TPU v7x, 32 devices: a whole 2x2x4 slice. The times are simulated.
32 devices in a mesh: dp: 8 (over y, x, core), mp: 4 (over z).
Axes of the slice: x: 2, y: 2, z: 4, core: 2. Of those that a mesh axis runs over, the one named last changes fastest.
Arguments:
- clean_patches: float32 [32, 12, 1024], P('dp'), may hold values from -1 to 1
- noise_patches: float32 [32, 12, 1024], P('dp'), may hold values from -6 to 6
- timesteps: int32 [32], P('dp'), may hold values from 0 to 999
- present_mask: int32 [32, 1024], P('dp'), may hold values from 0 to 1, as said below
- copy_widein: bfloat16 [1024, 10, 1024], P(None, None, 'mp'), may hold values from -0.1875 to 0.1875
- copy_narrowin: bfloat16 [512, 3, 1024], P(None, None, 'mp'), may hold values from -0.25 to 0.25
- copy_wideout: bfloat16 [6, 1024, 1024], P(None, 'mp')
- copy_narrowout: bfloat16 [1024, 512], P('mp'), may hold values from -1.5 to 1.5
- copy_latents: bfloat16 [128, 1024], replicated, may hold values from -3 to 3
- copy_gains: bfloat16 [11, 512], replicated, may hold values from 0.5 to 1.5
- copy_pixels: bfloat16 [2, 12, 512], replicated
- master_widein: float32 [1024, 10, 1024], P('dp', None, 'mp'), may hold values from -0.1875 to 0.1875
- first_widein: float32 [1024, 10, 1024], P('dp', None, 'mp'), may hold values from -1.8e-05 to 1.8e-05
- second_widein: float32 [1024, 10, 1024], P('dp', None, 'mp'), may hold values from 4.5e-12 to 7.2e-11
- master_narrowin: float32 [512, 3, 1024], P('dp', None, 'mp'), may hold values from -0.25 to 0.25
- first_narrowin: float32 [512, 3, 1024], P('dp', None, 'mp'), may hold values from -1.8e-05 to 1.8e-05
- second_narrowin: float32 [512, 3, 1024], P('dp', None, 'mp'), may hold values from 4.5e-12 to 7.2e-11
- master_wideout: float32 [6, 1024, 1024], P(None, 'mp', 'dp')
- first_wideout: float32 [6, 1024, 1024], P(None, 'mp', 'dp'), may hold values from -1.8e-05 to 1.8e-05
- second_wideout: float32 [6, 1024, 1024], P(None, 'mp', 'dp'), may hold values from 4.5e-12 to 7.2e-11
- master_narrowout: float32 [1024, 512], P('mp', 'dp'), may hold values from -1.5 to 1.5
- first_narrowout: float32 [1024, 512], P('mp', 'dp'), may hold values from -1.8e-05 to 1.8e-05
- second_narrowout: float32 [1024, 512], P('mp', 'dp'), may hold values from 4.5e-12 to 7.2e-11
- master_latents: float32 [128, 1024], P(None, 'dp'), may hold values from -3 to 3
- first_latents: float32 [128, 1024], P(None, 'dp'), may hold values from -1.7883438e-06 to 1.7883438e-06
- second_latents: float32 [128, 1024], P(None, 'dp'), may hold values from 8.8838144e-14 to 3.5535257e-13
- master_gains: float32 [11, 512], P(None, 'dp'), may hold values from 0.5 to 1.5
- first_gains: float32 [11, 512], P(None, 'dp'), may hold values from -6e-05 to 6e-05
- second_gains: float32 [11, 512], P(None, 'dp'), may hold values from 5e-11 to 8e-10
- master_pixels: float32 [2, 12, 512], P(None, None, 'dp')
- first_pixels: float32 [2, 12, 512], P(None, None, 'dp'), may hold values from -6e-05 to 6e-05
- second_pixels: float32 [2, 12, 512], P(None, None, 'dp'), may hold values from 5e-11 to 8e-10
Outputs:
- loss_value: float32 [], replicated
- grad_norm: float32 [], replicated
- updated_widein: float32 [1024, 10, 1024], P('dp', None, 'mp')
- moment_widein: float32 [1024, 10, 1024], P('dp', None, 'mp')
- square_widein: float32 [1024, 10, 1024], P('dp', None, 'mp')
- updated_narrowin: float32 [512, 3, 1024], P('dp', None, 'mp')
- moment_narrowin: float32 [512, 3, 1024], P('dp', None, 'mp')
- square_narrowin: float32 [512, 3, 1024], P('dp', None, 'mp')
- updated_wideout: float32 [6, 1024, 1024], P(None, 'mp', 'dp')
- moment_wideout: float32 [6, 1024, 1024], P(None, 'mp', 'dp')
- square_wideout: float32 [6, 1024, 1024], P(None, 'mp', 'dp')
- updated_narrowout: float32 [1024, 512], P('mp', 'dp')
- moment_narrowout: float32 [1024, 512], P('mp', 'dp')
- square_narrowout: float32 [1024, 512], P('mp', 'dp')
- updated_latents: float32 [128, 1024], P(None, 'dp')
- moment_latents: float32 [128, 1024], P(None, 'dp')
- square_latents: float32 [128, 1024], P(None, 'dp')
- updated_gains: float32 [11, 512], P(None, 'dp')
- moment_gains: float32 [11, 512], P(None, 'dp')
- square_gains: float32 [11, 512], P(None, 'dp')
- updated_pixels: float32 [2, 12, 512], P(None, None, 'dp')
- moment_pixels: float32 [2, 12, 512], P(None, None, 'dp')
- square_pixels: float32 [2, 12, 512], P(None, None, 'dp')
Inputs may be any that keep to these rules, and one draw needn't show every extreme that they name: `present_mask`: every image has at least one present patch.
All inputs are finite; a program needn't handle non-finite values.
Results may differ from a plain program's by a relative error of at most 0.0035.
Values sent between devices are 32-bit elements; how exact they have to be, the bound alone decides.
A program may use at most 256 MiB of HBM per device.

v0:
```python
from functools import partial
import math

import jax
import jax.numpy as jnp
from jax import lax
from jax.sharding import PartitionSpec as P

HEAD_DIM = 64
PIX = 12
NSTEPS = 1000
STEP = 10


precise = lax.Precision.HIGHEST
clip_level = 0.01
learning_rate = 0.05
weight_decay = 0.1
adam_beta = 0.5
adam_eps = 1e-08


def layer_norm(values, gain):
    centered = values - jnp.mean(values, -1, keepdims=True)
    scale = lax.rsqrt(jnp.mean(centered * centered, -1, keepdims=True) + 1e-05)
    normed = centered * scale
    return (normed * gain, (normed, scale))


def norm_back(upstream, gain, stats):
    normed, scale = stats
    inner = upstream * gain
    values = scale * (
        inner
        - jnp.mean(inner, -1, keepdims=True)
        - normed * jnp.mean(inner * normed, -1, keepdims=True)
    )
    gain_grad = jnp.sum((upstream * normed).reshape(-1, normed.shape[-1]), 0)
    return (values, gain_grad)


def positions(count, width):
    place = jnp.arange(count, dtype=jnp.float32)[:, None]
    index = jnp.arange(width // 2, dtype=jnp.float32)[None, :]
    angle = place * jnp.exp(-math.log(10000.0) * 2.0 * index / width)
    return jnp.concatenate([jnp.sin(angle), jnp.cos(angle)], -1)


def split_heads(values):
    return values.reshape(values.shape[:-1] + (values.shape[-1] // HEAD_DIM, HEAD_DIM))


def attend_scores(queries, keys, keep_mask):
    scores = jnp.einsum(
        "bqhe,bkhe->bhqk",
        split_heads(queries),
        split_heads(keys),
        preferred_element_type=jnp.float32,
    ) * HEAD_DIM ** (-0.5)
    if keep_mask is not None:
        scores = jnp.where(keep_mask[:, None, None, :] > 0, scores, -1e30)
    return scores


def attend_forward(queries, keys, values, keep_mask):
    scores = attend_scores(queries, keys, keep_mask)
    top = jnp.max(scores, -1, keepdims=True)
    log_total = top + jnp.log(jnp.sum(jnp.exp(scores - top), -1, keepdims=True))
    probs = jnp.exp(scores - log_total).astype(jnp.bfloat16)
    output = jnp.einsum(
        "bhqk,bkhe->bqhe", probs, split_heads(values), preferred_element_type=jnp.float32
    )
    return (output.reshape(queries.shape).astype(jnp.bfloat16), log_total)


def attend_back(queries, keys, values, keep_mask, log_total, upstream):
    scores = attend_scores(queries, keys, keep_mask)
    probs = jnp.exp(scores - log_total)
    value_grad = jnp.einsum(
        "bhqk,bqhe->bkhe",
        probs.astype(jnp.bfloat16),
        split_heads(upstream),
        preferred_element_type=jnp.float32,
    )
    prob_grad = jnp.einsum(
        "bqhe,bkhe->bhqk",
        split_heads(upstream),
        split_heads(values),
        preferred_element_type=jnp.float32,
    )
    score_grad = (probs * (prob_grad - jnp.sum(prob_grad * probs, -1, keepdims=True))).astype(
        jnp.bfloat16
    )
    query_grad = jnp.einsum(
        "bhqk,bkhe->bqhe", score_grad, split_heads(keys), preferred_element_type=jnp.float32
    ) * HEAD_DIM ** (-0.5)
    key_grad = jnp.einsum(
        "bhqk,bqhe->bkhe", score_grad, split_heads(queries), preferred_element_type=jnp.float32
    ) * HEAD_DIM ** (-0.5)
    return (
        query_grad.reshape(queries.shape).astype(jnp.bfloat16),
        key_grad.reshape(keys.shape).astype(jnp.bfloat16),
        value_grad.reshape(values.shape).astype(jnp.bfloat16),
    )


def latent_mix(partial_sum):
    return lax.psum(partial_sum, "mp")


def latent_return(latent_part, gain_part):
    return lax.psum((latent_part, gain_part), "mp")


def adam_update(master, first, second, gradient, scale):
    clipped = gradient * scale
    moment = adam_beta * first + (1.0 - adam_beta) * clipped
    square = adam_beta * second + (1.0 - adam_beta) * clipped * clipped
    fixed_first = moment / (1.0 - adam_beta**STEP)
    fixed_second = square / (1.0 - adam_beta**STEP)
    updated = master - learning_rate * (
        fixed_first / (jnp.sqrt(fixed_second) + adam_eps) + weight_decay * master
    )
    return (updated, moment, square)


def body(
    clean_patches,
    noise_patches,
    timesteps,
    present_mask,
    copy_widein,
    copy_narrowin,
    copy_wideout,
    copy_narrowout,
    copy_latents,
    copy_gains,
    copy_pixels,
    master_widein,
    first_widein,
    second_widein,
    master_narrowin,
    first_narrowin,
    second_narrowin,
    master_wideout,
    first_wideout,
    second_wideout,
    master_narrowout,
    first_narrowout,
    second_narrowout,
    master_latents,
    first_latents,
    second_latents,
    master_gains,
    first_gains,
    second_gains,
    master_pixels,
    first_pixels,
    second_pixels,
):
    images = clean_patches.shape[0]
    signal = jnp.cos(0.5 * math.pi * (timesteps.astype(jnp.float32) + 0.5) / NSTEPS) ** 2
    noisy = (
        jnp.sqrt(signal)[:, None, None] * clean_patches
        + jnp.sqrt(1.0 - signal)[:, None, None] * noise_patches
    )
    loss_weight = 0.5 + signal
    keep_float = present_mask.astype(jnp.float32)
    weight_total = lax.psum(jnp.sum(loss_weight * PIX * jnp.sum(keep_float, 1)), "dp")
    gain_rows = copy_gains.astype(jnp.float32)

    def wide_gain(index):
        return gain_rows[2 * index : 2 * index + 2].reshape(-1)

    pixel_rows = copy_pixels.astype(jnp.float32)
    interface = jnp.einsum("bcp,cd->bpd", noisy, pixel_rows[0], precision=precise) + positions(
        noisy.shape[2], pixel_rows.shape[2]
    )
    latent_zero = jnp.broadcast_to(
        copy_latents.astype(jnp.float32)[None], (images,) + copy_latents.shape
    )
    read_norm, read_stats = layer_norm(latent_zero, wide_gain(0))
    read_low = read_norm.astype(jnp.bfloat16)
    side_norm, side_stats = layer_norm(interface, gain_rows[8])
    side_low = side_norm.astype(jnp.bfloat16)
    read_query = jnp.einsum(
        "bld,dc->blc", read_low, copy_widein[:, 0], preferred_element_type=jnp.float32
    ).astype(jnp.bfloat16)
    read_pairs = jnp.einsum(
        "bpd,dsc->bpsc", side_low, copy_narrowin[:, 0:2], preferred_element_type=jnp.float32
    ).astype(jnp.bfloat16)
    read_out, read_total = attend_forward(
        read_query, read_pairs[:, :, 0], read_pairs[:, :, 1], present_mask
    )
    latent_one = latent_zero + latent_mix(
        jnp.einsum("blc,cd->bld", read_out, copy_wideout[0], preferred_element_type=jnp.float32)
    )
    self_norm, self_stats = layer_norm(latent_one, wide_gain(1))
    self_low = self_norm.astype(jnp.bfloat16)
    self_triple = jnp.einsum(
        "bld,dsc->blsc", self_low, copy_widein[:, 1:4], preferred_element_type=jnp.float32
    ).astype(jnp.bfloat16)
    self_out, self_total = attend_forward(
        self_triple[:, :, 0], self_triple[:, :, 1], self_triple[:, :, 2], None
    )
    latent_two = latent_one + latent_mix(
        jnp.einsum("blc,cd->bld", self_out, copy_wideout[1], preferred_element_type=jnp.float32)
    )
    feed_norm, feed_stats = layer_norm(latent_two, wide_gain(2))
    feed_low = feed_norm.astype(jnp.bfloat16)
    hidden = jnp.einsum(
        "bld,dsc->blsc", feed_low, copy_widein[:, 4:8], preferred_element_type=jnp.float32
    )
    active, gelu_pull = jax.vjp(partial(jax.nn.gelu, approximate=False), hidden)
    active_low = active.astype(jnp.bfloat16)
    latent_three = latent_two + latent_mix(
        jnp.einsum(
            "blsc,scd->bld", active_low, copy_wideout[2:6], preferred_element_type=jnp.float32
        )
    )
    write_norm, write_stats = layer_norm(latent_three, wide_gain(3))
    write_low = write_norm.astype(jnp.bfloat16)
    outer_norm, outer_stats = layer_norm(interface, gain_rows[9])
    outer_low = outer_norm.astype(jnp.bfloat16)
    write_query = jnp.einsum(
        "bpd,dc->bpc", outer_low, copy_narrowin[:, 2], preferred_element_type=jnp.float32
    ).astype(jnp.bfloat16)
    write_pairs = jnp.einsum(
        "bld,dsc->blsc", write_low, copy_widein[:, 8:10], preferred_element_type=jnp.float32
    ).astype(jnp.bfloat16)
    write_out, write_total = attend_forward(
        write_query, write_pairs[:, :, 0], write_pairs[:, :, 1], None
    )
    outer = interface + lax.psum(
        jnp.einsum("bpc,cd->bpd", write_out, copy_narrowout, preferred_element_type=jnp.float32),
        "mp",
    )
    final_norm, final_stats = layer_norm(outer, gain_rows[10])
    final_low = final_norm.astype(jnp.bfloat16)
    predicted = jnp.einsum(
        "bpd,cd->bcp", final_low, copy_pixels[1], preferred_element_type=jnp.float32
    )
    difference = predicted - noise_patches
    masked = loss_weight[:, None, None] * keep_float[:, None, :] * difference
    loss_local = jnp.sum(masked * difference)
    predict_grad = (2.0 * masked / weight_total).astype(jnp.bfloat16)
    head_grad = jnp.einsum(
        "bcp,bpd->cd", predict_grad, final_low, preferred_element_type=jnp.float32
    )
    final_grad = jnp.einsum(
        "bcp,cd->bpd", predict_grad, copy_pixels[1], preferred_element_type=jnp.float32
    )
    outer_grad, gain_final = norm_back(final_grad, gain_rows[10], final_stats)
    branch_low = outer_grad.astype(jnp.bfloat16)
    narrowout_grad = jnp.einsum(
        "bpc,bpd->cd", write_out, branch_low, preferred_element_type=jnp.float32
    )
    write_upstream = jnp.einsum(
        "bpd,cd->bpc", branch_low, copy_narrowout, preferred_element_type=jnp.float32
    ).astype(jnp.bfloat16)
    query_grad, key_grad, value_grad = attend_back(
        write_query, write_pairs[:, :, 0], write_pairs[:, :, 1], None, write_total, write_upstream
    )
    write_query_grad = jnp.einsum(
        "bpd,bpc->dc", outer_low, query_grad, preferred_element_type=jnp.float32
    )
    outer_part = jnp.einsum(
        "bpc,dc->bpd", query_grad, copy_narrowin[:, 2], preferred_element_type=jnp.float32
    )
    pair_grad = jnp.stack([key_grad, value_grad], 2)
    write_pair_grad = jnp.einsum(
        "bld,blsc->dsc", write_low, pair_grad, preferred_element_type=jnp.float32
    )
    write_part = jnp.einsum(
        "blsc,dsc->bld", pair_grad, copy_widein[:, 8:10], preferred_element_type=jnp.float32
    )
    latent_part, gain_part = norm_back(write_part, wide_gain(3), write_stats)
    latent_grad, gain_write = latent_return(latent_part, gain_part)
    outer_back, gain_outer_part = norm_back(outer_part, gain_rows[9], outer_stats)
    branch_low = latent_grad.astype(jnp.bfloat16)
    down_grad = jnp.einsum(
        "blsc,bld->scd", active_low, branch_low, preferred_element_type=jnp.float32
    )
    active_grad = jnp.einsum(
        "bld,scd->blsc", branch_low, copy_wideout[2:6], preferred_element_type=jnp.float32
    )
    hidden_grad = gelu_pull(active_grad)[0].astype(jnp.bfloat16)
    up_grad = jnp.einsum("bld,blsc->dsc", feed_low, hidden_grad, preferred_element_type=jnp.float32)
    feed_part = jnp.einsum(
        "blsc,dsc->bld", hidden_grad, copy_widein[:, 4:8], preferred_element_type=jnp.float32
    )
    latent_part, gain_part = norm_back(feed_part, wide_gain(2), feed_stats)
    returned, gain_feed = latent_return(latent_part, gain_part)
    latent_grad = latent_grad + returned
    branch_low = latent_grad.astype(jnp.bfloat16)
    self_out_grad = jnp.einsum(
        "blc,bld->cd", self_out, branch_low, preferred_element_type=jnp.float32
    )
    self_upstream = jnp.einsum(
        "bld,cd->blc", branch_low, copy_wideout[1], preferred_element_type=jnp.float32
    ).astype(jnp.bfloat16)
    query_grad, key_grad, value_grad = attend_back(
        self_triple[:, :, 0],
        self_triple[:, :, 1],
        self_triple[:, :, 2],
        None,
        self_total,
        self_upstream,
    )
    triple_grad = jnp.stack([query_grad, key_grad, value_grad], 2)
    self_in_grad = jnp.einsum(
        "bld,blsc->dsc", self_low, triple_grad, preferred_element_type=jnp.float32
    )
    self_part = jnp.einsum(
        "blsc,dsc->bld", triple_grad, copy_widein[:, 1:4], preferred_element_type=jnp.float32
    )
    latent_part, gain_part = norm_back(self_part, wide_gain(1), self_stats)
    returned, gain_self = latent_return(latent_part, gain_part)
    latent_grad = latent_grad + returned
    branch_low = latent_grad.astype(jnp.bfloat16)
    read_out_grad = jnp.einsum(
        "blc,bld->cd", read_out, branch_low, preferred_element_type=jnp.float32
    )
    read_upstream = jnp.einsum(
        "bld,cd->blc", branch_low, copy_wideout[0], preferred_element_type=jnp.float32
    ).astype(jnp.bfloat16)
    query_grad, key_grad, value_grad = attend_back(
        read_query,
        read_pairs[:, :, 0],
        read_pairs[:, :, 1],
        present_mask,
        read_total,
        read_upstream,
    )
    read_query_grad = jnp.einsum(
        "bld,blc->dc", read_low, query_grad, preferred_element_type=jnp.float32
    )
    read_part = jnp.einsum(
        "blc,dc->bld", query_grad, copy_widein[:, 0], preferred_element_type=jnp.float32
    )
    latent_part, gain_part = norm_back(read_part, wide_gain(0), read_stats)
    returned, gain_read = latent_return(latent_part, gain_part)
    latent_total = jnp.sum(latent_grad + returned, 0)
    pair_grad = jnp.stack([key_grad, value_grad], 2)
    read_pair_grad = jnp.einsum(
        "bpd,bpsc->dsc", side_low, pair_grad, preferred_element_type=jnp.float32
    )
    side_part = jnp.einsum(
        "bpsc,dsc->bpd", pair_grad, copy_narrowin[:, 0:2], preferred_element_type=jnp.float32
    )
    side_back, gain_side_part = norm_back(side_part, gain_rows[8], side_stats)
    interface_part, gain_outer, gain_side = lax.psum(
        (outer_back + side_back, gain_outer_part, gain_side_part), "mp"
    )
    embed_grad = jnp.einsum("bcp,bpd->cd", noisy, outer_grad + interface_part, precision=precise)
    widein_grad = jnp.concatenate(
        [read_query_grad[:, None], self_in_grad, up_grad, write_pair_grad], 1
    )
    narrowin_grad = jnp.concatenate([read_pair_grad, write_query_grad[:, None]], 1)
    wideout_grad = jnp.concatenate([read_out_grad[None], self_out_grad[None], down_grad], 0)
    gains_grad = jnp.concatenate(
        [
            gain_read.reshape(2, -1),
            gain_self.reshape(2, -1),
            gain_feed.reshape(2, -1),
            gain_write.reshape(2, -1),
            gain_side[None],
            gain_outer[None],
            gain_final[None],
        ],
        0,
    )
    pixels_grad = jnp.stack([embed_grad, head_grad], 0)
    shares = (
        lax.psum_scatter(widein_grad, "dp", scatter_dimension=0, tiled=True),
        lax.psum_scatter(narrowin_grad, "dp", scatter_dimension=0, tiled=True),
        lax.psum_scatter(wideout_grad, "dp", scatter_dimension=2, tiled=True),
        lax.psum_scatter(narrowout_grad, "dp", scatter_dimension=1, tiled=True),
        lax.psum_scatter(latent_total, "dp", scatter_dimension=1, tiled=True),
        lax.psum_scatter(gains_grad, "dp", scatter_dimension=1, tiled=True),
        lax.psum_scatter(pixels_grad, "dp", scatter_dimension=2, tiled=True),
    )
    leading = (lax.axis_index("mp") == 0).astype(jnp.float32)
    split_square = sum((jnp.sum(item * item) for item in shares[:4]))
    copied_square = sum((jnp.sum(item * item) for item in shares[4:]))
    square_total, loss_total = lax.psum(
        (split_square + leading * copied_square, leading * loss_local), ("dp", "mp")
    )
    grad_norm = jnp.sqrt(square_total)
    loss_value = loss_total / weight_total
    scale = clip_level / jnp.maximum(grad_norm, clip_level)
    states = (
        (master_widein, first_widein, second_widein),
        (master_narrowin, first_narrowin, second_narrowin),
        (master_wideout, first_wideout, second_wideout),
        (master_narrowout, first_narrowout, second_narrowout),
        (master_latents, first_latents, second_latents),
        (master_gains, first_gains, second_gains),
        (master_pixels, first_pixels, second_pixels),
    )
    results = []
    for state, gradient in zip(states, shares):
        results.extend(adam_update(state[0], state[1], state[2], gradient, scale))
    return (
        loss_value,
        grad_norm,
        results[0],
        results[1],
        results[2],
        results[3],
        results[4],
        results[5],
        results[6],
        results[7],
        results[8],
        results[9],
        results[10],
        results[11],
        results[12],
        results[13],
        results[14],
        results[15],
        results[16],
        results[17],
        results[18],
        results[19],
        results[20],
    )


def solution(mesh):
    in_specs = (
        P("dp", None, None),
        P("dp", None, None),
        P("dp"),
        P("dp", None),
        P(None, None, "mp"),
        P(None, None, "mp"),
        P(None, "mp", None),
        P("mp", None),
        P(),
        P(),
        P(),
        P("dp", None, "mp"),
        P("dp", None, "mp"),
        P("dp", None, "mp"),
        P("dp", None, "mp"),
        P("dp", None, "mp"),
        P("dp", None, "mp"),
        P(None, "mp", "dp"),
        P(None, "mp", "dp"),
        P(None, "mp", "dp"),
        P("mp", "dp"),
        P("mp", "dp"),
        P("mp", "dp"),
        P(None, "dp"),
        P(None, "dp"),
        P(None, "dp"),
        P(None, "dp"),
        P(None, "dp"),
        P(None, "dp"),
        P(None, None, "dp"),
        P(None, None, "dp"),
        P(None, None, "dp"),
    )
    out_specs = (
        P(),
        P(),
        P("dp", None, "mp"),
        P("dp", None, "mp"),
        P("dp", None, "mp"),
        P("dp", None, "mp"),
        P("dp", None, "mp"),
        P("dp", None, "mp"),
        P(None, "mp", "dp"),
        P(None, "mp", "dp"),
        P(None, "mp", "dp"),
        P("mp", "dp"),
        P("mp", "dp"),
        P("mp", "dp"),
        P(None, "dp"),
        P(None, "dp"),
        P(None, "dp"),
        P(None, "dp"),
        P(None, "dp"),
        P(None, "dp"),
        P(None, None, "dp"),
        P(None, None, "dp"),
        P(None, None, "dp"),
    )
    return jax.shard_map(body, mesh=mesh, in_specs=in_specs, out_specs=out_specs, check_vma=False)
```

profile of v0, /device:TPU:0, one launch (start us, length us, event | category | flops | bytes accessed | tf_op | source)
XLA Modules:
  0.0 1829.3 jit_solution(12102948035297369412)
XLA Ops:
  17.9 3.7 fusion.104
  22.8 5.1 add_reduce_fusion
  31.1 3.5 fusion.16
  45.6 89.3 %all-reduce.12.cloned.1.call-done = f32[4,128,1024]{2,1,0:T(8,128)} async-done(((f32[4,128,1024]{2,1,0:T(8,128)}), f32[4,128,1024]{2,1,0:T(8,128)}) %all-reduce.12.cloned.1.call-update) | async-done | bytes 2097168 | tf_op jit(solution)/shard_map/psum | solution.py:108
  148.3 85.5 %all-reduce.14.cloned.1.call-done = f32[4,128,1024]{2,1,0:T(8,128)} async-done(((f32[4,128,1024]{2,1,0:T(8,128)}), f32[4,128,1024]{2,1,0:T(8,128)}) %all-reduce.14.cloned.1.call-update) | async-done | bytes 2097168 | tf_op jit(solution)/shard_map/psum | solution.py:108
  236.9 3.8 fusion.129
  240.7 6.1 multiply_convert_fusion.8
  250.5 6.6 convolution_convert_fusion
  257.1 79.0 %all-reduce.16.cloned.1.call-done = f32[4,128,1024]{2,1,0:T(8,128)} async-done(((f32[4,128,1024]{2,1,0:T(8,128)}), f32[4,128,1024]{2,1,0:T(8,128)}) %all-reduce.16.cloned.1.call-update) | async-done | bytes 2097168 | tf_op jit(solution)/shard_map/psum | solution.py:108
  355.0 4.8 fusion.148
  359.9 14.9 psum.131
  375.5 274.2 %all-reduce.18.cloned.1.call-done = f32[4,1024,512]{1,2,0:T(8,128)} async-done(((f32[4,1024,512]{1,2,0:T(8,128)}), f32[4,1024,512]{1,2,0:T(8,128)}) %all-reduce.18.cloned.1.call-update) | async-done | bytes 8388624 | tf_op jit(solution)/shard_map/psum | solution.py:234
  649.8 12.1 fusion.191
  661.9 4.7 multiply_reduce_fusion.7
  671.3 6.3 multiply_reduce_fusion.2
  677.6 4.8 subtract_multiply_fusion
  688.1 5.3 multiply_reduce_fusion.5
  695.2 7.2 multiply_convert_fusion.1
  710.7 85.6 %all-reduce.20.cloned.1.call-done = f32[4,128,1024]{2,1,0:T(8,128)} async-done(((f32[4,128,1024]{2,1,0:T(8,128)}), f32[4,128,1024]{2,1,0:T(8,128)}) %all-reduce.20.cloned.1.call-update) | async-done | bytes 2097168 | tf_op jit(solution)/shard_map/psum | solution.py:112
  796.3 5.4 add_convert_fusion
  801.8 3.6 fusion.27
  807.8 85.2 %all-reduce.22.cloned.1.call-done = f32[4,128,1024]{2,1,0:T(8,128)} async-done(((f32[4,128,1024]{2,1,0:T(8,128)}), f32[4,128,1024]{2,1,0:T(8,128)}) %all-reduce.22.cloned.1.call-update) | async-done | bytes 2097168 | tf_op jit(solution)/shard_map/psum | solution.py:112
  908.7 3.7 fusion.26
  919.7 5.4 fusion.144
  925.1 75.0 %all-reduce.24.cloned.1.call-done = f32[4,128,1024]{2,1,0:T(8,128)} async-done(((f32[4,128,1024]{2,1,0:T(8,128)}), f32[4,128,1024]{2,1,0:T(8,128)}) %all-reduce.24.cloned.1.call-update) | async-done | bytes 2097168 | tf_op jit(solution)/shard_map/psum | solution.py:112
  1005.8 7.0 convolution_convert_fusion.1
  1012.8 5.7 multiply_reduce_fusion.4
  1024.5 4.0 copy.232
  1028.5 4.0 copy.231
  1034.9 12.0 multiply_reduce_fusion
  1048.8 9.9 add_multiply_fusion
  1059.0 6.1 fusion.74
  1065.1 5.5 convolution_bitcast_fusion.7
  1070.7 21.0 %all-reduce.1 = (f32[2,512]{1,0:T(2,128)S(1)}, f32[2,512]{1,0:T(2,128)S(1)}, f32[2,512]{1,0:T(2,128)S(1)}, f32[2,512]{1,0:T(2,128)S(1)}, f32[1,512]{1,0:T(1,128)S(1)}, /*index=5*/f32[1,512]{1,0:T(1,128)S(1)}) all-reduce(f32[2,512]{1,0:T(2,128)S(1)} %reshape.375, f32[2,512]{1,0:T(2,128)S(1)} %reshape.376, ...), channel_id=1, replica_groups=mesh['dp'=8,'mp'=4] {'mp'}, use_global_device_ids=true, to_apply=%region_56.57 | all-reduce | flops 5120 | bytes 40960 | tf_op jit(solution)/shard_map/psum | solution.py:112
  1092.6 8.0 fusion.68
  1108.7 3.7 pad_maximum_fusion.1
  1122.6 295.3 %all-reduce.26.cloned.1.call-done = (f32[4,128,1024]{2,1,0:T(8,128)}, f32[4,1024,512]{1,2,0:T(8,128)}) async-done(((f32[4,128,1024]{2,1,0:T(8,128)}, f32[4,1024,512]{1,2,0:T(8,128)}), (f32[4,128,1024]{2,1,0:T(8,128)}, f32[4,1024,512]{1,2,0:T(8,128)})) %all-reduce.26.cloned.1.call-update) | async-done | bytes 10485776 | tf_op jit(solution)/shard_map/psum | solution.py:112
  1418.0 10.2 fusion.84
  1429.6 3.7 add_reduce_fusion.1
  1437.5 4.3 pad_maximum_fusion
  1442.6 12.2 reduce-scatter.18.cloned.1.call-done
  1456.3 35.2 %reduce-scatter.22.cloned.1.call-done = f32[64,11]{1,0:T(8,128)} async-done(((f32[512,11]{1,0:T(8,128)}), f32[64,11]{1,0:T(8,128)}) %reduce-scatter.22.cloned.1.call-update) | async-done | bytes 2832
  1493.0 40.4 %reduce-scatter.14.cloned.1.call-done = f32[64,3,256]{2,0,1:T(8,128)} async-done(((f32[512,3,256]{2,0,1:T(8,128)}), f32[64,3,256]{2,0,1:T(8,128)}) %reduce-scatter.14.cloned.1.call-update) | async-done | bytes 196624 | tf_op jit(solution)/shard_map/reduce_scatter | solution.py:376
  1535.0 63.3 %reduce-scatter.16.cloned.1.call-done = f32[6,256,128]{2,1,0:T(8,128)} async-done(((f32[6,256,1024]{2,1,0:T(8,128)}), f32[6,256,128]{2,1,0:T(8,128)}) %reduce-scatter.16.cloned.1.call-update) | async-done | bytes 786448 | tf_op jit(solution)/shard_map/reduce_scatter | solution.py:377
  1600.3 35.6 %reduce-scatter.24.cloned.1.call-done = f32[64,24]{1,0:T(8,128)} async-done(((f32[512,24]{1,0:T(8,128)}), f32[64,24]{1,0:T(8,128)}) %reduce-scatter.24.cloned.1.call-update) | async-done | bytes 6160
  1637.4 36.1 %reduce-scatter.20.cloned.1.call-done = f32[128,128]{1,0:T(8,128)} async-done(((f32[128,1024]{1,0:T(8,128)}), f32[128,128]{1,0:T(8,128)}) %reduce-scatter.20.cloned.1.call-update) | async-done | bytes 65552 | tf_op jit(solution)/shard_map/reduce_scatter | solution.py:379
  1676.9 81.9 %reduce-scatter.12.cloned.1.call-done = f32[128,10,256]{2,0,1:T(8,128)} async-done(((f32[1024,10,256]{2,0,1:T(8,128)}), f32[128,10,256]{2,0,1:T(8,128)}) %reduce-scatter.12.cloned.1.call-update) | async-done | bytes 1310736 | tf_op jit(solution)/shard_map/reduce_scatter | solution.py:375
  1763.7 39.7 %all-reduce = (f32[]{:T(128)}, f32[]{:T(128)}) all-reduce(f32[]{:T(128)S(6)} %mul.780, f32[]{:T(128)S(6)} %add.318), channel_id=1, replica_groups=mesh['dp'=8,'mp'=4] {'dp','mp'}, use_global_device_ids=true, to_apply=%region_23.24 | all-reduce | flops 2 | bytes 16 | tf_op jit(solution)/shard_map/psum | solution.py:386
  (430 shorter events, 177.5 us)
Async XLA Ops:
  7.2 347.8 %copy-start = (bf16[256,512]{1,0:T(8,128)(2,1)S(1)}, bf16[256,512]{1,0:T(8,128)(2,1)}, u32[]{:S(2)}) copy-start(bf16[256,512]{1,0:T(8,128)(2,1)} %param.39) | copy-start | bytes 786436
  7.2 127.7 %all-reduce.12.cloned.1.call-start = ((), (), s32[]{:S(2)}) async-start(), calls=%async_computation.7 | async-start | bytes 4194304 | tf_op jit(solution)/shard_map/psum | solution.py:108
  9.7 19.6 %copy-start.82 = (f32[1,512]{1,0:T(1,128)}, f32[1,512]{1,0:T(1,128)S(1)}, u32[]{:S(2)}) copy-start(f32[1,512]{1,0:T(1,128)S(1)} %get-tuple-element.174) | copy-start | bytes 6148
  9.7 240.8 %copy-start.110 = (f32[1,512]{1,0:T(1,128)}, f32[1,512]{1,0:T(1,128)S(1)}, u32[]{:S(2)}) copy-start(f32[1,512]{1,0:T(1,128)S(1)} %get-tuple-element.173) | copy-start | bytes 6148
  12.5 125.1 %copy-start.20 = (f32[128,1024]{1,0:T(8,128)}, f32[128,1024]{1,0:T(8,128)S(1)}, u32[]{:S(2)}) copy-start(f32[128,1024]{1,0:T(8,128)S(1)} %convert_element_type.268) | copy-start | bytes 1572868
  17.9 17.3 copy-start.36
  45.6 188.3 %all-reduce.14.cloned.1.call-start = ((), (), s32[]{:S(2)}) async-start(), calls=%async_computation.8 | async-start | bytes 4194304 | tf_op jit(solution)/shard_map/psum | solution.py:108
  45.6 92.0 %copy-start.92 = (f32[1,4,2,128]{3,1,2,0:T(4,128)}, f32[1,4,2,128]{3,1,2,0:T(4,128)S(1)}, u32[]{:S(2)}) copy-start(f32[1,4,2,128]{3,1,2,0:T(4,128)S(1)} %copy.310) | copy-start | bytes 12292
  148.3 187.8 %all-reduce.16.cloned.1.call-start = ((), (), s32[]{:S(2)}) async-start(), calls=%async_computation.9 | async-start | bytes 4194304 | tf_op jit(solution)/shard_map/psum | solution.py:108
  148.3 88.6 %copy-start.94 = (f32[1,4,2,128]{3,1,2,0:T(4,128)}, f32[1,4,2,128]{3,1,2,0:T(4,128)S(1)}, u32[]{:S(2)}) copy-start(f32[1,4,2,128]{3,1,2,0:T(4,128)S(1)} %copy.311) | copy-start | bytes 12292
  240.7 6.1 copy-start.51
  240.7 7.1 copy-start.54
  250.4 399.4 %all-reduce.18.cloned.1.call-start = ((), (), s32[]{:S(2)}) async-start(), calls=%async_computation.10 | async-start | bytes 16777216 | tf_op jit(solution)/shard_map/psum | solution.py:234
  250.5 88.5 %copy-start.96 = (f32[1,4,2,128]{3,1,2,0:T(4,128)}, f32[1,4,2,128]{3,1,2,0:T(4,128)S(1)}, u32[]{:S(2)}) copy-start(f32[1,4,2,128]{3,1,2,0:T(4,128)S(1)} %copy.312) | copy-start | bytes 12292
  359.8 15.0 copy-start.78
  359.8 436.5 %all-reduce.20.cloned.1.call-start = ((), (), s32[]{:S(2)}) async-start(), calls=%async_computation.11 | async-start | bytes 4194304 | tf_op jit(solution)/shard_map/psum | solution.py:112
  671.3 6.3 copy-start.34
  671.3 14.4 slice-start
  677.6 8.1 slice-start.1
  695.2 7.2 copy-start.31
  710.6 182.4 %all-reduce.22.cloned.1.call-start = ((), (), s32[]{:S(2)}) async-start(), calls=%async_computation.12 | async-start | bytes 4194304 | tf_op jit(solution)/shard_map/psum | solution.py:112
  807.4 192.8 %all-reduce.24.cloned.1.call-start = ((), (), s32[]{:S(2)}) async-start(), calls=%async_computation.13 | async-start | bytes 4194304 | tf_op jit(solution)/shard_map/psum | solution.py:112
  897.0 6.2 copy-start.44
  914.6 503.4 %all-reduce.26.cloned.1.call-start = ((), (), s32[]{:S(2)}) async-start(), calls=%async_computation.21 | async-start | bytes 20971520 | tf_op jit(solution)/shard_map/psum | solution.py:112
  1005.8 7.0 copy-start.29
  1005.8 12.7 slice-start.2
  1022.4 10.0 copy-start.68
  1032.5 16.3 slice-start.4
  1034.9 13.9 slice-start.5
  1058.7 396.1 %reduce-scatter.18.cloned.1.call-start = ((), (), s32[]{:S(2)}) async-start(), calls=%async_computation.17 | async-start | bytes 589824 | tf_op jit(solution)/shard_map/reduce_scatter | solution.py:378
  1070.6 420.9 %reduce-scatter.22.cloned.1.call-start = ((), (), s32[]{:S(2)}) async-start(), calls=%async_computation.19 | async-start | bytes 294912
  1100.6 432.7 %reduce-scatter.14.cloned.1.call-start = ((), (), s32[]{:S(2)}) async-start(), calls=%async_computation.15 | async-start | bytes 1769472 | tf_op jit(solution)/shard_map/reduce_scatter | solution.py:376
  1103.2 495.1 %reduce-scatter.16.cloned.1.call-start = ((), (), s32[]{:S(2)}) async-start(), calls=%async_computation.16 | async-start | bytes 7077888 | tf_op jit(solution)/shard_map/reduce_scatter | solution.py:377
  1112.5 523.4 %reduce-scatter.24.cloned.1.call-start = ((), (), s32[]{:S(2)}) async-start(), calls=%async_computation.20 | async-start | bytes 294912
  1119.2 298.8 %copy-start.40 = (f32[4,12,1024]{2,0,1:T(4,128)S(1)}, f32[4,12,1024]{2,0,1:T(4,128)}, u32[]{:S(2)}) copy-start(f32[4,12,1024]{2,0,1:T(4,128)} %copy-done.39) | copy-start | bytes 589828
  1429.5 244.0 %reduce-scatter.20.cloned.1.call-start = ((), (), s32[]{:S(2)}) async-start(), calls=%async_computation.18 | async-start | bytes 589824 | tf_op jit(solution)/shard_map/reduce_scatter | solution.py:379
  1433.4 325.5 %reduce-scatter.12.cloned.1.call-start = ((), (), s32[]{:S(2)}) async-start(), calls=%async_computation.14 | async-start | bytes 11796480 | tf_op jit(solution)/shard_map/reduce_scatter | solution.py:375
  1441.8 363.7 %copy-start.98 = (f32[2,12,64]{2,0,1:T(2,128)S(1)}, f32[2,12,64]{2,0,1:T(2,128)}, u32[]{:S(2)}) copy-start(f32[2,12,64]{2,0,1:T(2,128)} %param.61) | copy-start | bytes 18436
  1441.8 363.7 %copy-start.99 = (f32[2,12,64]{2,0,1:T(2,128)S(1)}, f32[2,12,64]{2,0,1:T(2,128)}, u32[]{:S(2)}) copy-start(f32[2,12,64]{2,0,1:T(2,128)} %param.62) | copy-start | bytes 18436
  1441.9 363.7 %copy-start.100 = (f32[2,12,64]{2,0,1:T(2,128)S(1)}, f32[2,12,64]{2,0,1:T(2,128)}, u32[]{:S(2)}) copy-start(f32[2,12,64]{2,0,1:T(2,128)} %param.63) | copy-start | bytes 18436
  1441.9 365.5 %copy-start.112 = (f32[11,64]{1,0:T(8,128)S(1)}, f32[11,64]{1,0:T(8,128)}, u32[]{:S(2)}) copy-start(f32[11,64]{1,0:T(8,128)} %param.58) | copy-start | bytes 8452
  1441.9 365.5 %copy-start.113 = (f32[11,64]{1,0:T(8,128)S(1)}, f32[11,64]{1,0:T(8,128)}, u32[]{:S(2)}) copy-start(f32[11,64]{1,0:T(8,128)} %param.59) | copy-start | bytes 8452
  1454.8 355.6 %copy-start.76 = (f32[256,64]{0,1:T(8,128)S(1)}, f32[256,64]{0,1:T(8,128)}, u32[]{:S(2)}) copy-start(f32[256,64]{0,1:T(8,128)} %reduce-scatter.18.cloned.1.call-done) | copy-start | bytes 196612
  1533.4 278.6 %copy-start.64 = (f32[64,3,256]{2,0,1:T(8,128)S(1)}, f32[64,3,256]{2,0,1:T(8,128)}, u32[]{:S(2)}) copy-start(f32[64,3,256]{2,0,1:T(8,128)} %reduce-scatter.14.cloned.1.call-done) | copy-start | bytes 589828
  1600.3 213.7 %copy-start.38 = (f32[6,256,128]{2,1,0:T(8,128)S(1)}, f32[6,256,128]{2,1,0:T(8,128)}, u32[]{:S(2)}) copy-start(f32[6,256,128]{2,1,0:T(8,128)} %reduce-scatter.16.cloned.1.call-done) | copy-start | bytes 2359300
  1600.3 213.7 %copy-start.65 = (f32[6,256,128]{2,1,0:T(8,128)S(1)}, f32[6,256,128]{2,1,0:T(8,128)}, u32[]{:S(2)}) copy-start(f32[6,256,128]{2,1,0:T(8,128)} %param.49) | copy-start | bytes 2359300
  1600.3 213.7 %copy-start.66 = (f32[6,256,128]{2,1,0:T(8,128)S(1)}, f32[6,256,128]{2,1,0:T(8,128)}, u32[]{:S(2)}) copy-start(f32[6,256,128]{2,1,0:T(8,128)} %param.50) | copy-start | bytes 2359300
  1600.3 213.7 %copy-start.67 = (f32[6,256,128]{2,1,0:T(8,128)S(1)}, f32[6,256,128]{2,1,0:T(8,128)}, u32[]{:S(2)}) copy-start(f32[6,256,128]{2,1,0:T(8,128)} %param.51) | copy-start | bytes 2359300
  (92 other events, 266.1 us)
Sparse Core Ops, SparseCore 0:
  45.7 89.2 all-reduce.11
  148.4 85.4 all-reduce.13
  250.5 85.4 all-reduce.15
  360.0 289.7 all-reduce.17
  710.7 85.5 all-reduce.19
  807.5 85.4 all-reduce.21
  914.7 85.4 all-reduce.23
  1058.8 359.1 all-reduce.25
  1421.6 33.1 reduce-scatter.17
  1457.9 33.5 reduce-scatter.21
  1494.8 38.4 reduce-scatter.13
  1536.6 61.7 reduce-scatter.15
  1602.2 33.5 reduce-scatter.23
  1639.4 34.1 reduce-scatter.19
  1677.3 81.5 reduce-scatter.11
where the time goes:
time: 1840 us; the launch traced here: 1830 us
  waiting for transfers between devices  1370 us (74%)
  matrix products  176 us (10%)
  other arithmetic  122 us (7%)
  blocking collectives  75.6 us (4%)
  local copies, waits for them, and re-layouts  54.3 us (3%)
  between operations  25.9 us (1%)
    psum x4, waiting for transfers between devices, latent_return(): return lax.psum((latent_part, gain_part), 'mp')  541 us
    psum x1, waiting for transfers between devices, body(): lax.psum(jnp.einsum('bpc,cd->bpd', write_out, copy_narrowout, preferred_e...  274 us
    psum x3, waiting for transfers between devices, latent_mix(): return lax.psum(partial_sum, 'mp')  254 us
    reduce_scatter x1, waiting for transfers between devices, body(): lax.psum_scatter(widein_grad, 'dp', scatter_dimension=0, tiled=True)  81.9 us
    unnamed x17, waiting for transfers between devices  71.1 us
    reduce_scatter x1, waiting for transfers between devices, body(): lax.psum_scatter(wideout_grad, 'dp', scatter_dimension=2, tiled=True)  63.3 us
    reduce_scatter x1, waiting for transfers between devices, body(): lax.psum_scatter(narrowin_grad, 'dp', scatter_dimension=0, tiled=True)  40.4 us
    psum x1, blocking collectives, body(): lax.psum((split_square + leading * copied_square, leading * loss_local),...  39.7 us
  transfers between devices with their start and end apart: 15, of which 15 were waited for; matrix products, arithmetic and copies ran while one was open for 5% of the time, Pallas kernels for 0%

commit v1 on v0

v1 whole, which is shorter than its diff:
```python
from functools import partial
import math

import jax
import jax.numpy as jnp
from jax import lax
from jax.experimental import pallas as pl
from jax.experimental.pallas import tpu as pltpu
from jax.sharding import PartitionSpec as P

HEAD_DIM = 64
PIX = 12
NSTEPS = 1000
STEP = 10


precise = lax.Precision.HIGHEST
clip_level = 0.01
learning_rate = 0.05
weight_decay = 0.1
adam_beta = 0.5
adam_eps = 1e-08


def layer_norm(values, gain):
    centered = values - jnp.mean(values, -1, keepdims=True)
    scale = lax.rsqrt(jnp.mean(centered * centered, -1, keepdims=True) + 1e-05)
    normed = centered * scale
    return (normed * gain, (normed, scale))


def norm_back(upstream, gain, stats):
    normed, scale = stats
    inner = upstream * gain
    values = scale * (
        inner
        - jnp.mean(inner, -1, keepdims=True)
        - normed * jnp.mean(inner * normed, -1, keepdims=True)
    )
    gain_grad = jnp.sum((upstream * normed).reshape(-1, normed.shape[-1]), 0)
    return (values, gain_grad)


def positions(count, width):
    place = jnp.arange(count, dtype=jnp.float32)[:, None]
    index = jnp.arange(width // 2, dtype=jnp.float32)[None, :]
    angle = place * jnp.exp(-math.log(10000.0) * 2.0 * index / width)
    return jnp.concatenate([jnp.sin(angle), jnp.cos(angle)], -1)


def split_heads(values):
    return values.reshape(values.shape[:-1] + (values.shape[-1] // HEAD_DIM, HEAD_DIM))


def attend_scores(queries, keys, keep_mask):
    scores = jnp.einsum(
        "bqhe,bkhe->bhqk",
        split_heads(queries),
        split_heads(keys),
        preferred_element_type=jnp.float32,
    ) * HEAD_DIM ** (-0.5)
    if keep_mask is not None:
        scores = jnp.where(keep_mask[:, None, None, :] > 0, scores, -1e30)
    return scores


def attend_forward(queries, keys, values, keep_mask):
    scores = attend_scores(queries, keys, keep_mask)
    top = jnp.max(scores, -1, keepdims=True)
    log_total = top + jnp.log(jnp.sum(jnp.exp(scores - top), -1, keepdims=True))
    probs = jnp.exp(scores - log_total).astype(jnp.bfloat16)
    output = jnp.einsum(
        "bhqk,bkhe->bqhe", probs, split_heads(values), preferred_element_type=jnp.float32
    )
    return (output.reshape(queries.shape).astype(jnp.bfloat16), log_total)


def attend_back(queries, keys, values, keep_mask, log_total, upstream):
    scores = attend_scores(queries, keys, keep_mask)
    probs = jnp.exp(scores - log_total)
    value_grad = jnp.einsum(
        "bhqk,bqhe->bkhe",
        probs.astype(jnp.bfloat16),
        split_heads(upstream),
        preferred_element_type=jnp.float32,
    )
    prob_grad = jnp.einsum(
        "bqhe,bkhe->bhqk",
        split_heads(upstream),
        split_heads(values),
        preferred_element_type=jnp.float32,
    )
    score_grad = (probs * (prob_grad - jnp.sum(prob_grad * probs, -1, keepdims=True))).astype(
        jnp.bfloat16
    )
    query_grad = jnp.einsum(
        "bhqk,bkhe->bqhe", score_grad, split_heads(keys), preferred_element_type=jnp.float32
    ) * HEAD_DIM ** (-0.5)
    key_grad = jnp.einsum(
        "bhqk,bqhe->bkhe", score_grad, split_heads(queries), preferred_element_type=jnp.float32
    ) * HEAD_DIM ** (-0.5)
    return (
        query_grad.reshape(queries.shape).astype(jnp.bfloat16),
        key_grad.reshape(keys.shape),
        value_grad.reshape(values.shape),
    )


MESH_ID = pl.DeviceIdType.MESH
VMEM_SPEC = pl.BlockSpec(memory_space=pltpu.VMEM)
CHUNKS = 32


def remote(source, target, send_sem, recv_sem, device):
    return pltpu.make_async_remote_copy(
        src_ref=source,
        dst_ref=target,
        send_sem=send_sem,
        recv_sem=recv_sem,
        device_id=device,
        device_id_type=MESH_ID,
    )


def greet_line(place, count):
    barrier = pltpu.get_barrier_semaphore()
    below, above = {"mp": place - 1}, {"mp": place + 1}

    @pl.when(place > 0)
    def _():
        pl.semaphore_signal(barrier, inc=1, device_id=below, device_id_type=MESH_ID)

    @pl.when(place < count - 1)
    def _():
        pl.semaphore_signal(barrier, inc=1, device_id=above, device_id_type=MESH_ID)

    inside = jnp.logical_and(place > 0, place < count - 1)

    @pl.when(inside)
    def _():
        pl.semaphore_wait(barrier, 2)

    @pl.when(jnp.logical_not(inside))
    def _():
        pl.semaphore_wait(barrier, 1)


def line_sum_kernel(
    count,
    part_ref,
    base_ref,
    out_ref,
    inner,
    from_away,
    from_toward,
    toward_send,
    away_send,
    away_recv,
    toward_recv,
):
    place = lax.axis_index("mp")
    half = count // 2
    low_side = place < half
    toward = {"mp": jnp.where(low_side, place + 1, place - 1)}
    away = {"mp": jnp.where(low_side, place - 1, place + 1)}
    middle = jnp.logical_or(place == half - 1, place == half)
    outermost = jnp.logical_or(place == 0, place == count - 1)
    chunks = toward_send.shape[0]
    rows = part_ref.shape[0] // chunks
    greet_line(place, count)

    def window(step):
        return pl.ds(pl.multiple_of(step * rows, rows), rows)

    def push(step, source, inside):
        target = from_toward if inside else from_away
        recv = toward_recv if inside else away_recv
        return remote(
            source.at[window(step)],
            target.at[window(step)],
            toward_send.at[step],
            recv.at[step],
            toward,
        )

    def back(step, source):
        return remote(
            source.at[window(step)],
            from_toward.at[window(step)],
            away_send.at[step],
            toward_recv.at[step],
            away,
        )

    def gather_in(step):
        push(step, part_ref, False).wait_recv()
        inner[window(step)] = part_ref[window(step)] + from_away[window(step)]

    @pl.when(outermost)
    def _():
        def leave(step, carry):
            push(step, part_ref, False).start()
            return carry

        lax.fori_loop(0, chunks, leave, 0)

        def arrive(step, carry):
            push(step, part_ref, True).wait_recv()
            out_ref[window(step)] = from_toward[window(step)] + base_ref[window(step)]
            push(step, part_ref, False).wait_send()
            return carry

        lax.fori_loop(0, chunks, arrive, 0)

    lag = 2

    @pl.when(middle)
    def _():
        def finish(step):
            push(step, inner, True).wait_recv()
            push(step, inner, True).wait_send()
            total = inner[window(step)] + from_toward[window(step)]
            inner[window(step)] = total
            back(step, inner).start()
            out_ref[window(step)] = total + base_ref[window(step)]

        def first(step, carry):
            gather_in(step)
            push(step, inner, True).start()
            return carry

        def both(step, carry):
            first(step, carry)
            finish(step - lag)
            return carry

        def last(step, carry):
            finish(step)
            return carry

        def drain(step, carry):
            back(step, inner).wait_send()
            return carry

        lax.fori_loop(0, lag, first, 0)
        lax.fori_loop(lag, chunks, both, 0)
        lax.fori_loop(chunks - lag, chunks, last, 0)
        lax.fori_loop(0, chunks, drain, 0)

    if count > 4:

        @pl.when(jnp.logical_not(jnp.logical_or(middle, outermost)))
        def _():
            def inwards(step, carry):
                gather_in(step)
                push(step, inner, False).start()
                return carry

            def outwards(step, carry):
                push(step, inner, True).wait_recv()
                back(step, from_toward).start()
                out_ref[window(step)] = from_toward[window(step)] + base_ref[window(step)]
                return carry

            def drain(step, carry):
                push(step, inner, False).wait_send()
                back(step, from_toward).wait_send()
                return carry

            lax.fori_loop(0, chunks, inwards, 0)
            lax.fori_loop(0, chunks, outwards, 0)
            lax.fori_loop(0, chunks, drain, 0)


def line_sum(part, base, call_id):
    shape = part.shape
    part = part.reshape(-1, shape[-1])
    rows, width = part.shape
    buffer = pltpu.VMEM((rows, width), jnp.float32)
    sems = pltpu.SemaphoreType.DMA((CHUNKS,))
    out = pl.pallas_call(
        partial(line_sum_kernel, lax.axis_size("mp")),
        out_shape=jax.ShapeDtypeStruct((rows, width), jnp.float32),
        in_specs=[VMEM_SPEC] * 2,
        out_specs=VMEM_SPEC,
        scratch_shapes=[buffer] * 3 + [sems] * 4,
        compiler_params=pltpu.CompilerParams(
            collective_id=call_id, has_side_effects=True, vmem_limit_bytes=24 << 20
        ),
        cost_estimate=pl.CostEstimate(
            flops=4 * rows * width, bytes_accessed=16 * rows * width, transcendentals=0
        ),
    )(part, base.reshape(part.shape))
    return out.reshape(shape)


def line_scatter_kernel(
    count, part_ref, out_ref, up_acc, down_acc, from_below, from_above, up_send, down_send, up_recv, down_recv
):
    place = lax.axis_index("mp")
    steps = up_send.shape[1]
    block = part_ref.shape[0] // count
    rows = block // steps
    below, above = {"mp": place - 1}, {"mp": place + 1}
    greet_line(place, count)

    def window(owner, step):
        return pl.ds(pl.multiple_of(owner * block + step * rows, rows), rows)

    def up(owner, step, source):
        where = window(owner, step)
        return remote(
            source.at[where], from_below.at[where], up_send.at[owner, step], up_recv.at[owner, step], above
        )

    def down(owner, step, source):
        where = window(owner, step)
        return remote(
            source.at[where], from_above.at[where], down_send.at[owner, step], down_recv.at[owner, step], below
        )

    def up_turn(index):
        owner, step = count - 1 - index // steps, lax.rem(index, steps)

        @pl.when(jnp.logical_and(owner > place, place == 0))
        def _():
            up(owner, step, part_ref).start()

        @pl.when(jnp.logical_and(owner > place, place > 0))
        def _():
            up(owner, step, part_ref).wait_recv()
            where = window(owner, step)
            up_acc[where] = part_ref[where] + from_below[where]
            up(owner, step, up_acc).start()

    def down_turn(index):
        owner, step = index // steps, lax.rem(index, steps)

        @pl.when(jnp.logical_and(owner < place, place == count - 1))
        def _():
            down(owner, step, part_ref).start()

        @pl.when(jnp.logical_and(owner < place, place < count - 1))
        def _():
            down(owner, step, part_ref).wait_recv()
            where = window(owner, step)
            down_acc[where] = part_ref[where] + from_above[where]
            down(owner, step, down_acc).start()

    turns, lag = count * steps, steps

    def staggered(first, second):
        def begin(index, carry):
            first(index)
            return carry

        def both(index, carry):
            first(index)
            second(index - lag)
            return carry

        def end(index, carry):
            second(index)
            return carry

        lax.fori_loop(0, lag, begin, 0)
        lax.fori_loop(lag, turns, both, 0)
        lax.fori_loop(turns - lag, turns, end, 0)

    @pl.when(place < count // 2)
    def _():
        staggered(up_turn, down_turn)

    @pl.when(place >= count // 2)
    def _():
        staggered(down_turn, up_turn)

    def settle(step, carry):
        where = window(place, step)
        mine = pl.ds(pl.multiple_of(step * rows, rows), rows)
        out_ref[mine] = part_ref[where]

        @pl.when(place > 0)
        def _():
            up(place, step, part_ref).wait_recv()
            out_ref[mine] += from_below[where]

        @pl.when(place < count - 1)
        def _():
            down(place, step, part_ref).wait_recv()
            out_ref[mine] += from_above[where]

        return carry

    lax.fori_loop(0, steps, settle, 0)

    def drain(index, carry):
        owner, step = index // steps, lax.rem(index, steps)

        @pl.when(owner > place)
        def _():
            up(owner, step, part_ref).wait_send()

        @pl.when(owner < place)
        def _():
            down(owner, step, part_ref).wait_send()

        return carry

    lax.fori_loop(0, count * steps, drain, 0)


def line_scatter(part, call_id):
    rows, width = part.shape
    count = lax.axis_size("mp")
    steps = 8
    buffer = pltpu.VMEM((rows, width), jnp.float32)
    sems = pltpu.SemaphoreType.DMA((count, steps))
    return pl.pallas_call(
        partial(line_scatter_kernel, count),
        out_shape=jax.ShapeDtypeStruct((rows // count, width), jnp.float32),
        in_specs=[VMEM_SPEC],
        out_specs=VMEM_SPEC,
        scratch_shapes=[buffer] * 4 + [sems] * 4,
        compiler_params=pltpu.CompilerParams(
            collective_id=call_id, has_side_effects=True, vmem_limit_bytes=24 << 20
        ),
        cost_estimate=pl.CostEstimate(
            flops=2 * rows * width, bytes_accessed=8 * rows * width, transcendentals=0
        ),
    )(part)


def line_gather_kernel(count, own_ref, out_ref, up_send, down_send, up_recv, down_recv):
    place = lax.axis_index("mp")
    steps = up_send.shape[1]
    block = own_ref.shape[0]
    rows = block // steps
    below, above = {"mp": place - 1}, {"mp": place + 1}
    greet_line(place, count)

    def window(owner, step):
        return pl.ds(pl.multiple_of(owner * block + step * rows, rows), rows)

    def up(owner, step):
        part = out_ref.at[window(owner, step)]
        return remote(part, part, up_send.at[owner, step], up_recv.at[owner, step], above)

    def down(owner, step):
        part = out_ref.at[window(owner, step)]
        return remote(part, part, down_send.at[owner, step], down_recv.at[owner, step], below)

    def begin(step, carry):
        out_ref[window(place, step)] = own_ref[pl.ds(pl.multiple_of(step * rows, rows), rows)]

        @pl.when(place < count - 1)
        def _():
            up(place, step).start()

        @pl.when(place > 0)
        def _():
            down(place, step).start()

        return carry

    lax.fori_loop(0, steps, begin, 0)

    def pass_on(index, carry):
        away, step = 1 + index // steps, lax.rem(index, steps)

        @pl.when(place - away >= 0)
        def _():
            up(place - away, step).wait_recv()

        @pl.when(jnp.logical_and(place - away >= 0, place < count - 1))
        def _():
            up(place - away, step).start()

        @pl.when(place + away < count)
        def _():
            down(place + away, step).wait_recv()

        @pl.when(jnp.logical_and(place + away < count, place > 0))
        def _():
            down(place + away, step).start()

        return carry

    lax.fori_loop(0, (count - 1) * steps, pass_on, 0)

    def drain(index, carry):
        owner, step = index // steps, lax.rem(index, steps)

        @pl.when(jnp.logical_and(owner <= place, place < count - 1))
        def _():
            up(owner, step).wait_send()

        @pl.when(jnp.logical_and(owner >= place, place > 0))
        def _():
            down(owner, step).wait_send()

        return carry

    lax.fori_loop(0, count * steps, drain, 0)


def line_gather(own, call_id):
    rows, width = own.shape
    count = lax.axis_size("mp")
    steps = 8
    sems = pltpu.SemaphoreType.DMA((count, steps))
    return pl.pallas_call(
        partial(line_gather_kernel, count),
        out_shape=jax.ShapeDtypeStruct((rows * count, width), jnp.float32),
        in_specs=[VMEM_SPEC],
        out_specs=VMEM_SPEC,
        scratch_shapes=[sems] * 4,
        compiler_params=pltpu.CompilerParams(
            collective_id=call_id, has_side_effects=True, vmem_limit_bytes=16 << 20
        ),
        cost_estimate=pl.CostEstimate(
            flops=rows * width, bytes_accessed=8 * rows * width * count, transcendentals=0
        ),
    )(own)


def mesh_sum_kernel(axes, tile_ref, out_ref, held, send_sem, recv_sem):
    barrier = pltpu.get_barrier_semaphore()
    places = {name: lax.axis_index(name) for name, _ in axes}

    def peer(name, count, step):
        return {name: lax.rem(places[name] + step, count)}

    for name, count in axes:

        def greet(step, carry, name=name, count=count):
            pl.semaphore_signal(
                barrier, inc=1, device_id=peer(name, count, step), device_id_type=MESH_ID
            )
            return carry

        lax.fori_loop(1, count, greet, 0)
    pl.semaphore_wait(barrier, sum(count - 1 for _, count in axes))
    value = tile_ref[...]
    first = 0
    for name, count in axes:
        place = places[name]
        held[first + place] = value

        def copy(step, slot, name=name, count=count, first=first, place=place):
            return remote(
                held.at[first + place],
                held.at[first + slot],
                send_sem.at[first + step],
                recv_sem.at[first + slot],
                peer(name, count, step),
            )

        def send(step, carry, copy=copy, place=place):
            copy(step, place).start()
            return carry

        def take(step, carry, copy=copy, count=count, place=place):
            copy(step, lax.rem(place + step, count)).wait_recv()
            return carry

        def add(slot, carry, first=first):
            return carry + held[first + slot]

        def drain(step, carry, copy=copy, place=place):
            copy(step, place).wait_send()
            return carry

        lax.fori_loop(1, count, send, 0)
        lax.fori_loop(1, count, take, 0)
        value = lax.fori_loop(1, count, add, held[first])
        lax.fori_loop(1, count, drain, 0)
        first += count
    out_ref[...] = value


def mesh_sum(tile, names, call_id):
    axes = [(name, lax.axis_size(name)) for name in names]
    slots = sum(count for _, count in axes)
    return pl.pallas_call(
        partial(mesh_sum_kernel, axes),
        out_shape=jax.ShapeDtypeStruct(tile.shape, jnp.float32),
        in_specs=[VMEM_SPEC],
        out_specs=VMEM_SPEC,
        scratch_shapes=[
            pltpu.VMEM((slots,) + tile.shape, jnp.float32),
            pltpu.SemaphoreType.DMA((slots,)),
            pltpu.SemaphoreType.DMA((slots,)),
        ],
        compiler_params=pltpu.CompilerParams(collective_id=call_id, has_side_effects=True),
    )(tile)


def adam_update(master, first, second, gradient, scale):
    clipped = gradient * scale
    moment = adam_beta * first + (1.0 - adam_beta) * clipped
    square = adam_beta * second + (1.0 - adam_beta) * clipped * clipped
    fixed_first = moment / (1.0 - adam_beta**STEP)
    fixed_second = square / (1.0 - adam_beta**STEP)
    updated = master - learning_rate * (
        fixed_first / (jnp.sqrt(fixed_second) + adam_eps) + weight_decay * master
    )
    return (updated, moment, square)


def body(
    clean_patches,
    noise_patches,
    timesteps,
    present_mask,
    copy_widein,
    copy_narrowin,
    copy_wideout,
    copy_narrowout,
    copy_latents,
    copy_gains,
    copy_pixels,
    master_widein,
    first_widein,
    second_widein,
    master_narrowin,
    first_narrowin,
    second_narrowin,
    master_wideout,
    first_wideout,
    second_wideout,
    master_narrowout,
    first_narrowout,
    second_narrowout,
    master_latents,
    first_latents,
    second_latents,
    master_gains,
    first_gains,
    second_gains,
    master_pixels,
    first_pixels,
    second_pixels,
):
    images = clean_patches.shape[0]
    patches = clean_patches.shape[2]
    count_mp, count_dp = lax.axis_size("mp"), lax.axis_size("dp")
    mp_index, dp_index = lax.axis_index("mp"), lax.axis_index("dp")
    lead = (mp_index == 0).astype(jnp.float32)
    latents, d_lat = copy_latents.shape
    d_if = copy_gains.shape[1]
    local = copy_widein.shape[2]
    sharers = max(1, count_mp // images)
    own_images = max(1, images // count_mp)
    own_patches, own_latents = patches // sharers, latents // sharers
    first_image = mp_index * own_images // sharers
    share = lax.rem(mp_index, sharers)

    def dp_piece(values, axis):
        size = values.shape[axis] // count_dp
        return lax.dynamic_slice_in_dim(values, dp_index * size, size, axis).astype(jnp.float32)

    key_piece = dp_piece(copy_widein[:, 8], 0)
    value_piece = dp_piece(copy_widein[:, 9], 0)
    query_piece = dp_piece(copy_narrowin[:, 2], 0)
    out_piece = dp_piece(copy_narrowout, 1).T
    gathered = lax.all_gather(
        jnp.concatenate([key_piece, value_piece, query_piece, out_piece], 0), ("mp", "dp")
    ).reshape(count_mp, count_dp, -1, local)
    nothing = jnp.where(timesteps[0] > 0, 0.0, -0.0)
    gathered = gathered + nothing
    edges = [0, d_lat, 2 * d_lat, 2 * d_lat + d_if, 2 * d_lat + 2 * d_if]
    write_key_weight, write_value_weight, write_query_weight, write_out_weight = (
        gathered[:, :, low // count_dp : high // count_dp]
        .reshape(count_mp, high - low, local)
        .astype(jnp.bfloat16)
        for low, high in zip(edges[:-1], edges[1:])
    )

    signal = jnp.cos(0.5 * math.pi * (timesteps.astype(jnp.float32) + 0.5) / NSTEPS) ** 2
    noisy = (
        jnp.sqrt(signal)[:, None, None] * clean_patches
        + jnp.sqrt(1.0 - signal)[:, None, None] * noise_patches
    )
    loss_weight = 0.5 + signal
    keep_float = present_mask.astype(jnp.float32)
    weight_here = jnp.sum(loss_weight * PIX * jnp.sum(keep_float, 1))
    weight_total = mesh_sum(jnp.full((8, 128), weight_here), ("dp",), 1)[0, 0]
    gain_rows = copy_gains.astype(jnp.float32)

    def wide_gain(index):
        return gain_rows[2 * index : 2 * index + 2].reshape(-1)

    pixel_rows = copy_pixels.astype(jnp.float32)
    interface = jnp.einsum("bcp,cd->bpd", noisy, pixel_rows[0], precision=precise) + positions(
        noisy.shape[2], pixel_rows.shape[2]
    )
    latent_zero = copy_latents.astype(jnp.float32)
    read_norm, read_stats = layer_norm(latent_zero, wide_gain(0))
    read_low = read_norm.astype(jnp.bfloat16)
    side_norm, side_stats = layer_norm(interface, gain_rows[8])
    side_low = side_norm.astype(jnp.bfloat16)
    read_query = jnp.einsum(
        "ld,dc->lc", read_low, copy_widein[:, 0], preferred_element_type=jnp.float32
    ).astype(jnp.bfloat16)
    read_query = jnp.broadcast_to(read_query[None], (images,) + read_query.shape)
    read_key = jnp.einsum(
        "bpd,dc->bpc", side_low, copy_narrowin[:, 0], preferred_element_type=jnp.float32
    ).astype(jnp.bfloat16)
    read_value = jnp.einsum(
        "bpd,dc->bpc", side_low, copy_narrowin[:, 1], preferred_element_type=jnp.float32
    ).astype(jnp.bfloat16)
    read_out, read_total = attend_forward(read_query, read_key, read_value, present_mask)
    latent_one = line_sum(
        jnp.einsum("blc,cd->bld", read_out, copy_wideout[0], preferred_element_type=jnp.float32),
        jnp.broadcast_to(latent_zero[None], (images, latents, d_lat)),
        2,
    )
    self_norm, self_stats = layer_norm(latent_one, wide_gain(1))
    self_low = self_norm.astype(jnp.bfloat16)
    self_triple = jnp.einsum(
        "bld,dsc->blsc", self_low, copy_widein[:, 1:4], preferred_element_type=jnp.float32
    ).astype(jnp.bfloat16)
    self_out, self_total = attend_forward(
        self_triple[:, :, 0], self_triple[:, :, 1], self_triple[:, :, 2], None
    )
    latent_two = line_sum(
        jnp.einsum("blc,cd->bld", self_out, copy_wideout[1], preferred_element_type=jnp.float32),
        latent_one,
        3,
    )
    feed_norm, feed_stats = layer_norm(latent_two, wide_gain(2))
    feed_low = feed_norm.astype(jnp.bfloat16)
    hidden = jnp.einsum(
        "bld,dsc->blsc", feed_low, copy_widein[:, 4:8], preferred_element_type=jnp.float32
    )
    active, gelu_pull = jax.vjp(partial(jax.nn.gelu, approximate=False), hidden)
    active_low = active.astype(jnp.bfloat16)
    feed_partial = jnp.einsum(
        "blsc,scd->bld", active_low, copy_wideout[2:6], preferred_element_type=jnp.float32
    )

    def own_rows(values):
        values = values.reshape((images * sharers, own_latents) + values.shape[2:])
        return lax.dynamic_slice_in_dim(values, mp_index * own_images, own_images, 0)

    latent_three = own_rows(latent_two) + line_scatter(
        feed_partial.reshape(-1, d_lat), 4
    ).reshape(own_images, own_latents, d_lat)
    write_norm, write_stats = layer_norm(latent_three, wide_gain(3))
    write_low = write_norm.astype(jnp.bfloat16)

    def own_tokens(values, axis):
        values = lax.dynamic_slice_in_dim(values, first_image, own_images, 0)
        return lax.dynamic_slice_in_dim(values, share * own_patches, own_patches, axis)

    own_interface = own_tokens(interface, 1)
    own_noisy, own_noise = own_tokens(noisy, 2), own_tokens(noise_patches, 2)
    own_keep = own_tokens(keep_float, 1)
    own_weight = lax.dynamic_slice_in_dim(loss_weight, first_image, own_images, 0)

    outer_norm, outer_stats = layer_norm(own_interface, gain_rows[9])
    outer_low = outer_norm.astype(jnp.bfloat16)

    def join(spec, values, weight):
        product = jnp.einsum(spec, values, weight, preferred_element_type=jnp.float32)
        return product.astype(jnp.bfloat16).reshape(product.shape[:2] + (-1,))

    def image_rows(values):
        if sharers == 1:
            return values
        whole = lax.all_gather(values.astype(jnp.float32), "mp", axis=0, tiled=True)
        whole = whole + nothing
        whole = whole.reshape(images, latents, d_lat).astype(jnp.bfloat16)
        return lax.dynamic_slice_in_dim(whole, first_image, own_images, 0)

    write_query = join("bpd,mdc->bpmc", outer_low, write_query_weight)
    write_key = image_rows(join("bld,mdc->blmc", write_low, write_key_weight))
    write_value = image_rows(join("bld,mdc->blmc", write_low, write_value_weight))
    write_out, write_total = attend_forward(write_query, write_key, write_value, None)
    write_split = write_out.reshape(write_out.shape[:2] + (count_mp, local))
    outer = own_interface + jnp.einsum(
        "bpmc,mdc->bpd", write_split, write_out_weight, preferred_element_type=jnp.float32
    )
    final_norm, final_stats = layer_norm(outer, gain_rows[10])
    final_low = final_norm.astype(jnp.bfloat16)
    predicted = jnp.einsum(
        "bpd,cd->bcp", final_low, copy_pixels[1], preferred_element_type=jnp.float32
    )
    difference = predicted - own_noise
    masked = own_weight[:, None, None] * own_keep[:, None, :] * difference
    loss_local = jnp.sum(masked * difference)
    predict_grad = (2.0 * masked / weight_total).astype(jnp.bfloat16)
    head_grad = jnp.einsum(
        "bcp,bpd->cd", predict_grad, final_low, preferred_element_type=jnp.float32
    )
    final_grad = jnp.einsum(
        "bcp,cd->bpd", predict_grad, copy_pixels[1], preferred_element_type=jnp.float32
    )
    outer_grad, gain_final = norm_back(final_grad, gain_rows[10], final_stats)
    branch_low = outer_grad.astype(jnp.bfloat16)
    narrowout_grad = jnp.einsum(
        "bpd,bpmc->mdc", branch_low, write_split, preferred_element_type=jnp.float32
    )
    write_upstream = join("bpd,mdc->bpmc", branch_low, write_out_weight)
    query_grad, key_grad, value_grad = attend_back(
        write_query, write_key, write_value, None, write_total, write_upstream
    )
    query_split = query_grad.reshape(query_grad.shape[:2] + (count_mp, local))
    write_query_grad = jnp.einsum(
        "bpd,bpmc->mdc", outer_low, query_split, preferred_element_type=jnp.float32
    )
    outer_part = jnp.einsum(
        "bpmc,mdc->bpd", query_split, write_query_weight, preferred_element_type=jnp.float32
    )

    def row_grad(values):
        if sharers > 1:
            whole = jnp.zeros((images, latents, d_lat), jnp.float32)
            whole = lax.dynamic_update_slice_in_dim(whole, values, first_image, 0)
            values = lax.psum_scatter(
                whole.reshape(images * sharers, own_latents, d_lat),
                "mp",
                scatter_dimension=0,
                tiled=True,
            )
        values = values.astype(jnp.bfloat16)
        return values.reshape(values.shape[:2] + (count_mp, local))

    key_grad, value_grad = row_grad(key_grad), row_grad(value_grad)
    write_key_grad = jnp.einsum(
        "bld,blmc->mdc", write_low, key_grad, preferred_element_type=jnp.float32
    )
    write_value_grad = jnp.einsum(
        "bld,blmc->mdc", write_low, value_grad, preferred_element_type=jnp.float32
    )
    write_part = jnp.einsum(
        "blmc,mdc->bld", key_grad, write_key_weight, preferred_element_type=jnp.float32
    ) + jnp.einsum(
        "blmc,mdc->bld", value_grad, write_value_weight, preferred_element_type=jnp.float32
    )
    own_grad, gain_write = norm_back(write_part, wide_gain(3), write_stats)
    latent_grad = line_gather(own_grad.reshape(-1, d_lat), 5).reshape(latent_one.shape)
    outer_back, gain_outer = norm_back(outer_part, gain_rows[9], outer_stats)

    def pieces(values, groups):
        return values.reshape(groups, -1, local)

    def both_pieces(values):
        values = values.reshape(count_mp, count_dp, -1, local)
        return jnp.swapaxes(values, 0, 1)

    write_joined = jnp.concatenate(
        [
            both_pieces(item)
            for item in (write_key_grad, write_value_grad, write_query_grad, narrowout_grad)
        ],
        2,
    )
    write_share = lax.psum_scatter(
        lax.psum_scatter(write_joined, "dp", scatter_dimension=0), "mp", scatter_dimension=0
    )

    def dp_scatter(items):
        joined = jnp.concatenate([pieces(item, count_dp) for item in items], 1)
        return lax.psum_scatter(joined, "dp", scatter_dimension=0)

    branch_low = latent_grad.astype(jnp.bfloat16)
    down_grad = [
        jnp.einsum(
            "bld,blc->dc", branch_low, active_low[:, :, slot], preferred_element_type=jnp.float32
        )
        for slot in range(4)
    ]
    active_grad = jnp.einsum(
        "bld,scd->blsc", branch_low, copy_wideout[2:6], preferred_element_type=jnp.float32
    )
    hidden_grad = gelu_pull(active_grad)[0].astype(jnp.bfloat16)
    up_grad = [
        jnp.einsum(
            "bld,blc->dc", feed_low, hidden_grad[:, :, slot], preferred_element_type=jnp.float32
        )
        for slot in range(4)
    ]
    feed_part = jnp.einsum(
        "blsc,dsc->bld", hidden_grad, copy_widein[:, 4:8], preferred_element_type=jnp.float32
    )
    feed_share = dp_scatter(up_grad + down_grad)
    latent_part, gain_feed = norm_back(feed_part, wide_gain(2), feed_stats)
    latent_grad = line_sum(latent_part, latent_grad, 6)
    branch_low = latent_grad.astype(jnp.bfloat16)
    self_out_grad = jnp.einsum(
        "bld,blc->dc", branch_low, self_out, preferred_element_type=jnp.float32
    )
    self_upstream = jnp.einsum(
        "bld,cd->blc", branch_low, copy_wideout[1], preferred_element_type=jnp.float32
    ).astype(jnp.bfloat16)
    triple_grad = [
        item.astype(jnp.bfloat16)
        for item in attend_back(
            self_triple[:, :, 0],
            self_triple[:, :, 1],
            self_triple[:, :, 2],
            None,
            self_total,
            self_upstream,
        )
    ]
    self_in_grad = [
        jnp.einsum("bld,blc->dc", self_low, item, preferred_element_type=jnp.float32)
        for item in triple_grad
    ]
    self_part = jnp.einsum(
        "blsc,dsc->bld",
        jnp.stack(triple_grad, 2),
        copy_widein[:, 1:4],
        preferred_element_type=jnp.float32,
    )
    self_share = dp_scatter(self_in_grad + [self_out_grad])
    latent_part, gain_self = norm_back(self_part, wide_gain(1), self_stats)
    latent_grad = line_sum(latent_part, latent_grad, 7)
    branch_low = latent_grad.astype(jnp.bfloat16)
    read_out_grad = jnp.einsum(
        "bld,blc->dc", branch_low, read_out, preferred_element_type=jnp.float32
    )
    read_upstream = jnp.einsum(
        "bld,cd->blc", branch_low, copy_wideout[0], preferred_element_type=jnp.float32
    ).astype(jnp.bfloat16)
    query_grad, key_grad, value_grad = (
        item.astype(jnp.bfloat16)
        for item in attend_back(
            read_query, read_key, read_value, present_mask, read_total, read_upstream
        )
    )
    read_query_grad = jnp.einsum(
        "ld,blc->dc", read_low, query_grad, preferred_element_type=jnp.float32
    )
    read_part = jnp.einsum(
        "blc,dc->bld", query_grad, copy_widein[:, 0], preferred_element_type=jnp.float32
    )
    normed, scale = read_stats
    latent_part, gain_read = norm_back(
        read_part, wide_gain(0), (normed[None], scale[None])
    )
    latent_total = jnp.sum(lead * latent_grad + latent_part, 0)
    read_key_grad = jnp.einsum(
        "bpd,bpc->dc", side_low, key_grad, preferred_element_type=jnp.float32
    )
    read_value_grad = jnp.einsum(
        "bpd,bpc->dc", side_low, value_grad, preferred_element_type=jnp.float32
    )
    side_part = jnp.einsum(
        "bpc,dc->bpd", key_grad, copy_narrowin[:, 0], preferred_element_type=jnp.float32
    ) + jnp.einsum(
        "bpc,dc->bpd", value_grad, copy_narrowin[:, 1], preferred_element_type=jnp.float32
    )
    side_back, gain_side = norm_back(side_part, gain_rows[8], side_stats)
    embed_grad = jnp.einsum("bcp,bpd->cd", noisy, side_back, precision=precise) + jnp.einsum(
        "bcp,bpd->cd", own_noisy, outer_grad + outer_back, precision=precise
    )
    gains_grad = jnp.concatenate(
        [
            gain_read.reshape(2, -1),
            gain_self.reshape(2, -1),
            gain_feed.reshape(2, -1),
            gain_write.reshape(2, -1),
            gain_side[None],
            gain_outer[None],
            gain_final[None],
        ],
        0,
    )

    def dp_columns(values):
        values = values.reshape(-1, count_dp, values.shape[-1] // count_dp)
        return jnp.swapaxes(values, 0, 1).reshape(count_dp, -1)

    small_parts = [
        dp_columns(item)
        for item in (latent_total, gains_grad, embed_grad, head_grad)
    ]
    small_sizes = [item.shape[1] for item in small_parts]
    small = jnp.concatenate(small_parts, 1)
    fill = -small.shape[1] % (8 * local)
    small = jnp.pad(small, ((0, 0), (0, fill))).reshape(count_dp, -1, local)
    read_joined = jnp.concatenate(
        [
            pieces(item, count_dp)
            for item in (read_query_grad, read_key_grad, read_value_grad, read_out_grad)
        ]
        + [small],
        1,
    )
    read_share = lax.psum_scatter(read_joined, "dp", scatter_dimension=0)
    lat_rows, if_rows = d_lat // count_dp, d_if // count_dp
    small_share = lax.psum(read_share[2 * lat_rows + 2 * if_rows :], "mp")
    small_flat = small_share.reshape(-1)
    latents_grad, gains_grad, embed_grad, head_grad = (
        small_flat[sum(small_sizes[:i]) : sum(small_sizes[: i + 1])].reshape(rows, -1)
        for i, rows in enumerate((latents, gains_grad.shape[0], PIX, PIX))
    )
    pixels_grad = jnp.stack([embed_grad, head_grad], 0)

    def cut(share, index, rows, start=0):
        return share[start + index * rows : start + (index + 1) * rows]

    widein_grad = jnp.stack(
        [cut(read_share, 0, lat_rows)]
        + [cut(self_share, i, lat_rows) for i in range(3)]
        + [cut(feed_share, i, lat_rows) for i in range(4)]
        + [cut(write_share, i, lat_rows) for i in range(2)],
        1,
    )
    narrowin_grad = jnp.stack(
        [
            cut(read_share, 0, if_rows, lat_rows),
            cut(read_share, 1, if_rows, lat_rows),
            cut(write_share, 0, if_rows, 2 * lat_rows),
        ],
        1,
    )
    wideout_grad = jnp.stack(
        [
            cut(read_share, 0, lat_rows, lat_rows + 2 * if_rows).T,
            cut(self_share, 3, lat_rows).T,
        ]
        + [cut(feed_share, 4 + i, lat_rows).T for i in range(4)],
        0,
    )
    narrowout_grad = cut(write_share, 1, if_rows, 2 * lat_rows).T
    shares = (
        widein_grad,
        narrowin_grad,
        wideout_grad,
        narrowout_grad,
        latents_grad,
        gains_grad,
        pixels_grad,
    )
    split_square = sum((jnp.sum(item * item) for item in shares[:4]))
    copied_square = sum((jnp.sum(item * item) for item in shares[4:]))
    lane = lax.broadcasted_iota(jnp.int32, (8, 128), 1)
    totals = mesh_sum(
        jnp.where(lane == 0, split_square + lead * copied_square, loss_local), ("dp", "mp"), 8
    )
    square_total, loss_total = totals[0, 0], totals[0, 1]
    grad_norm = jnp.sqrt(square_total)
    loss_value = loss_total / weight_total
    scale = clip_level / jnp.maximum(grad_norm, clip_level)
    states = (
        (master_widein, first_widein, second_widein),
        (master_narrowin, first_narrowin, second_narrowin),
        (master_wideout, first_wideout, second_wideout),
        (master_narrowout, first_narrowout, second_narrowout),
        (master_latents, first_latents, second_latents),
        (master_gains, first_gains, second_gains),
        (master_pixels, first_pixels, second_pixels),
    )
    results = []
    for state, gradient in zip(states, shares):
        results.extend(adam_update(state[0], state[1], state[2], gradient, scale))
    return (
        loss_value,
        grad_norm,
        results[0],
        results[1],
        results[2],
        results[3],
        results[4],
        results[5],
        results[6],
        results[7],
        results[8],
        results[9],
        results[10],
        results[11],
        results[12],
        results[13],
        results[14],
        results[15],
        results[16],
        results[17],
        results[18],
        results[19],
        results[20],
    )


def solution(mesh):
    in_specs = (
        P("dp", None, None),
        P("dp", None, None),
        P("dp"),
        P("dp", None),
        P(None, None, "mp"),
        P(None, None, "mp"),
        P(None, "mp", None),
        P("mp", None),
        P(),
        P(),
        P(),
        P("dp", None, "mp"),
        P("dp", None, "mp"),
        P("dp", None, "mp"),
        P("dp", None, "mp"),
        P("dp", None, "mp"),
        P("dp", None, "mp"),
        P(None, "mp", "dp"),
        P(None, "mp", "dp"),
        P(None, "mp", "dp"),
        P("mp", "dp"),
        P("mp", "dp"),
        P("mp", "dp"),
        P(None, "dp"),
        P(None, "dp"),
        P(None, "dp"),
        P(None, "dp"),
        P(None, "dp"),
        P(None, "dp"),
        P(None, None, "dp"),
        P(None, None, "dp"),
        P(None, None, "dp"),
    )
    out_specs = (
        P(),
        P(),
        P("dp", None, "mp"),
        P("dp", None, "mp"),
        P("dp", None, "mp"),
        P("dp", None, "mp"),
        P("dp", None, "mp"),
        P("dp", None, "mp"),
        P(None, "mp", "dp"),
        P(None, "mp", "dp"),
        P(None, "mp", "dp"),
        P("mp", "dp"),
        P("mp", "dp"),
        P("mp", "dp"),
        P(None, "dp"),
        P(None, "dp"),
        P(None, "dp"),
        P(None, "dp"),
        P(None, "dp"),
        P(None, "dp"),
        P(None, None, "dp"),
        P(None, None, "dp"),
        P(None, None, "dp"),
    )
    return jax.shard_map(body, mesh=mesh, in_specs=in_specs, out_specs=out_specs, check_vma=False)
```

time: 1840 us -> 983 us (0.53)
  waiting for transfers between devices: 1370 us -> 239 us
  Pallas kernels: 0 us -> 344 us
  blocking collectives: 75.6 us -> 0 us
  local copies, waits for them, and re-layouts: 54.3 us -> 116 us
  other arithmetic: 122 us -> 83.3 us
    psum x8 -> x1, waiting for transfers between devices: 1070 us -> 0.02 us  [body(): small_share = lax.psum(read_share[2 * lat_rows + 2 * if_rows:], 'mp')]
    pallas_call x0 -> x8, Pallas kernels: none -> 344 us  [the longest x4 256 us: line_sum(): pl.pallas_call(partial(line_sum_kernel, lax.axis_size('mp')), out_shape=j...]
    psum x3 -> x0, blocking collectives: 75.6 us -> none  [the longest x1 39.7 us: body(): lax.psum((split_square + leading * copied_square, leading * loss_local),...]
    unnamed x17 -> x7, waiting for transfers between devices: 71.1 us -> 0.11 us
    unnamed x264 -> x332, local copies, waits for them, and re-layouts: 29.7 us -> 43.5 us
    dot_general x21 -> x36, matrix products: 87.3 us -> 92.2 us  [the longest x1 11.2 us: body(): jnp.einsum('bcp,bpd->cd', noisy, side_back, precision=precise)]
  transfers between devices with their start and end apart: 15 -> 7, of which waited for: 15 -> 5; matrix products, arithmetic and copies ran while one was open for 5% -> 17% of each run, Pallas kernels for 0% -> 20%
where the time goes in v1:
time: 983 us; the launch traced here: 971 us
  Pallas kernels  344 us (35%)
  waiting for transfers between devices  239 us (24%)
  matrix products  162 us (16%)
  local copies, waits for them, and re-layouts  116 us (12%)
  other arithmetic  83.3 us (8%)
  between operations  26.2 us (3%)
    pallas_call x4, Pallas kernels, line_sum(): pl.pallas_call(partial(line_sum_kernel, lax.axis_size('mp')), out_shape=j...  256 us
    reduce_scatter x2, waiting for transfers between devices, dp_scatter(): return lax.psum_scatter(joined, 'dp', scatter_dimension=0)  123 us
    reduce_scatter x1, waiting for transfers between devices, body(): lax.psum_scatter(write_joined, 'dp', scatter_dimension=0)  85.7 us
    unnamed x332, local copies, waits for them, and re-layouts  43.5 us
    pallas_call x1, Pallas kernels, line_gather(): pl.pallas_call(partial(line_gather_kernel, count), out_shape=jax.ShapeDty...  36.2 us
    pallas_call x1, Pallas kernels, line_scatter(): pl.pallas_call(partial(line_scatter_kernel, count), out_shape=jax.ShapeDt...  32.8 us
    reduce_scatter x1, waiting for transfers between devices, body(): lax.psum_scatter(lax.psum_scatter(write_joined, 'dp', scatter_dimension=0...  29.6 us
  transfers between devices with their start and end apart: 7, of which 5 were waited for; matrix products, arithmetic and copies ran while one was open for 17% of the time, Pallas kernels for 20%

profile of v1, /device:TPU:0, one launch (start us, length us, event | category | flops | bytes accessed | tf_op | source)
XLA Modules:
  0.0 971.2 jit_solution(5604241951854628806)
XLA Ops:
  14.2 7.6 shard_map.482
  27.3 3.7 fusion.99
  34.9 7.4 fusion.211
  47.3 2.5 exponential_reduce_fusion.1
  55.9 95.7 %shard_map.479.base_ref = f32[512,1024]{1,0:T(8,128)S(1)} custom-call(f32[512,1024]{1,0:T(8,128)S(1)} %fusion.119.part_ref, f32[512,1024]{1,0:T(8,128)S(1)} %bitcast.778), custom_call_target="tpu_custom_call" | custom-call | flops 2097152 | bytes 8388608 | tf_op jit(solution)/shard_map/pallas_call | solution.py:281
  152.5 2.8 fusion.57
  160.8 54.6 %shard_map.480 = f32[512,1024]{1,0:T(8,128)S(1)} custom-call(f32[512,1024]{1,0:T(8,128)S(1)} %fusion.117.part_ref, f32[512,1024]{1,0:T(8,128)S(1)} %shard_map.479.base_ref), custom_call_target="tpu_custom_call" | custom-call | flops 2097152 | bytes 8388608 | tf_op jit(solution)/shard_map/pallas_call | solution.py:281
  224.8 3.8 fusion.125
  228.6 5.7 multiply_convert_fusion.7
  235.6 32.8 %shard_map.481 = f32[128,1024]{1,0:T(8,128)S(1)} custom-call(f32[512,1024]{1,0:T(8,128)S(1)} %bitcast.779), custom_call_target="tpu_custom_call" | custom-call | flops 1048576 | bytes 4194304 | tf_op jit(solution)/shard_map/pallas_call | solution.py:419
  272.5 3.2 fusion.3
  275.7 5.5 broadcast_add_fusion
  288.8 2.7 convolution_convert_fusion.11
  293.4 3.3 convolution_convert_fusion.5
  301.4 3.7 fusion.222
  317.3 2.5 multiply_convert_fusion.1
  324.9 36.2 %shard_map.483.base_ref = f32[512,1024]{1,0:T(8,128)S(1)} custom-call(f32[128,1024]{1,0:T(8,128)S(1)} %fusion.116.own_ref), custom_call_target="tpu_custom_call" | custom-call | flops 131072 | bytes 4194304 | tf_op jit(solution)/shard_map/pallas_call | solution.py:512
  365.0 3.7 fusion.28
  369.4 53.1 %shard_map.484.base_ref = f32[512,1024]{1,0:T(8,128)S(1)} custom-call(f32[512,1024]{1,0:T(8,128)S(1)} %bitcast.776, f32[512,1024]{1,0:T(8,128)S(1)} %shard_map.483.base_ref), custom_call_target="tpu_custom_call" | custom-call | flops 2097152 | bytes 8388608 | tf_op jit(solution)/shard_map/pallas_call | solution.py:281
  434.0 3.6 fusion.27
  439.1 52.5 %shard_map.485 = f32[512,1024]{1,0:T(8,128)S(1)} custom-call(f32[512,1024]{1,0:T(8,128)S(1)} %bitcast.777, f32[512,1024]{1,0:T(8,128)S(1)} %copy-done.6), custom_call_target="tpu_custom_call" | custom-call | flops 2097152 | bytes 8388608 | tf_op jit(solution)/shard_map/pallas_call | solution.py:281
  496.5 7.0 convolution_convert_fusion.2
  503.5 5.5 multiply_reduce_fusion.2
  511.4 2.9 convert_reduce_fusion
  518.6 5.0 fusion.21
  532.6 7.7 multiply_reduce_fusion
  540.4 5.1 fusion.19
  545.6 11.2 %fusion.85 = f32[12,512]{1,0:T(8,128)S(1)} fusion(f32[12,512]{1,0:T(8,128)S(1)} %fusion.19, f32[4,12,1024]{2,1,0:T(8,128)S(1)} %copy-done.41, f32[4,1024,512]{1,2,0:T(8,128)} %get-tuple-element.187, f32[4,1024,512]{1,2,0:T(8,128)} %copy-done.7, f32[4,1024]{1,0:T(4,128)S(1)} %broadcast_multiply_fusion.1, f32[4,1024]{1,0:T(4,128)S(1)} %broadcast_multiply_fusion.2, ...), kind=kOutput, calls=%fused_computation.210 | convolution fusion | flops 316676096 | bytes 17090560 | tf_op jit(solution)/shard_map/bcp,bpd->cd/dot_general | solution.py:958
  561.6 4.4 fusion.75
  572.3 4.2 convolution_bitcast_fusion.2
  576.5 3.5 copy.212
  581.9 2.7 convolution_bitcast_fusion
  584.7 5.4 copy.206
  590.1 5.4 copy.368
  595.5 4.3 convolution_bitcast_fusion.3
  599.8 2.9 copy.209
  602.7 3.3 copy.371
  606.0 2.7 convolution_bitcast_fusion.1
  608.6 5.4 copy.204
  614.1 4.6 copy.369
  620.7 8.7 pad_maximum_fusion
  666.5 85.7 %reduce-scatter.12.cloned.1.call-done = f32[1,4,384,256]{3,2,1,0:T(8,128)} async-done(((f32[8,4,384,256]{3,2,1,0:T(8,128)}), f32[1,4,384,256]{3,2,1,0:T(8,128)}) %reduce-scatter.12.cloned.1.call-update) | async-done | bytes 1572880 | tf_op jit(solution)/shard_map/reduce_scatter | solution.py:861
  754.9 52.3 %reduce-scatter.8.cloned.1.call-done = f32[1,512,256]{2,1,0:T(8,128)} async-done(((f32[8,512,256]{2,1,0:T(8,128)}), f32[1,512,256]{2,1,0:T(8,128)}) %reduce-scatter.8.cloned.1.call-update) | async-done | bytes 524304 | tf_op jit(solution)/shard_map/reduce_scatter | solution.py:866
  810.9 70.9 %reduce-scatter.10.cloned.1.call-done = f32[1,1024,256]{2,1,0:T(8,128)} async-done(((f32[8,1024,256]{2,1,0:T(8,128)}), f32[1,1024,256]{2,1,0:T(8,128)}) %reduce-scatter.10.cloned.1.call-update) | async-done | bytes 1048592 | tf_op jit(solution)/shard_map/reduce_scatter | solution.py:866
  889.9 29.6 %reduce-scatter.14.cloned.1.call-done = f32[1,384,256]{2,1,0:T(8,128)} async-done(((f32[4,384,256]{2,1,0:T(8,128)}), f32[1,384,256]{2,1,0:T(8,128)}) %reduce-scatter.14.cloned.1.call-update) | async-done | bytes 393232 | tf_op jit(solution)/shard_map/reduce_scatter | solution.py:860
  928.3 10.9 %shard_map.486 = f32[8,128]{1,0:T(8,128)} custom-call(f32[8,128]{1,0:T(8,128)} %iota.19.tile_ref), custom_call_target="tpu_custom_call" | custom-call | tf_op jit(solution)/shard_map/pallas_call | solution.py:585
  942.6 3.2 multiply_subtract_fusion.1
  955.1 4.5 multiply_subtract_fusion
  (552 shorter events, 199.1 us)
Async XLA Ops:
  7.2 268.5 %all-gather.3.cloned.1.call-start = ((), (), s32[]{:S(2)}) async-start(), calls=%async_computation.11 | async-start | bytes 12976128 | tf_op jit(solution)/shard_map/all_gather | solution.py:667
  8.2 14.8 %copy-start.111 = (bf16[11,512]{1,0:T(8,128)(2,1)S(1)}, bf16[11,512]{1,0:T(8,128)(2,1)}, u32[]{:S(2)}) copy-start(bf16[11,512]{1,0:T(8,128)(2,1)} %param.41) | copy-start | bytes 33796
  8.3 15.3 %copy-start.33 = (bf16[128,1024]{1,0:T(8,128)(2,1)S(1)}, bf16[128,1024]{1,0:T(8,128)(2,1)}, u32[]{:S(2)}) copy-start(bf16[128,1024]{1,0:T(8,128)(2,1)} %param.40) | copy-start | bytes 786436
  11.5 607.6 %reduce-scatter.6.cloned.1.call-start = ((), (), s32[]{:S(2)}) async-start(), calls=%async_computation.5 | async-start | bytes 4276224 | tf_op jit(solution)/shard_map/reduce_scatter | solution.py:994
  23.6 128.5 %copy-start.104 = (f32[1,4,2,128]{3,1,2,0:T(4,128)}, f32[1,4,2,128]{3,1,2,0:T(4,128)S(1)}, u32[]{:S(2)}) copy-start(f32[1,4,2,128]{3,1,2,0:T(4,128)S(1)} %copy.313) | copy-start | bytes 12292
  23.6 7.5 copy-start.91
  24.0 7.1 copy-start.137
  33.9 15.9 %copy-start.88 = (f32[1,512]{1,0:T(1,128)}, f32[1,512]{1,0:T(1,128)S(1)}, u32[]{:S(2)}) copy-start(f32[1,512]{1,0:T(1,128)S(1)} %get-tuple-element.150) | copy-start | bytes 6148
  34.9 7.4 copy-start.40
  42.3 7.5 copy-start.7
  159.1 56.4 %copy-start.45 = (bf16[4,4,64,128]{3,2,1,0:T(8,128)(2,1)}, bf16[4,4,64,128]{3,2,1,0:T(8,128)(2,1)S(1)}, u32[]{:S(2)}) copy-start(bf16[4,4,64,128]{3,2,1,0:T(8,128)(2,1)S(1)} %convolution_convert_fusion.12) | copy-start | bytes 786436
  219.1 5.3 copy-start.106
  219.1 5.3 copy-start.3
  224.7 9.5 copy-start.81
  224.7 43.6 %slice-start = ((s8[8388608]{0:T(1024)(128)(4,1)}), s8[4194304]{0:T(1024)(128)(4,1)S(1)}, s32[]{:S(2)}) async-start(s8[8388608]{0:T(1024)(128)(4,1)} %bitcast.780), calls=%async_computation.12 | async-start | bytes 8388608
  228.6 5.7 copy-start.64
  228.6 39.8 %slice-start.1 = ((s8[8388608]{0:T(1024)(128)(4,1)}), s8[4194304]{0:T(1024)(128)(4,1)S(1)}, s32[]{:S(2)}) async-start(s8[8388608]{0:T(1024)(128)(4,1)} %bitcast.780), calls=%async_computation.13 | async-start | bytes 8388608
  234.3 37.7 %slice-start.4 = ((s8[8388608]{0:T(1024)(128)(4,1)}), s8[4194304]{0:T(1024)(128)(4,1)S(1)}, s32[]{:S(2)}) async-start(s8[8388608]{0:T(1024)(128)(4,1)} %bitcast.784), calls=%async_computation.16 | async-start | bytes 8388608
  235.6 36.4 %slice-start.5 = ((s8[8388608]{0:T(1024)(128)(4,1)}), s8[4194304]{0:T(1024)(128)(4,1)S(1)}, s32[]{:S(2)}) async-start(s8[8388608]{0:T(1024)(128)(4,1)} %bitcast.784), calls=%async_computation.17 | async-start | bytes 8388608
  322.9 38.4 %copy-start.82 = (bf16[6,256,1024]{2,1,0:T(8,128)(2,1)S(1)}, bf16[6,256,1024]{2,1,0:T(8,128)(2,1)}, u32[]{:S(2)}) copy-start(bf16[6,256,1024]{2,1,0:T(8,128)(2,1)} %param.38) | copy-start | bytes 9437188
  324.9 36.4 %copy-start.66 = (f32[4,128,4,256]{3,1,2,0:T(8,128)S(1)}, f32[4,128,4,256]{3,1,2,0:T(8,128)}, u32[]{:S(2)}) copy-start(f32[4,128,4,256]{3,1,2,0:T(8,128)} %get-tuple-element.116) | copy-start | bytes 6291460
  496.5 7.0 copy-start.15
  496.5 12.5 %slice-start.2 = ((s8[8388608]{0:T(1024)(128)(4,1)}), s8[4194304]{0:T(1024)(128)(4,1)S(1)}, s32[]{:S(2)}) async-start(s8[8388608]{0:T(1024)(128)(4,1)} %bitcast.782), calls=%async_computation.14 | async-start | bytes 8388608
  503.5 5.6 slice-start.3
  532.6 7.8 copy-start.41
  545.5 12.1 %copy-start.110 = (f32[2,8,64]{2,1,0:T(8,128)S(1)}, f32[2,8,64]{2,1,0:T(8,128)}, u32[]{:S(2)}) copy-start(f32[2,8,64]{2,1,0:T(8,128)} %concatenate.43) | copy-start | bytes 12292
  545.5 12.1 %copy-start.109 = (f32[2,8,64]{2,1,0:T(8,128)S(1)}, f32[2,8,64]{2,1,0:T(8,128)}, u32[]{:S(2)}) copy-start(f32[2,8,64]{2,1,0:T(8,128)} %concatenate.44) | copy-start | bytes 12292
  545.5 12.1 %copy-start.108 = (f32[2,8,64]{2,1,0:T(8,128)S(1)}, f32[2,8,64]{2,1,0:T(8,128)}, u32[]{:S(2)}) copy-start(f32[2,8,64]{2,1,0:T(8,128)} %concatenate.45) | copy-start | bytes 12292
  545.6 12.1 %copy-start.124 = (f32[1,8,64]{2,1,0:T(8,128)S(1)}, f32[1,8,64]{2,1,0:T(8,128)}, u32[]{:S(2)}) copy-start(f32[1,8,64]{2,1,0:T(8,128)} %concatenate.47) | copy-start | bytes 6148
  545.6 12.1 %copy-start.123 = (f32[1,8,64]{2,1,0:T(8,128)S(1)}, f32[1,8,64]{2,1,0:T(8,128)}, u32[]{:S(2)}) copy-start(f32[1,8,64]{2,1,0:T(8,128)} %concatenate.48) | copy-start | bytes 6148
  570.7 91.7 %all-reduce.3.cloned.1.call-start = ((), (), s32[]{:S(2)}) async-start(), calls=%async_computation.10 | async-start | bytes 163840 | tf_op jit(solution)/shard_map/psum | solution.py:996
  590.1 5.4 copy-start.61
  590.1 5.4 copy-start.122
  620.7 131.6 %reduce-scatter.12.cloned.1.call-start = ((), (), s32[]{:S(2)}) async-start(), calls=%async_computation.8 | async-start | bytes 14155776 | tf_op jit(solution)/shard_map/reduce_scatter | solution.py:861
  629.4 177.8 %reduce-scatter.8.cloned.1.call-start = ((), (), s32[]{:S(2)}) async-start(), calls=%async_computation.6 | async-start | bytes 4718592 | tf_op jit(solution)/shard_map/reduce_scatter | solution.py:866
  637.3 244.4 %reduce-scatter.10.cloned.1.call-start = ((), (), s32[]{:S(2)}) async-start(), calls=%async_computation.7 | async-start | bytes 9437184 | tf_op jit(solution)/shard_map/reduce_scatter | solution.py:866
  654.8 264.7 %reduce-scatter.14.cloned.1.call-start = ((), (), s32[]{:S(2)}) async-start(), calls=%async_computation.9 | async-start | bytes 1966080 | tf_op jit(solution)/shard_map/reduce_scatter | solution.py:860
  885.5 57.1 %copy-start.69 = (f32[80,256]{1,0:T(8,128)S(1)}, f32[80,256]{1,0:T(8,128)}, u32[]{:S(2)}) copy-start(f32[80,256]{1,0:T(8,128)} %all-reduce.3.cloned.1.call-done) | copy-start | bytes 245764
  942.6 5.7 copy-start.125
  942.6 5.7 copy-start.126
  942.6 5.7 copy-start.127
  945.8 5.4 copy-start.38
  945.8 6.6 copy-start.129
  945.8 6.6 copy-start.130
  945.8 6.6 copy-start.131
  955.1 5.2 copy-start.96
  955.1 5.2 copy-start.97
  955.1 6.7 copy-start.1
  (105 other events, 249.9 us)
Sparse Core Ops, SparseCore 0:
  11.6 128.8 all-gather.2
  570.8 48.2 reduce-scatter.5
  622.0 33.9 all-reduce.2
  659.8 92.4 reduce-scatter.11
  755.8 51.3 reduce-scatter.7
  810.5 71.2 reduce-scatter.9
  884.2 35.2 reduce-scatter.13

commit v2 on v1

--- a/solution.py
+++ b/solution.py
@@ -109,6 +109,7 @@
 MESH_ID = pl.DeviceIdType.MESH
 VMEM_SPEC = pl.BlockSpec(memory_space=pltpu.VMEM)
 CHUNKS = 32
+VMEM_LIMIT = 56 << 20
 
 
 def remote(source, target, send_sem, recv_sem, device):
@@ -122,7 +123,148 @@
     )
 
 
-def greet_line(place, count):
+class PieceSums:
+    def __init__(self, count, items, outs, scratch):
+        self.count, self.items, self.outs = count, items, outs
+        self.bits = count.bit_length() - 1
+        self.place = lax.axis_index("dp") if items else None
+        self.held = []
+        for index in range(len(items)):
+            self.held.append(scratch[index * (self.bits + 2) : (index + 1) * (self.bits + 2)])
+
+    @staticmethod
+    def scratch(count, shapes):
+        bits = count.bit_length() - 1
+        result = []
+        for rows, width in shapes:
+            result.append(pltpu.VMEM((count // 2, rows, width), jnp.float32))
+            for phase in range(2, bits + 1):
+                result.append(
+                    pltpu.VMEM((2 * (count >> phase), rows // 2, width), jnp.float32)
+                )
+            copies = count // 2 + 2 * sum(count >> phase for phase in range(2, bits + 1))
+            result += [pltpu.SemaphoreType.DMA((copies,))] * 2
+        return result
+
+    def peers(self):
+        return [{"dp": self.place ^ (1 << bit)} for bit in range(self.bits)] if self.items else []
+
+    def order(self, half):
+        later = list(range(1, self.bits))
+        turn = half * (len(later) // 2)
+        return later[turn:] + later[:turn]
+
+    def first_copy(self, index, piece):
+        item, held = self.items[index], self.held[index]
+        other = 1 - (self.place & 1)
+        return remote(
+            item.at[2 * piece + other],
+            held[0].at[piece],
+            held[-2].at[piece],
+            held[-1].at[piece],
+            {"dp": self.place ^ 1},
+        )
+
+    def member(self, half, phase, entry, flip):
+        bits = self.order(half)
+        settled, now, rest = bits[: phase - 2], bits[phase - 2], bits[phase - 1 :]
+        piece = 0
+        for bit in settled:
+            piece = piece | (self.place & (1 << bit))
+        own = self.place & (1 << now)
+        piece = piece | ((own ^ (1 << now)) if flip else own)
+        for position, bit in enumerate(rest):
+            if (entry >> position) & 1:
+                piece = piece | (1 << bit)
+        return piece >> 1
+
+    def later_copy(self, index, half, phase, entry):
+        held = self.held[index]
+        rows = self.items[index].shape[1] // 2
+        size = self.count >> phase
+        sem = self.count // 2 + 2 * sum(self.count >> p for p in range(2, phase)) + half * size + entry
+        return remote(
+            held[0].at[self.member(half, phase, entry, True), pl.ds(half * rows, rows)],
+            held[phase - 1].at[half * size + entry],
+            held[-2].at[sem],
+            held[-1].at[sem],
+            {"dp": self.place ^ (1 << self.order(half)[phase - 2])},
+        )
+
+    def entries(self, phase):
+        return [
+            (index, half, entry)
+            for index in range(len(self.items))
+            for half in range(2)
+            for entry in range(self.count >> phase)
+        ]
+
+    def begin(self):
+        for index in range(len(self.items)):
+            for piece in range(self.count // 2):
+                self.first_copy(index, piece).start()
+
+    def send(self, phase):
+        for index, half, entry in self.entries(phase):
+            self.later_copy(index, half, phase, entry).start()
+
+    def advance(self, phase):
+        if not self.items:
+            return
+        if phase == 1:
+            own = self.place & 1
+            for index, item in enumerate(self.items):
+                total = self.held[index][0]
+                for piece in range(self.count // 2):
+                    self.first_copy(index, piece).wait_recv()
+                    add_rows(total.at[piece], total.at[piece], item.at[2 * piece + own])
+        else:
+            for index, half, entry in self.entries(phase):
+                self.later_copy(index, half, phase, entry).wait_recv()
+                held, rows = self.held[index], self.items[index].shape[1] // 2
+                where = pl.ds(half * rows, rows)
+                came = held[phase - 1].at[half * (self.count >> phase) + entry]
+                kept = held[0].at[self.member(half, phase, entry, False), where]
+                if phase == self.bits:
+                    add_rows(self.outs[index].at[where], kept, came)
+                else:
+                    add_rows(kept, kept, came)
+        if phase < self.bits:
+            self.send(phase + 1)
+
+    def finish(self):
+        for index in range(len(self.items)):
+            for piece in range(self.count // 2):
+                self.first_copy(index, piece).wait_send()
+        for phase in range(2, self.bits + 1):
+            for index, half, entry in self.entries(phase):
+                self.later_copy(index, half, phase, entry).wait_send()
+
+    def moments(self, total):
+        if not self.items:
+            return [(0, total, None)]
+        marks, low = [], 0
+        for phase in range(1, self.bits + 1):
+            share = (1 - 0.5 ** (phase - 1)) / (1 - 0.5 ** (self.bits - 1))
+            high = total if phase == self.bits else int(total * (0.22 + 0.78 * share))
+            marks.append((low, high, phase))
+            low = high
+        return marks
+
+
+def add_rows(target, left, right):
+    rows, width = target.shape
+    step = math.gcd(rows, max(8, 8192 // width))
+
+    def one(index, carry):
+        where = pl.ds(pl.multiple_of(index * step, step), step)
+        target[where] = left[where] + right[where]
+        return carry
+
+    lax.fori_loop(0, rows // step, one, 0)
+
+
+def greet(place, count, others=()):
     barrier = pltpu.get_barrier_semaphore()
     below, above = {"mp": place - 1}, {"mp": place + 1}
 
@@ -134,30 +276,24 @@
     def _():
         pl.semaphore_signal(barrier, inc=1, device_id=above, device_id_type=MESH_ID)
 
+    for other in others:
+        pl.semaphore_signal(barrier, inc=1, device_id=other, device_id_type=MESH_ID)
     inside = jnp.logical_and(place > 0, place < count - 1)
 
     @pl.when(inside)
     def _():
-        pl.semaphore_wait(barrier, 2)
+        pl.semaphore_wait(barrier, 2 + len(others))
 
     @pl.when(jnp.logical_not(inside))
     def _():
-        pl.semaphore_wait(barrier, 1)
-
-
-def line_sum_kernel(
-    count,
-    part_ref,
-    base_ref,
-    out_ref,
-    inner,
-    from_away,
-    from_toward,
-    toward_send,
-    away_send,
-    away_recv,
-    toward_recv,
-):
+        pl.semaphore_wait(barrier, 1 + len(others))
+
+
+def line_sum_kernel(count, count_dp, extra, part_ref, base_ref, *refs):
+    items, out_ref, outs = refs[:extra], refs[extra], refs[extra + 1 : 2 * extra + 1]
+    inner, from_away, from_toward = refs[2 * extra + 1 : 2 * extra + 4]
+    toward_send, away_send, away_recv, toward_recv = refs[2 * extra + 4 : 2 * extra + 8]
+    sums = PieceSums(count_dp, items, outs, refs[2 * extra + 8 :])
     place = lax.axis_index("mp")
     half = count // 2
     low_side = place < half
@@ -167,7 +303,8 @@
     outermost = jnp.logical_or(place == 0, place == count - 1)
     chunks = toward_send.shape[0]
     rows = part_ref.shape[0] // chunks
-    greet_line(place, count)
+    greet(place, count, sums.peers())
+    sums.begin()
 
     def window(step):
         return pl.ds(pl.multiple_of(step * rows, rows), rows)
@@ -210,7 +347,9 @@
             push(step, part_ref, False).wait_send()
             return carry
 
-        lax.fori_loop(0, chunks, arrive, 0)
+        for low, high, phase in sums.moments(chunks):
+            lax.fori_loop(low, high, arrive, 0)
+            sums.advance(phase)
 
     lag = 2
 
@@ -243,8 +382,11 @@
             return carry
 
         lax.fori_loop(0, lag, first, 0)
-        lax.fori_loop(lag, chunks, both, 0)
-        lax.fori_loop(chunks - lag, chunks, last, 0)
+        for low, high, phase in sums.moments(chunks):
+            lax.fori_loop(max(low, lag), high, both, 0)
+            if high == chunks:
+                lax.fori_loop(chunks - lag, chunks, last, 0)
+            sums.advance(phase)
         lax.fori_loop(0, chunks, drain, 0)
 
     if count > 4:
@@ -268,30 +410,45 @@
                 return carry
 
             lax.fori_loop(0, chunks, inwards, 0)
-            lax.fori_loop(0, chunks, outwards, 0)
+            for low, high, phase in sums.moments(chunks):
+                lax.fori_loop(low, high, outwards, 0)
+                sums.advance(phase)
             lax.fori_loop(0, chunks, drain, 0)
 
-
-def line_sum(part, base, call_id):
+    sums.finish()
+
+
+def piece_shapes(items):
+    count = lax.axis_size("dp")
+    items = [item.reshape(count, -1, item.shape[-1]) for item in items]
+    shapes = [item.shape[1:] for item in items]
+    return items, shapes, [jax.ShapeDtypeStruct(shape, jnp.float32) for shape in shapes]
+
+
+def line_sum(part, base, call_id, items=()):
     shape = part.shape
+    items, shapes, shares = piece_shapes(items)
+    extra = len(items)
     part = part.reshape(-1, shape[-1])
     rows, width = part.shape
     buffer = pltpu.VMEM((rows, width), jnp.float32)
     sems = pltpu.SemaphoreType.DMA((CHUNKS,))
-    out = pl.pallas_call(
-        partial(line_sum_kernel, lax.axis_size("mp")),
-        out_shape=jax.ShapeDtypeStruct((rows, width), jnp.float32),
-        in_specs=[VMEM_SPEC] * 2,
-        out_specs=VMEM_SPEC,
-        scratch_shapes=[buffer] * 3 + [sems] * 4,
+    results = pl.pallas_call(
+        partial(line_sum_kernel, lax.axis_size("mp"), lax.axis_size("dp"), extra),
+        out_shape=[jax.ShapeDtypeStruct((rows, width), jnp.float32)] + shares,
+        in_specs=[VMEM_SPEC] * (2 + extra),
+        out_specs=[VMEM_SPEC] * (1 + extra),
+        scratch_shapes=[buffer] * 3
+        + [sems] * 4
+        + PieceSums.scratch(lax.axis_size("dp"), shapes),
         compiler_params=pltpu.CompilerParams(
-            collective_id=call_id, has_side_effects=True, vmem_limit_bytes=24 << 20
+            collective_id=call_id, has_side_effects=True, vmem_limit_bytes=VMEM_LIMIT
         ),
         cost_estimate=pl.CostEstimate(
-            flops=4 * rows * width, bytes_accessed=16 * rows * width, transcendentals=0
+            flops=4 * rows * width, bytes_accessed=350 * rows * width, transcendentals=0
         ),
-    )(part, base.reshape(part.shape))
-    return out.reshape(shape)
+    )(part, base.reshape(part.shape), *items)
+    return results[0].reshape(shape), results[1:]
 
 
 def line_scatter_kernel(
@@ -302,7 +459,7 @@
     block = part_ref.shape[0] // count
     rows = block // steps
     below, above = {"mp": place - 1}, {"mp": place + 1}
-    greet_line(place, count)
+    greet(place, count)
 
     def window(owner, step):
         return pl.ds(pl.multiple_of(owner * block + step * rows, rows), rows)
@@ -426,18 +583,22 @@
             collective_id=call_id, has_side_effects=True, vmem_limit_bytes=24 << 20
         ),
         cost_estimate=pl.CostEstimate(
-            flops=2 * rows * width, bytes_accessed=8 * rows * width, transcendentals=0
+            flops=2 * rows * width, bytes_accessed=230 * rows * width, transcendentals=0
         ),
     )(part)
 
 
-def line_gather_kernel(count, own_ref, out_ref, up_send, down_send, up_recv, down_recv):
+def line_gather_kernel(count, count_dp, extra, own_ref, *refs):
+    items, out_ref, outs = refs[:extra], refs[extra], refs[extra + 1 : 2 * extra + 1]
+    up_send, down_send, up_recv, down_recv = refs[2 * extra + 1 : 2 * extra + 5]
+    sums = PieceSums(count_dp, items, outs, refs[2 * extra + 5 :])
     place = lax.axis_index("mp")
     steps = up_send.shape[1]
     block = own_ref.shape[0]
     rows = block // steps
     below, above = {"mp": place - 1}, {"mp": place + 1}
-    greet_line(place, count)
+    greet(place, count, sums.peers())
+    sums.begin()
 
     def window(owner, step):
         return pl.ds(pl.multiple_of(owner * block + step * rows, rows), rows)
@@ -486,7 +647,9 @@
 
         return carry
 
-    lax.fori_loop(0, (count - 1) * steps, pass_on, 0)
+    for low, high, phase in sums.moments((count - 1) * steps):
+        lax.fori_loop(low, high, pass_on, 0)
+        sums.advance(phase)
 
     def drain(index, carry):
         owner, step = index // steps, lax.rem(index, steps)
@@ -502,26 +665,56 @@
         return carry
 
     lax.fori_loop(0, count * steps, drain, 0)
-
-
-def line_gather(own, call_id):
+    sums.finish()
+
+
+def line_gather(own, call_id, items=()):
     rows, width = own.shape
     count = lax.axis_size("mp")
     steps = 8
     sems = pltpu.SemaphoreType.DMA((count, steps))
-    return pl.pallas_call(
-        partial(line_gather_kernel, count),
-        out_shape=jax.ShapeDtypeStruct((rows * count, width), jnp.float32),
-        in_specs=[VMEM_SPEC],
-        out_specs=VMEM_SPEC,
-        scratch_shapes=[sems] * 4,
+    items, shapes, shares = piece_shapes(items)
+    extra = len(items)
+    results = pl.pallas_call(
+        partial(line_gather_kernel, count, lax.axis_size("dp"), extra),
+        out_shape=[jax.ShapeDtypeStruct((rows * count, width), jnp.float32)] + shares,
+        in_specs=[VMEM_SPEC] * (1 + extra),
+        out_specs=[VMEM_SPEC] * (1 + extra),
+        scratch_shapes=[sems] * 4 + PieceSums.scratch(lax.axis_size("dp"), shapes),
         compiler_params=pltpu.CompilerParams(
-            collective_id=call_id, has_side_effects=True, vmem_limit_bytes=16 << 20
+            collective_id=call_id, has_side_effects=True, vmem_limit_bytes=VMEM_LIMIT
         ),
         cost_estimate=pl.CostEstimate(
-            flops=rows * width, bytes_accessed=8 * rows * width * count, transcendentals=0
+            flops=rows * width, bytes_accessed=250 * rows * width * count, transcendentals=0
         ),
-    )(own)
+    )(own, *items)
+    return results[0], results[1:]
+
+
+def piece_sums_kernel(count_dp, extra, *refs):
+    sums = PieceSums(count_dp, refs[:extra], refs[extra : 2 * extra], refs[2 * extra :])
+    barrier = pltpu.get_barrier_semaphore()
+    for other in sums.peers():
+        pl.semaphore_signal(barrier, inc=1, device_id=other, device_id_type=MESH_ID)
+    pl.semaphore_wait(barrier, len(sums.peers()))
+    sums.begin()
+    for phase in range(1, sums.bits + 1):
+        sums.advance(phase)
+    sums.finish()
+
+
+def piece_sums(items, call_id):
+    items, shapes, shares = piece_shapes(items)
+    return pl.pallas_call(
+        partial(piece_sums_kernel, lax.axis_size("dp"), len(items)),
+        out_shape=shares,
+        in_specs=[VMEM_SPEC] * len(items),
+        out_specs=[VMEM_SPEC] * len(items),
+        scratch_shapes=PieceSums.scratch(lax.axis_size("dp"), shapes),
+        compiler_params=pltpu.CompilerParams(
+            collective_id=call_id, has_side_effects=True, vmem_limit_bytes=VMEM_LIMIT
+        ),
+    )(*items)
 
 
 def mesh_sum_kernel(axes, tile_ref, out_ref, held, send_sem, recv_sem):
@@ -665,14 +858,15 @@
     query_piece = dp_piece(copy_narrowin[:, 2], 0)
     out_piece = dp_piece(copy_narrowout, 1).T
     gathered = lax.all_gather(
-        jnp.concatenate([key_piece, value_piece, query_piece, out_piece], 0), ("mp", "dp")
-    ).reshape(count_mp, count_dp, -1, local)
+        jnp.concatenate([key_piece, value_piece, query_piece, out_piece], 0), "mp"
+    )
+    gathered = lax.all_gather(gathered, "dp")
     nothing = jnp.where(timesteps[0] > 0, 0.0, -0.0)
     gathered = gathered + nothing
     edges = [0, d_lat, 2 * d_lat, 2 * d_lat + d_if, 2 * d_lat + 2 * d_if]
     write_key_weight, write_value_weight, write_query_weight, write_out_weight = (
-        gathered[:, :, low // count_dp : high // count_dp]
-        .reshape(count_mp, high - low, local)
+        jnp.swapaxes(gathered[:, :, low // count_dp : high // count_dp], 1, 2)
+        .reshape(high - low, count_mp * local)
         .astype(jnp.bfloat16)
         for low, high in zip(edges[:-1], edges[1:])
     )
@@ -715,7 +909,7 @@
         jnp.einsum("blc,cd->bld", read_out, copy_wideout[0], preferred_element_type=jnp.float32),
         jnp.broadcast_to(latent_zero[None], (images, latents, d_lat)),
         2,
-    )
+    )[0]
     self_norm, self_stats = layer_norm(latent_one, wide_gain(1))
     self_low = self_norm.astype(jnp.bfloat16)
     self_triple = jnp.einsum(
@@ -728,7 +922,7 @@
         jnp.einsum("blc,cd->bld", self_out, copy_wideout[1], preferred_element_type=jnp.float32),
         latent_one,
         3,
-    )
+    )[0]
     feed_norm, feed_stats = layer_norm(latent_two, wide_gain(2))
     feed_low = feed_norm.astype(jnp.bfloat16)
     hidden = jnp.einsum(
@@ -764,7 +958,7 @@
 
     def join(spec, values, weight):
         product = jnp.einsum(spec, values, weight, preferred_element_type=jnp.float32)
-        return product.astype(jnp.bfloat16).reshape(product.shape[:2] + (-1,))
+        return product.astype(jnp.bfloat16)
 
     def image_rows(values):
         if sharers == 1:
@@ -774,13 +968,12 @@
         whole = whole.reshape(images, latents, d_lat).astype(jnp.bfloat16)
         return lax.dynamic_slice_in_dim(whole, first_image, own_images, 0)
 
-    write_query = join("bpd,mdc->bpmc", outer_low, write_query_weight)
-    write_key = image_rows(join("bld,mdc->blmc", write_low, write_key_weight))
-    write_value = image_rows(join("bld,mdc->blmc", write_low, write_value_weight))
+    write_query = join("bpd,dc->bpc", outer_low, write_query_weight)
+    write_key = image_rows(join("bld,dc->blc", write_low, write_key_weight))
+    write_value = image_rows(join("bld,dc->blc", write_low, write_value_weight))
     write_out, write_total = attend_forward(write_query, write_key, write_value, None)
-    write_split = write_out.reshape(write_out.shape[:2] + (count_mp, local))
     outer = own_interface + jnp.einsum(
-        "bpmc,mdc->bpd", write_split, write_out_weight, preferred_element_type=jnp.float32
+        "bpc,dc->bpd", write_out, write_out_weight, preferred_element_type=jnp.float32
     )
     final_norm, final_stats = layer_norm(outer, gain_rows[10])
     final_low = final_norm.astype(jnp.bfloat16)
@@ -800,18 +993,17 @@
     outer_grad, gain_final = norm_back(final_grad, gain_rows[10], final_stats)
     branch_low = outer_grad.astype(jnp.bfloat16)
     narrowout_grad = jnp.einsum(
-        "bpd,bpmc->mdc", branch_low, write_split, preferred_element_type=jnp.float32
-    )
-    write_upstream = join("bpd,mdc->bpmc", branch_low, write_out_weight)
+        "bpd,bpc->dc", branch_low, write_out, preferred_element_type=jnp.float32
+    )
+    write_upstream = join("bpd,dc->bpc", branch_low, write_out_weight)
     query_grad, key_grad, value_grad = attend_back(
         write_query, write_key, write_value, None, write_total, write_upstream
     )
-    query_split = query_grad.reshape(query_grad.shape[:2] + (count_mp, local))
     write_query_grad = jnp.einsum(
-        "bpd,bpmc->mdc", outer_low, query_split, preferred_element_type=jnp.float32
+        "bpd,bpc->dc", outer_low, query_grad, preferred_element_type=jnp.float32
     )
     outer_part = jnp.einsum(
-        "bpmc,mdc->bpd", query_split, write_query_weight, preferred_element_type=jnp.float32
+        "bpc,dc->bpd", query_grad, write_query_weight, preferred_element_type=jnp.float32
     )
 
     def row_grad(values):
@@ -824,46 +1016,28 @@
                 scatter_dimension=0,
                 tiled=True,
             )
-        values = values.astype(jnp.bfloat16)
-        return values.reshape(values.shape[:2] + (count_mp, local))
+        return values.astype(jnp.bfloat16)
 
     key_grad, value_grad = row_grad(key_grad), row_grad(value_grad)
     write_key_grad = jnp.einsum(
-        "bld,blmc->mdc", write_low, key_grad, preferred_element_type=jnp.float32
+        "bld,blc->dc", write_low, key_grad, preferred_element_type=jnp.float32
     )
     write_value_grad = jnp.einsum(
-        "bld,blmc->mdc", write_low, value_grad, preferred_element_type=jnp.float32
+        "bld,blc->dc", write_low, value_grad, preferred_element_type=jnp.float32
     )
     write_part = jnp.einsum(
-        "blmc,mdc->bld", key_grad, write_key_weight, preferred_element_type=jnp.float32
+        "blc,dc->bld", key_grad, write_key_weight, preferred_element_type=jnp.float32
     ) + jnp.einsum(
-        "blmc,mdc->bld", value_grad, write_value_weight, preferred_element_type=jnp.float32
+        "blc,dc->bld", value_grad, write_value_weight, preferred_element_type=jnp.float32
     )
     own_grad, gain_write = norm_back(write_part, wide_gain(3), write_stats)
-    latent_grad = line_gather(own_grad.reshape(-1, d_lat), 5).reshape(latent_one.shape)
     outer_back, gain_outer = norm_back(outer_part, gain_rows[9], outer_stats)
 
-    def pieces(values, groups):
-        return values.reshape(groups, -1, local)
-
-    def both_pieces(values):
-        values = values.reshape(count_mp, count_dp, -1, local)
-        return jnp.swapaxes(values, 0, 1)
-
-    write_joined = jnp.concatenate(
-        [
-            both_pieces(item)
-            for item in (write_key_grad, write_value_grad, write_query_grad, narrowout_grad)
-        ],
-        2,
-    )
-    write_share = lax.psum_scatter(
-        lax.psum_scatter(write_joined, "dp", scatter_dimension=0), "mp", scatter_dimension=0
-    )
-
-    def dp_scatter(items):
-        joined = jnp.concatenate([pieces(item, count_dp) for item in items], 1)
-        return lax.psum_scatter(joined, "dp", scatter_dimension=0)
+    latent_grad, (key_share, query_share) = line_gather(
+        own_grad.reshape(-1, d_lat), 5, [write_key_grad, write_query_grad]
+    )
+    latent_grad = latent_grad.reshape(latent_one.shape)
+    outer_back, gain_outer = norm_back(outer_part, gain_rows[9], outer_stats)
 
     branch_low = latent_grad.astype(jnp.bfloat16)
     down_grad = [
@@ -885,9 +1059,10 @@
     feed_part = jnp.einsum(
         "blsc,dsc->bld", hidden_grad, copy_widein[:, 4:8], preferred_element_type=jnp.float32
     )
-    feed_share = dp_scatter(up_grad + down_grad)
     latent_part, gain_feed = norm_back(feed_part, wide_gain(2), feed_stats)
-    latent_grad = line_sum(latent_part, latent_grad, 6)
+    latent_grad, five_shares = line_sum(
+        latent_part, latent_grad, 6, [write_value_grad, narrowout_grad] + up_grad[:2]
+    )
     branch_low = latent_grad.astype(jnp.bfloat16)
     self_out_grad = jnp.einsum(
         "bld,blc->dc", branch_low, self_out, preferred_element_type=jnp.float32
@@ -916,9 +1091,13 @@
         copy_widein[:, 1:4],
         preferred_element_type=jnp.float32,
     )
-    self_share = dp_scatter(self_in_grad + [self_out_grad])
     latent_part, gain_self = norm_back(self_part, wide_gain(1), self_stats)
-    latent_grad = line_sum(latent_part, latent_grad, 7)
+    latent_grad, six_shares = line_sum(
+        latent_part, latent_grad, 7, up_grad[2:] + down_grad + self_in_grad[:2]
+    )
+    write_share = jnp.concatenate([key_share, five_shares[0], query_share, five_shares[1]], 0)
+    write_share = lax.optimization_barrier((write_share, latent_grad))[0]
+    write_share = lax.psum_scatter(write_share, "mp", scatter_dimension=1, tiled=True)
     branch_low = latent_grad.astype(jnp.bfloat16)
     read_out_grad = jnp.einsum(
         "bld,blc->dc", branch_low, read_out, preferred_element_type=jnp.float32
@@ -981,19 +1160,22 @@
     ]
     small_sizes = [item.shape[1] for item in small_parts]
     small = jnp.concatenate(small_parts, 1)
-    fill = -small.shape[1] % (8 * local)
-    small = jnp.pad(small, ((0, 0), (0, fill))).reshape(count_dp, -1, local)
-    read_joined = jnp.concatenate(
+    fill = -small.shape[1] % (16 * local)
+    small = jnp.pad(small, ((0, 0), (0, fill))).reshape(-1, local)
+    last_shares = piece_sums(
         [
-            pieces(item, count_dp)
-            for item in (read_query_grad, read_key_grad, read_value_grad, read_out_grad)
-        ]
-        + [small],
-        1,
-    )
-    read_share = lax.psum_scatter(read_joined, "dp", scatter_dimension=0)
+            self_in_grad[2],
+            self_out_grad,
+            read_query_grad,
+            read_key_grad,
+            read_value_grad,
+            read_out_grad,
+            small,
+        ],
+        9,
+    )
     lat_rows, if_rows = d_lat // count_dp, d_if // count_dp
-    small_share = lax.psum(read_share[2 * lat_rows + 2 * if_rows :], "mp")
+    small_share = mesh_sum(last_shares[6], ("mp",), 10)
     small_flat = small_share.reshape(-1)
     latents_grad, gains_grad, embed_grad, head_grad = (
         small_flat[sum(small_sizes[:i]) : sum(small_sizes[: i + 1])].reshape(rows, -1)
@@ -1005,27 +1187,17 @@
         return share[start + index * rows : start + (index + 1) * rows]
 
     widein_grad = jnp.stack(
-        [cut(read_share, 0, lat_rows)]
-        + [cut(self_share, i, lat_rows) for i in range(3)]
-        + [cut(feed_share, i, lat_rows) for i in range(4)]
+        [last_shares[2], six_shares[6], six_shares[7], last_shares[0]]
+        + list(five_shares[2:])
+        + list(six_shares[:2])
         + [cut(write_share, i, lat_rows) for i in range(2)],
         1,
     )
     narrowin_grad = jnp.stack(
-        [
-            cut(read_share, 0, if_rows, lat_rows),
-            cut(read_share, 1, if_rows, lat_rows),
-            cut(write_share, 0, if_rows, 2 * lat_rows),
-        ],
-        1,
+        [last_shares[3], last_shares[4], cut(write_share, 0, if_rows, 2 * lat_rows)], 1
     )
     wideout_grad = jnp.stack(
-        [
-            cut(read_share, 0, lat_rows, lat_rows + 2 * if_rows).T,
-            cut(self_share, 3, lat_rows).T,
-        ]
-        + [cut(feed_share, 4 + i, lat_rows).T for i in range(4)],
-        0,
+        [last_shares[5].T, last_shares[1].T] + [item.T for item in six_shares[2:6]], 0
     )
     narrowout_grad = cut(write_share, 1, if_rows, 2 * lat_rows).T
     shares = (

time: 983 us -> 829 us (0.84)
  waiting for transfers between devices: 239 us -> 64.6 us
  Pallas kernels: 344 us -> 389 us
  local copies, waits for them, and re-layouts: 116 us -> 81.2 us
    reduce_scatter x5 -> x1, waiting for transfers between devices: 239 us -> 24.7 us  [body(): lax.psum_scatter(write_share, 'mp', scatter_dimension=1, tiled=True)]
    all_gather x1, waiting for transfers between devices: 0.01 us -> 39.9 us  [body(): lax.all_gather(jnp.concatenate([key_piece, value_piece, query_piece, out_...]
    pallas_call x5 -> x6, Pallas kernels: 292 us -> 330 us  [the longest x4 247 us: line_sum(): pl.pallas_call(partial(line_sum_kernel, lax.axis_size('mp'), lax.axis_siz...]
    convert_element_type x2 -> x8, local copies, waits for them, and re-layouts: 3.59 us -> 22.7 us  [the longest x6 19.8 us: body(): write_key_weight, write_value_weight, write_query_weight, write_out_weigh...]
    transpose x4 -> x2, local copies, waits for them, and re-layouts: 17.2 us -> 0.18 us  [body(): out_piece = dp_piece(copy_narrowout, 1).T]
    reshape x4 -> x0, local copies, waits for them, and re-layouts: 15.3 us -> none  [both_pieces(): values = values.reshape(count_mp, count_dp, -1, local)]
    unnamed x332 -> x374, local copies, waits for them, and re-layouts: 43.5 us -> 31.2 us
    pallas_call x2 -> x3, Pallas kernels: 18.6 us -> 28 us  [mesh_sum(): pl.pallas_call(partial(mesh_sum_kernel, axes), out_shape=jax.ShapeDtypeSt...]
  transfers between devices with their start and end apart: 7 -> 3, of which waited for: 5 -> 2; matrix products, arithmetic and copies ran while one was open for 17% -> 11% of each run, Pallas kernels for 20% -> 19%
where the time goes in v2:
time: 829 us; the launch traced here: 818 us
  Pallas kernels  389 us (47%)
  matrix products  166 us (20%)
  other arithmetic  91.1 us (11%)
  local copies, waits for them, and re-layouts  81.2 us (10%)
  waiting for transfers between devices  64.6 us (8%)
  between operations  25.5 us (3%)
    pallas_call x4, Pallas kernels, line_sum(): pl.pallas_call(partial(line_sum_kernel, lax.axis_size('mp'), lax.axis_siz...  247 us
    pallas_call x1, Pallas kernels, line_gather(): pl.pallas_call(partial(line_gather_kernel, count, lax.axis_size('dp'), ex...  45 us
    all_gather x1, waiting for transfers between devices, body(): lax.all_gather(jnp.concatenate([key_piece, value_piece, query_piece, out_...  39.9 us
    pallas_call x1, Pallas kernels, piece_sums(): pl.pallas_call(partial(piece_sums_kernel, lax.axis_size('dp'), len(items)...  38.5 us
    pallas_call x1, Pallas kernels, line_scatter(): pl.pallas_call(partial(line_scatter_kernel, count), out_shape=jax.ShapeDt...  31.3 us
    unnamed x374, local copies, waits for them, and re-layouts  31.2 us
    pallas_call x3, Pallas kernels, mesh_sum(): pl.pallas_call(partial(mesh_sum_kernel, axes), out_shape=jax.ShapeDtypeSt...  28 us
    reduce_scatter x1, waiting for transfers between devices, body(): lax.psum_scatter(write_share, 'mp', scatter_dimension=1, tiled=True)  24.7 us
  transfers between devices with their start and end apart: 3, of which 2 were waited for; matrix products, arithmetic and copies ran while one was open for 11% of the time, Pallas kernels for 19%

profile of v2, /device:TPU:0, one launch (start us, length us, event | category | flops | bytes accessed | tf_op | source)
XLA Modules:
  0.0 817.6 jit_solution(991089021576244649)
XLA Ops:
  11.6 39.9 %all-gather.5.cloned.1.call-done = f32[1536,256]{1,0:T(8,128)} async-done(((f32[384,256]{1,0:T(8,128)}), f32[1536,256]{1,0:T(8,128)}) %all-gather.5.cloned.1.call-update) | async-done | bytes 1572880 | tf_op jit(solution)/shard_map/all_gather | solution.py:860
  53.6 6.1 shard_map.482
  68.4 3.7 fusion.109
  75.4 7.4 fusion.206
  94.2 2.9 fusion.129.part_ref
  98.7 59.2 %shard_map.479.base_ref = f32[512,1024]{1,0:T(8,128)} custom-call(f32[512,1024]{1,0:T(8,128)} %fusion.129.part_ref, f32[512,1024]{1,0:T(8,128)} %bitcast.739), custom_call_target="tpu_custom_call" | custom-call | flops 2097152 | bytes 183500800 | tf_op jit(solution)/shard_map/pallas_call | solution.py:436
  166.7 2.9 fusion.127.part_ref
  169.6 58.4 %shard_map.480 = f32[512,1024]{1,0:T(8,128)} custom-call(f32[512,1024]{1,0:T(8,128)} %fusion.127.part_ref, f32[512,1024]{1,0:T(8,128)} %shard_map.479.base_ref), custom_call_target="tpu_custom_call" | custom-call | flops 2097152 | bytes 183500800 | tf_op jit(solution)/shard_map/pallas_call | solution.py:436
  233.8 3.7 fusion.133
  237.5 5.9 multiply_convert_fusion.7
  244.7 31.3 %shard_map.481 = f32[128,1024]{1,0:T(8,128)S(1)} custom-call(f32[512,1024]{1,0:T(8,128)S(1)} %bitcast.719), custom_call_target="tpu_custom_call" | custom-call | flops 1048576 | bytes 120586240 | tf_op jit(solution)/shard_map/pallas_call | solution.py:576
  282.8 3.0 multiply_convert_fusion.6
  285.9 5.7 fusion.3
  291.5 8.6 %add_convert_fusion = bf16[32,384,256]{2,1,0:T(8,128)(2,1)} fusion(f32[32,384,256]{2,1,0:T(8,128)} %all-gather.7.cloned.1.call-done, f32[]{:T(128)} %bitcast.44), kind=kLoop, calls=%fused_computation | loop fusion | flops 6291456 | bytes 18874372 | tf_op jit(solution)/shard_map/convert.9
  300.1 3.1 slice_bitcast_fusion.3
  303.2 4.8 slice_bitcast_fusion.1
  308.0 4.3 copy.318
  317.6 4.7 copy.320
  322.3 3.3 fusion.87
  326.8 3.3 fusion.84
  331.9 2.9 convolution_convert_fusion.5
  339.4 3.6 fusion.215
  368.0 2.7 fusion.216.refs_0_
  373.2 45.0 %shard_map.483 = (f32[512,1024]{1,0:T(8,128)}, f32[128,1024]{1,0:T(8,128)}, f32[64,1024]{1,0:T(8,128)}) custom-call(f32[128,1024]{1,0:T(8,128)} %fusion.126.own_ref, f32[8,128,1024]{2,1,0:T(8,128)} %fusion.216.refs_0_, f32[8,64,1024]{2,1,0:T(8,128)} %fusion.217.refs_1_), custom_call_target="tpu_custom_call" | custom-call | flops 131072 | bytes 131072000 | tf_op jit(solution)/shard_map/pallas_call | solution.py:678
  418.1 2.7 convert_element_type.424
  423.1 2.8 convolution_bitcast_fusion.3.refs_5_
  430.3 3.6 add_convert_fusion.1
  439.6 4.0 fusion.36
  443.6 2.7 fusion.218.refs_0_
  446.3 2.7 fusion.219.refs_1_
  450.9 64.0 %shard_map.484 = (f32[512,1024]{1,0:T(8,128)}, f32[128,1024]{1,0:T(8,128)}, f32[64,1024]{1,0:T(8,128)}, f32[128,256]{1,0:T(8,128)}, f32[128,256]{1,0:T(8,128)}) custom-call(f32[512,1024]{1,0:T(8,128)} %bitcast.749, f32[512,1024]{1,0:T(8,128)} %get-tuple-element.48.base_ref, f32[8,128,1024]{2,1,0:T(8,128)} %fusion.218.refs_0_, ...), custom_call_target="tpu_custom_call" | custom-call | flops 2097152 | bytes 183500800 | tf_op jit(solution)/shard_map/pallas_call | solution.py:436
  525.8 3.5 fusion.35
  531.3 65.0 %shard_map.485 = (f32[512,1024]{1,0:T(8,128)}, f32[128,256]{1,0:T(8,128)}, f32[128,256]{1,0:T(8,128)}, f32[128,256]{1,0:T(8,128)}, f32[128,256]{1,0:T(8,128)}, /...) custom-call(f32[512,1024]{1,0:T(8,128)} %bitcast.748, ...), custom_call_target="tpu_custom_call" | custom-call | flops 2097152 | bytes 183500800 | tf_op jit(solution)/shard_map/pallas_call | solution.py:436
  596.3 3.6 convert_bitcast_fusion
  601.7 7.0 convolution_convert_fusion.2
  608.7 5.7 multiply_reduce_fusion.2
  616.8 2.9 convert_reduce_fusion
  623.5 5.3 fusion.29
  634.1 5.1 convolution_bitcast_fusion.13.refs_4_
  648.0 7.8 multiply_reduce_fusion
  656.0 5.8 fusion.27
  661.9 10.1 %fusion.94 = f32[12,512]{1,0:T(8,128)S(1)} fusion(f32[12,512]{1,0:T(8,128)S(1)} %fusion.27, f32[4,12,1024]{2,1,0:T(8,128)S(1)} %copy-done.40, f32[4,1024,512]{1,2,0:T(8,128)S(1)} %copy-done.9, f32[4,1024,512]{1,2,0:T(8,128)} %copy-done.2, f32[4,1024]{1,0:T(4,128)S(1)} %broadcast_multiply_fusion, f32[4,1024]{1,0:T(4,128)S(1)} %broadcast_multiply_fusion.1, ...), kind=kOutput, calls=%fused_computation.197 | convolution fusion | flops 316676096 | bytes 17090560 | tf_op jit(solution)/shard_map/bcp,bpd->cd/dot_general | solution.py:1137
  677.9 38.5 %shard_map.486 = (f32[128,256]{1,0:T(8,128)}, f32[128,256]{1,0:T(8,128)}, f32[128,256]{1,0:T(8,128)}, f32[64,256]{1,0:T(8,128)}, f32[64,256]{1,0:T(8,128)}, /*index=5*/f32[128,256]{1,0:T(8,128)}, f32[80,256]{1,0:T(8,128)}) custom-call(f32[8,128,256]{2,1,0:T(8,128)} %convolution_bitcast_fusion.10.refs_0_, f32[8,128,256]{2,1,0:T(8,128)} %convolution_bitcast_fusion.9.refs_1_, ...), custom_call_target="tpu_custom_call" | custom-call | tf_op jit(solution)/shard_map/pallas_call | solution.py:708
  716.4 10.9 %shard_map.487 = f32[80,256]{1,0:T(8,128)} custom-call(f32[80,256]{1,0:T(8,128)} %get-tuple-element.72.tile_ref), custom_call_target="tpu_custom_call" | custom-call | tf_op jit(solution)/shard_map/pallas_call | solution.py:778
  741.2 24.7 %reduce-scatter.2.cloned.1.call-done = f32[384,256]{1,0:T(8,128)} async-done(((f32[384,1024]{1,0:T(8,128)}), f32[384,256]{1,0:T(8,128)}) %reduce-scatter.2.cloned.1.call-update) | async-done | bytes 393232 | tf_op jit(solution)/shard_map/reduce_scatter | solution.py:1100
  774.7 10.9 %shard_map.488 = f32[8,128]{1,0:T(8,128)} custom-call(f32[8,128]{1,0:T(8,128)} %iota.19.tile_ref), custom_call_target="tpu_custom_call" | custom-call | tf_op jit(solution)/shard_map/pallas_call | solution.py:778
  789.1 3.2 multiply_subtract_fusion.1
  801.6 4.5 multiply_subtract_fusion
  (576 shorter events, 178.5 us)
Async XLA Ops:
  7.2 44.3 %all-gather.5.cloned.1.call-start = ((), (), s32[]{:S(2)}) async-start(), calls=%async_computation.2 | async-start | bytes 1966080 | tf_op jit(solution)/shard_map/all_gather | solution.py:860
  9.3 42.2 %copy-start.91 = (s32[4,1024]{1,0:T(4,128)S(1)}, s32[4,1024]{1,0:T(4,128)}, u32[]{:S(2)}) copy-start(s32[4,1024]{1,0:T(4,128)} %param.35) | copy-start | bytes 49156
  9.3 42.4 %copy-start.163 = (s32[4]{0:T(128)S(1)}, s32[4]{0:T(128)}, u32[]{:S(2)}) copy-start(s32[4]{0:T(128)} %param.34) | copy-start | bytes 52
  9.4 51.6 %copy-start.136 = (bf16[11,512]{1,0:T(8,128)(2,1)S(1)}, bf16[11,512]{1,0:T(8,128)(2,1)}, u32[]{:S(2)}) copy-start(bf16[11,512]{1,0:T(8,128)(2,1)} %param.41) | copy-start | bytes 33796
  9.4 51.7 %copy-start.29 = (bf16[128,1024]{1,0:T(8,128)(2,1)S(1)}, bf16[128,1024]{1,0:T(8,128)(2,1)}, u32[]{:S(2)}) copy-start(bf16[128,1024]{1,0:T(8,128)(2,1)} %param.40) | copy-start | bytes 786436
  11.5 280.0 %all-gather.7.cloned.1.call-start = ((), (), s32[]{:S(2)}) async-start(), calls=%async_computation.3 | async-start | bytes 14155776 | tf_op jit(solution)/shard_map/all_gather | solution.py:863
  51.5 13.4 %copy-start.78 = (f32[6,256,128]{2,1,0:T(8,128)S(1)}, f32[6,256,128]{2,1,0:T(8,128)}, u32[]{:S(2)}) copy-start(f32[6,256,128]{2,1,0:T(8,128)} %param.49) | copy-start | bytes 2359300
  51.5 714.4 %reduce-scatter.2.cloned.1.call-start = ((), (), s32[]{:S(2)}) async-start(), calls=%async_computation.1 | async-start | bytes 1966080 | tf_op jit(solution)/shard_map/reduce_scatter | solution.py:1100
  61.0 169.6 %copy-start.128 = (f32[1,4,2,128]{3,1,2,0:T(4,128)}, f32[1,4,2,128]{3,1,2,0:T(4,128)S(1)}, u32[]{:S(2)}) copy-start(f32[1,4,2,128]{3,1,2,0:T(4,128)S(1)} %copy.469) | copy-start | bytes 12292
  61.0 99.5 %copy-start.126 = (f32[1,4,2,128]{3,1,2,0:T(4,128)}, f32[1,4,2,128]{3,1,2,0:T(4,128)S(1)}, u32[]{:S(2)}) copy-start(f32[1,4,2,128]{3,1,2,0:T(4,128)S(1)} %copy.466) | copy-start | bytes 12292
  63.0 23.2 %copy-start.67 = (bf16[128,256]{0,1:T(8,128)(2,1)}, bf16[128,256]{0,1:T(8,128)(2,1)S(1)}, u32[]{:S(2)}) copy-start(bf16[128,256]{0,1:T(8,128)(2,1)S(1)} %copy.307) | copy-start | bytes 196612
  74.3 208.4 %copy-start.133 = (f32[1,512]{1,0:T(1,128)}, f32[1,512]{1,0:T(1,128)S(1)}, u32[]{:S(2)}) copy-start(f32[1,512]{1,0:T(1,128)S(1)} %get-tuple-element.243) | copy-start | bytes 6148
  74.3 211.5 %copy-start.105 = (f32[1,512]{1,0:T(1,128)}, f32[1,512]{1,0:T(1,128)S(1)}, u32[]{:S(2)}) copy-start(f32[1,512]{1,0:T(1,128)S(1)} %get-tuple-element.244) | copy-start | bytes 6148
  75.4 7.4 copy-start.39
  82.8 7.2 copy-start.2
  166.5 61.5 %copy-start.43 = (bf16[4,4,64,128]{3,2,1,0:T(8,128)(2,1)}, bf16[4,4,64,128]{3,2,1,0:T(8,128)(2,1)S(1)}, u32[]{:S(2)}) copy-start(bf16[4,4,64,128]{3,2,1,0:T(8,128)(2,1)S(1)} %convolution_convert_fusion.10) | copy-start | bytes 786436
  237.5 5.9 copy-start.61
  237.5 5.9 copy-start.83
  276.1 50.7 %copy-start.155 = (f32[128]{0:T(128)}, f32[128]{0:T(128)S(1)}, u32[]{:S(2)}) copy-start(f32[128]{0:T(128)S(1)} %broadcast_multiply_fusion.19) | copy-start | bytes 1540
  276.3 50.4 %copy-start.157 = (f32[128]{0:T(128)}, f32[128]{0:T(128)S(1)}, u32[]{:S(2)}) copy-start(f32[128]{0:T(128)S(1)} %add_rsqrt_fusion.3) | copy-start | bytes 1540
  282.8 8.8 %copy-start.120 = (f32[1024]{0:T(1024)}, f32[1024]{0:T(1024)S(1)}, u32[]{:S(2)}) copy-start(f32[1024]{0:T(1024)S(1)} %add_rsqrt_fusion.2) | copy-start | bytes 12292
  601.7 7.1 copy-start.17
  601.7 12.8 %slice-start = ((s8[8388608]{0:T(1024)(128)(4,1)}), s8[4194304]{0:T(1024)(128)(4,1)S(1)}, s32[]{:S(2)}) async-start(s8[8388608]{0:T(1024)(128)(4,1)} %bitcast.720), calls=%async_computation.4 | async-start | bytes 8388608
  648.0 8.0 copy-start.8
  648.0 8.0 copy-start.40
  648.0 8.0 copy-start.104
  648.0 8.0 copy-start.123
  648.0 8.0 copy-start.125
  648.0 8.0 copy-start.135
  661.8 10.4 %copy-start.119 = (f32[11,8,64]{2,1,0:T(8,128)S(1)}, f32[11,8,64]{2,1,0:T(8,128)}, u32[]{:S(2)}) copy-start(f32[11,8,64]{2,1,0:T(8,128)} %constant_dynamic-update-slice_fusion.6) | copy-start | bytes 67588
  661.8 10.4 %copy-start.132 = (f32[2,8,64]{2,1,0:T(8,128)S(1)}, f32[2,8,64]{2,1,0:T(8,128)}, u32[]{:S(2)}) copy-start(f32[2,8,64]{2,1,0:T(8,128)} %concatenate.34) | copy-start | bytes 12292
  661.8 10.4 %copy-start.131 = (f32[2,8,64]{2,1,0:T(8,128)S(1)}, f32[2,8,64]{2,1,0:T(8,128)}, u32[]{:S(2)}) copy-start(f32[2,8,64]{2,1,0:T(8,128)} %concatenate.35) | copy-start | bytes 12292
  661.9 10.4 %copy-start.130 = (f32[2,8,64]{2,1,0:T(8,128)S(1)}, f32[2,8,64]{2,1,0:T(8,128)}, u32[]{:S(2)}) copy-start(f32[2,8,64]{2,1,0:T(8,128)} %concatenate.36) | copy-start | bytes 12292
  661.9 10.4 %copy-start.147 = (f32[1,8,64]{2,1,0:T(8,128)S(1)}, f32[1,8,64]{2,1,0:T(8,128)}, u32[]{:S(2)}) copy-start(f32[1,8,64]{2,1,0:T(8,128)} %concatenate.38) | copy-start | bytes 6148
  661.9 10.4 %copy-start.146 = (f32[1,8,64]{2,1,0:T(8,128)S(1)}, f32[1,8,64]{2,1,0:T(8,128)}, u32[]{:S(2)}) copy-start(f32[1,8,64]{2,1,0:T(8,128)} %concatenate.39) | copy-start | bytes 6148
  661.9 10.5 %copy-start.60 = (f32[16,8,8,128]{3,2,1,0:T(8,128)S(1)}, f32[16,8,8,128]{3,2,1,0:T(8,128)}, u32[]{:S(2)}) copy-start(f32[16,8,8,128]{3,2,1,0:T(8,128)} %copy.476) | copy-start | bytes 1572868
  677.8 51.9 %copy-start.81 = (f32[128,1024]{1,0:T(8,128)S(1)}, f32[128,1024]{1,0:T(8,128)}, u32[]{:S(2)}) copy-start(f32[128,1024]{1,0:T(8,128)} %get-tuple-element.59) | copy-start | bytes 1572868
  677.8 51.9 %copy-start.82 = (f32[128,1024]{1,0:T(8,128)S(1)}, f32[128,1024]{1,0:T(8,128)}, u32[]{:S(2)}) copy-start(f32[128,1024]{1,0:T(8,128)} %get-tuple-element.60) | copy-start | bytes 1572868
  677.8 51.9 %copy-start.85 = (f32[64,1024]{1,0:T(8,128)S(1)}, f32[64,1024]{1,0:T(8,128)}, u32[]{:S(2)}) copy-start(f32[64,1024]{1,0:T(8,128)} %get-tuple-element.61) | copy-start | bytes 786436
  677.8 51.9 %copy-start.86 = (f32[64,1024]{1,0:T(8,128)S(1)}, f32[64,1024]{1,0:T(8,128)}, u32[]{:S(2)}) copy-start(f32[64,1024]{1,0:T(8,128)} %get-tuple-element.62) | copy-start | bytes 786436
  731.1 8.2 %copy-start.92 = (f32[128,256]{1,0:T(8,128)S(1)}, f32[128,256]{1,0:T(8,128)}, u32[]{:S(2)}) copy-start(f32[128,256]{1,0:T(8,128)} %get-tuple-element.56) | copy-start | bytes 393220
  736.4 33.7 %copy-start.87 = (f32[64,256]{1,0:T(8,128)S(1)}, f32[64,256]{1,0:T(8,128)}, u32[]{:S(2)}) copy-start(f32[64,256]{1,0:T(8,128)} %get-tuple-element.64) | copy-start | bytes 196612
  736.4 33.7 %copy-start.88 = (f32[64,256]{1,0:T(8,128)S(1)}, f32[64,256]{1,0:T(8,128)}, u32[]{:S(2)}) copy-start(f32[64,256]{1,0:T(8,128)} %get-tuple-element.65) | copy-start | bytes 196612
  736.5 52.6 %copy-start.36 = (f32[6,256,128]{1,2,0:T(8,128)S(1)}, f32[6,256,128]{1,2,0:T(8,128)}, u32[]{:S(2)}) copy-start(f32[6,256,128]{1,2,0:T(8,128)} %copy.378) | copy-start | bytes 2359300
  792.3 6.6 copy-start.152
  792.3 6.6 copy-start.153
  792.3 6.6 copy-start.154
  801.6 6.7 copy-start.1
  (121 other events, 359.5 us)
Sparse Core Ops, SparseCore 0:
  11.6 39.7 all-gather.4
  53.4 70.9 all-gather.6
  731.2 34.6 reduce-scatter.1

commit v3 on v2

--- a/solution.py
+++ b/solution.py
@@ -264,6 +264,99 @@
     lax.fori_loop(0, rows // step, one, 0)
 
 
+class Spread:
+    def __init__(self, name, count, held, send_sem, recv_sem):
+        self.name, self.count, self.held = name, count, held
+        self.send_sem, self.recv_sem = send_sem, recv_sem
+        self.place = lax.axis_index(name)
+
+    @staticmethod
+    def scratch(count, shape):
+        sems = pltpu.SemaphoreType.DMA((count,))
+        return [pltpu.VMEM((count,) + shape, jnp.float32), sems, sems]
+
+    def peer(self, step):
+        return {self.name: lax.rem(self.place + step, self.count)}
+
+    def copy(self, step, slot):
+        return remote(
+            self.held.at[slot],
+            self.held.at[slot],
+            self.send_sem.at[step],
+            self.recv_sem.at[slot],
+            self.peer(step),
+        )
+
+    def each(self, action):
+        def one(step, carry):
+            action(step)
+            return carry
+
+        lax.fori_loop(1, self.count, one, 0)
+
+    def start(self):
+        self.each(lambda step: self.copy(step, self.place).start())
+
+    def take(self):
+        self.each(lambda step: self.copy(step, lax.rem(self.place + step, self.count)).wait_recv())
+
+    def finish(self):
+        self.each(lambda step: self.copy(step, self.place).wait_send())
+
+    def total(self):
+        return lax.fori_loop(
+            1, self.count, lambda slot, carry: carry + self.held[slot], self.held[0]
+        )
+
+
+class Convert:
+    def __init__(self, count_mp, steps, blocks, outs, buffer, sems):
+        self.count_mp, self.blocks, self.outs = count_mp, blocks, outs
+        self.buffer, self.sems = buffer, sems
+        self.number = blocks.shape[0]
+        self.each = -(-self.number // steps)
+
+    @staticmethod
+    def scratch(block):
+        return [pltpu.VMEM((3,) + block, jnp.float32), pltpu.SemaphoreType.DMA((3,))]
+
+    def copy(self, index):
+        slot = lax.rem(index, 3)
+        return pltpu.make_async_copy(
+            self.blocks.at[index], self.buffer.at[slot], self.sems.at[slot]
+        )
+
+    def begin(self):
+        self.copy(0).start()
+        self.copy(1).start()
+
+    def one(self, index):
+        self.copy(index).wait()
+
+        @pl.when(index + 2 < self.number)
+        def _():
+            self.copy(index + 2).start()
+
+        block = self.buffer.at[lax.rem(index, 3)]
+        local = block.shape[1]
+        columns = pl.ds(pl.multiple_of(lax.rem(index, self.count_mp) * local, local), local)
+        low = 0
+        for out in self.outs:
+            rows = out.shape[0] * self.count_mp // self.number
+            where = pl.ds(pl.multiple_of(index // self.count_mp * rows, rows), rows)
+            out[where, columns] = block[pl.ds(low, rows)].astype(jnp.bfloat16)
+            low += rows
+
+    def step(self, index):
+        for entry in range(self.each):
+            self.one(index * self.each + entry)
+
+
+def signal_all(barrier, others):
+    for other in others:
+        pl.semaphore_signal(barrier, inc=1, device_id=other, device_id_type=MESH_ID)
+
+
 def greet(place, count, others=()):
     barrier = pltpu.get_barrier_semaphore()
     below, above = {"mp": place - 1}, {"mp": place + 1}
@@ -276,8 +369,7 @@
     def _():
         pl.semaphore_signal(barrier, inc=1, device_id=above, device_id_type=MESH_ID)
 
-    for other in others:
-        pl.semaphore_signal(barrier, inc=1, device_id=other, device_id_type=MESH_ID)
+    signal_all(barrier, others)
     inside = jnp.logical_and(place > 0, place < count - 1)
 
     @pl.when(inside)
@@ -289,11 +381,23 @@
         pl.semaphore_wait(barrier, 1 + len(others))
 
 
-def line_sum_kernel(count, count_dp, extra, part_ref, base_ref, *refs):
-    items, out_ref, outs = refs[:extra], refs[extra], refs[extra + 1 : 2 * extra + 1]
-    inner, from_away, from_toward = refs[2 * extra + 1 : 2 * extra + 4]
-    toward_send, away_send, away_recv, toward_recv = refs[2 * extra + 4 : 2 * extra + 8]
-    sums = PieceSums(count_dp, items, outs, refs[2 * extra + 8 :])
+def line_sum_kernel(count, count_dp, extra, tiled, converted, *refs):
+    refs = list(refs)
+
+    def pull(number):
+        taken = refs[:number]
+        del refs[:number]
+        return taken
+
+    part_ref, base_ref = pull(2)
+    items, tile, blocks = pull(extra), pull(tiled), pull(min(1, converted))
+    (out_ref,) = pull(1)
+    outs, tile_out, wide = pull(extra), pull(tiled), pull(converted)
+    inner, from_away, from_toward, toward_send, away_send, away_recv, toward_recv = pull(7)
+    chunks = toward_send.shape[0]
+    spread = Spread("dp", count_dp, *pull(3)) if tiled else None
+    convert = Convert(count, chunks, blocks[0], wide, *pull(2)) if converted else None
+    sums = PieceSums(count_dp, items, outs, refs)
     place = lax.axis_index("mp")
     half = count // 2
     low_side = place < half
@@ -301,9 +405,15 @@
     away = {"mp": jnp.where(low_side, place - 1, place + 1)}
     middle = jnp.logical_or(place == half - 1, place == half)
     outermost = jnp.logical_or(place == 0, place == count - 1)
-    chunks = toward_send.shape[0]
     rows = part_ref.shape[0] // chunks
-    greet(place, count, sums.peers())
+    others = [spread.peer(step) for step in range(1, count_dp)] if tiled else sums.peers()
+    if tiled:
+        spread.held[spread.place] = tile[0][...]
+    greet(place, count, others)
+    if tiled:
+        spread.start()
+    if converted:
+        convert.begin()
     sums.begin()
 
     def window(step):
@@ -345,6 +455,8 @@
             push(step, part_ref, True).wait_recv()
             out_ref[window(step)] = from_toward[window(step)] + base_ref[window(step)]
             push(step, part_ref, False).wait_send()
+            if converted:
+                convert.step(step)
             return carry
 
         for low, high, phase in sums.moments(chunks):
@@ -366,6 +478,8 @@
         def first(step, carry):
             gather_in(step)
             push(step, inner, True).start()
+            if converted:
+                convert.step(step)
             return carry
 
         def both(step, carry):
@@ -402,6 +516,8 @@
                 push(step, inner, True).wait_recv()
                 back(step, from_toward).start()
                 out_ref[window(step)] = from_toward[window(step)] + base_ref[window(step)]
+                if converted:
+                    convert.step(step)
                 return carry
 
             def drain(step, carry):
@@ -416,6 +532,27 @@
             lax.fori_loop(0, chunks, drain, 0)
 
     sums.finish()
+    if tiled:
+        spread.take()
+        tile_out[0][...] = spread.total()
+        spread.finish()
+
+
+def room(*groups):
+    total = 8 << 20
+    for group in groups:
+        for item in group:
+            if hasattr(item, "shape") and hasattr(item, "dtype"):
+                total += math.prod(item.shape) * jnp.dtype(item.dtype).itemsize
+    return min(total, VMEM_LIMIT)
+
+
+def room_of(scratch):
+    return [
+        jax.ShapeDtypeStruct(item.shape, item.dtype)
+        for item in scratch
+        if getattr(item, "dtype", None) in (jnp.float32, jnp.bfloat16)
+    ]
 
 
 def piece_shapes(items):
@@ -425,160 +562,208 @@
     return items, shapes, [jax.ShapeDtypeStruct(shape, jnp.float32) for shape in shapes]
 
 
-def line_sum(part, base, call_id, items=()):
+def line_sum(part, base, call_id, items=(), tile=None, blocks=None):
     shape = part.shape
     items, shapes, shares = piece_shapes(items)
-    extra = len(items)
+    count, count_dp = lax.axis_size("mp"), lax.axis_size("dp")
     part = part.reshape(-1, shape[-1])
     rows, width = part.shape
     buffer = pltpu.VMEM((rows, width), jnp.float32)
     sems = pltpu.SemaphoreType.DMA((CHUNKS,))
+    inputs, specs = [part, base.reshape(part.shape), *items], [VMEM_SPEC] * (2 + len(items))
+    outs = [jax.ShapeDtypeStruct((rows, width), jnp.float32)] + shares
+    scratch = [buffer] * 3 + [sems] * 4
+    if tile is not None:
+        inputs.append(tile)
+        specs.append(VMEM_SPEC)
+        outs.append(jax.ShapeDtypeStruct(tile.shape, jnp.float32))
+        scratch += Spread.scratch(count_dp, tile.shape)
+    sizes = []
+    if blocks is not None:
+        blocks, sizes = blocks
+        outs += [
+            jax.ShapeDtypeStruct((size, count * blocks.shape[2]), jnp.bfloat16) for size in sizes
+        ]
+        scratch += Convert.scratch(blocks.shape[1:])
+    scratch += PieceSums.scratch(count_dp, shapes)
+    limit = room(inputs, outs, room_of(scratch))
+    if blocks is not None:
+        inputs.append(blocks)
+        specs.append(pl.BlockSpec(memory_space=pl.ANY))
     results = pl.pallas_call(
-        partial(line_sum_kernel, lax.axis_size("mp"), lax.axis_size("dp"), extra),
-        out_shape=[jax.ShapeDtypeStruct((rows, width), jnp.float32)] + shares,
-        in_specs=[VMEM_SPEC] * (2 + extra),
-        out_specs=[VMEM_SPEC] * (1 + extra),
-        scratch_shapes=[buffer] * 3
-        + [sems] * 4
-        + PieceSums.scratch(lax.axis_size("dp"), shapes),
+        partial(line_sum_kernel, count, count_dp, len(items), int(tile is not None), len(sizes)),
+        out_shape=outs,
+        in_specs=specs,
+        out_specs=[VMEM_SPEC] * len(outs),
+        scratch_shapes=scratch,
         compiler_params=pltpu.CompilerParams(
-            collective_id=call_id, has_side_effects=True, vmem_limit_bytes=VMEM_LIMIT
+            collective_id=call_id, has_side_effects=True, vmem_limit_bytes=limit
         ),
         cost_estimate=pl.CostEstimate(
             flops=4 * rows * width, bytes_accessed=350 * rows * width, transcendentals=0
         ),
-    )(part, base.reshape(part.shape), *items)
+    )(*inputs)
     return results[0].reshape(shape), results[1:]
 
 
-def line_scatter_kernel(
-    count, part_ref, out_ref, up_acc, down_acc, from_below, from_above, up_send, down_send, up_recv, down_recv
-):
-    place = lax.axis_index("mp")
-    steps = up_send.shape[1]
-    block = part_ref.shape[0] // count
-    rows = block // steps
-    below, above = {"mp": place - 1}, {"mp": place + 1}
-    greet(place, count)
-
-    def window(owner, step):
-        return pl.ds(pl.multiple_of(owner * block + step * rows, rows), rows)
-
-    def up(owner, step, source):
-        where = window(owner, step)
+class LineScatter:
+    def __init__(self, count, part, out, buffers, sems):
+        self.count, self.part, self.out = count, part, out
+        self.up_acc, self.down_acc, self.from_below, self.from_above = buffers
+        self.up_send, self.down_send, self.up_recv, self.down_recv = sems
+        self.place = lax.axis_index("mp")
+        self.steps = self.up_send.shape[1]
+        self.block = part.shape[0] // count
+        self.rows = self.block // self.steps
+
+    @staticmethod
+    def scratch(count, shape, steps):
+        sems = pltpu.SemaphoreType.DMA((count, steps))
+        return [pltpu.VMEM(shape, jnp.float32)] * 4 + [sems] * 4
+
+    def window(self, owner, step):
+        return pl.ds(pl.multiple_of(owner * self.block + step * self.rows, self.rows), self.rows)
+
+    def up(self, owner, step, source):
+        where = self.window(owner, step)
         return remote(
-            source.at[where], from_below.at[where], up_send.at[owner, step], up_recv.at[owner, step], above
+            source.at[where],
+            self.from_below.at[where],
+            self.up_send.at[owner, step],
+            self.up_recv.at[owner, step],
+            {"mp": self.place + 1},
         )
 
-    def down(owner, step, source):
-        where = window(owner, step)
+    def down(self, owner, step, source):
+        where = self.window(owner, step)
         return remote(
-            source.at[where], from_above.at[where], down_send.at[owner, step], down_recv.at[owner, step], below
+            source.at[where],
+            self.from_above.at[where],
+            self.down_send.at[owner, step],
+            self.down_recv.at[owner, step],
+            {"mp": self.place - 1},
         )
 
-    def up_turn(index):
-        owner, step = count - 1 - index // steps, lax.rem(index, steps)
+    def up_turn(self, index):
+        place, part = self.place, self.part
+        owner, step = self.count - 1 - index // self.steps, lax.rem(index, self.steps)
 
         @pl.when(jnp.logical_and(owner > place, place == 0))
         def _():
-            up(owner, step, part_ref).start()
+            self.up(owner, step, part).start()
 
         @pl.when(jnp.logical_and(owner > place, place > 0))
         def _():
-            up(owner, step, part_ref).wait_recv()
-            where = window(owner, step)
-            up_acc[where] = part_ref[where] + from_below[where]
-            up(owner, step, up_acc).start()
-
-    def down_turn(index):
-        owner, step = index // steps, lax.rem(index, steps)
+            self.up(owner, step, part).wait_recv()
+            where = self.window(owner, step)
+            self.up_acc[where] = part[where] + self.from_below[where]
+            self.up(owner, step, self.up_acc).start()
+
+    def down_turn(self, index):
+        place, part, count = self.place, self.part, self.count
+        owner, step = index // self.steps, lax.rem(index, self.steps)
 
         @pl.when(jnp.logical_and(owner < place, place == count - 1))
         def _():
-            down(owner, step, part_ref).start()
+            self.down(owner, step, part).start()
 
         @pl.when(jnp.logical_and(owner < place, place < count - 1))
         def _():
-            down(owner, step, part_ref).wait_recv()
-            where = window(owner, step)
-            down_acc[where] = part_ref[where] + from_above[where]
-            down(owner, step, down_acc).start()
-
-    turns, lag = count * steps, steps
-
-    def staggered(first, second):
-        def begin(index, carry):
-            first(index)
+            self.down(owner, step, part).wait_recv()
+            where = self.window(owner, step)
+            self.down_acc[where] = part[where] + self.from_above[where]
+            self.down(owner, step, self.down_acc).start()
+
+    def run(self, pause=None):
+        turns, lag = self.count * self.steps, self.steps
+
+        def staggered(first, second):
+            def begin(index, carry):
+                first(index)
+                return carry
+
+            def both(index, carry):
+                first(index)
+                second(index - lag)
+                return carry
+
+            def end(index, carry):
+                second(index)
+                return carry
+
+            lax.fori_loop(0, lag, begin, 0)
+            if pause is not None:
+                pause()
+            lax.fori_loop(lag, turns, both, 0)
+            lax.fori_loop(turns - lag, turns, end, 0)
+
+        @pl.when(self.place < self.count // 2)
+        def _():
+            staggered(self.up_turn, self.down_turn)
+
+        @pl.when(self.place >= self.count // 2)
+        def _():
+            staggered(self.down_turn, self.up_turn)
+
+    def settle(self):
+        place, rows = self.place, self.rows
+
+        def one(step, carry):
+            where = self.window(place, step)
+            mine = pl.ds(pl.multiple_of(step * rows, rows), rows)
+            self.out[mine] = self.part[where]
+
+            @pl.when(place > 0)
+            def _():
+                self.up(place, step, self.part).wait_recv()
+                self.out[mine] += self.from_below[where]
+
+            @pl.when(place < self.count - 1)
+            def _():
+                self.down(place, step, self.part).wait_recv()
+                self.out[mine] += self.from_above[where]
+
             return carry
 
-        def both(index, carry):
-            first(index)
-            second(index - lag)
+        lax.fori_loop(0, self.steps, one, 0)
+
+    def finish(self):
+        place = self.place
+
+        def one(index, carry):
+            owner, step = index // self.steps, lax.rem(index, self.steps)
+
+            @pl.when(owner > place)
+            def _():
+                self.up(owner, step, self.part).wait_send()
+
+            @pl.when(owner < place)
+            def _():
+                self.down(owner, step, self.part).wait_send()
+
             return carry
 
-        def end(index, carry):
-            second(index)
-            return carry
-
-        lax.fori_loop(0, lag, begin, 0)
-        lax.fori_loop(lag, turns, both, 0)
-        lax.fori_loop(turns - lag, turns, end, 0)
-
-    @pl.when(place < count // 2)
-    def _():
-        staggered(up_turn, down_turn)
-
-    @pl.when(place >= count // 2)
-    def _():
-        staggered(down_turn, up_turn)
-
-    def settle(step, carry):
-        where = window(place, step)
-        mine = pl.ds(pl.multiple_of(step * rows, rows), rows)
-        out_ref[mine] = part_ref[where]
-
-        @pl.when(place > 0)
-        def _():
-            up(place, step, part_ref).wait_recv()
-            out_ref[mine] += from_below[where]
-
-        @pl.when(place < count - 1)
-        def _():
-            down(place, step, part_ref).wait_recv()
-            out_ref[mine] += from_above[where]
-
-        return carry
-
-    lax.fori_loop(0, steps, settle, 0)
-
-    def drain(index, carry):
-        owner, step = index // steps, lax.rem(index, steps)
-
-        @pl.when(owner > place)
-        def _():
-            up(owner, step, part_ref).wait_send()
-
-        @pl.when(owner < place)
-        def _():
-            down(owner, step, part_ref).wait_send()
-
-        return carry
-
-    lax.fori_loop(0, count * steps, drain, 0)
+        lax.fori_loop(0, self.count * self.steps, one, 0)
+
+
+def line_scatter_kernel(count, part_ref, out_ref, *scratch):
+    scatter = LineScatter(count, part_ref, out_ref, scratch[:4], scratch[4:])
+    greet(scatter.place, count)
+    scatter.run()
+    scatter.settle()
+    scatter.finish()
 
 
 def line_scatter(part, call_id):
     rows, width = part.shape
     count = lax.axis_size("mp")
     steps = 8
-    buffer = pltpu.VMEM((rows, width), jnp.float32)
-    sems = pltpu.SemaphoreType.DMA((count, steps))
     return pl.pallas_call(
         partial(line_scatter_kernel, count),
         out_shape=jax.ShapeDtypeStruct((rows // count, width), jnp.float32),
         in_specs=[VMEM_SPEC],
         out_specs=VMEM_SPEC,
-        scratch_shapes=[buffer] * 4 + [sems] * 4,
+        scratch_shapes=LineScatter.scratch(count, (rows, width), steps),
         compiler_params=pltpu.CompilerParams(
             collective_id=call_id, has_side_effects=True, vmem_limit_bytes=24 << 20
         ),
@@ -670,123 +855,27 @@
 
 def line_gather(own, call_id, items=()):
     rows, width = own.shape
-    count = lax.axis_size("mp")
+    count, count_dp = lax.axis_size("mp"), lax.axis_size("dp")
     steps = 8
     sems = pltpu.SemaphoreType.DMA((count, steps))
     items, shapes, shares = piece_shapes(items)
     extra = len(items)
+    scratch = PieceSums.scratch(count_dp, shapes)
+    limit = room(items, shares, room_of(scratch)) + 2 * rows * count * width * 4
     results = pl.pallas_call(
-        partial(line_gather_kernel, count, lax.axis_size("dp"), extra),
+        partial(line_gather_kernel, count, count_dp, extra),
         out_shape=[jax.ShapeDtypeStruct((rows * count, width), jnp.float32)] + shares,
         in_specs=[VMEM_SPEC] * (1 + extra),
         out_specs=[VMEM_SPEC] * (1 + extra),
-        scratch_shapes=[sems] * 4 + PieceSums.scratch(lax.axis_size("dp"), shapes),
+        scratch_shapes=[sems] * 4 + scratch,
         compiler_params=pltpu.CompilerParams(
-            collective_id=call_id, has_side_effects=True, vmem_limit_bytes=VMEM_LIMIT
+            collective_id=call_id, has_side_effects=True, vmem_limit_bytes=limit
         ),
         cost_estimate=pl.CostEstimate(
             flops=rows * width, bytes_accessed=250 * rows * width * count, transcendentals=0
         ),
     )(own, *items)
     return results[0], results[1:]
-
-
-def piece_sums_kernel(count_dp, extra, *refs):
-    sums = PieceSums(count_dp, refs[:extra], refs[extra : 2 * extra], refs[2 * extra :])
-    barrier = pltpu.get_barrier_semaphore()
-    for other in sums.peers():
-        pl.semaphore_signal(barrier, inc=1, device_id=other, device_id_type=MESH_ID)
-    pl.semaphore_wait(barrier, len(sums.peers()))
-    sums.begin()
-    for phase in range(1, sums.bits + 1):
-        sums.advance(phase)
-    sums.finish()
-
-
-def piece_sums(items, call_id):
-    items, shapes, shares = piece_shapes(items)
-    return pl.pallas_call(
-        partial(piece_sums_kernel, lax.axis_size("dp"), len(items)),
-        out_shape=shares,
-        in_specs=[VMEM_SPEC] * len(items),
-        out_specs=[VMEM_SPEC] * len(items),
-        scratch_shapes=PieceSums.scratch(lax.axis_size("dp"), shapes),
-        compiler_params=pltpu.CompilerParams(
-            collective_id=call_id, has_side_effects=True, vmem_limit_bytes=VMEM_LIMIT
-        ),
-    )(*items)
-
-
-def mesh_sum_kernel(axes, tile_ref, out_ref, held, send_sem, recv_sem):
-    barrier = pltpu.get_barrier_semaphore()
-    places = {name: lax.axis_index(name) for name, _ in axes}
-
-    def peer(name, count, step):
-        return {name: lax.rem(places[name] + step, count)}
-
-    for name, count in axes:
-
-        def greet(step, carry, name=name, count=count):
-            pl.semaphore_signal(
-                barrier, inc=1, device_id=peer(name, count, step), device_id_type=MESH_ID
-            )
-            return carry
-
-        lax.fori_loop(1, count, greet, 0)
-    pl.semaphore_wait(barrier, sum(count - 1 for _, count in axes))
-    value = tile_ref[...]
-    first = 0
-    for name, count in axes:
-        place = places[name]
-        held[first + place] = value
-
-        def copy(step, slot, name=name, count=count, first=first, place=place):
-            return remote(
-                held.at[first + place],
-                held.at[first + slot],
-                send_sem.at[first + step],
-                recv_sem.at[first + slot],
-                peer(name, count, step),
-            )
-
-        def send(step, carry, copy=copy, place=place):
-            copy(step, place).start()
-            return carry
-
-        def take(step, carry, copy=copy, count=count, place=place):
-            copy(step, lax.rem(place + step, count)).wait_recv()
-            return carry
-
-        def add(slot, carry, first=first):
-            return carry + held[first + slot]
-
-        def drain(step, carry, copy=copy, place=place):
-            copy(step, place).wait_send()
-            return carry
-
-        lax.fori_loop(1, count, send, 0)
-        lax.fori_loop(1, count, take, 0)
-        value = lax.fori_loop(1, count, add, held[first])
-        lax.fori_loop(1, count, drain, 0)
-        first += count
-    out_ref[...] = value
-
-
-def mesh_sum(tile, names, call_id):
-    axes = [(name, lax.axis_size(name)) for name in names]
-    slots = sum(count for _, count in axes)
-    return pl.pallas_call(
-        partial(mesh_sum_kernel, axes),
-        out_shape=jax.ShapeDtypeStruct(tile.shape, jnp.float32),
-        in_specs=[VMEM_SPEC],
-        out_specs=VMEM_SPEC,
-        scratch_shapes=[
-            pltpu.VMEM((slots,) + tile.shape, jnp.float32),
-            pltpu.SemaphoreType.DMA((slots,)),
-            pltpu.SemaphoreType.DMA((slots,)),
-        ],
-        compiler_params=pltpu.CompilerParams(collective_id=call_id, has_side_effects=True),
-    )(tile)
 
 
 def adam_update(master, first, second, gradient, scale):
@@ -799,6 +888,171 @@
         fixed_first / (jnp.sqrt(fixed_second) + adam_eps) + weight_decay * master
     )
     return (updated, moment, square)
+
+
+def sum_rows(values):
+    return jnp.sum(values.reshape(-1, 8, values.shape[-1]), 0)
+
+
+def closing_kernel(count, count_dp, sizes, *refs):
+    refs = list(refs)
+
+    def pull(number):
+        taken = refs[:number]
+        del refs[:number]
+        return taken
+
+    number, finished, states = sizes
+    items, (columns, tile), done = pull(number), pull(2), pull(finished)
+    state_in, state_out, (stats,) = pull(states), pull(states), pull(1)
+    shares = pull(number)
+    sums = PieceSums(count_dp, items, shares, pull(number * (count_dp.bit_length() + 1)))
+    (write_share,) = pull(1)
+    scatter = LineScatter(count, columns, write_share, pull(4), pull(4))
+    small = [Spread("mp", count, *pull(3)) for _ in range(2)]
+    over_dp, over_mp = Spread("dp", count_dp, *pull(3)), Spread("mp", count, *pull(3))
+    held, (turned, in_sems, out_sems) = pull(states), pull(3)
+
+    barrier = pltpu.get_barrier_semaphore()
+    others = [over_dp.peer(step) for step in range(1, count_dp)]
+    others += [over_mp.peer(step) for step in range(1, count)]
+    signal_all(barrier, others)
+    loads = [
+        pltpu.make_async_copy(source, target, in_sems.at[index])
+        for index, (source, target) in enumerate(zip(state_in, held))
+    ]
+    for load in loads:
+        load.start()
+    pl.semaphore_wait(barrier, len(others))
+
+    sums.begin()
+    scatter.run(lambda: sums.advance(1))
+    for phase in range(2, sums.bits + 1):
+        sums.advance(phase)
+    for spread, share in zip(small, shares[-2:]):
+        spread.held[spread.place] = share[...]
+        spread.start()
+    scatter.settle()
+
+    self_in_2, self_out, read_query, read_key, read_value, read_out = shares[:6]
+    self_in_0, self_in_1 = done[:2]
+    up, down = done[2:6], done[6:10]
+    lat_rows, if_rows = self_out.shape[0], read_key.shape[0]
+    write_key, write_value = (write_share.at[pl.ds(i * lat_rows, lat_rows)] for i in range(2))
+    write_query, write_out = (
+        write_share.at[pl.ds(2 * lat_rows + i * if_rows, if_rows)] for i in range(2)
+    )
+    for index, share in enumerate([read_out, self_out] + down):
+        turned[index] = share[...].T
+    split = [read_query, read_key, read_value, read_out, self_in_0, self_in_1, self_in_2, self_out]
+    square = sum(sum_rows(ref[...] * ref[...]) for ref in split + up + down + [write_share])
+    for spread in small:
+        spread.take()
+    latents, rest = (spread.total() for spread in small)
+    lead = (over_mp.place == 0).astype(jnp.float32)
+    local = jnp.sum(square) + lead * (
+        jnp.sum(sum_rows(latents * latents)) + jnp.sum(sum_rows(rest * rest))
+    )
+    lane = lax.broadcasted_iota(jnp.int32, (8, 128), 1)
+    value = jnp.where(lane == 0, local, tile[...])
+    for spread in (over_dp, over_mp):
+        spread.held[spread.place] = value
+        spread.start()
+        spread.take()
+        value = spread.total()
+    norm = jnp.sqrt(value)
+    stats[...] = jnp.where(lane == 0, norm, value)
+    first = jnp.logical_and(lane == 0, lax.broadcasted_iota(jnp.int32, (8, 128), 0) == 0)
+    scale = jnp.sum(jnp.where(first, clip_level / jnp.maximum(norm, clip_level), 0.0))
+
+    def update(kind, at, gradient):
+        refs = held[3 * kind : 3 * kind + 3]
+        results = adam_update(refs[0][at], refs[1][at], refs[2][at], gradient, scale)
+        for ref, result in zip(refs, results):
+            ref[at] = result
+
+    def update_rows(kind, slot, gradient):
+        rows, width = gradient.shape
+        step = math.gcd(rows, max(8, 8192 // width))
+
+        def one(index, carry):
+            where = pl.ds(pl.multiple_of(index * step, step), step)
+            at = (where,) if slot is None else (slot, where)
+            update(kind, at, gradient[where])
+            return carry
+
+        lax.fori_loop(0, rows // step, one, 0)
+
+    def store(kind):
+        for index in range(3 * kind, 3 * kind + 3):
+            pltpu.make_async_copy(held[index], state_out[index], out_sems.at[index]).start()
+
+    for load in loads:
+        load.wait()
+    wide = [read_query, self_in_0, self_in_1, self_in_2] + up + [write_key, write_value]
+    for slot, gradient in enumerate(wide):
+        update_rows(0, slot, gradient)
+    store(0)
+    for slot in range(turned.shape[0]):
+        update_rows(2, slot, turned.at[slot])
+    store(2)
+    for slot, gradient in enumerate([read_key, read_value, write_query]):
+        update_rows(1, slot, gradient)
+    store(1)
+    update_rows(3, None, write_out)
+    store(3)
+    update(4, (slice(None),), latents)
+    store(4)
+    gains, lanes = held[15].shape
+    update(5, (slice(None),), rest[:gains, :lanes])
+    store(5)
+    for slot in range(2):
+        low = 16 * (slot + 1)
+        update(6, (slot,), rest[low : low + PIX, :lanes])
+    store(6)
+    sums.finish()
+    scatter.finish()
+    for spread in small + [over_dp, over_mp]:
+        spread.finish()
+    for index in range(states):
+        pltpu.make_async_copy(held[index], state_out[index], out_sems.at[index]).wait()
+
+
+def closing(items, columns, tile, done, states, call_id):
+    items, shapes, shares = piece_shapes(items)
+    count, count_dp = lax.axis_size("mp"), lax.axis_size("dp")
+    shares = [pltpu.VMEM(item.shape, jnp.float32) for item in shares]
+    held = [pltpu.VMEM(item.shape, jnp.float32) for item in states]
+    turned = (6,) + done[0].shape[::-1]
+    state_sems = pltpu.SemaphoreType.DMA((len(states),))
+    scratch = (
+        shares
+        + PieceSums.scratch(count_dp, shapes)
+        + [pltpu.VMEM((columns.shape[0] // count, columns.shape[1]), jnp.float32)]
+        + LineScatter.scratch(count, columns.shape, 4)
+        + Spread.scratch(count, tuple(shares[-2].shape))
+        + Spread.scratch(count, tuple(shares[-1].shape))
+        + Spread.scratch(count_dp, tile.shape)
+        + Spread.scratch(count, tile.shape)
+        + held
+        + [pltpu.VMEM(turned, jnp.float32), state_sems, state_sems]
+    )
+    here = [*items, columns, tile, *done]
+    any_spec = pl.BlockSpec(memory_space=pl.ANY)
+    results = pl.pallas_call(
+        partial(closing_kernel, count, count_dp, (len(items), len(done), len(states))),
+        out_shape=[jax.ShapeDtypeStruct(item.shape, jnp.float32) for item in states]
+        + [jax.ShapeDtypeStruct((8, 128), jnp.float32)],
+        in_specs=[VMEM_SPEC] * len(here) + [any_spec] * len(states),
+        out_specs=[any_spec] * len(states) + [VMEM_SPEC],
+        scratch_shapes=scratch,
+        compiler_params=pltpu.CompilerParams(
+            collective_id=call_id,
+            has_side_effects=True,
+            vmem_limit_bytes=room(here, room_of(scratch)),
+        ),
+    )(*here, *states)
+    return results[:-1], results[-1]
 
 
 def body(
@@ -860,16 +1114,6 @@
     gathered = lax.all_gather(
         jnp.concatenate([key_piece, value_piece, query_piece, out_piece], 0), "mp"
     )
-    gathered = lax.all_gather(gathered, "dp")
-    nothing = jnp.where(timesteps[0] > 0, 0.0, -0.0)
-    gathered = gathered + nothing
-    edges = [0, d_lat, 2 * d_lat, 2 * d_lat + d_if, 2 * d_lat + 2 * d_if]
-    write_key_weight, write_value_weight, write_query_weight, write_out_weight = (
-        jnp.swapaxes(gathered[:, :, low // count_dp : high // count_dp], 1, 2)
-        .reshape(high - low, count_mp * local)
-        .astype(jnp.bfloat16)
-        for low, high in zip(edges[:-1], edges[1:])
-    )
 
     signal = jnp.cos(0.5 * math.pi * (timesteps.astype(jnp.float32) + 0.5) / NSTEPS) ** 2
     noisy = (
@@ -879,7 +1123,6 @@
     loss_weight = 0.5 + signal
     keep_float = present_mask.astype(jnp.float32)
     weight_here = jnp.sum(loss_weight * PIX * jnp.sum(keep_float, 1))
-    weight_total = mesh_sum(jnp.full((8, 128), weight_here), ("dp",), 1)[0, 0]
     gain_rows = copy_gains.astype(jnp.float32)
 
     def wide_gain(index):
@@ -905,11 +1148,18 @@
         "bpd,dc->bpc", side_low, copy_narrowin[:, 1], preferred_element_type=jnp.float32
     ).astype(jnp.bfloat16)
     read_out, read_total = attend_forward(read_query, read_key, read_value, present_mask)
-    latent_one = line_sum(
-        jnp.einsum("blc,cd->bld", read_out, copy_wideout[0], preferred_element_type=jnp.float32),
+    read_part = jnp.einsum(
+        "blc,cd->bld", read_out, copy_wideout[0], preferred_element_type=jnp.float32
+    )
+    gathered, read_part = lax.optimization_barrier((gathered, read_part))
+    gathered = lax.all_gather(gathered, "dp").reshape(count_dp * count_mp, -1, local)
+    latent_one, (weight_tile,) = line_sum(
+        read_part,
         jnp.broadcast_to(latent_zero[None], (images, latents, d_lat)),
         2,
-    )[0]
+        tile=jnp.full((8, 128), weight_here),
+    )
+    weight_total = weight_tile[0, 0]
     self_norm, self_stats = layer_norm(latent_one, wide_gain(1))
     self_low = self_norm.astype(jnp.bfloat16)
     self_triple = jnp.einsum(
@@ -918,11 +1168,13 @@
     self_out, self_total = attend_forward(
         self_triple[:, :, 0], self_triple[:, :, 1], self_triple[:, :, 2], None
     )
-    latent_two = line_sum(
+    latent_two, write_weights = line_sum(
         jnp.einsum("blc,cd->bld", self_out, copy_wideout[1], preferred_element_type=jnp.float32),
         latent_one,
         3,
-    )[0]
+        blocks=(gathered, [d_lat, d_lat, d_if, d_if]),
+    )
+    write_key_weight, write_value_weight, write_query_weight, write_out_weight = write_weights
     feed_norm, feed_stats = layer_norm(latent_two, wide_gain(2))
     feed_low = feed_norm.astype(jnp.bfloat16)
     hidden = jnp.einsum(
@@ -963,6 +1215,7 @@
     def image_rows(values):
         if sharers == 1:
             return values
+        nothing = jnp.where(timesteps[0] > 0, 0.0, -0.0)
         whole = lax.all_gather(values.astype(jnp.float32), "mp", axis=0, tiled=True)
         whole = whole + nothing
         whole = whole.reshape(images, latents, d_lat).astype(jnp.bfloat16)
@@ -1096,8 +1349,7 @@
         latent_part, latent_grad, 7, up_grad[2:] + down_grad + self_in_grad[:2]
     )
     write_share = jnp.concatenate([key_share, five_shares[0], query_share, five_shares[1]], 0)
-    write_share = lax.optimization_barrier((write_share, latent_grad))[0]
-    write_share = lax.psum_scatter(write_share, "mp", scatter_dimension=1, tiled=True)
+    write_columns = jnp.concatenate(jnp.split(write_share, count_mp, 1), 0)
     branch_low = latent_grad.astype(jnp.bfloat16)
     read_out_grad = jnp.einsum(
         "bld,blc->dc", branch_low, read_out, preferred_element_type=jnp.float32
@@ -1150,19 +1402,34 @@
         0,
     )
 
-    def dp_columns(values):
-        values = values.reshape(-1, count_dp, values.shape[-1] // count_dp)
-        return jnp.swapaxes(values, 0, 1).reshape(count_dp, -1)
-
-    small_parts = [
-        dp_columns(item)
-        for item in (latent_total, gains_grad, embed_grad, head_grad)
-    ]
-    small_sizes = [item.shape[1] for item in small_parts]
-    small = jnp.concatenate(small_parts, 1)
-    fill = -small.shape[1] % (16 * local)
-    small = jnp.pad(small, ((0, 0), (0, fill))).reshape(-1, local)
-    last_shares = piece_sums(
+    def dp_pieces(values):
+        values = values.reshape(values.shape[0], count_dp, -1)
+        return jnp.swapaxes(values, 0, 1)
+
+    low_rows = [gains_grad, embed_grad, head_grad]
+    low_rows = [jnp.pad(item, ((0, 16 - item.shape[0]), (0, 0))) for item in low_rows]
+    rest = dp_pieces(jnp.concatenate(low_rows, 0))
+    rest = jnp.pad(rest, ((0, 0), (0, 0), (0, 128 - rest.shape[2])))
+    latents_item = dp_pieces(latent_total)
+
+    states = (
+        *(jnp.swapaxes(item, 0, 1) for item in (master_widein, first_widein, second_widein)),
+        *(jnp.swapaxes(item, 0, 1) for item in (master_narrowin, first_narrowin, second_narrowin)),
+        master_wideout,
+        first_wideout,
+        second_wideout,
+        *(item.T for item in (master_narrowout, first_narrowout, second_narrowout)),
+        master_latents,
+        first_latents,
+        second_latents,
+        master_gains,
+        first_gains,
+        second_gains,
+        master_pixels,
+        first_pixels,
+        second_pixels,
+    )
+    results, stats = closing(
         [
             self_in_grad[2],
             self_out_grad,
@@ -1170,92 +1437,20 @@
             read_key_grad,
             read_value_grad,
             read_out_grad,
-            small,
+            latents_item.reshape(-1, latents_item.shape[2]),
+            rest.reshape(-1, rest.shape[2]),
         ],
-        9,
-    )
-    lat_rows, if_rows = d_lat // count_dp, d_if // count_dp
-    small_share = mesh_sum(last_shares[6], ("mp",), 10)
-    small_flat = small_share.reshape(-1)
-    latents_grad, gains_grad, embed_grad, head_grad = (
-        small_flat[sum(small_sizes[:i]) : sum(small_sizes[: i + 1])].reshape(rows, -1)
-        for i, rows in enumerate((latents, gains_grad.shape[0], PIX, PIX))
-    )
-    pixels_grad = jnp.stack([embed_grad, head_grad], 0)
-
-    def cut(share, index, rows, start=0):
-        return share[start + index * rows : start + (index + 1) * rows]
-
-    widein_grad = jnp.stack(
-        [last_shares[2], six_shares[6], six_shares[7], last_shares[0]]
-        + list(five_shares[2:])
-        + list(six_shares[:2])
-        + [cut(write_share, i, lat_rows) for i in range(2)],
-        1,
-    )
-    narrowin_grad = jnp.stack(
-        [last_shares[3], last_shares[4], cut(write_share, 0, if_rows, 2 * lat_rows)], 1
-    )
-    wideout_grad = jnp.stack(
-        [last_shares[5].T, last_shares[1].T] + [item.T for item in six_shares[2:6]], 0
-    )
-    narrowout_grad = cut(write_share, 1, if_rows, 2 * lat_rows).T
-    shares = (
-        widein_grad,
-        narrowin_grad,
-        wideout_grad,
-        narrowout_grad,
-        latents_grad,
-        gains_grad,
-        pixels_grad,
-    )
-    split_square = sum((jnp.sum(item * item) for item in shares[:4]))
-    copied_square = sum((jnp.sum(item * item) for item in shares[4:]))
-    lane = lax.broadcasted_iota(jnp.int32, (8, 128), 1)
-    totals = mesh_sum(
-        jnp.where(lane == 0, split_square + lead * copied_square, loss_local), ("dp", "mp"), 8
-    )
-    square_total, loss_total = totals[0, 0], totals[0, 1]
-    grad_norm = jnp.sqrt(square_total)
-    loss_value = loss_total / weight_total
-    scale = clip_level / jnp.maximum(grad_norm, clip_level)
-    states = (
-        (master_widein, first_widein, second_widein),
-        (master_narrowin, first_narrowin, second_narrowin),
-        (master_wideout, first_wideout, second_wideout),
-        (master_narrowout, first_narrowout, second_narrowout),
-        (master_latents, first_latents, second_latents),
-        (master_gains, first_gains, second_gains),
-        (master_pixels, first_pixels, second_pixels),
-    )
-    results = []
-    for state, gradient in zip(states, shares):
-        results.extend(adam_update(state[0], state[1], state[2], gradient, scale))
-    return (
-        loss_value,
-        grad_norm,
-        results[0],
-        results[1],
-        results[2],
-        results[3],
-        results[4],
-        results[5],
-        results[6],
-        results[7],
-        results[8],
-        results[9],
-        results[10],
-        results[11],
-        results[12],
-        results[13],
-        results[14],
-        results[15],
-        results[16],
-        results[17],
-        results[18],
-        results[19],
-        results[20],
-    )
+        write_columns,
+        jnp.full((8, 128), loss_local),
+        [*six_shares[6:8], *five_shares[2:], *six_shares[:6]],
+        states,
+        8,
+    )
+    results = [
+        jnp.swapaxes(item, 0, 1) if index < 6 or 9 <= index < 12 else item
+        for index, item in enumerate(results)
+    ]
+    return (stats[0, 1] / weight_total, stats[0, 0], *results)
 
 
 def solution(mesh):

time: 829 us -> 716 us (0.86)
  waiting for transfers between devices: 64.6 us -> 8.7 us
  other arithmetic: 91.1 us -> 52.5 us
  local copies, waits for them, and re-layouts: 81.2 us -> 107 us
  Pallas kernels: 389 us -> 366 us
  matrix products: 166 us -> 156 us
    unnamed x374 -> x536, local copies, waits for them, and re-layouts: 31.2 us -> 68.6 us
    all_gather x1, waiting for transfers between devices: 39.9 us -> 8.67 us  [body(): lax.all_gather(jnp.concatenate([key_piece, value_piece, query_piece, out_...]
    pallas_call x9 -> x6, Pallas kernels: 358 us -> 333 us  [the longest x4 230 us: line_sum(): pl.pallas_call(partial(line_sum_kernel, count, count_dp, len(items), int(...]
    reduce_scatter x1 -> x0, waiting for transfers between devices: 24.7 us -> none  [body(): lax.psum_scatter(write_share, 'mp', scatter_dimension=1, tiled=True)]
    convert_element_type x6 -> x0, local copies, waits for them, and re-layouts: 19.8 us -> none  [body(): write_key_weight, write_value_weight, write_query_weight, write_out_weigh...]
    sub x7 -> x0, other arithmetic: 12.6 us -> none  [adam_update(): master - learning_rate * (fixed_first / (jnp.sqrt(fixed_second) + adam_ep...]
    another operation x1, other arithmetic: 8.57 us -> 0.26 us
  transfers between devices with their start and end apart: 3 -> 2, of which waited for: 2 -> 1; matrix products, arithmetic and copies ran while one was open for 11% -> 9% of each run, Pallas kernels for 19% -> 8%
where the time goes in v3:
time: 716 us; the launch traced here: 710 us
  Pallas kernels  366 us (51%)
  matrix products  156 us (22%)
  local copies, waits for them, and re-layouts  107 us (15%)
  other arithmetic  52.5 us (7%)
  between operations  20.1 us (3%)
  waiting for transfers between devices  8.7 us (1%)
    pallas_call x4, Pallas kernels, line_sum(): pl.pallas_call(partial(line_sum_kernel, count, count_dp, len(items), int(...  230 us
    unnamed x536, local copies, waits for them, and re-layouts  68.6 us
    pallas_call x1, Pallas kernels, closing(): pl.pallas_call(partial(closing_kernel, count, count_dp, (len(items), len(...  62.2 us
    pallas_call x1, Pallas kernels, line_gather(): pl.pallas_call(partial(line_gather_kernel, count, count_dp, extra), out_s...  40.5 us
    pallas_call x1, Pallas kernels, line_scatter(): pl.pallas_call(partial(line_scatter_kernel, count), out_shape=jax.ShapeDt...  33.1 us
  transfers between devices with their start and end apart: 2, of which 1 were waited for; matrix products, arithmetic and copies ran while one was open for 9% of the time, Pallas kernels for 8%

profile of v3, /device:TPU:0, one launch (start us, length us, event | category | flops | bytes accessed | tf_op | source)
XLA Modules:
  0.0 710.4 jit_solution(18208508716804804324)
XLA Ops:
  14.8 3.7 fusion.85
  21.1 7.5 %fusion.165 = (f32[4,1024]{1,0:T(4,128)S(1)}, f32[4,1024,512]{1,2,0:T(8,128)S(1)}, f32[4,1024,512]{1,2,0:T(8,128)}) fusion(f32[1024,512]{0,1:T(8,128)S(1)} %get-tuple-element.222, f32[4,12,1024]{2,1,0:T(8,128)S(1)} %get-tuple-element.233, bf16[1,12,512]{2,0,1:T(2,128)(2,1)S(1)} %get-tuple-element.239), kind=kOutput, calls=%fused_computation.346 | convolution fusion | flops 306180096 | bytes 19099648 | tf_op jit(solution)/shard_map/bcp,cd->bpd/dot_general | solution.py:1132
  37.5 2.3 convolution_convert_fusion.13
  39.8 2.9 fusion.104
  42.8 8.7 %all-gather.5.cloned.1.call-done = f32[1536,256]{1,0:T(8,128)} async-done(((f32[384,256]{1,0:T(8,128)}), f32[1536,256]{1,0:T(8,128)}) %all-gather.5.cloned.1.call-update) | async-done | bytes 1572880 | tf_op jit(solution)/shard_map/all_gather | solution.py:1114
  60.4 3.0 multiply_convert_fusion.6
  63.5 5.9 fusion.3
  71.0 57.6 %shard_map.479 = (f32[512,1024]{1,0:T(8,128)S(1)}, f32[8,128]{1,0:T(8,128)S(1)}) custom-call(f32[512,1024]{1,0:T(8,128)S(1)} %bitcast.621, f32[512,1024]{1,0:T(8,128)S(1)} %bitcast.620, f32[8,128]{1,0:T(8,128)S(1)} %broadcast_in_dim.37.refs_2_), custom_call_target="tpu_custom_call" | custom-call | flops 2097152 | bytes 183500800 | tf_op jit(solution)/shard_map/pallas_call | solution.py:593
  130.1 2.4 fusion.57
  139.5 2.4 copy.237
  144.0 2.8 fusion.101.refs_0_
  146.8 4.6 copy-done.5
  153.0 55.4 %shard_map.480 = (f32[512,1024]{1,0:T(8,128)S(1)}, bf16[1024,1024]{1,0:T(8,128)(2,1)S(1)}, bf16[1024,1024]{1,0:T(8,128)(2,1)S(1)}, bf16[512,1024]{1,0:T(8,128)(2,1)S(1)}, bf16[512,1024]{1,0:T(8,128)(2,1)S(1)}) custom-call(f32[512,1024]{1,0:T(8,128)S(1)} %copy-done.15, f32[512,1024]{1,0:T(8,128)S(1)} %get-tuple-element.72.refs_1_, f32[32,384,256]{2,1,0:T(8,128)S(1)} %copy-done.5), custom_call_target="tpu_custom_call" | custom-call | flops 2097152 | bytes 183500800 | tf_op jit(solution)/shard_map/pallas_call | solution.py:593
  213.4 2.1 reduce_sum.426
  218.1 3.7 fusion.108
  221.9 5.7 multiply_convert_fusion.7
  228.8 33.1 %shard_map.481 = f32[128,1024]{1,0:T(8,128)S(1)} custom-call(f32[512,1024]{1,0:T(8,128)S(1)} %bitcast.624), custom_call_target="tpu_custom_call" | custom-call | flops 1048576 | bytes 120586240 | tf_op jit(solution)/shard_map/pallas_call | solution.py:761
  266.2 3.0 convolution_convert_fusion.11
  270.9 2.6 convolution_convert_fusion.5
  278.2 3.6 fusion.174
  290.1 2.5 convolution_convert_fusion.9
  292.6 2.5 multiply_reduce_fusion.3
  295.1 2.6 multiply_convert_fusion.1
  301.5 2.6 fusion.175
  309.6 40.5 %shard_map.482 = (f32[512,1024]{1,0:T(8,128)S(1)}, f32[128,1024]{1,0:T(8,128)S(1)}, f32[64,1024]{1,0:T(8,128)S(1)}) custom-call(f32[128,1024]{1,0:T(8,128)S(1)} %fusion.100.own_ref, f32[8,128,1024]{2,1,0:T(8,128)S(1)} %fusion.176.refs_0_, f32[8,64,1024]{2,1,0:T(8,128)S(1)} %fusion.177.refs_1_), custom_call_target="tpu_custom_call" | custom-call | flops 131072 | bytes 131072000 | tf_op jit(solution)/shard_map/pallas_call | solution.py:865
  361.0 2.4 copy.233
  363.4 5.1 add_convert_fusion
  373.0 3.4 fusion.28
  381.2 57.5 %shard_map.483 = (f32[512,1024]{1,0:T(8,128)S(1)}, f32[128,1024]{1,0:T(8,128)S(1)}, f32[64,1024]{1,0:T(8,128)S(1)}, f32[128,256]{1,0:T(8,128)S(1)}, f32[128,256]{1,0:T(8,128)S(1)}) custom-call(f32[512,1024]{1,0:T(8,128)S(1)} %bitcast.623, f32[512,1024]{1,0:T(8,128)S(1)} %copy-done.14, f32[8,128,1024]{2,1,0:T(8,128)S(1)} %fusion.178.refs_2_, ...), custom_call_target="tpu_custom_call" | custom-call | flops 2097152 | bytes 183500800 | tf_op jit(solution)/shard_map/pallas_call | solution.py:593
  441.9 2.2 convolution_convert_fusion.8
  444.1 2.3 copy.239
  448.2 2.6 convolution_convert_fusion.7
  461.5 2.9 fusion.27
  467.3 59.4 %shard_map.484 = (f32[512,1024]{1,0:T(8,128)S(1)}, f32[128,256]{1,0:T(8,128)S(1)}, f32[128,256]{1,0:T(8,128)S(1)}, f32[128,256]{1,0:T(8,128)S(1)}, f32[128,256]{...) custom-call(f32[512,1024]{1,0:T(8,128)S(1)} %bitcast.622, ...), custom_call_target="tpu_custom_call" | custom-call | flops 2097152 | bytes 183500800 | tf_op jit(solution)/shard_map/pallas_call | solution.py:593
  531.7 7.0 convolution_convert_fusion.2
  538.7 5.5 multiply_reduce_fusion.2
  544.3 2.4 multiply_convert_fusion
  546.7 2.9 convert_reduce_fusion
  551.8 3.7 fusion.26
  560.1 2.6 fusion.167
  563.2 5.1 convolution_bitcast_fusion.13.refs_4_
  568.3 2.2 convolution_bitcast_fusion.14.refs_3_
  575.5 3.0 fusion.117
  578.7 9.1 %multiply_reduce_fusion.1 = (f32[512]{0:T(512)S(1)}, f32[4,1024]{1,0:T(4,128)S(1)}, f32[4,1024]{1,0:T(4,128)S(1)}, f32[4,1024,512]{1,2,0:T(8,128)}) fusion(f32[4,1024,512]{1,2,0:T(8,128)} %copy-done.104, f32[4,1024]{1,0:T(4,128)S(1)} %copy-done.182, f32[4,1024]{1,0:T(4,128)S(1)} %copy-done.180, f32[512]{0:T(512)S(1)} %bitcast.748, ...), kind=kOutput, calls=%fused_computation.11 | convolution fusion | flops 1092607488 | bytes 27594752 | tf_op jit(solution)/shard_map/bpc,dc->bpd/dot_general | solution.py:1385
  588.7 2.8 fusion.19
  592.1 8.3 %fusion.72 = f32[12,512]{1,0:T(8,128)S(1)} fusion(f32[12,512]{1,0:T(8,128)S(1)} %fusion.19, f32[4,12,1024]{2,1,0:T(8,128)S(1)} %copy-done.141, f32[4,1024,512]{1,2,0:T(8,128)S(1)} %copy-done.110, f32[4,1024,512]{1,2,0:T(8,128)S(1)} %bitcast.642, f32[4,1024]{1,0:T(4,128)S(1)} %broadcast_multiply_fusion.1, f32[4,1024]{1,0:T(4,128)S(1)} %broadcast_multiply_fusion.2, ...), kind=kOutput, calls=%fused_computation.174 | convolution fusion | flops 316676096 | bytes 17090560 | tf_op jit(solution)/shard_map/bcp,bpd->cd/dot_general | solution.py:1389
  606.3 62.2 %shard_map.485 = (f32[10,128,256]{2,1,0:T(8,128)S(1)}, f32[10,128,256]{2,1,0:T(8,128)S(1)}, f32[10,128,256]{2,1,0:T(8,128)S(1)}, f32[3,64,256]{2,1,0:T(8,128)S(1...) custom-call(f32[8,128,256]{2,1,0:T(8,128)S(1)} %convolution_bitcast_, ...), custom_call_target="tpu_custom_call" | custom-call | tf_op jit(solution)/shard_map/pallas_call | solution.py:1042
  687.3 2.5 copy.407
  (699 shorter events, 169.5 us)
Async XLA Ops:
  7.2 44.2 %all-gather.5.cloned.1.call-start = ((), (), s32[]{:S(2)}) async-start(), calls=%async_computation | async-start | bytes 1966080 | tf_op jit(solution)/shard_map/all_gather | solution.py:1114
  11.5 135.3 %all-gather.7.cloned.1.call-start = ((), (), s32[]{:S(2)}) async-start(), calls=%async_computation.1 | async-start | bytes 14155776 | tf_op jit(solution)/shard_map/all_gather | solution.py:1155
  11.7 25.8 %copy-start.183 = (pred[4,1024]{1,0:T(4,128)(4,1)}, pred[4,1024]{1,0:T(4,128)(4,1)S(1)}, u32[]{:S(2)}) copy-start(pred[4,1024]{1,0:T(4,128)(4,1)S(1)} %broadcast_compare_fusion) | copy-start | bytes 12292
  12.2 48.2 %copy-start.225 = (f32[1,512]{1,0:T(1,128)}, f32[1,512]{1,0:T(1,128)S(1)}, u32[]{:S(2)}) copy-start(f32[1,512]{1,0:T(1,128)S(1)} %get-tuple-element.241) | copy-start | bytes 6148
  12.2 51.2 %copy-start.207 = (f32[1,512]{1,0:T(1,128)}, f32[1,512]{1,0:T(1,128)S(1)}, u32[]{:S(2)}) copy-start(f32[1,512]{1,0:T(1,128)S(1)} %get-tuple-element.242) | copy-start | bytes 6148
  12.6 40.1 %copy-start.244 = (f32[128]{0:T(128)}, f32[128]{0:T(128)S(1)}, u32[]{:S(2)}) copy-start(f32[128]{0:T(128)S(1)} %add_rsqrt_fusion.4) | copy-start | bytes 1540
  12.7 40.0 %copy-start.209 = (f32[1,4,2,128]{3,1,2,0:T(4,128)}, f32[1,4,2,128]{3,1,2,0:T(4,128)S(1)}, u32[]{:S(2)}) copy-start(f32[1,4,2,128]{3,1,2,0:T(4,128)S(1)} %copy.357) | copy-start | bytes 12292
  14.8 17.3 %copy-start.166 = (bf16[128,256]{0,1:T(8,128)(2,1)}, bf16[128,256]{0,1:T(8,128)(2,1)S(1)}, u32[]{:S(2)}) copy-start(bf16[128,256]{0,1:T(8,128)(2,1)S(1)} %copy.210) | copy-start | bytes 196612
  21.1 7.5 %copy-start.140 = (f32[4,12,1024]{2,1,0:T(8,128)}, f32[4,12,1024]{2,1,0:T(8,128)S(1)}, u32[]{:S(2)}) copy-start(f32[4,12,1024]{2,1,0:T(8,128)S(1)} %get-tuple-element.233) | copy-start | bytes 589828
  28.6 7.1 copy-start.104
  28.6 34.8 %copy-start.179 = (f32[4,1024]{1,0:T(4,128)}, f32[4,1024]{1,0:T(4,128)S(1)}, u32[]{:S(2)}) copy-start(f32[4,1024]{1,0:T(4,128)S(1)} %broadcast_multiply_fusion.3) | copy-start | bytes 49156
  29.8 33.6 %copy-start.181 = (f32[4,1024]{1,0:T(4,128)}, f32[4,1024]{1,0:T(4,128)S(1)}, u32[]{:S(2)}) copy-start(f32[4,1024]{1,0:T(4,128)S(1)} %add_rsqrt_fusion) | copy-start | bytes 49156
  39.8 11.7 %copy-start.177 = (bf16[4,4,64,128]{3,2,1,0:T(8,128)(2,1)}, bf16[4,4,64,128]{3,2,1,0:T(8,128)(2,1)S(1)}, u32[]{:S(2)}) copy-start(bf16[4,4,64,128]{3,2,1,0:T(8,128)(2,1)S(1)} %convolution_convert_fusion.13) | copy-start | bytes 786436
  39.8 11.7 %copy-start.240 = (f32[2,12,64]{2,0,1:T(2,128)S(1)}, f32[2,12,64]{2,0,1:T(2,128)}, u32[]{:S(2)}) copy-start(f32[2,12,64]{2,0,1:T(2,128)} %param.61) | copy-start | bytes 18436
  39.8 11.7 %copy-start.241 = (f32[2,12,64]{2,0,1:T(2,128)S(1)}, f32[2,12,64]{2,0,1:T(2,128)}, u32[]{:S(2)}) copy-start(f32[2,12,64]{2,0,1:T(2,128)} %param.62) | copy-start | bytes 18436
  39.8 12.3 %copy-start.242 = (f32[2,12,64]{2,0,1:T(2,128)S(1)}, f32[2,12,64]{2,0,1:T(2,128)}, u32[]{:S(2)}) copy-start(f32[2,12,64]{2,0,1:T(2,128)} %param.63) | copy-start | bytes 18436
  52.7 213.4 %copy-start.192 = (f32[1,4,2,128]{3,1,2,0:T(4,128)}, f32[1,4,2,128]{3,1,2,0:T(4,128)S(1)}, u32[]{:S(2)}) copy-start(f32[1,4,2,128]{3,1,2,0:T(4,128)S(1)} %copy.361) | copy-start | bytes 12292
  52.7 164.9 %copy-start.223 = (f32[1,4,2,128]{3,1,2,0:T(4,128)}, f32[1,4,2,128]{3,1,2,0:T(4,128)S(1)}, u32[]{:S(2)}) copy-start(f32[1,4,2,128]{3,1,2,0:T(4,128)S(1)} %copy.360) | copy-start | bytes 12292
  52.8 77.0 %copy-start.221 = (f32[1,4,2,128]{3,1,2,0:T(4,128)}, f32[1,4,2,128]{3,1,2,0:T(4,128)S(1)}, u32[]{:S(2)}) copy-start(f32[1,4,2,128]{3,1,2,0:T(4,128)S(1)} %copy.358) | copy-start | bytes 12292
  60.4 9.0 %copy-start.215 = (f32[1024]{0:T(1024)}, f32[1024]{0:T(1024)S(1)}, u32[]{:S(2)}) copy-start(f32[1024]{0:T(1024)S(1)} %add_rsqrt_fusion.2) | copy-start | bytes 12292
  134.6 7.3 %copy-start.153 = (bf16[4,128,1,256]{1,3,0,2:T(8,128)(2,1)}, bf16[4,128,1,256]{1,3,0,2:T(8,128)(2,1)S(1)}, u32[]{:S(2)}) copy-start(bf16[4,128,1,256]{1,3,0,2:T(8,128)(2,1)S(1)} %copy.216) | copy-start | bytes 786436
  143.8 64.6 %copy-start.144 = (bf16[4,4,64,128]{3,2,1,0:T(8,128)(2,1)}, bf16[4,4,64,128]{3,2,1,0:T(8,128)(2,1)S(1)}, u32[]{:S(2)}) copy-start(bf16[4,4,64,128]{3,2,1,0:T(8,128)(2,1)S(1)} %convolution_convert_fusion.12) | copy-start | bytes 786436
  213.4 57.6 %copy-start.100 = (bf16[512,1024]{1,0:T(8,128)(2,1)}, bf16[512,1024]{1,0:T(8,128)(2,1)S(1)}, u32[]{:S(2)}) copy-start(bf16[512,1024]{1,0:T(8,128)(2,1)S(1)} %get-tuple-element.75) | copy-start | bytes 3145732
  221.9 5.7 copy-start.163
  221.9 5.7 copy-start.185
  301.5 5.8 copy-start.142
  441.9 6.3 copy-start.191
  531.7 7.0 copy-start.122
  531.7 12.5 %slice-start.2 = ((s8[8388608]{0:T(1024)(128)(4,1)}), s8[4194304]{0:T(1024)(128)(4,1)S(1)}, s32[]{:S(2)}) async-start(s8[8388608]{0:T(1024)(128)(4,1)} %bitcast.643), calls=%async_computation.4 | async-start | bytes 8388608
  575.5 12.3 %slice-start = ((s8[8388608]{0:T(1024)(128)(4,1)}), s8[4194304]{0:T(1024)(128)(4,1)S(1)}, s32[]{:S(2)}) async-start(s8[8388608]{0:T(1024)(128)(4,1)} %bitcast.641), calls=%async_computation.2 | async-start | bytes 8388608
  578.6 9.2 %slice-start.1 = ((s8[8388608]{0:T(1024)(128)(4,1)}), s8[4194304]{0:T(1024)(128)(4,1)S(1)}, s32[]{:S(2)}) async-start(s8[8388608]{0:T(1024)(128)(4,1)} %bitcast.641), calls=%async_computation.3 | async-start | bytes 8388608
  578.6 9.2 %copy-start.107 = (f32[1,1024,512]{1,2,0:T(8,128)S(1)}, f32[1,1024,512]{1,2,0:T(8,128)}, u32[]{:S(2)}) copy-start(f32[1,1024,512]{1,2,0:T(8,128)} %copy-done.106) | copy-start | bytes 6291460
  578.6 9.2 %copy-start.112 = (f32[1024,512]{0,1:T(8,128)S(1)}, f32[1024,512]{0,1:T(8,128)}, u32[]{:S(2)}) copy-start(f32[1024,512]{0,1:T(8,128)} %copy-done.111) | copy-start | bytes 6291460
  578.6 10.0 %copy-start.128 = (f32[1024,512]{0,1:T(8,128)S(1)}, f32[1024,512]{0,1:T(8,128)}, u32[]{:S(2)}) copy-start(f32[1024,512]{0,1:T(8,128)} %copy-done.127) | copy-start | bytes 6291460
  578.6 10.0 %copy-start.141 = (f32[4,12,1024]{2,1,0:T(8,128)S(1)}, f32[4,12,1024]{2,1,0:T(8,128)}, u32[]{:S(2)}) copy-start(f32[4,12,1024]{2,1,0:T(8,128)} %copy-done.140) | copy-start | bytes 589828
  578.6 10.0 %copy-start.198 = (f32[1024]{0:T(1024)S(1)}, f32[1024]{0:T(1024)}, u32[]{:S(2)}) copy-start(f32[1024]{0:T(1024)} %copy-done.197) | copy-start | bytes 12292
  578.6 10.0 %copy-start.201 = (f32[1024]{0:T(1024)S(1)}, f32[1024]{0:T(1024)}, u32[]{:S(2)}) copy-start(f32[1024]{0:T(1024)} %copy-done.200) | copy-start | bytes 12292
  578.6 10.0 %copy-start.206 = (f32[1,512]{1,0:T(1,128)S(1)}, f32[1,512]{1,0:T(1,128)}, u32[]{:S(2)}) copy-start(f32[1,512]{1,0:T(1,128)} %get-tuple-element.240) | copy-start | bytes 6148
  578.6 10.0 %copy-start.218 = (f32[1024]{0:T(1024)S(1)}, f32[1024]{0:T(1024)}, u32[]{:S(2)}) copy-start(f32[1024]{0:T(1024)} %copy-done.217) | copy-start | bytes 12292
  578.6 10.0 %copy-start.220 = (f32[1024]{0:T(1024)S(1)}, f32[1024]{0:T(1024)}, u32[]{:S(2)}) copy-start(f32[1024]{0:T(1024)} %copy-done.219) | copy-start | bytes 12292
  592.1 8.3 %copy-start.243 = (f32[512]{0:T(512)S(1)}, f32[512]{0:T(512)}, u32[]{:S(2)}) copy-start(f32[512]{0:T(512)} %get-tuple-element.193) | copy-start | bytes 6148
  592.1 8.6 %copy-start.135 = (bf16[4,128,1024]{1,2,0:T(8,128)(2,1)S(1)}, bf16[4,128,1024]{1,2,0:T(8,128)(2,1)}, u32[]{:S(2)}) copy-start(bf16[4,128,1024]{1,2,0:T(8,128)(2,1)} %copy.239) | copy-start | bytes 3145732
  592.1 8.6 %copy-start.145 = (bf16[4,4,64,128]{3,2,1,0:T(8,128)(2,1)S(1)}, bf16[4,4,64,128]{3,2,1,0:T(8,128)(2,1)}, u32[]{:S(2)}) copy-start(bf16[4,4,64,128]{3,2,1,0:T(8,128)(2,1)} %copy-done.144) | copy-start | bytes 786436
  681.3 8.4 %copy-start.22 = (f32[10,128,256]{2,1,0:T(8,128)S(1)}, f32[10,128,256]{2,1,0:T(8,128)}, u32[]{:S(2)}) copy-start(f32[10,128,256]{2,1,0:T(8,128)} %copy-done.21) | copy-start | bytes 3932164
  693.9 8.3 %copy-start.1 = (bf16[256,512]{1,0:T(8,128)(2,1)S(1)}, bf16[256,512]{1,0:T(8,128)(2,1)}, u32[]{:S(2)}) copy-start(bf16[256,512]{1,0:T(8,128)(2,1)} %param.39) | copy-start | bytes 786436
  694.8 5.6 copy-start.99
  694.8 6.2 copy-start.97
  694.8 6.8 copy-start.95
  (205 other events, 512.0 us)
Sparse Core Ops, SparseCore 0:
  11.6 39.7 all-gather.4
  53.3 71.3 all-gather.6

commit v4 on v3

--- a/solution.py
+++ b/solution.py
@@ -3,6 +3,7 @@
 
 import jax
 import jax.numpy as jnp
+import numpy as np
 from jax import lax
 from jax.experimental import pallas as pl
 from jax.experimental.pallas import tpu as pltpu
@@ -39,6 +40,12 @@
     )
     gain_grad = jnp.sum((upstream * normed).reshape(-1, normed.shape[-1]), 0)
     return (values, gain_grad)
+
+
+def position_table(count, width):
+    place = np.arange(count, dtype=np.float64)[:, None]
+    angle = place * 10000.0 ** (-2.0 * np.arange(width // 2) / width)
+    return jnp.asarray(np.concatenate([np.sin(angle), np.cos(angle)], -1), jnp.float32)
 
 
 def positions(count, width):
@@ -381,6 +388,13 @@
         pl.semaphore_wait(barrier, 1 + len(others))
 
 
+def views(refs):
+    result = []
+    for ref in refs:
+        result += [ref] if len(ref.shape) == 3 else [ref.at[slot] for slot in range(ref.shape[0])]
+    return result
+
+
 def line_sum_kernel(count, count_dp, extra, tiled, converted, *refs):
     refs = list(refs)
 
@@ -390,9 +404,9 @@
         return taken
 
     part_ref, base_ref = pull(2)
-    items, tile, blocks = pull(extra), pull(tiled), pull(min(1, converted))
+    items, tile, blocks = views(pull(extra)), pull(tiled), pull(min(1, converted))
     (out_ref,) = pull(1)
-    outs, tile_out, wide = pull(extra), pull(tiled), pull(converted)
+    outs, tile_out, wide = pull(len(items)), pull(tiled), pull(converted)
     inner, from_away, from_toward, toward_send, away_send, away_recv, toward_recv = pull(7)
     chunks = toward_send.shape[0]
     spread = Spread("dp", count_dp, *pull(3)) if tiled else None
@@ -557,8 +571,10 @@
 
 def piece_shapes(items):
     count = lax.axis_size("dp")
-    items = [item.reshape(count, -1, item.shape[-1]) for item in items]
-    shapes = [item.shape[1:] for item in items]
+    items = [item.reshape(item.shape[:-2] + (count, -1, item.shape[-1])) for item in items]
+    shapes = []
+    for item in items:
+        shapes += [item.shape[-2:]] * (item.shape[0] if item.ndim == 4 else 1)
     return items, shapes, [jax.ShapeDtypeStruct(shape, jnp.float32) for shape in shapes]
 
 
@@ -774,9 +790,10 @@
 
 
 def line_gather_kernel(count, count_dp, extra, own_ref, *refs):
-    items, out_ref, outs = refs[:extra], refs[extra], refs[extra + 1 : 2 * extra + 1]
-    up_send, down_send, up_recv, down_recv = refs[2 * extra + 1 : 2 * extra + 5]
-    sums = PieceSums(count_dp, items, outs, refs[2 * extra + 5 :])
+    items, out_ref, refs = views(refs[:extra]), refs[extra], refs[extra + 1 :]
+    outs, refs = refs[: len(items)], refs[len(items) :]
+    up_send, down_send, up_recv, down_recv = refs[:4]
+    sums = PieceSums(count_dp, items, outs, refs[4:])
     place = lax.axis_index("mp")
     steps = up_send.shape[1]
     block = own_ref.shape[0]
@@ -866,7 +883,7 @@
         partial(line_gather_kernel, count, count_dp, extra),
         out_shape=[jax.ShapeDtypeStruct((rows * count, width), jnp.float32)] + shares,
         in_specs=[VMEM_SPEC] * (1 + extra),
-        out_specs=[VMEM_SPEC] * (1 + extra),
+        out_specs=[VMEM_SPEC] * (1 + len(shares)),
         scratch_shapes=[sems] * 4 + scratch,
         compiler_params=pltpu.CompilerParams(
             collective_id=call_id, has_side_effects=True, vmem_limit_bytes=limit
@@ -878,6 +895,639 @@
     return results[0], results[1:]
 
 
+def dot(left, right, left_dim=1, right_dim=0):
+    return lax.dot_general(
+        left, right, (((left_dim,), (right_dim,)), ((), ())), preferred_element_type=jnp.float32
+    )
+
+
+def head_mask(width, copies):
+    lane = lax.broadcasted_iota(jnp.int32, (1, width), 1)
+    return [lane // HEAD_DIM == head for head in range(copies)]
+
+
+def spread_heads(values):
+    masks = head_mask(values.shape[1], values.shape[1] // HEAD_DIM)
+    return jnp.concatenate([jnp.where(mask, values, jnp.zeros_like(values)) for mask in masks], 0)
+
+
+def join_heads(values, heads):
+    rows = values.shape[0] // heads
+    masks = head_mask(values.shape[1], heads)
+    return sum(
+        jnp.where(mask, values[head * rows : (head + 1) * rows], 0.0)
+        for head, mask in enumerate(masks)
+    )
+
+
+def split_three(values):
+    first = values.astype(jnp.bfloat16)
+    left = values - first.astype(jnp.float32)
+    second = left.astype(jnp.bfloat16)
+    third = (left - second.astype(jnp.float32)).astype(jnp.bfloat16)
+    return first, second, third
+
+
+def norm_rows(values):
+    centered = values - jnp.mean(values, -1, keepdims=True)
+    scale = lax.rsqrt(jnp.mean(centered * centered, -1, keepdims=True) + 1e-05)
+    return centered * scale, scale
+
+
+def norm_rows_back(upstream, gain, normed, scale):
+    inner = upstream * gain
+    return scale * (
+        inner
+        - jnp.mean(inner, -1, keepdims=True)
+        - normed * jnp.mean(inner * normed, -1, keepdims=True)
+    )
+
+
+def embed(noisy, pixels, place):
+    stacked = jnp.concatenate(split_three(noisy), 0)
+    return dot(stacked, jnp.concatenate([pixels] * 3, 0), 0, 0) + place
+
+
+def read_forward_kernel(
+    noisy_ref,
+    keep_ref,
+    place_ref,
+    pixels_ref,
+    latents_ref,
+    wide_gain_ref,
+    gain_ref,
+    query_weight_ref,
+    pair_weight_ref,
+    out_weight_ref,
+    part_ref,
+    pairs_ref,
+    output_ref,
+    total_ref,
+    queries_ref,
+):
+    heads = query_weight_ref.shape[2] // HEAD_DIM
+
+    @pl.when(pl.program_id(0) == 0)
+    def _():
+        normed, _ = norm_rows(latents_ref[...].astype(jnp.float32))
+        low = (normed * wide_gain_ref[...]).astype(jnp.bfloat16)
+        queries = dot(low, query_weight_ref[0]).astype(jnp.bfloat16)
+        queries_ref[...] = spread_heads(queries * jnp.bfloat16(HEAD_DIM ** (-0.5)))
+
+    normed, _ = norm_rows(embed(noisy_ref[0], pixels_ref[...], place_ref[...]))
+    side = (normed * gain_ref[...]).astype(jnp.bfloat16)
+    keys = dot(side, pair_weight_ref[0]).astype(jnp.bfloat16)
+    values = dot(side, pair_weight_ref[1]).astype(jnp.bfloat16)
+    pairs_ref[0, 0] = keys
+    pairs_ref[0, 1] = values
+    scores = dot(keys, queries_ref[...], 1, 1)
+    scores = jnp.where(keep_ref[0] > 0, scores, -1e30)
+    top = jnp.max(scores, 0, keepdims=True)
+    grown = jnp.exp(scores - top)
+    summed = jnp.sum(grown, 0, keepdims=True)
+    total_ref[0] = top + jnp.log(summed)
+    probs = (grown / summed).astype(jnp.bfloat16)
+    output = join_heads(dot(probs, values, 0, 0), heads).astype(jnp.bfloat16)
+    output_ref[0] = output
+    part_ref[...] = dot(output, out_weight_ref[0])
+
+
+def whole(shape):
+    return pl.BlockSpec(shape, lambda b: (0,) * len(shape))
+
+
+def each(shape):
+    return pl.BlockSpec((1,) + shape, lambda b: (b,) + (0,) * len(shape))
+
+
+def slot_of(shape, slot):
+    return pl.BlockSpec(shape, lambda b: (slot,) + (0,) * (len(shape) - 1))
+
+
+def read_forward(noisy, keep, place, pixels, latents, wide_gain, gain, wide, narrow, wideout):
+    images, _, patches = noisy.shape
+    count, d_lat = latents.shape
+    d_if, local = narrow.shape[1:]
+    stacked = local // HEAD_DIM * count
+    return pl.pallas_call(
+        read_forward_kernel,
+        grid=(images,),
+        out_shape=[
+            jax.ShapeDtypeStruct((images * count, d_lat), jnp.float32),
+            jax.ShapeDtypeStruct((images, 2, patches, local), jnp.bfloat16),
+            jax.ShapeDtypeStruct((images, count, local), jnp.bfloat16),
+            jax.ShapeDtypeStruct((images, 1, stacked), jnp.float32),
+            jax.ShapeDtypeStruct((stacked, local), jnp.bfloat16),
+        ],
+        in_specs=[
+            each(noisy.shape[1:]),
+            each((patches, 1)),
+            whole((patches, d_if)),
+            whole(pixels.shape),
+            whole(latents.shape),
+            whole((1, d_lat)),
+            whole((1, d_if)),
+            slot_of((1, d_lat, local), 0),
+            slot_of((2, d_if, local), 0),
+            slot_of((1, local, d_lat), 0),
+        ],
+        out_specs=[
+            pl.BlockSpec((count, d_lat), lambda b: (b, 0)),
+            each((2, patches, local)),
+            each((count, local)),
+            each((1, stacked)),
+            whole((stacked, local)),
+        ],
+        compiler_params=pltpu.CompilerParams(vmem_limit_bytes=40 << 20),
+        cost_estimate=pl.CostEstimate(
+            flops=10**10, bytes_accessed=30 * 10**6, transcendentals=2 * 10**6
+        ),
+    )(noisy, keep, place, pixels, latents, wide_gain, gain, wide, narrow, wideout)
+
+
+def read_backward_kernel(
+    noisy_ref,
+    keep_ref,
+    place_ref,
+    pixels_ref,
+    latents_ref,
+    wide_gain_ref,
+    gain_ref,
+    query_weight_ref,
+    pair_weight_ref,
+    out_weight_ref,
+    pairs_ref,
+    output_ref,
+    total_ref,
+    queries_ref,
+    grad_ref,
+    lead_ref,
+    query_grad_ref,
+    key_grad_ref,
+    value_grad_ref,
+    out_grad_ref,
+    latents_grad_ref,
+    wide_gain_grad_ref,
+    gain_grad_ref,
+    embed_grad_ref,
+    low_ref,
+    returned_ref,
+):
+    step, steps = pl.program_id(0), pl.num_programs(0)
+    heads = query_weight_ref.shape[2] // HEAD_DIM
+
+    @pl.when(step == 0)
+    def _():
+        normed, _ = norm_rows(latents_ref[...].astype(jnp.float32))
+        low_ref[...] = (normed * wide_gain_ref[...]).astype(jnp.bfloat16)
+        for ref in (
+            query_grad_ref,
+            key_grad_ref,
+            value_grad_ref,
+            out_grad_ref,
+            latents_grad_ref,
+            gain_grad_ref,
+            embed_grad_ref,
+            returned_ref,
+        ):
+            ref[...] = jnp.zeros_like(ref)
+
+    normed, scale = norm_rows(embed(noisy_ref[0], pixels_ref[...], place_ref[...]))
+    side = (normed * gain_ref[...]).astype(jnp.bfloat16)
+    keys, values, queries = pairs_ref[0, 0], pairs_ref[0, 1], queries_ref[...]
+    branch = grad_ref[...].astype(jnp.bfloat16)
+    latents_grad_ref[...] += lead_ref[...] * grad_ref[...]
+    out_grad_ref[...] += dot(branch, output_ref[0], 0, 0)
+    upstream = spread_heads(dot(branch, out_weight_ref[0], 1, 1).astype(jnp.bfloat16))
+    scores = dot(keys, queries, 1, 1)
+    scores = jnp.where(keep_ref[0] > 0, scores, -1e30)
+    probs = jnp.exp(scores - total_ref[0])
+    value_grad = dot(probs.astype(jnp.bfloat16), upstream).astype(jnp.bfloat16)
+    prob_grad = dot(values, upstream, 1, 1)
+    inner = jnp.sum(prob_grad * probs, 0, keepdims=True)
+    score_grad = (probs * (prob_grad - inner)).astype(jnp.bfloat16)
+    key_grad = dot(score_grad, queries).astype(jnp.bfloat16)
+    query_grad = join_heads(dot(score_grad, keys, 0, 0), heads) * HEAD_DIM ** (-0.5)
+    query_grad = query_grad.astype(jnp.bfloat16)
+    query_grad_ref[...] += dot(low_ref[...], query_grad, 0, 0)
+    returned_ref[...] += dot(query_grad, query_weight_ref[0], 1, 1)
+    key_grad_ref[...] += dot(side, key_grad, 0, 0)
+    value_grad_ref[...] += dot(side, value_grad, 0, 0)
+    side_grad = dot(key_grad, pair_weight_ref[0], 1, 1) + dot(value_grad, pair_weight_ref[1], 1, 1)
+    gain_grad_ref[...] += jnp.sum(side_grad * normed, 0, keepdims=True)
+    back = norm_rows_back(side_grad, gain_ref[...], normed, scale)
+    embed_grad_ref[...] += embed_back(noisy_ref[0], back)
+
+    @pl.when(step == steps - 1)
+    def _():
+        normed, scale = norm_rows(latents_ref[...].astype(jnp.float32))
+        returned = returned_ref[...]
+        wide_gain_grad_ref[...] = jnp.sum(returned * normed, 0, keepdims=True)
+        latents_grad_ref[...] += norm_rows_back(returned, wide_gain_ref[...], normed, scale)
+
+
+def embed_back(noisy, back):
+    first, second, _ = split_three(noisy)
+    high = back.astype(jnp.bfloat16)
+    low = (back - high.astype(jnp.float32)).astype(jnp.bfloat16)
+    rows = noisy.shape[0]
+    both = dot(jnp.concatenate([first, second], 0), high)
+    return both[:rows] + both[rows:] + dot(first, low)
+
+
+def read_backward(
+    noisy,
+    keep,
+    place,
+    pixels,
+    latents,
+    wide_gain,
+    gain,
+    wide,
+    narrow,
+    wideout,
+    pairs,
+    output,
+    total,
+    queries,
+    grad,
+    lead,
+):
+    images, rows, patches = noisy.shape
+    count, d_lat = latents.shape
+    d_if, local = narrow.shape[1:]
+    stacked = local // HEAD_DIM * count
+    results = [
+        (d_lat, local),
+        (d_if, local),
+        (d_if, local),
+        (d_lat, local),
+        (count, d_lat),
+        (1, d_lat),
+        (1, d_if),
+        (rows, d_if),
+    ]
+    return pl.pallas_call(
+        read_backward_kernel,
+        grid=(images,),
+        out_shape=[jax.ShapeDtypeStruct(shape, jnp.float32) for shape in results],
+        in_specs=[
+            each(noisy.shape[1:]),
+            each((patches, 1)),
+            whole((patches, d_if)),
+            whole(pixels.shape),
+            whole(latents.shape),
+            whole((1, d_lat)),
+            whole((1, d_if)),
+            slot_of((1, d_lat, local), 0),
+            slot_of((2, d_if, local), 0),
+            slot_of((1, local, d_lat), 0),
+            each((2, patches, local)),
+            each((count, local)),
+            each((1, stacked)),
+            whole((stacked, local)),
+            pl.BlockSpec((count, d_lat), lambda b: (b, 0)),
+            whole((1, 1)),
+        ],
+        out_specs=[whole(shape) for shape in results],
+        scratch_shapes=[
+            pltpu.VMEM((count, d_lat), jnp.bfloat16),
+            pltpu.VMEM((count, d_lat), jnp.float32),
+        ],
+        compiler_params=pltpu.CompilerParams(vmem_limit_bytes=48 << 20),
+        cost_estimate=pl.CostEstimate(
+            flops=2 * 10**10, bytes_accessed=30 * 10**6, transcendentals=2 * 10**6
+        ),
+    )(
+        noisy,
+        keep,
+        place,
+        pixels,
+        latents,
+        wide_gain,
+        gain,
+        wide,
+        narrow,
+        wideout,
+        pairs,
+        output,
+        total,
+        queries,
+        grad,
+        lead,
+    )
+
+
+def rows_of(rows, width):
+    return pl.BlockSpec((rows, width), lambda b: (b, 0))
+
+
+def attend_few(keys, values, queries):
+    scores = dot(keys, queries, 1, 1)
+    top = jnp.max(scores, 0, keepdims=True)
+    grown = jnp.exp(scores - top)
+    summed = jnp.sum(grown, 0, keepdims=True)
+    probs = (grown / summed).astype(jnp.bfloat16)
+    return dot(probs, values, 0, 0), top + jnp.log(summed)
+
+
+def scaled_heads(queries):
+    return spread_heads(queries * jnp.bfloat16(HEAD_DIM ** (-0.5)))
+
+
+def self_forward_kernel(
+    latent_ref, gain_ref, q_ref, k_ref, v_ref, out_weight_ref, part_ref, triple_ref, output_ref, total_ref, low_ref
+):
+    heads = q_ref.shape[2] // HEAD_DIM
+    normed, _ = norm_rows(latent_ref[...])
+    low = (normed * gain_ref[...]).astype(jnp.bfloat16)
+    low_ref[...] = low
+    queries, keys, values = (dot(low, ref[0]).astype(jnp.bfloat16) for ref in (q_ref, k_ref, v_ref))
+    for index, item in enumerate((queries, keys, values)):
+        triple_ref[0, index] = item
+    output, total_ref[0] = attend_few(keys, values, scaled_heads(queries))
+    output = join_heads(output, heads).astype(jnp.bfloat16)
+    output_ref[0] = output
+    part_ref[...] = dot(output, out_weight_ref[0])
+
+
+def self_forward(latent, gain, wide, wideout, images):
+    total, d_lat = latent.shape
+    count, local = total // images, wide.shape[2]
+    stacked = local // HEAD_DIM * count
+    return pl.pallas_call(
+        self_forward_kernel,
+        grid=(images,),
+        out_shape=[
+            jax.ShapeDtypeStruct((total, d_lat), jnp.float32),
+            jax.ShapeDtypeStruct((images, 3, count, local), jnp.bfloat16),
+            jax.ShapeDtypeStruct((images, count, local), jnp.bfloat16),
+            jax.ShapeDtypeStruct((images, 1, stacked), jnp.float32),
+            jax.ShapeDtypeStruct((total, d_lat), jnp.bfloat16),
+        ],
+        in_specs=[rows_of(count, d_lat), whole((1, d_lat))]
+        + [slot_of((1, d_lat, local), slot) for slot in (1, 2, 3)]
+        + [slot_of((1, local, d_lat), 1)],
+        out_specs=[
+            rows_of(count, d_lat),
+            each((3, count, local)),
+            each((count, local)),
+            each((1, stacked)),
+            rows_of(count, d_lat),
+        ],
+        compiler_params=pltpu.CompilerParams(vmem_limit_bytes=20 << 20),
+        cost_estimate=pl.CostEstimate(
+            flops=3 * 10**9, bytes_accessed=12 * 10**6, transcendentals=3 * 10**5
+        ),
+    )(latent, gain, wide, wide, wide, wideout)
+
+
+def self_backward_kernel(
+    grad_ref,
+    latent_ref,
+    gain_ref,
+    q_ref,
+    k_ref,
+    v_ref,
+    out_weight_ref,
+    triple_ref,
+    output_ref,
+    total_ref,
+    low_ref,
+    part_ref,
+    q_grad_ref,
+    k_grad_ref,
+    v_grad_ref,
+    out_grad_ref,
+    gain_grad_ref,
+    branches,
+    outputs,
+    grads,
+    lows,
+):
+    step, steps = pl.program_id(0), pl.num_programs(0)
+    heads = q_ref.shape[2] // HEAD_DIM
+    count = grad_ref.shape[0]
+    mine = pl.ds(pl.multiple_of(step * count, count), count)
+    normed, scale = norm_rows(latent_ref[...])
+    branch = grad_ref[...].astype(jnp.bfloat16)
+    branches[mine] = branch
+    outputs[mine] = output_ref[0]
+    lows[mine] = low_ref[...]
+    upstream = spread_heads(dot(branch, out_weight_ref[0], 1, 1).astype(jnp.bfloat16))
+    keys, values = triple_ref[0, 1], triple_ref[0, 2]
+    queries = scaled_heads(triple_ref[0, 0])
+    probs = jnp.exp(dot(keys, queries, 1, 1) - total_ref[0])
+    value_grad = dot(probs.astype(jnp.bfloat16), upstream).astype(jnp.bfloat16)
+    prob_grad = dot(values, upstream, 1, 1)
+    inner = jnp.sum(prob_grad * probs, 0, keepdims=True)
+    score_grad = (probs * (prob_grad - inner)).astype(jnp.bfloat16)
+    key_grad = dot(score_grad, queries).astype(jnp.bfloat16)
+    query_grad = join_heads(dot(score_grad, keys, 0, 0), heads) * HEAD_DIM ** (-0.5)
+    query_grad = query_grad.astype(jnp.bfloat16)
+    part = (
+        dot(query_grad, q_ref[0], 1, 1)
+        + dot(key_grad, k_ref[0], 1, 1)
+        + dot(value_grad, v_ref[0], 1, 1)
+    )
+    for index, item in enumerate((query_grad, key_grad, value_grad)):
+        grads[index, mine] = item
+    gain_part = jnp.sum(part * normed, 0, keepdims=True)
+    gain_grad_ref[...] = gain_part + jnp.where(step == 0, 0.0, gain_grad_ref[...])
+    part_ref[...] = norm_rows_back(part, gain_ref[...], normed, scale)
+
+    @pl.when(step == steps - 1)
+    def _():
+        turned = lows[...].T
+        for index, ref in enumerate((q_grad_ref, k_grad_ref, v_grad_ref)):
+            ref[...] = dot(turned, grads[index])
+        out_grad_ref[...] = dot(branches[...], outputs[...], 0, 0)
+
+
+def self_backward(grad, latent, gain, wide, wideout, triple, output, total, low):
+    rows, d_lat = latent.shape
+    images, _, count, local = triple.shape
+    stacked = local // HEAD_DIM * count
+    weight = jax.ShapeDtypeStruct((d_lat, local), jnp.float32)
+    return pl.pallas_call(
+        self_backward_kernel,
+        grid=(images,),
+        out_shape=[jax.ShapeDtypeStruct((rows, d_lat), jnp.float32)]
+        + [weight] * 4
+        + [jax.ShapeDtypeStruct((1, d_lat), jnp.float32)],
+        in_specs=[rows_of(count, d_lat), rows_of(count, d_lat), whole((1, d_lat))]
+        + [slot_of((1, d_lat, local), slot) for slot in (1, 2, 3)]
+        + [
+            slot_of((1, local, d_lat), 1),
+            each((3, count, local)),
+            each((count, local)),
+            each((1, stacked)),
+            rows_of(count, d_lat),
+        ],
+        out_specs=[rows_of(count, d_lat)] + [whole((d_lat, local))] * 4 + [whole((1, d_lat))],
+        scratch_shapes=[
+            pltpu.VMEM((rows, d_lat), jnp.bfloat16),
+            pltpu.VMEM((rows, local), jnp.bfloat16),
+            pltpu.VMEM((3, rows, local), jnp.bfloat16),
+            pltpu.VMEM((rows, d_lat), jnp.bfloat16),
+        ],
+        compiler_params=pltpu.CompilerParams(vmem_limit_bytes=28 << 20),
+        cost_estimate=pl.CostEstimate(
+            flops=6 * 10**9, bytes_accessed=16 * 10**6, transcendentals=3 * 10**5
+        ),
+    )(grad, latent, gain, wide, wide, wide, wideout, triple, output, total, low)
+
+
+def feed_forward_kernel(
+    latent_ref, gain_ref, up_ref, down_ref, part_ref, active_ref, slope_ref, low_ref
+):
+    @pl.when(pl.program_id(0) == 0)
+    def _():
+        normed, _ = norm_rows(latent_ref[...])
+        low_ref[...] = (normed * gain_ref[...]).astype(jnp.bfloat16)
+
+    hidden = dot(low_ref[...], up_ref[0])
+    share = 0.5 * (1.0 + lax.erf(hidden * math.sqrt(0.5)))
+    density = jnp.exp(-0.5 * hidden * hidden) * (1.0 / math.sqrt(2.0 * math.pi))
+    active = (hidden * share).astype(jnp.bfloat16)
+    active_ref[0] = active
+    slope_ref[0] = share + hidden * density
+    part = dot(active, down_ref[0])
+
+    @pl.when(pl.program_id(0) == 0)
+    def _():
+        part_ref[...] = part
+
+    @pl.when(pl.program_id(0) > 0)
+    def _():
+        part_ref[...] += part
+
+
+def feed_forward(latent, gain, wide, wideout):
+    rows, d_lat = latent.shape
+    local = wide.shape[2]
+    return pl.pallas_call(
+        feed_forward_kernel,
+        grid=(4,),
+        out_shape=[
+            jax.ShapeDtypeStruct((rows, d_lat), jnp.float32),
+            jax.ShapeDtypeStruct((4, rows, local), jnp.bfloat16),
+            jax.ShapeDtypeStruct((4, rows, local), jnp.float32),
+            jax.ShapeDtypeStruct((rows, d_lat), jnp.bfloat16),
+        ],
+        in_specs=[
+            whole((rows, d_lat)),
+            whole((1, d_lat)),
+            pl.BlockSpec((1, d_lat, local), lambda s: (4 + s, 0, 0)),
+            pl.BlockSpec((1, local, d_lat), lambda s: (2 + s, 0, 0)),
+        ],
+        out_specs=[
+            whole((rows, d_lat)),
+            each((rows, local)),
+            each((rows, local)),
+            whole((rows, d_lat)),
+        ],
+        compiler_params=pltpu.CompilerParams(vmem_limit_bytes=24 << 20),
+        cost_estimate=pl.CostEstimate(
+            flops=4 * 10**9, bytes_accessed=14 * 10**6, transcendentals=10**6
+        ),
+    )(latent, gain, wide, wideout)
+
+
+def feed_backward_kernel(
+    grad_ref,
+    latent_ref,
+    gain_ref,
+    up_ref,
+    down_ref,
+    active_ref,
+    slope_ref,
+    low_ref,
+    part_ref,
+    up_first_ref,
+    up_last_ref,
+    down_grad_ref,
+    gain_grad_ref,
+    branch,
+    branch_turned,
+    low_turned,
+    total,
+):
+    step, steps = pl.program_id(0), pl.num_programs(0)
+
+    @pl.when(step == 0)
+    def _():
+        low = grad_ref[...].astype(jnp.bfloat16)
+        branch[...] = low
+        branch_turned[...] = low.T
+        low_turned[...] = low_ref[...].T
+        total[...] = jnp.zeros_like(total)
+
+    active_grad = dot(branch[...], down_ref[0], 1, 1)
+    hidden_grad = (active_grad * slope_ref[0]).astype(jnp.bfloat16)
+    down_grad_ref[0] = dot(branch_turned[...], active_ref[0])
+    total[...] += dot(hidden_grad, up_ref[0], 1, 1)
+    up_grad = dot(low_turned[...], hidden_grad)
+
+    @pl.when(step < 2)
+    def _():
+        up_first_ref[0] = up_grad
+
+    @pl.when(step >= 2)
+    def _():
+        up_last_ref[0] = up_grad
+
+    @pl.when(step == steps - 1)
+    def _():
+        normed, scale = norm_rows(latent_ref[...])
+        part = total[...]
+        gain_grad_ref[...] = jnp.sum(part * normed, 0, keepdims=True)
+        part_ref[...] = norm_rows_back(part, gain_ref[...], normed, scale)
+
+
+def feed_backward(grad, latent, gain, wide, wideout, active, slope, low):
+    rows, d_lat = latent.shape
+    local = wide.shape[2]
+    return pl.pallas_call(
+        feed_backward_kernel,
+        grid=(4,),
+        out_shape=[
+            jax.ShapeDtypeStruct((rows, d_lat), jnp.float32),
+            jax.ShapeDtypeStruct((2, d_lat, local), jnp.float32),
+            jax.ShapeDtypeStruct((2, d_lat, local), jnp.float32),
+            jax.ShapeDtypeStruct((4, d_lat, local), jnp.float32),
+            jax.ShapeDtypeStruct((1, d_lat), jnp.float32),
+        ],
+        in_specs=[
+            whole((rows, d_lat)),
+            whole((rows, d_lat)),
+            whole((1, d_lat)),
+            pl.BlockSpec((1, d_lat, local), lambda s: (4 + s, 0, 0)),
+            pl.BlockSpec((1, local, d_lat), lambda s: (2 + s, 0, 0)),
+            each((rows, local)),
+            each((rows, local)),
+            whole((rows, d_lat)),
+        ],
+        out_specs=[
+            whole((rows, d_lat)),
+            pl.BlockSpec((1, d_lat, local), lambda s: (jnp.minimum(s, 1), 0, 0)),
+            pl.BlockSpec((1, d_lat, local), lambda s: (jnp.maximum(s - 2, 0), 0, 0)),
+            each((d_lat, local)),
+            whole((1, d_lat)),
+        ],
+        scratch_shapes=[
+            pltpu.VMEM((rows, d_lat), jnp.bfloat16),
+            pltpu.VMEM((d_lat, rows), jnp.bfloat16),
+            pltpu.VMEM((d_lat, rows), jnp.bfloat16),
+            pltpu.VMEM((rows, d_lat), jnp.float32),
+        ],
+        compiler_params=pltpu.CompilerParams(vmem_limit_bytes=36 << 20),
+        cost_estimate=pl.CostEstimate(
+            flops=9 * 10**9, bytes_accessed=26 * 10**6, transcendentals=0
+        ),
+    )(grad, latent, gain, wide, wideout, active, slope, low)
+
+
 def adam_update(master, first, second, gradient, scale):
     clipped = gradient * scale
     moment = adam_beta * first + (1.0 - adam_beta) * clipped
@@ -902,27 +1552,20 @@
         del refs[:number]
         return taken
 
-    number, finished, states = sizes
+    number, finished = sizes
     items, (columns, tile), done = pull(number), pull(2), pull(finished)
-    state_in, state_out, (stats,) = pull(states), pull(states), pull(1)
+    wide_out, narrow_out, turned_out, last_out, latents_out, rest_out, stats = pull(7)
     shares = pull(number)
     sums = PieceSums(count_dp, items, shares, pull(number * (count_dp.bit_length() + 1)))
     (write_share,) = pull(1)
     scatter = LineScatter(count, columns, write_share, pull(4), pull(4))
     small = [Spread("mp", count, *pull(3)) for _ in range(2)]
     over_dp, over_mp = Spread("dp", count_dp, *pull(3)), Spread("mp", count, *pull(3))
-    held, (turned, in_sems, out_sems) = pull(states), pull(3)
 
     barrier = pltpu.get_barrier_semaphore()
     others = [over_dp.peer(step) for step in range(1, count_dp)]
     others += [over_mp.peer(step) for step in range(1, count)]
     signal_all(barrier, others)
-    loads = [
-        pltpu.make_async_copy(source, target, in_sems.at[index])
-        for index, (source, target) in enumerate(zip(state_in, held))
-    ]
-    for load in loads:
-        load.start()
     pl.semaphore_wait(barrier, len(others))
 
     sums.begin()
@@ -942,13 +1585,27 @@
     write_query, write_out = (
         write_share.at[pl.ds(2 * lat_rows + i * if_rows, if_rows)] for i in range(2)
     )
-    for index, share in enumerate([read_out, self_out] + down):
-        turned[index] = share[...].T
-    split = [read_query, read_key, read_value, read_out, self_in_0, self_in_1, self_in_2, self_out]
-    square = sum(sum_rows(ref[...] * ref[...]) for ref in split + up + down + [write_share])
+    square = 0.0
+
+    def keep(out, gradient, turn=False):
+        nonlocal square
+        value = gradient[...]
+        square = square + sum_rows(value * value)
+        out[...] = value.T if turn else value
+
+    wide = [read_query, self_in_0, self_in_1, self_in_2] + up + [write_key, write_value]
+    for slot, gradient in enumerate(wide):
+        keep(wide_out.at[slot], gradient)
+    for slot, gradient in enumerate([read_key, read_value, write_query]):
+        keep(narrow_out.at[slot], gradient)
+    for slot, gradient in enumerate([read_out, self_out] + down):
+        keep(turned_out.at[slot], gradient, True)
+    keep(last_out, write_out)
     for spread in small:
         spread.take()
     latents, rest = (spread.total() for spread in small)
+    latents_out[...] = latents
+    rest_out[...] = rest
     lead = (over_mp.place == 0).astype(jnp.float32)
     local = jnp.sum(square) + lead * (
         jnp.sum(sum_rows(latents * latents)) + jnp.sum(sum_rows(rest * rest))
@@ -960,99 +1617,121 @@
         spread.start()
         spread.take()
         value = spread.total()
-    norm = jnp.sqrt(value)
-    stats[...] = jnp.where(lane == 0, norm, value)
-    first = jnp.logical_and(lane == 0, lax.broadcasted_iota(jnp.int32, (8, 128), 0) == 0)
-    scale = jnp.sum(jnp.where(first, clip_level / jnp.maximum(norm, clip_level), 0.0))
-
-    def update(kind, at, gradient):
-        refs = held[3 * kind : 3 * kind + 3]
-        results = adam_update(refs[0][at], refs[1][at], refs[2][at], gradient, scale)
-        for ref, result in zip(refs, results):
-            ref[at] = result
-
-    def update_rows(kind, slot, gradient):
-        rows, width = gradient.shape
-        step = math.gcd(rows, max(8, 8192 // width))
-
-        def one(index, carry):
-            where = pl.ds(pl.multiple_of(index * step, step), step)
-            at = (where,) if slot is None else (slot, where)
-            update(kind, at, gradient[where])
-            return carry
-
-        lax.fori_loop(0, rows // step, one, 0)
-
-    def store(kind):
-        for index in range(3 * kind, 3 * kind + 3):
-            pltpu.make_async_copy(held[index], state_out[index], out_sems.at[index]).start()
-
-    for load in loads:
-        load.wait()
-    wide = [read_query, self_in_0, self_in_1, self_in_2] + up + [write_key, write_value]
-    for slot, gradient in enumerate(wide):
-        update_rows(0, slot, gradient)
-    store(0)
-    for slot in range(turned.shape[0]):
-        update_rows(2, slot, turned.at[slot])
-    store(2)
-    for slot, gradient in enumerate([read_key, read_value, write_query]):
-        update_rows(1, slot, gradient)
-    store(1)
-    update_rows(3, None, write_out)
-    store(3)
-    update(4, (slice(None),), latents)
-    store(4)
-    gains, lanes = held[15].shape
-    update(5, (slice(None),), rest[:gains, :lanes])
-    store(5)
-    for slot in range(2):
-        low = 16 * (slot + 1)
-        update(6, (slot,), rest[low : low + PIX, :lanes])
-    store(6)
+    stats[...] = jnp.where(lane == 0, jnp.sqrt(value), value)
     sums.finish()
     scatter.finish()
     for spread in small + [over_dp, over_mp]:
         spread.finish()
-    for index in range(states):
-        pltpu.make_async_copy(held[index], state_out[index], out_sems.at[index]).wait()
-
-
-def closing(items, columns, tile, done, states, call_id):
+
+
+def closing(items, columns, tile, done, call_id):
     items, shapes, shares = piece_shapes(items)
     count, count_dp = lax.axis_size("mp"), lax.axis_size("dp")
+    lat_rows, local = done[0].shape
+    if_rows = shapes[3][0]
+    outs = [
+        (10, lat_rows, local),
+        (3, if_rows, local),
+        (6, local, lat_rows),
+        (if_rows, local),
+        shapes[-2],
+        shapes[-1],
+        (8, 128),
+    ]
+    outs = [jax.ShapeDtypeStruct(shape, jnp.float32) for shape in outs]
     shares = [pltpu.VMEM(item.shape, jnp.float32) for item in shares]
-    held = [pltpu.VMEM(item.shape, jnp.float32) for item in states]
-    turned = (6,) + done[0].shape[::-1]
-    state_sems = pltpu.SemaphoreType.DMA((len(states),))
     scratch = (
         shares
         + PieceSums.scratch(count_dp, shapes)
         + [pltpu.VMEM((columns.shape[0] // count, columns.shape[1]), jnp.float32)]
         + LineScatter.scratch(count, columns.shape, 4)
-        + Spread.scratch(count, tuple(shares[-2].shape))
-        + Spread.scratch(count, tuple(shares[-1].shape))
+        + Spread.scratch(count, tuple(shapes[-2]))
+        + Spread.scratch(count, tuple(shapes[-1]))
         + Spread.scratch(count_dp, tile.shape)
         + Spread.scratch(count, tile.shape)
-        + held
-        + [pltpu.VMEM(turned, jnp.float32), state_sems, state_sems]
     )
     here = [*items, columns, tile, *done]
-    any_spec = pl.BlockSpec(memory_space=pl.ANY)
-    results = pl.pallas_call(
-        partial(closing_kernel, count, count_dp, (len(items), len(done), len(states))),
-        out_shape=[jax.ShapeDtypeStruct(item.shape, jnp.float32) for item in states]
-        + [jax.ShapeDtypeStruct((8, 128), jnp.float32)],
-        in_specs=[VMEM_SPEC] * len(here) + [any_spec] * len(states),
-        out_specs=[any_spec] * len(states) + [VMEM_SPEC],
+    return pl.pallas_call(
+        partial(closing_kernel, count, count_dp, (len(items), len(done))),
+        out_shape=outs,
+        in_specs=[VMEM_SPEC] * len(here),
+        out_specs=[VMEM_SPEC] * len(outs),
         scratch_shapes=scratch,
         compiler_params=pltpu.CompilerParams(
             collective_id=call_id,
             has_side_effects=True,
-            vmem_limit_bytes=room(here, room_of(scratch)),
+            vmem_limit_bytes=room(here, outs, room_of(scratch)),
         ),
-    )(*here, *states)
-    return results[:-1], results[-1]
+        cost_estimate=pl.CostEstimate(
+            flops=10**7, bytes_accessed=150 * 10**6, transcendentals=0
+        ),
+    )(*here)
+
+
+def clip_scale(norm):
+    return clip_level / jnp.maximum(norm, clip_level)
+
+
+def update_kernel(kinds, stats, *refs):
+    gradients, refs = refs[:kinds], refs[kinds:]
+    states, outs, held = (refs[index * 3 * kinds : (index + 1) * 3 * kinds] for index in range(3))
+    sems = refs[9 * kinds]
+    lane = lax.broadcasted_iota(jnp.int32, (8, 128), 1)
+    first = jnp.logical_and(lane == 0, lax.broadcasted_iota(jnp.int32, (8, 128), 0) == 0)
+    scale = jnp.sum(jnp.where(first, clip_scale(stats[...]), 0.0))
+    copies = []
+
+    def update(kind, at, gradient):
+        refs = [3 * kind + index for index in range(3)]
+        results = adam_update(*(states[index][at] for index in refs), gradient, scale)
+        for index, result in zip(refs, results):
+            held[index][at] = result
+
+    def send(kind, slot):
+        for index in range(3 * kind, 3 * kind + 3):
+            source, target = held[index], outs[index]
+            if slot is not None:
+                source, target = source.at[slot], target.at[slot]
+            copies.append(pltpu.make_async_copy(source, target, sems.at[len(copies)]))
+            copies[-1].start()
+
+    for kind, gradient in enumerate(gradients):
+        slots = range(gradient.shape[0]) if len(gradient.shape) == 3 else [None]
+        for slot in slots:
+            rows, width = states[3 * kind].shape[-2:]
+            step = math.gcd(rows, max(8, 8192 // width)) if rows % 8 == 0 else rows
+            source = gradient if slot is None else gradient.at[slot]
+
+            def one(index, carry, kind=kind, slot=slot, source=source, step=step, width=width):
+                where = pl.ds(pl.multiple_of(index * step, step), step)
+                update(kind, (where,) if slot is None else (slot, where), source[where, :width])
+                return carry
+
+            lax.fori_loop(0, rows // step, one, 0)
+            send(kind, slot)
+    for copy in copies:
+        copy.wait()
+
+
+def update_states(stats, gradients, states):
+    kinds = len(gradients)
+    hbm = pl.BlockSpec(memory_space=pltpu.HBM)
+    outs = [jax.ShapeDtypeStruct(item.shape, jnp.float32) for item in states]
+    copies = sum(3 * (item.shape[0] if item.ndim == 3 else 1) for item in gradients)
+    return pl.pallas_call(
+        partial(update_kernel, kinds),
+        out_shape=outs,
+        in_specs=[VMEM_SPEC] * (1 + kinds + len(states)),
+        out_specs=[hbm] * len(states),
+        scratch_shapes=[pltpu.VMEM(item.shape, jnp.float32) for item in states]
+        + [pltpu.SemaphoreType.DMA((copies,))],
+        compiler_params=pltpu.CompilerParams(
+            vmem_limit_bytes=room(gradients, states, outs)
+        ),
+        cost_estimate=pl.CostEstimate(
+            flops=2 * 10**7, bytes_accessed=14 * 10**6, transcendentals=0
+        ),
+    )(stats, *gradients, *states)
 
 
 def body(
@@ -1128,71 +1807,42 @@
     def wide_gain(index):
         return gain_rows[2 * index : 2 * index + 2].reshape(-1)
 
-    pixel_rows = copy_pixels.astype(jnp.float32)
-    interface = jnp.einsum("bcp,cd->bpd", noisy, pixel_rows[0], precision=precise) + positions(
-        noisy.shape[2], pixel_rows.shape[2]
-    )
-    latent_zero = copy_latents.astype(jnp.float32)
-    read_norm, read_stats = layer_norm(latent_zero, wide_gain(0))
-    read_low = read_norm.astype(jnp.bfloat16)
-    side_norm, side_stats = layer_norm(interface, gain_rows[8])
-    side_low = side_norm.astype(jnp.bfloat16)
-    read_query = jnp.einsum(
-        "ld,dc->lc", read_low, copy_widein[:, 0], preferred_element_type=jnp.float32
-    ).astype(jnp.bfloat16)
-    read_query = jnp.broadcast_to(read_query[None], (images,) + read_query.shape)
-    read_key = jnp.einsum(
-        "bpd,dc->bpc", side_low, copy_narrowin[:, 0], preferred_element_type=jnp.float32
-    ).astype(jnp.bfloat16)
-    read_value = jnp.einsum(
-        "bpd,dc->bpc", side_low, copy_narrowin[:, 1], preferred_element_type=jnp.float32
-    ).astype(jnp.bfloat16)
-    read_out, read_total = attend_forward(read_query, read_key, read_value, present_mask)
-    read_part = jnp.einsum(
-        "blc,cd->bld", read_out, copy_wideout[0], preferred_element_type=jnp.float32
-    )
+    wide_in = jnp.swapaxes(copy_widein, 0, 1)
+    narrow_in = jnp.swapaxes(copy_narrowin, 0, 1)
+    place = position_table(patches, d_if)
+    read_args = (
+        jnp.pad(noisy, ((0, 0), (0, 16 - PIX), (0, 0))),
+        keep_float[:, :, None],
+        place,
+        jnp.pad(copy_pixels[0], ((0, 16 - PIX), (0, 0))),
+        copy_latents,
+        wide_gain(0)[None],
+        gain_rows[8:9],
+        wide_in,
+        narrow_in,
+        copy_wideout,
+    )
+    read_part, *read_kept = read_forward(*read_args)
     gathered, read_part = lax.optimization_barrier((gathered, read_part))
     gathered = lax.all_gather(gathered, "dp").reshape(count_dp * count_mp, -1, local)
+    latent_zero = copy_latents.astype(jnp.float32)
+    latent_base = jnp.broadcast_to(latent_zero[None], (images, latents, d_lat))
     latent_one, (weight_tile,) = line_sum(
-        read_part,
-        jnp.broadcast_to(latent_zero[None], (images, latents, d_lat)),
-        2,
-        tile=jnp.full((8, 128), weight_here),
+        read_part, latent_base.reshape(-1, d_lat), 2, tile=jnp.full((8, 128), weight_here)
     )
     weight_total = weight_tile[0, 0]
-    self_norm, self_stats = layer_norm(latent_one, wide_gain(1))
-    self_low = self_norm.astype(jnp.bfloat16)
-    self_triple = jnp.einsum(
-        "bld,dsc->blsc", self_low, copy_widein[:, 1:4], preferred_element_type=jnp.float32
-    ).astype(jnp.bfloat16)
-    self_out, self_total = attend_forward(
-        self_triple[:, :, 0], self_triple[:, :, 1], self_triple[:, :, 2], None
+    self_part, *self_kept = self_forward(
+        latent_one, wide_gain(1)[None], wide_in, copy_wideout, images
     )
     latent_two, write_weights = line_sum(
-        jnp.einsum("blc,cd->bld", self_out, copy_wideout[1], preferred_element_type=jnp.float32),
-        latent_one,
-        3,
-        blocks=(gathered, [d_lat, d_lat, d_if, d_if]),
+        self_part, latent_one, 3, blocks=(gathered, [d_lat, d_lat, d_if, d_if])
     )
     write_key_weight, write_value_weight, write_query_weight, write_out_weight = write_weights
-    feed_norm, feed_stats = layer_norm(latent_two, wide_gain(2))
-    feed_low = feed_norm.astype(jnp.bfloat16)
-    hidden = jnp.einsum(
-        "bld,dsc->blsc", feed_low, copy_widein[:, 4:8], preferred_element_type=jnp.float32
-    )
-    active, gelu_pull = jax.vjp(partial(jax.nn.gelu, approximate=False), hidden)
-    active_low = active.astype(jnp.bfloat16)
-    feed_partial = jnp.einsum(
-        "blsc,scd->bld", active_low, copy_wideout[2:6], preferred_element_type=jnp.float32
-    )
-
-    def own_rows(values):
-        values = values.reshape((images * sharers, own_latents) + values.shape[2:])
-        return lax.dynamic_slice_in_dim(values, mp_index * own_images, own_images, 0)
-
-    latent_three = own_rows(latent_two) + line_scatter(
-        feed_partial.reshape(-1, d_lat), 4
-    ).reshape(own_images, own_latents, d_lat)
+    feed_part, *feed_kept = feed_forward(latent_two, wide_gain(2)[None], wide_in, copy_wideout)
+    own_two = lax.dynamic_slice_in_dim(
+        latent_two, mp_index * (own_images * own_latents), own_images * own_latents, 0
+    )
+    latent_three = (own_two + line_scatter(feed_part, 4)).reshape(own_images, own_latents, d_lat)
     write_norm, write_stats = layer_norm(latent_three, wide_gain(3))
     write_low = write_norm.astype(jnp.bfloat16)
 
@@ -1200,8 +1850,10 @@
         values = lax.dynamic_slice_in_dim(values, first_image, own_images, 0)
         return lax.dynamic_slice_in_dim(values, share * own_patches, own_patches, axis)
 
-    own_interface = own_tokens(interface, 1)
     own_noisy, own_noise = own_tokens(noisy, 2), own_tokens(noise_patches, 2)
+    own_interface = jnp.einsum(
+        "bcp,cd->bpd", own_noisy, copy_pixels[0].astype(jnp.float32), precision=precise
+    ) + lax.dynamic_slice_in_dim(place, share * own_patches, own_patches, 0)
     own_keep = own_tokens(keep_float, 1)
     own_weight = lax.dynamic_slice_in_dim(loss_weight, first_image, own_images, 0)
 
@@ -1289,104 +1941,39 @@
     latent_grad, (key_share, query_share) = line_gather(
         own_grad.reshape(-1, d_lat), 5, [write_key_grad, write_query_grad]
     )
+    outer_back, gain_outer = norm_back(outer_part, gain_rows[9], outer_stats)
+
+    latent_grad, (key_share, query_share) = line_gather(
+        own_grad.reshape(-1, d_lat), 5, [write_key_grad, write_query_grad]
+    )
     latent_grad = latent_grad.reshape(latent_one.shape)
     outer_back, gain_outer = norm_back(outer_part, gain_rows[9], outer_stats)
 
-    branch_low = latent_grad.astype(jnp.bfloat16)
-    down_grad = [
-        jnp.einsum(
-            "bld,blc->dc", branch_low, active_low[:, :, slot], preferred_element_type=jnp.float32
-        )
-        for slot in range(4)
-    ]
-    active_grad = jnp.einsum(
-        "bld,scd->blsc", branch_low, copy_wideout[2:6], preferred_element_type=jnp.float32
-    )
-    hidden_grad = gelu_pull(active_grad)[0].astype(jnp.bfloat16)
-    up_grad = [
-        jnp.einsum(
-            "bld,blc->dc", feed_low, hidden_grad[:, :, slot], preferred_element_type=jnp.float32
-        )
-        for slot in range(4)
-    ]
-    feed_part = jnp.einsum(
-        "blsc,dsc->bld", hidden_grad, copy_widein[:, 4:8], preferred_element_type=jnp.float32
-    )
-    latent_part, gain_feed = norm_back(feed_part, wide_gain(2), feed_stats)
+    latent_part, up_first, up_last, down_grad, gain_feed = feed_backward(
+        latent_grad, latent_two, wide_gain(2)[None], wide_in, copy_wideout, *feed_kept
+    )
     latent_grad, five_shares = line_sum(
-        latent_part, latent_grad, 6, [write_value_grad, narrowout_grad] + up_grad[:2]
-    )
-    branch_low = latent_grad.astype(jnp.bfloat16)
-    self_out_grad = jnp.einsum(
-        "bld,blc->dc", branch_low, self_out, preferred_element_type=jnp.float32
-    )
-    self_upstream = jnp.einsum(
-        "bld,cd->blc", branch_low, copy_wideout[1], preferred_element_type=jnp.float32
-    ).astype(jnp.bfloat16)
-    triple_grad = [
-        item.astype(jnp.bfloat16)
-        for item in attend_back(
-            self_triple[:, :, 0],
-            self_triple[:, :, 1],
-            self_triple[:, :, 2],
-            None,
-            self_total,
-            self_upstream,
-        )
-    ]
-    self_in_grad = [
-        jnp.einsum("bld,blc->dc", self_low, item, preferred_element_type=jnp.float32)
-        for item in triple_grad
-    ]
-    self_part = jnp.einsum(
-        "blsc,dsc->bld",
-        jnp.stack(triple_grad, 2),
-        copy_widein[:, 1:4],
-        preferred_element_type=jnp.float32,
-    )
-    latent_part, gain_self = norm_back(self_part, wide_gain(1), self_stats)
+        latent_part, latent_grad, 6, [write_value_grad, narrowout_grad, up_first]
+    )
+    latent_part, self_query_grad, self_key_grad, self_value_grad, self_out_grad, gain_self = (
+        self_backward(latent_grad, latent_one, wide_gain(1)[None], wide_in, copy_wideout, *self_kept)
+    )
     latent_grad, six_shares = line_sum(
-        latent_part, latent_grad, 7, up_grad[2:] + down_grad + self_in_grad[:2]
+        latent_part, latent_grad, 7, [up_last, down_grad, self_query_grad, self_key_grad]
     )
     write_share = jnp.concatenate([key_share, five_shares[0], query_share, five_shares[1]], 0)
     write_columns = jnp.concatenate(jnp.split(write_share, count_mp, 1), 0)
-    branch_low = latent_grad.astype(jnp.bfloat16)
-    read_out_grad = jnp.einsum(
-        "bld,blc->dc", branch_low, read_out, preferred_element_type=jnp.float32
-    )
-    read_upstream = jnp.einsum(
-        "bld,cd->blc", branch_low, copy_wideout[0], preferred_element_type=jnp.float32
-    ).astype(jnp.bfloat16)
-    query_grad, key_grad, value_grad = (
-        item.astype(jnp.bfloat16)
-        for item in attend_back(
-            read_query, read_key, read_value, present_mask, read_total, read_upstream
-        )
-    )
-    read_query_grad = jnp.einsum(
-        "ld,blc->dc", read_low, query_grad, preferred_element_type=jnp.float32
-    )
-    read_part = jnp.einsum(
-        "blc,dc->bld", query_grad, copy_widein[:, 0], preferred_element_type=jnp.float32
-    )
-    normed, scale = read_stats
-    latent_part, gain_read = norm_back(
-        read_part, wide_gain(0), (normed[None], scale[None])
-    )
-    latent_total = jnp.sum(lead * latent_grad + latent_part, 0)
-    read_key_grad = jnp.einsum(
-        "bpd,bpc->dc", side_low, key_grad, preferred_element_type=jnp.float32
-    )
-    read_value_grad = jnp.einsum(
-        "bpd,bpc->dc", side_low, value_grad, preferred_element_type=jnp.float32
-    )
-    side_part = jnp.einsum(
-        "bpc,dc->bpd", key_grad, copy_narrowin[:, 0], preferred_element_type=jnp.float32
-    ) + jnp.einsum(
-        "bpc,dc->bpd", value_grad, copy_narrowin[:, 1], preferred_element_type=jnp.float32
-    )
-    side_back, gain_side = norm_back(side_part, gain_rows[8], side_stats)
-    embed_grad = jnp.einsum("bcp,bpd->cd", noisy, side_back, precision=precise) + jnp.einsum(
+    (
+        read_query_grad,
+        read_key_grad,
+        read_value_grad,
+        read_out_grad,
+        latent_total,
+        gain_read,
+        gain_side,
+        side_embed,
+    ) = read_backward(*read_args, *read_kept, latent_grad, lead.reshape(1, 1))
+    embed_grad = side_embed[:PIX] + jnp.einsum(
         "bcp,bpd->cd", own_noisy, outer_grad + outer_back, precision=precise
     )
     gains_grad = jnp.concatenate(
@@ -1395,7 +1982,7 @@
             gain_self.reshape(2, -1),
             gain_feed.reshape(2, -1),
             gain_write.reshape(2, -1),
-            gain_side[None],
+            gain_side,
             gain_outer[None],
             gain_final[None],
         ],
@@ -1412,6 +1999,22 @@
     rest = jnp.pad(rest, ((0, 0), (0, 0), (0, 128 - rest.shape[2])))
     latents_item = dp_pieces(latent_total)
 
+    *gradients, rest_grad, stats = closing(
+        [
+            self_value_grad,
+            self_out_grad,
+            read_query_grad,
+            read_key_grad,
+            read_value_grad,
+            read_out_grad,
+            latents_item.reshape(-1, latents_item.shape[2]),
+            rest.reshape(-1, rest.shape[2]),
+        ],
+        write_columns,
+        jnp.full((8, 128), loss_local),
+        [*six_shares[6:8], *five_shares[2:], *six_shares[:6]],
+        8,
+    )
     states = (
         *(jnp.swapaxes(item, 0, 1) for item in (master_widein, first_widein, second_widein)),
         *(jnp.swapaxes(item, 0, 1) for item in (master_narrowin, first_narrowin, second_narrowin)),
@@ -1425,31 +2028,17 @@
         master_gains,
         first_gains,
         second_gains,
-        master_pixels,
-        first_pixels,
-        second_pixels,
-    )
-    results, stats = closing(
-        [
-            self_in_grad[2],
-            self_out_grad,
-            read_query_grad,
-            read_key_grad,
-            read_value_grad,
-            read_out_grad,
-            latents_item.reshape(-1, latents_item.shape[2]),
-            rest.reshape(-1, rest.shape[2]),
-        ],
-        write_columns,
-        jnp.full((8, 128), loss_local),
-        [*six_shares[6:8], *five_shares[2:], *six_shares[:6]],
-        states,
-        8,
-    )
+    )
+    results = update_states(stats, [*gradients, rest_grad], states)
     results = [
         jnp.swapaxes(item, 0, 1) if index < 6 or 9 <= index < 12 else item
         for index, item in enumerate(results)
     ]
+    lanes = master_pixels.shape[2]
+    pixels_grad = jnp.stack([rest_grad[16 : 16 + PIX, :lanes], rest_grad[32 : 32 + PIX, :lanes]])
+    results += adam_update(
+        master_pixels, first_pixels, second_pixels, pixels_grad, clip_scale(stats[0, 0])
+    )
     return (stats[0, 1] / weight_total, stats[0, 0], *results)
 
 

time: 716 us -> 702 us (0.980)
  Pallas kernels: 366 us -> 474 us
  matrix products: 156 us -> 52.6 us
  other arithmetic: 52.5 us -> 17.6 us
  local copies, waits for them, and re-layouts: 107 us -> 118 us
    dot_general x34 -> x1, matrix products: 85 us -> 2.93 us  [body(): jnp.einsum('bcp,cd->bpd', own_noisy, copy_pixels[0].astype(jnp.float32),...]
    pallas_call x0 -> x7, Pallas kernels: none -> 73.1 us  [the longest x1 24.2 us: read_backward(): pl.pallas_call(read_backward_kernel, grid=(images,), out_shape=[jax.Shape...]
    pallas_call x1 -> x2, Pallas kernels: 40.5 us -> 80.9 us  [line_gather(): pl.pallas_call(partial(line_gather_kernel, count, count_dp, extra), out_s...]
    unnamed x536 -> x392, local copies, waits for them, and re-layouts: 68.6 us -> 99.4 us
    convert_element_type x8 -> x1, other arithmetic: 16.2 us -> 0.35 us  [body(): final_low = final_norm.astype(jnp.bfloat16)]
    convert_element_type x10 -> x0, local copies, waits for them, and re-layouts: 11.7 us -> none  [the longest x3 4.87 us: body(): branch_low = latent_grad.astype(jnp.bfloat16)]
    dot_general x3 -> x1, matrix products: 12 us -> 2.43 us  [attend_back(): jnp.einsum('bhqk,bqhe->bkhe', probs.astype(jnp.bfloat16), split_heads(ups...]
    pallas_call x1, Pallas kernels: 62.2 us -> 54.7 us  [closing(): pl.pallas_call(partial(closing_kernel, count, count_dp, (len(items), len(...]
  transfers between devices with their start and end apart: 2 -> 2, of which waited for: 1 -> 1; matrix products, arithmetic and copies ran while one was open for 9% -> 2% of each run, Pallas kernels for 8% -> 11%
where the time goes in v4:
time: 702 us; the launch traced here: 692 us
  Pallas kernels  474 us (68%)
  local copies, waits for them, and re-layouts  118 us (17%)
  matrix products  52.6 us (7%)
  between operations  19.6 us (3%)
  other arithmetic  17.6 us (3%)
  waiting for transfers between devices  10.9 us (2%)
    pallas_call x4, Pallas kernels, line_sum(): pl.pallas_call(partial(line_sum_kernel, count, count_dp, len(items), int(...  231 us
    unnamed x392, local copies, waits for them, and re-layouts  99.4 us
    pallas_call x2, Pallas kernels, line_gather(): pl.pallas_call(partial(line_gather_kernel, count, count_dp, extra), out_s...  80.9 us
    pallas_call x1, Pallas kernels, closing(): pl.pallas_call(partial(closing_kernel, count, count_dp, (len(items), len(...  54.7 us
    pallas_call x1, Pallas kernels, line_scatter(): pl.pallas_call(partial(line_scatter_kernel, count), out_shape=jax.ShapeDt...  33.8 us
    pallas_call x1, Pallas kernels, read_backward(): pl.pallas_call(read_backward_kernel, grid=(images,), out_shape=[jax.Shape...  24.2 us
    pallas_call x1, Pallas kernels, read_forward(): pl.pallas_call(read_forward_kernel, grid=(images,), out_shape=[jax.ShapeD...  14.6 us
  transfers between devices with their start and end apart: 2, of which 1 were waited for; matrix products, arithmetic and copies ran while one was open for 2% of the time, Pallas kernels for 11%

profile of v4, /device:TPU:0, one launch (start us, length us, event | category | flops | bytes accessed | tf_op | source)
XLA Modules:
  0.0 692.4 jit_solution(1392349994547531675)
XLA Ops:
  10.5 2.0 copy.132.keep_ref
  13.3 2.0 fusion.48
  15.9 1.6 copy-done.17
  21.2 14.6 %shard_map.488 = (f32[512,1024]{1,0:T(8,128)S(1)}, bf16[4,2,1024,256]{3,2,1,0:T(8,128)(2,1)}, bf16[4,128,256]{2,1,0:T(8,128)(2,1)S(1)}, f32[4,1,512]{2,1,0:T(1,128)S(1)}, bf16[512,256]{1,0:T(8,128)(2,1)S(1)}) custom-call(f32[4,16,1024]{2,1,0:T(8,128)S(1)} %pad.23.noisy_ref, f32[4,1024,1]{2,1,0:T(8,128)S(1)} %copy-done.17, f32[1024,512]{1,0:T(8,128)S(1)} %copy-done.18, ...), custom_call_target="tpu_custom_call" | custom-call | flops 10000000000 | bytes 30000000 | tf_op jit(solution)/shard_map/pallas_call | solution.py:1012
  39.2 10.8 %all-gather.5.cloned.1.call-done = f32[1536,256]{1,0:T(8,128)} async-done(((f32[384,256]{1,0:T(8,128)}), f32[1536,256]{1,0:T(8,128)}) %all-gather.5.cloned.1.call-update) | async-done | bytes 1572880 | tf_op jit(solution)/shard_map/all_gather | solution.py:1793
  51.4 2.9 fusion.53
  56.5 57.6 %shard_map.489 = (f32[512,1024]{1,0:T(8,128)S(1)}, f32[8,128]{1,0:T(8,128)S(1)}) custom-call(f32[512,1024]{1,0:T(8,128)S(1)} %copy-done.16, f32[512,1024]{1,0:T(8,128)S(1)} %bitcast.198, f32[8,128]{1,0:T(8,128)S(1)} %broadcast_in_dim.14.refs_2_), custom_call_target="tpu_custom_call" | custom-call | flops 2097152 | bytes 183500800 | tf_op jit(solution)/shard_map/pallas_call | solution.py:609
  114.7 5.0 shard_map.490
  123.0 4.6 copy-done.5
  127.6 1.6 copy-done.32
  129.2 57.0 %shard_map.491 = (f32[512,1024]{1,0:T(8,128)S(1)}, bf16[1024,1024]{1,0:T(8,128)(2,1)S(1)}, bf16[1024,1024]{1,0:T(8,128)(2,1)S(1)}, bf16[512,1024]{1,0:T(8,128)(2,1)S(1)}, bf16[512,1024]{1,0:T(8,128)(2,1)S(1)}) custom-call(f32[512,1024]{1,0:T(8,128)S(1)} %copy-done.32, f32[512,1024]{1,0:T(8,128)S(1)} %get-tuple-element.109.latent_ref.refs_1_, ...), custom_call_target="tpu_custom_call" | custom-call | flops 2097152 | bytes 183500800 | tf_op jit(solution)/shard_map/pallas_call | solution.py:609
  187.5 3.6 copy-done.2
  191.1 6.6 shard_map.492
  197.8 33.8 %shard_map.493 = f32[128,1024]{1,0:T(8,128)S(1)} custom-call(f32[512,1024]{1,0:T(8,128)S(1)} %get-tuple-element.113.part_ref), custom_call_target="tpu_custom_call" | custom-call | flops 1048576 | bytes 120586240 | tf_op jit(solution)/shard_map/pallas_call | solution.py:777
  235.2 3.0 convolution_convert_fusion.5
  238.2 1.8 copy.134
  240.0 3.2 convolution_convert_fusion.2
  246.1 1.8 convolution_convert_fusion.1
  250.5 1.8 fusion.25
  252.4 2.4 multiply_reduce_fusion.3
  254.8 2.1 convert_bitcast_fusion
  258.3 2.5 multiply_reduce_fusion
  260.8 2.5 multiply_convert_fusion
  265.0 2.3 fusion.8
  267.3 2.4 convolution_convert_fusion.3
  271.1 1.7 multiply_reduce_fusion.4
  275.5 2.6 fusion.55
  280.0 2.7 fusion.57.refs_1_
  282.7 2.7 fusion.56.refs_0_
  285.7 2.2 copy-done.3
  289.5 41.7 %shard_map.494 = (f32[512,1024]{1,0:T(8,128)}, f32[128,1024]{1,0:T(8,128)}, f32[64,1024]{1,0:T(8,128)}) custom-call(f32[128,1024]{1,0:T(8,128)S(1)} %subtract_multiply_fusion.4.own_ref, f32[8,128,1024]{2,1,0:T(8,128)S(1)} %copy-done.3, f32[8,64,1024]{2,1,0:T(8,128)S(1)} %copy-done.13), custom_call_target="tpu_custom_call" | custom-call | flops 131072 | bytes 131072000 | tf_op jit(solution)/shard_map/pallas_call | solution.py:882
  331.2 39.2 %shard_map.495 = (f32[512,1024]{1,0:T(8,128)S(1)}, f32[128,1024]{1,0:T(8,128)S(1)}, f32[64,1024]{1,0:T(8,128)S(1)}) custom-call(f32[128,1024]{1,0:T(8,128)S(1)} %subtract_multiply_fusion.4.own_ref, f32[8,128,1024]{2,1,0:T(8,128)S(1)} %copy-done.3, f32[8,64,1024]{2,1,0:T(8,128)S(1)} %copy-done.13), custom_call_target="tpu_custom_call" | custom-call | flops 131072 | bytes 131072000 | tf_op jit(solution)/shard_map/pallas_call | solution.py:882
  371.7 1.6 fusion.30
  373.3 2.3 copy.150
  375.7 2.8 fusion.58.refs_2_
  379.4 4.4 fusion.59.refs_3_
  383.8 9.7 %shard_map.496 = (f32[512,1024]{1,0:T(8,128)S(1)}, f32[2,1024,256]{2,1,0:T(8,128)S(1)}, f32[2,1024,256]{2,1,0:T(8,128)S(1)}, f32[4,1024,256]{2,1,0:T(8,128)}, f32[1,1024]{1,0:T(1,128)S(1)}) custom-call(f32[512,1024]{1,0:T(8,128)S(1)} %copy-done.22, f32[512,1024]{1,0:T(8,128)S(1)} %copy-done.92, f32[1,1024]{1,0:T(1,128)S(1)} %bitcast.227, ...), custom_call_target="tpu_custom_call" | custom-call | flops 8999999488 | bytes 26000000 | tf_op jit(solution)/shard_map/pallas_call | solution.py:1491
  398.2 2.3 copy-done.4
  400.6 1.8 copy-done.23
  405.5 1.6 copy-done.30
  407.1 57.6 %shard_map.497 = (f32[512,1024]{1,0:T(8,128)S(1)}, f32[128,1024]{1,0:T(8,128)S(1)}, f32[64,1024]{1,0:T(8,128)S(1)}, f32[128,256]{1,0:T(8,128)S(1)}, f32[128,256]{1,0:T(8,128)S(1)}) custom-call(f32[512,1024]{1,0:T(8,128)S(1)} %copy-done.28, f32[512,1024]{1,0:T(8,128)S(1)} %copy-done.23, f32[8,128,1024]{2,1,0:T(8,128)S(1)} %copy-done.4, ...), custom_call_target="tpu_custom_call" | custom-call | flops 2097152 | bytes 183500800 | tf_op jit(solution)/shard_map/pallas_call | solution.py:609
  466.9 8.7 %shard_map.498 = (f32[512,1024]{1,0:T(8,128)S(1)}, f32[1024,256]{1,0:T(8,128)S(1)}, f32[1024,256]{1,0:T(8,128)S(1)}, f32[1024,256]{1,0:T(8,128)S(1)}, f32[1024,256]{1,0:T(8,128)S(1)}, /*index=5*/f32[1,1024]{1,0:T(1,128)S(1)}) custom-call(f32[512,1024]{1,0:T(8,128)S(1)} %get-tuple-element.125.grad_ref.refs_1_, ...), custom_call_target="tpu_custom_call" | custom-call | flops 6000000000 | bytes 16000000 | tf_op jit(solution)/shard_map/pallas_call | solution.py:1352
  478.0 2.0 copy-done.20
  481.6 59.0 %shard_map.499 = (f32[512,1024]{1,0:T(8,128)S(1)}, f32[128,256]{1,0:T(8,128)S(1)}, f32[128,256]{1,0:T(8,128)S(1)}, f32[128,256]{1,0:T(8,128)S(1)}, f32[128,256]{...) custom-call(f32[512,1024]{1,0:T(8,128)S(1)} %copy-done.25, ...), custom_call_target="tpu_custom_call" | custom-call | flops 2097152 | bytes 183500800 | tf_op jit(solution)/shard_map/pallas_call | solution.py:609
  546.0 24.2 %shard_map.500 = (f32[1024,256]{1,0:T(8,128)S(1)}, f32[512,256]{1,0:T(8,128)S(1)}, f32[512,256]{1,0:T(8,128)S(1)}, f32[1024,256]{1,0:T(8,128)S(1)}, f32[128,1024...) custom-call(f32[4,16,1024]{2,1,0:T(8,128)S(1)} %copy-done.65, ...), custom_call_target="tpu_custom_call" | custom-call | flops 20000000000 | bytes 30000000 | tf_op jit(solution)/shard_map/pallas_call | solution.py:1170
  576.5 4.6 fusion.10
  595.3 54.7 %shard_map.501 = (f32[10,128,256]{2,1,0:T(8,128)S(1)}, f32[3,64,256]{2,1,0:T(8,128)S(1)}, f32[6,256,128]{2,1,0:T(8,128)S(1)}, f32[64,256]{1,0:T(8,128)S(1)}, f32...) custom-call(f32[8,128,256]{2,1,0:T(8,128)S(1)} %bitcast.208, f32[8,128,256]{2,1,0:T(8,128)S(1)} %bitcast.209, ...), custom_call_target="tpu_custom_call" | custom-call | flops 10000000 | bytes 150000000 | tf_op jit(solution)/shard_map/pallas_call | solution.py:1654
  679.5 4.4 shard_map.502
  (465 shorter events, 108.8 us)
Async XLA Ops:
  7.2 42.8 %all-gather.5.cloned.1.call-start = ((), (), s32[]{:S(2)}) async-start(), calls=%async_computation | async-start | bytes 1966080 | tf_op jit(solution)/shard_map/all_gather | solution.py:1793
  9.7 113.2 %all-gather.7.cloned.1.call-start = ((), (), s32[]{:S(2)}) async-start(), calls=%async_computation.1 | async-start | bytes 14155776 | tf_op jit(solution)/shard_map/all_gather | solution.py:1827
  15.2 20.6 %copy-start.64 = (f32[4,16,1024]{2,1,0:T(8,128)}, f32[4,16,1024]{2,1,0:T(8,128)S(1)}, u32[]{:S(2)}) copy-start(f32[4,16,1024]{2,1,0:T(8,128)S(1)} %pad.23.noisy_ref) | copy-start | bytes 786436
  15.3 20.5 %copy-start.118 = (f32[1,512]{1,0:T(1,128)}, f32[1,512]{1,0:T(1,128)S(1)}, u32[]{:S(2)}) copy-start(f32[1,512]{1,0:T(1,128)S(1)} %get-tuple-element.299.gain_ref) | copy-start | bytes 6148
  15.3 255.8 %copy-start.176 = (f32[1,512]{1,0:T(1,128)}, f32[1,512]{1,0:T(1,128)S(1)}, u32[]{:S(2)}) copy-start(f32[1,512]{1,0:T(1,128)S(1)} %get-tuple-element.298) | copy-start | bytes 6148
  50.0 64.6 %slice-start = ((s8[5242880]{0:T(1024)(128)(4,1)}), s8[1048576]{0:T(1024)(128)(4,1)S(1)}, s32[]{:S(2)}) async-start(s8[5242880]{0:T(1024)(128)(4,1)} %bitcast.187), calls=%async_computation.2 | async-start | bytes 2097152
  54.3 216.7 %copy-start.171 = (f32[1024]{0:T(1024)}, f32[1024]{0:T(1024)S(1)}, u32[]{:S(2)}) copy-start(f32[1024]{0:T(1024)S(1)} %broadcast_multiply_fusion.5) | copy-start | bytes 12292
  54.3 60.3 %slice-start.1 = ((s8[5242880]{0:T(1024)(128)(4,1)}), s8[4194304]{0:T(1024)(128)(4,1)S(1)}, s32[]{:S(2)}) async-start(s8[5242880]{0:T(1024)(128)(4,1)} %bitcast.187), calls=%async_computation.3 | async-start | bytes 8388608
  54.8 216.3 %copy-start.173 = (f32[1024]{0:T(1024)}, f32[1024]{0:T(1024)S(1)}, u32[]{:S(2)}) copy-start(f32[1024]{0:T(1024)S(1)} %add_rsqrt_fusion.1) | copy-start | bytes 12292
  56.4 58.2 %copy-start.7 = (bf16[6,256,1024]{2,1,0:T(8,128)(2,1)S(1)}, bf16[6,256,1024]{2,1,0:T(8,128)(2,1)}, u32[]{:S(2)}) copy-start(bf16[6,256,1024]{2,1,0:T(8,128)(2,1)} %out_weight_ref.7) | copy-start | bytes 9437188
  122.9 63.2 %copy-start.59 = (bf16[4,128,256]{2,1,0:T(8,128)(2,1)}, bf16[4,128,256]{2,1,0:T(8,128)(2,1)S(1)}, u32[]{:S(2)}) copy-start(bf16[4,128,256]{2,1,0:T(8,128)(2,1)S(1)} %get-tuple-element.127.output_ref) | copy-start | bytes 786436
  129.2 58.3 %copy-start.8 = (bf16[6,256,1024]{2,1,0:T(8,128)(2,1)S(1)}, bf16[6,256,1024]{2,1,0:T(8,128)(2,1)}, u32[]{:S(2)}) copy-start(bf16[6,256,1024]{2,1,0:T(8,128)(2,1)} %out_weight_ref.7) | copy-start | bytes 9437188
  186.2 11.6 %copy-start.121 = (bf16[512,1024]{1,0:T(8,128)(2,1)}, bf16[512,1024]{1,0:T(8,128)(2,1)S(1)}, u32[]{:S(2)}) copy-start(bf16[512,1024]{1,0:T(8,128)(2,1)S(1)} %get-tuple-element.117) | copy-start | bytes 3145732
  186.2 45.4 %copy-start.91 = (f32[512,1024]{1,0:T(8,128)}, f32[512,1024]{1,0:T(8,128)S(1)}, u32[]{:S(2)}) copy-start(f32[512,1024]{1,0:T(8,128)S(1)} %get-tuple-element.112.latent_ref) | copy-start | bytes 6291460
  186.2 46.7 %copy-start.10 = (bf16[1024,1024]{1,0:T(8,128)(2,1)}, bf16[1024,1024]{1,0:T(8,128)(2,1)S(1)}, u32[]{:S(2)}) copy-start(bf16[1024,1024]{1,0:T(8,128)(2,1)S(1)} %get-tuple-element.116) | copy-start | bytes 6291460
  197.7 34.0 %copy-start.123 = (f32[4,512,256]{2,1,0:T(8,128)}, f32[4,512,256]{2,1,0:T(8,128)S(1)}, u32[]{:S(2)}) copy-start(f32[4,512,256]{2,1,0:T(8,128)S(1)} %get-tuple-element.121.slope_ref) | copy-start | bytes 6291460
  197.7 34.0 %copy-start.125 = (bf16[4,512,256]{2,1,0:T(8,128)(2,1)}, bf16[4,512,256]{2,1,0:T(8,128)(2,1)S(1)}, u32[]{:S(2)}) copy-start(bf16[4,512,256]{2,1,0:T(8,128)(2,1)S(1)} %get-tuple-element.120.active_ref) | copy-start | bytes 3145732
  197.7 34.0 %copy-start.127 = (bf16[512,1024]{1,0:T(8,128)(2,1)}, bf16[512,1024]{1,0:T(8,128)(2,1)S(1)}, u32[]{:S(2)}) copy-start(bf16[512,1024]{1,0:T(8,128)(2,1)S(1)} %get-tuple-element.122.low_ref) | copy-start | bytes 3145732
  331.2 40.5 %copy-start.140 = (bf16[1024,512]{1,0:T(8,128)(2,1)S(1)}, bf16[1024,512]{1,0:T(8,128)(2,1)}, u32[]{:S(2)}) copy-start(bf16[1024,512]{1,0:T(8,128)(2,1)} %copy-done.139) | copy-start | bytes 3145732
  331.2 40.5 %copy-start.166 = (f32[1,12,1024]{2,1,0:T(8,128)S(1)}, f32[1,12,1024]{2,1,0:T(8,128)}, u32[]{:S(2)}) copy-start(f32[1,12,1024]{2,1,0:T(8,128)} %copy-done.165) | copy-start | bytes 147460
  398.2 67.9 %slice-start.2 = ((s8[5242880]{0:T(1024)(128)(4,1)}), s8[4194304]{0:T(1024)(128)(4,1)S(1)}, s32[]{:S(2)}) async-start(s8[5242880]{0:T(1024)(128)(4,1)} %bitcast.193), calls=%async_computation.4 | async-start | bytes 8388608
  407.1 57.6 %copy-start.147 = (f32[384,1024]{1,0:T(8,128)S(1)}, f32[384,1024]{1,0:T(8,128)}, u32[]{:S(2)}) copy-start(f32[384,1024]{1,0:T(8,128)} %constant_dynamic-update-slice_fusion.3) | copy-start | bytes 4718596
  407.1 57.7 %copy-start.67 = (f32[64,1024]{1,0:T(8,128)S(1)}, f32[64,1024]{1,0:T(8,128)}, u32[]{:S(2)}) copy-start(f32[64,1024]{1,0:T(8,128)} %copy-done.66) | copy-start | bytes 786436
  407.1 59.0 %slice-start.3 = ((s8[5242880]{0:T(1024)(128)(4,1)}), s8[1048576]{0:T(1024)(128)(4,1)S(1)}, s32[]{:S(2)}) async-start(s8[5242880]{0:T(1024)(128)(4,1)} %bitcast.193), calls=%async_computation.5 | async-start | bytes 2097152
  478.0 62.6 %copy-start.42 = (f32[1024,256]{1,0:T(8,128)}, f32[1024,256]{1,0:T(8,128)S(1)}, u32[]{:S(2)}) copy-start(f32[1024,256]{1,0:T(8,128)S(1)} %get-tuple-element.131) | copy-start | bytes 3145732
  478.0 62.7 %copy-start.116 = (f32[1,1024]{1,0:T(1,128)}, f32[1,1024]{1,0:T(1,128)S(1)}, u32[]{:S(2)}) copy-start(f32[1,1024]{1,0:T(1,128)S(1)} %get-tuple-element.148) | copy-start | bytes 12292
  481.5 64.3 %copy-start.63 = (bf16[128,1024]{1,0:T(8,128)(2,1)S(1)}, bf16[128,1024]{1,0:T(8,128)(2,1)}, u32[]{:S(2)}) copy-start(bf16[128,1024]{1,0:T(8,128)(2,1)} %latents_ref.3) | copy-start | bytes 786436
  481.5 64.3 %copy-start.65 = (f32[4,16,1024]{2,1,0:T(8,128)S(1)}, f32[4,16,1024]{2,1,0:T(8,128)}, u32[]{:S(2)}) copy-start(f32[4,16,1024]{2,1,0:T(8,128)} %copy-done.64) | copy-start | bytes 786436
  481.5 64.3 %copy-start.94 = (bf16[512,3,256]{2,0,1:T(8,128)(2,1)S(1)}, bf16[512,3,256]{2,0,1:T(8,128)(2,1)}, u32[]{:S(2)}) copy-start(bf16[512,3,256]{2,0,1:T(8,128)(2,1)} %param.38) | copy-start | bytes 2359300
  481.5 64.3 %copy-start.108 = (bf16[16,512]{1,0:T(8,128)(2,1)S(1)}, bf16[16,512]{1,0:T(8,128)(2,1)}, u32[]{:S(2)}) copy-start(bf16[16,512]{1,0:T(8,128)(2,1)} %copy-done.107) | copy-start | bytes 49156
  481.6 64.4 %copy-start.119 = (f32[1,512]{1,0:T(1,128)S(1)}, f32[1,512]{1,0:T(1,128)}, u32[]{:S(2)}) copy-start(f32[1,512]{1,0:T(1,128)} %copy-done.118) | copy-start | bytes 6148
  481.6 64.4 %copy-start.130 = (bf16[4,128,256]{2,1,0:T(8,128)(2,1)S(1)}, bf16[4,128,256]{2,1,0:T(8,128)(2,1)}, u32[]{:S(2)}) copy-start(bf16[4,128,256]{2,1,0:T(8,128)(2,1)} %copy-done.129) | copy-start | bytes 786436
  481.6 64.4 %copy-start.132 = (bf16[512,256]{1,0:T(8,128)(2,1)S(1)}, bf16[512,256]{1,0:T(8,128)(2,1)}, u32[]{:S(2)}) copy-start(bf16[512,256]{1,0:T(8,128)(2,1)} %copy-done.131) | copy-start | bytes 786436
  481.6 64.4 %copy-start.134 = (f32[4,1,512]{2,1,0:T(1,128)S(1)}, f32[4,1,512]{2,1,0:T(1,128)}, u32[]{:S(2)}) copy-start(f32[4,1,512]{2,1,0:T(1,128)} %copy-done.133) | copy-start | bytes 24580
  545.9 24.4 %copy-start.75 = (f32[128,256]{1,0:T(8,128)}, f32[128,256]{1,0:T(8,128)S(1)}, u32[]{:S(2)}) copy-start(f32[128,256]{1,0:T(8,128)S(1)} %get-tuple-element.160.refs_14_) | copy-start | bytes 393220
  545.9 24.4 %copy-start.77 = (f32[128,256]{1,0:T(8,128)}, f32[128,256]{1,0:T(8,128)S(1)}, u32[]{:S(2)}) copy-start(f32[128,256]{1,0:T(8,128)S(1)} %get-tuple-element.161.refs_15_) | copy-start | bytes 393220
  545.9 29.0 %copy-start.117 = (f32[1,1024]{1,0:T(1,128)S(1)}, f32[1,1024]{1,0:T(1,128)}, u32[]{:S(2)}) copy-start(f32[1,1024]{1,0:T(1,128)} %copy-done.116) | copy-start | bytes 12292
  546.0 29.7 %copy-start.115 = (f32[1,1024]{1,0:T(1,128)S(1)}, f32[1,1024]{1,0:T(1,128)}, u32[]{:S(2)}) copy-start(f32[1,1024]{1,0:T(1,128)} %copy-done.114) | copy-start | bytes 12292
  546.0 30.4 %copy-start.178 = (f32[1024]{0:T(1024)S(1)}, f32[1024]{0:T(1024)}, u32[]{:S(2)}) copy-start(f32[1024]{0:T(1024)} %get-tuple-element.266) | copy-start | bytes 12292
  546.0 30.4 %copy-start.180 = (f32[1024]{0:T(1024)S(1)}, f32[1024]{0:T(1024)}, u32[]{:S(2)}) copy-start(f32[1024]{0:T(1024)} %get-tuple-element.263) | copy-start | bytes 12292
  546.0 30.4 %copy-start.179 = (f32[1024]{0:T(1024)S(1)}, f32[1024]{0:T(1024)}, u32[]{:S(2)}) copy-start(f32[1024]{0:T(1024)} %get-tuple-element.264) | copy-start | bytes 12292
  546.0 30.4 %copy-start.172 = (f32[1024]{0:T(1024)S(1)}, f32[1024]{0:T(1024)}, u32[]{:S(2)}) copy-start(f32[1024]{0:T(1024)} %copy-done.171) | copy-start | bytes 12292
  546.0 30.4 %copy-start.174 = (f32[1024]{0:T(1024)S(1)}, f32[1024]{0:T(1024)}, u32[]{:S(2)}) copy-start(f32[1024]{0:T(1024)} %copy-done.173) | copy-start | bytes 12292
  546.0 30.4 %copy-start.177 = (f32[1,512]{1,0:T(1,128)S(1)}, f32[1,512]{1,0:T(1,128)}, u32[]{:S(2)}) copy-start(f32[1,512]{1,0:T(1,128)} %copy-done.176) | copy-start | bytes 6148
  595.3 64.5 %copy-start.33 = (f32[128,10,256]{2,0,1:T(8,128)S(1)}, f32[128,10,256]{2,0,1:T(8,128)}, u32[]{:S(2)}) copy-start(f32[128,10,256]{2,0,1:T(8,128)} %param.44) | copy-start | bytes 3932164
  595.3 64.5 %copy-start.34 = (f32[128,10,256]{2,0,1:T(8,128)S(1)}, f32[128,10,256]{2,0,1:T(8,128)}, u32[]{:S(2)}) copy-start(f32[128,10,256]{2,0,1:T(8,128)} %param.45) | copy-start | bytes 3932164
  595.3 64.5 %copy-start.109 = (f32[11,64]{1,0:T(8,128)S(1)}, f32[11,64]{1,0:T(8,128)}, u32[]{:S(2)}) copy-start(f32[11,64]{1,0:T(8,128)} %refs_21_.1) | copy-start | bytes 8452
  595.3 64.5 %copy-start.110 = (f32[11,64]{1,0:T(8,128)S(1)}, f32[11,64]{1,0:T(8,128)}, u32[]{:S(2)}) copy-start(f32[11,64]{1,0:T(8,128)} %refs_22_.1) | copy-start | bytes 8452
  (145 other events, 304.6 us)
Sparse Core Ops, SparseCore 0:
  10.2 39.7 all-gather.4
  51.9 70.9 all-gather.6

commit v5 on v4

--- a/solution.py
+++ b/solution.py
@@ -114,9 +114,14 @@
 
 
 MESH_ID = pl.DeviceIdType.MESH
+HBM_SPEC = pl.BlockSpec(memory_space=pltpu.HBM)
 VMEM_SPEC = pl.BlockSpec(memory_space=pltpu.VMEM)
 CHUNKS = 32
 VMEM_LIMIT = 56 << 20
+
+
+def in_hbm(values):
+    return pltpu.with_memory_space_constraint(values, pltpu.HBM)
 
 
 def remote(source, target, send_sem, recv_sem, device):
@@ -364,38 +369,38 @@
         pl.semaphore_signal(barrier, inc=1, device_id=other, device_id_type=MESH_ID)
 
 
-def greet(place, count, others=()):
-    barrier = pltpu.get_barrier_semaphore()
-    below, above = {"mp": place - 1}, {"mp": place + 1}
-
-    @pl.when(place > 0)
-    def _():
-        pl.semaphore_signal(barrier, inc=1, device_id=below, device_id_type=MESH_ID)
-
-    @pl.when(place < count - 1)
-    def _():
-        pl.semaphore_signal(barrier, inc=1, device_id=above, device_id_type=MESH_ID)
-
-    signal_all(barrier, others)
-    inside = jnp.logical_and(place > 0, place < count - 1)
-
-    @pl.when(inside)
-    def _():
-        pl.semaphore_wait(barrier, 2 + len(others))
-
-    @pl.when(jnp.logical_not(inside))
-    def _():
-        pl.semaphore_wait(barrier, 1 + len(others))
-
-
-def views(refs):
-    result = []
-    for ref in refs:
-        result += [ref] if len(ref.shape) == 3 else [ref.at[slot] for slot in range(ref.shape[0])]
-    return result
-
-
-def line_sum_kernel(count, count_dp, extra, tiled, converted, *refs):
+class Stage:
+    def __init__(self, sources, held, in_sems, results, targets, out_sems):
+        self.loads = [
+            pltpu.make_async_copy(source, target, in_sems.at[index])
+            for index, (source, target) in enumerate(zip(sources, held))
+        ]
+        self.stores = [
+            pltpu.make_async_copy(source, target, out_sems.at[index])
+            for index, (source, target) in enumerate(zip(results, targets))
+        ]
+        self.stored = []
+
+    def start(self):
+        for load in self.loads:
+            load.start()
+
+    def wait(self, *indices):
+        for index in indices or range(len(self.loads)):
+            self.loads[index].wait()
+
+    def store(self, *indices):
+        for index in indices:
+            self.stores[index].start()
+            self.stored.append(index)
+
+    def finish(self):
+        self.store(*(index for index in range(len(self.stores)) if index not in self.stored))
+        for store in self.stores:
+            store.wait()
+
+
+def staged_kernel(body, counts, *refs):
     refs = list(refs)
 
     def pull(number):
@@ -403,10 +408,85 @@
         del refs[:number]
         return taken
 
-    part_ref, base_ref = pull(2)
-    items, tile, blocks = views(pull(extra)), pull(tiled), pull(min(1, converted))
-    (out_ref,) = pull(1)
-    outs, tile_out, wide = pull(len(items)), pull(tiled), pull(converted)
+    number, raw, results = counts
+    sources, raws, targets = pull(number), pull(raw), pull(results)
+    held, outs, (in_sems, out_sems) = pull(number), pull(results), pull(2)
+    stage = Stage(sources, held, in_sems, outs, targets, out_sems)
+    stage.start()
+    body(stage, held, raws, outs, refs)
+    stage.finish()
+
+
+def staged(body, inputs, outs, scratch, flops, raw=(), call_id=None, length=0):
+    copies = [pltpu.VMEM(item.shape, item.dtype) for item in (*inputs, *outs)]
+    sems = [pltpu.SemaphoreType.DMA((max(1, len(group)),)) for group in (inputs, outs)]
+    needed = sum(
+        math.prod(item.shape) * jnp.dtype(item.dtype).itemsize
+        for item in copies + list(scratch)
+        if getattr(item, "dtype", None) in (jnp.float32, jnp.bfloat16)
+    )
+    params = {} if call_id is None else {"collective_id": call_id, "has_side_effects": True}
+    results = pl.pallas_call(
+        partial(staged_kernel, body, (len(inputs), len(raw), len(outs))),
+        out_shape=[pltpu.HBM(item.shape, item.dtype) for item in outs],
+        in_specs=[HBM_SPEC] * (len(inputs) + len(raw)),
+        out_specs=[HBM_SPEC] * len(outs),
+        scratch_shapes=copies + sems + list(scratch),
+        compiler_params=pltpu.CompilerParams(vmem_limit_bytes=needed + (6 << 20), **params),
+        cost_estimate=pl.CostEstimate(
+            flops=flops, bytes_accessed=length * 3_500_000, transcendentals=0
+        ),
+    )(*(in_hbm(item) for item in (*inputs, *raw)))
+    return list(results)
+
+
+def greet(place, count, others=()):
+    barrier = pltpu.get_barrier_semaphore()
+    below, above = {"mp": place - 1}, {"mp": place + 1}
+
+    @pl.when(place > 0)
+    def _():
+        pl.semaphore_signal(barrier, inc=1, device_id=below, device_id_type=MESH_ID)
+
+    @pl.when(place < count - 1)
+    def _():
+        pl.semaphore_signal(barrier, inc=1, device_id=above, device_id_type=MESH_ID)
+
+    signal_all(barrier, others)
+    inside = jnp.logical_and(place > 0, place < count - 1)
+
+    @pl.when(inside)
+    def _():
+        pl.semaphore_wait(barrier, 2 + len(others))
+
+    @pl.when(jnp.logical_not(inside))
+    def _():
+        pl.semaphore_wait(barrier, 1 + len(others))
+
+
+def views(refs, base=3):
+    result = []
+    for ref in refs:
+        if len(ref.shape) == base:
+            result.append(ref)
+        else:
+            result += [ref.at[slot] for slot in range(ref.shape[0])]
+    return result
+
+
+def line_sum_kernel(count, count_dp, extra, tiled, stage, held, blocks, results, scratch):
+    refs = list(scratch)
+
+    def pull(number):
+        taken = refs[:number]
+        del refs[:number]
+        return taken
+
+    part_ref, base_ref, tile = held[0], held[1], held[2 + extra :]
+    items, outs = views(held[2 : 2 + extra]), views(results[1 : 1 + extra], 2)
+    out_ref, tile_out = results[0], results[1 + extra : 1 + extra + tiled]
+    wide = results[1 + extra + tiled :]
+    converted = len(wide)
     inner, from_away, from_toward, toward_send, away_send, away_recv, toward_recv = pull(7)
     chunks = toward_send.shape[0]
     spread = Spread("dp", count_dp, *pull(3)) if tiled else None
@@ -421,10 +501,10 @@
     outermost = jnp.logical_or(place == 0, place == count - 1)
     rows = part_ref.shape[0] // chunks
     others = [spread.peer(step) for step in range(1, count_dp)] if tiled else sums.peers()
+    greet(place, count, others)
+    stage.wait()
     if tiled:
         spread.held[spread.place] = tile[0][...]
-    greet(place, count, others)
-    if tiled:
         spread.start()
     if converted:
         convert.begin()
@@ -552,74 +632,49 @@
         spread.finish()
 
 
-def room(*groups):
-    total = 8 << 20
-    for group in groups:
-        for item in group:
-            if hasattr(item, "shape") and hasattr(item, "dtype"):
-                total += math.prod(item.shape) * jnp.dtype(item.dtype).itemsize
-    return min(total, VMEM_LIMIT)
-
-
-def room_of(scratch):
-    return [
-        jax.ShapeDtypeStruct(item.shape, item.dtype)
-        for item in scratch
-        if getattr(item, "dtype", None) in (jnp.float32, jnp.bfloat16)
-    ]
-
-
 def piece_shapes(items):
     count = lax.axis_size("dp")
     items = [item.reshape(item.shape[:-2] + (count, -1, item.shape[-1])) for item in items]
-    shapes = []
+    shapes, shares = [], []
     for item in items:
         shapes += [item.shape[-2:]] * (item.shape[0] if item.ndim == 4 else 1)
-    return items, shapes, [jax.ShapeDtypeStruct(shape, jnp.float32) for shape in shapes]
+        shares.append(jax.ShapeDtypeStruct(item.shape[:-3] + item.shape[-2:], jnp.float32))
+    return items, shapes, shares
 
 
 def line_sum(part, base, call_id, items=(), tile=None, blocks=None):
     shape = part.shape
     items, shapes, shares = piece_shapes(items)
     count, count_dp = lax.axis_size("mp"), lax.axis_size("dp")
-    part = part.reshape(-1, shape[-1])
     rows, width = part.shape
     buffer = pltpu.VMEM((rows, width), jnp.float32)
     sems = pltpu.SemaphoreType.DMA((CHUNKS,))
-    inputs, specs = [part, base.reshape(part.shape), *items], [VMEM_SPEC] * (2 + len(items))
+    inputs, raw = [part, base, *items], []
     outs = [jax.ShapeDtypeStruct((rows, width), jnp.float32)] + shares
     scratch = [buffer] * 3 + [sems] * 4
     if tile is not None:
         inputs.append(tile)
-        specs.append(VMEM_SPEC)
         outs.append(jax.ShapeDtypeStruct(tile.shape, jnp.float32))
         scratch += Spread.scratch(count_dp, tile.shape)
-    sizes = []
     if blocks is not None:
         blocks, sizes = blocks
+        raw.append(blocks)
         outs += [
             jax.ShapeDtypeStruct((size, count * blocks.shape[2]), jnp.bfloat16) for size in sizes
         ]
         scratch += Convert.scratch(blocks.shape[1:])
     scratch += PieceSums.scratch(count_dp, shapes)
-    limit = room(inputs, outs, room_of(scratch))
-    if blocks is not None:
-        inputs.append(blocks)
-        specs.append(pl.BlockSpec(memory_space=pl.ANY))
-    results = pl.pallas_call(
-        partial(line_sum_kernel, count, count_dp, len(items), int(tile is not None), len(sizes)),
-        out_shape=outs,
-        in_specs=specs,
-        out_specs=[VMEM_SPEC] * len(outs),
-        scratch_shapes=scratch,
-        compiler_params=pltpu.CompilerParams(
-            collective_id=call_id, has_side_effects=True, vmem_limit_bytes=limit
-        ),
-        cost_estimate=pl.CostEstimate(
-            flops=4 * rows * width, bytes_accessed=350 * rows * width, transcendentals=0
-        ),
-    )(*inputs)
-    return results[0].reshape(shape), results[1:]
+    results = staged(
+        partial(line_sum_kernel, count, count_dp, len(items), int(tile is not None)),
+        inputs,
+        outs,
+        scratch,
+        4 * rows * width,
+        raw,
+        call_id,
+        55,
+    )
+    return results[0], results[1:]
 
 
 class LineScatter:
@@ -762,9 +817,10 @@
         lax.fori_loop(0, self.count * self.steps, one, 0)
 
 
-def line_scatter_kernel(count, part_ref, out_ref, *scratch):
-    scatter = LineScatter(count, part_ref, out_ref, scratch[:4], scratch[4:])
+def line_scatter_kernel(count, stage, held, raws, results, scratch):
+    scatter = LineScatter(count, held[0], results[0], scratch[:4], scratch[4:])
     greet(scatter.place, count)
+    stage.wait()
     scatter.run()
     scatter.settle()
     scatter.finish()
@@ -773,33 +829,30 @@
 def line_scatter(part, call_id):
     rows, width = part.shape
     count = lax.axis_size("mp")
-    steps = 8
-    return pl.pallas_call(
+    (result,) = staged(
         partial(line_scatter_kernel, count),
-        out_shape=jax.ShapeDtypeStruct((rows // count, width), jnp.float32),
-        in_specs=[VMEM_SPEC],
-        out_specs=VMEM_SPEC,
-        scratch_shapes=LineScatter.scratch(count, (rows, width), steps),
-        compiler_params=pltpu.CompilerParams(
-            collective_id=call_id, has_side_effects=True, vmem_limit_bytes=24 << 20
-        ),
-        cost_estimate=pl.CostEstimate(
-            flops=2 * rows * width, bytes_accessed=230 * rows * width, transcendentals=0
-        ),
-    )(part)
-
-
-def line_gather_kernel(count, count_dp, extra, own_ref, *refs):
-    items, out_ref, refs = views(refs[:extra]), refs[extra], refs[extra + 1 :]
-    outs, refs = refs[: len(items)], refs[len(items) :]
-    up_send, down_send, up_recv, down_recv = refs[:4]
-    sums = PieceSums(count_dp, items, outs, refs[4:])
+        [part],
+        [jax.ShapeDtypeStruct((rows // count, width), jnp.float32)],
+        LineScatter.scratch(count, (rows, width), 8),
+        2 * rows * width,
+        call_id=call_id,
+        length=33,
+    )
+    return result
+
+
+def line_gather_kernel(count, count_dp, extra, stage, held, raws, results, scratch):
+    own_ref, out_ref = held[0], results[0]
+    items, outs = views(held[1:]), views(results[1:], 2)
+    up_send, down_send, up_recv, down_recv = scratch[:4]
+    sums = PieceSums(count_dp, items, outs, scratch[4:])
     place = lax.axis_index("mp")
     steps = up_send.shape[1]
     block = own_ref.shape[0]
     rows = block // steps
     below, above = {"mp": place - 1}, {"mp": place + 1}
     greet(place, count, sums.peers())
+    stage.wait()
     sums.begin()
 
     def window(owner, step):
@@ -873,25 +926,17 @@
 def line_gather(own, call_id, items=()):
     rows, width = own.shape
     count, count_dp = lax.axis_size("mp"), lax.axis_size("dp")
-    steps = 8
-    sems = pltpu.SemaphoreType.DMA((count, steps))
+    sems = pltpu.SemaphoreType.DMA((count, 8))
     items, shapes, shares = piece_shapes(items)
-    extra = len(items)
-    scratch = PieceSums.scratch(count_dp, shapes)
-    limit = room(items, shares, room_of(scratch)) + 2 * rows * count * width * 4
-    results = pl.pallas_call(
-        partial(line_gather_kernel, count, count_dp, extra),
-        out_shape=[jax.ShapeDtypeStruct((rows * count, width), jnp.float32)] + shares,
-        in_specs=[VMEM_SPEC] * (1 + extra),
-        out_specs=[VMEM_SPEC] * (1 + len(shares)),
-        scratch_shapes=[sems] * 4 + scratch,
-        compiler_params=pltpu.CompilerParams(
-            collective_id=call_id, has_side_effects=True, vmem_limit_bytes=limit
-        ),
-        cost_estimate=pl.CostEstimate(
-            flops=rows * width, bytes_accessed=250 * rows * width * count, transcendentals=0
-        ),
-    )(own, *items)
+    results = staged(
+        partial(line_gather_kernel, count, count_dp, len(items)),
+        [own, *items],
+        [jax.ShapeDtypeStruct((rows * count, width), jnp.float32)] + shares,
+        [sems] * 4 + PieceSums.scratch(count_dp, shapes),
+        rows * width,
+        call_id=call_id,
+        length=38,
+    )
     return results[0], results[1:]
 
 
@@ -1013,11 +1058,11 @@
         read_forward_kernel,
         grid=(images,),
         out_shape=[
-            jax.ShapeDtypeStruct((images * count, d_lat), jnp.float32),
-            jax.ShapeDtypeStruct((images, 2, patches, local), jnp.bfloat16),
-            jax.ShapeDtypeStruct((images, count, local), jnp.bfloat16),
-            jax.ShapeDtypeStruct((images, 1, stacked), jnp.float32),
-            jax.ShapeDtypeStruct((stacked, local), jnp.bfloat16),
+            pltpu.HBM((images * count, d_lat), jnp.float32),
+            pltpu.HBM((images, 2, patches, local), jnp.bfloat16),
+            pltpu.HBM((images, count, local), jnp.bfloat16),
+            pltpu.HBM((images, 1, stacked), jnp.float32),
+            pltpu.HBM((stacked, local), jnp.bfloat16),
         ],
         in_specs=[
             each(noisy.shape[1:]),
@@ -1042,7 +1087,7 @@
         cost_estimate=pl.CostEstimate(
             flops=10**10, bytes_accessed=30 * 10**6, transcendentals=2 * 10**6
         ),
-    )(noisy, keep, place, pixels, latents, wide_gain, gain, wide, narrow, wideout)
+    )(*map(in_hbm, (noisy, keep, place, pixels, latents, wide_gain, gain, wide, narrow, wideout)))
 
 
 def read_backward_kernel(
@@ -1062,10 +1107,8 @@
     queries_ref,
     grad_ref,
     lead_ref,
-    query_grad_ref,
-    key_grad_ref,
-    value_grad_ref,
-    out_grad_ref,
+    wide_grad_ref,
+    narrow_grad_ref,
     latents_grad_ref,
     wide_gain_grad_ref,
     gain_grad_ref,
@@ -1081,10 +1124,8 @@
         normed, _ = norm_rows(latents_ref[...].astype(jnp.float32))
         low_ref[...] = (normed * wide_gain_ref[...]).astype(jnp.bfloat16)
         for ref in (
-            query_grad_ref,
-            key_grad_ref,
-            value_grad_ref,
-            out_grad_ref,
+            wide_grad_ref,
+            narrow_grad_ref,
             latents_grad_ref,
             gain_grad_ref,
             embed_grad_ref,
@@ -1097,7 +1138,7 @@
     keys, values, queries = pairs_ref[0, 0], pairs_ref[0, 1], queries_ref[...]
     branch = grad_ref[...].astype(jnp.bfloat16)
     latents_grad_ref[...] += lead_ref[...] * grad_ref[...]
-    out_grad_ref[...] += dot(branch, output_ref[0], 0, 0)
+    wide_grad_ref[1] += dot(branch, output_ref[0], 0, 0)
     upstream = spread_heads(dot(branch, out_weight_ref[0], 1, 1).astype(jnp.bfloat16))
     scores = dot(keys, queries, 1, 1)
     scores = jnp.where(keep_ref[0] > 0, scores, -1e30)
@@ -1109,10 +1150,10 @@
     key_grad = dot(score_grad, queries).astype(jnp.bfloat16)
     query_grad = join_heads(dot(score_grad, keys, 0, 0), heads) * HEAD_DIM ** (-0.5)
     query_grad = query_grad.astype(jnp.bfloat16)
-    query_grad_ref[...] += dot(low_ref[...], query_grad, 0, 0)
+    wide_grad_ref[0] += dot(low_ref[...], query_grad, 0, 0)
     returned_ref[...] += dot(query_grad, query_weight_ref[0], 1, 1)
-    key_grad_ref[...] += dot(side, key_grad, 0, 0)
-    value_grad_ref[...] += dot(side, value_grad, 0, 0)
+    narrow_grad_ref[0] += dot(side, key_grad, 0, 0)
+    narrow_grad_ref[1] += dot(side, value_grad, 0, 0)
     side_grad = dot(key_grad, pair_weight_ref[0], 1, 1) + dot(value_grad, pair_weight_ref[1], 1, 1)
     gain_grad_ref[...] += jnp.sum(side_grad * normed, 0, keepdims=True)
     back = norm_rows_back(side_grad, gain_ref[...], normed, scale)
@@ -1158,10 +1199,8 @@
     d_if, local = narrow.shape[1:]
     stacked = local // HEAD_DIM * count
     results = [
-        (d_lat, local),
-        (d_if, local),
-        (d_if, local),
-        (d_lat, local),
+        (2, d_lat, local),
+        (2, d_if, local),
         (count, d_lat),
         (1, d_lat),
         (1, d_if),
@@ -1170,7 +1209,7 @@
     return pl.pallas_call(
         read_backward_kernel,
         grid=(images,),
-        out_shape=[jax.ShapeDtypeStruct(shape, jnp.float32) for shape in results],
+        out_shape=[pltpu.HBM(shape, jnp.float32) for shape in results],
         in_specs=[
             each(noisy.shape[1:]),
             each((patches, 1)),
@@ -1198,8 +1237,7 @@
         cost_estimate=pl.CostEstimate(
             flops=2 * 10**10, bytes_accessed=30 * 10**6, transcendentals=2 * 10**6
         ),
-    )(
-        noisy,
+    )(*map(in_hbm, (noisy,
         keep,
         place,
         pixels,
@@ -1214,8 +1252,7 @@
         total,
         queries,
         grad,
-        lead,
-    )
+        lead)))
 
 
 def rows_of(rows, width):
@@ -1259,11 +1296,11 @@
         self_forward_kernel,
         grid=(images,),
         out_shape=[
-            jax.ShapeDtypeStruct((total, d_lat), jnp.float32),
-            jax.ShapeDtypeStruct((images, 3, count, local), jnp.bfloat16),
-            jax.ShapeDtypeStruct((images, count, local), jnp.bfloat16),
-            jax.ShapeDtypeStruct((images, 1, stacked), jnp.float32),
-            jax.ShapeDtypeStruct((total, d_lat), jnp.bfloat16),
+            pltpu.HBM((total, d_lat), jnp.float32),
+            pltpu.HBM((images, 3, count, local), jnp.bfloat16),
+            pltpu.HBM((images, count, local), jnp.bfloat16),
+            pltpu.HBM((images, 1, stacked), jnp.float32),
+            pltpu.HBM((total, d_lat), jnp.bfloat16),
         ],
         in_specs=[rows_of(count, d_lat), whole((1, d_lat))]
         + [slot_of((1, d_lat, local), slot) for slot in (1, 2, 3)]
@@ -1279,7 +1316,7 @@
         cost_estimate=pl.CostEstimate(
             flops=3 * 10**9, bytes_accessed=12 * 10**6, transcendentals=3 * 10**5
         ),
-    )(latent, gain, wide, wide, wide, wideout)
+    )(*map(in_hbm, (latent, gain, wide, wide, wide, wideout)))
 
 
 def self_backward_kernel(
@@ -1295,10 +1332,8 @@
     total_ref,
     low_ref,
     part_ref,
-    q_grad_ref,
-    k_grad_ref,
-    v_grad_ref,
-    out_grad_ref,
+    first_ref,
+    last_ref,
     gain_grad_ref,
     branches,
     outputs,
@@ -1339,22 +1374,23 @@
     @pl.when(step == steps - 1)
     def _():
         turned = lows[...].T
-        for index, ref in enumerate((q_grad_ref, k_grad_ref, v_grad_ref)):
-            ref[...] = dot(turned, grads[index])
-        out_grad_ref[...] = dot(branches[...], outputs[...], 0, 0)
+        first_ref[0] = dot(turned, grads[0])
+        first_ref[1] = dot(turned, grads[1])
+        last_ref[0] = dot(turned, grads[2])
+        last_ref[1] = dot(branches[...], outputs[...], 0, 0)
 
 
 def self_backward(grad, latent, gain, wide, wideout, triple, output, total, low):
     rows, d_lat = latent.shape
     images, _, count, local = triple.shape
     stacked = local // HEAD_DIM * count
-    weight = jax.ShapeDtypeStruct((d_lat, local), jnp.float32)
+    weight = pltpu.HBM((2, d_lat, local), jnp.float32)
     return pl.pallas_call(
         self_backward_kernel,
         grid=(images,),
-        out_shape=[jax.ShapeDtypeStruct((rows, d_lat), jnp.float32)]
-        + [weight] * 4
-        + [jax.ShapeDtypeStruct((1, d_lat), jnp.float32)],
+        out_shape=[pltpu.HBM((rows, d_lat), jnp.float32)]
+        + [weight] * 2
+        + [pltpu.HBM((1, d_lat), jnp.float32)],
         in_specs=[rows_of(count, d_lat), rows_of(count, d_lat), whole((1, d_lat))]
         + [slot_of((1, d_lat, local), slot) for slot in (1, 2, 3)]
         + [
@@ -1364,7 +1400,7 @@
             each((1, stacked)),
             rows_of(count, d_lat),
         ],
-        out_specs=[rows_of(count, d_lat)] + [whole((d_lat, local))] * 4 + [whole((1, d_lat))],
+        out_specs=[rows_of(count, d_lat)] + [whole((2, d_lat, local))] * 2 + [whole((1, d_lat))],
         scratch_shapes=[
             pltpu.VMEM((rows, d_lat), jnp.bfloat16),
             pltpu.VMEM((rows, local), jnp.bfloat16),
@@ -1375,7 +1411,7 @@
         cost_estimate=pl.CostEstimate(
             flops=6 * 10**9, bytes_accessed=16 * 10**6, transcendentals=3 * 10**5
         ),
-    )(grad, latent, gain, wide, wide, wide, wideout, triple, output, total, low)
+    )(*map(in_hbm, (grad, latent, gain, wide, wide, wide, wideout, triple, output, total, low)))
 
 
 def feed_forward_kernel(
@@ -1410,10 +1446,10 @@
         feed_forward_kernel,
         grid=(4,),
         out_shape=[
-            jax.ShapeDtypeStruct((rows, d_lat), jnp.float32),
-            jax.ShapeDtypeStruct((4, rows, local), jnp.bfloat16),
-            jax.ShapeDtypeStruct((4, rows, local), jnp.float32),
-            jax.ShapeDtypeStruct((rows, d_lat), jnp.bfloat16),
+            pltpu.HBM((rows, d_lat), jnp.float32),
+            pltpu.HBM((4, rows, local), jnp.bfloat16),
+            pltpu.HBM((4, rows, local), jnp.float32),
+            pltpu.HBM((rows, d_lat), jnp.bfloat16),
         ],
         in_specs=[
             whole((rows, d_lat)),
@@ -1431,7 +1467,7 @@
         cost_estimate=pl.CostEstimate(
             flops=4 * 10**9, bytes_accessed=14 * 10**6, transcendentals=10**6
         ),
-    )(latent, gain, wide, wideout)
+    )(*map(in_hbm, (latent, gain, wide, wideout)))
 
 
 def feed_backward_kernel(
@@ -1492,11 +1528,11 @@
         feed_backward_kernel,
         grid=(4,),
         out_shape=[
-            jax.ShapeDtypeStruct((rows, d_lat), jnp.float32),
-            jax.ShapeDtypeStruct((2, d_lat, local), jnp.float32),
-            jax.ShapeDtypeStruct((2, d_lat, local), jnp.float32),
-            jax.ShapeDtypeStruct((4, d_lat, local), jnp.float32),
-            jax.ShapeDtypeStruct((1, d_lat), jnp.float32),
+            pltpu.HBM((rows, d_lat), jnp.float32),
+            pltpu.HBM((2, d_lat, local), jnp.float32),
+            pltpu.HBM((2, d_lat, local), jnp.float32),
+            pltpu.HBM((4, d_lat, local), jnp.float32),
+            pltpu.HBM((1, d_lat), jnp.float32),
         ],
         in_specs=[
             whole((rows, d_lat)),
@@ -1525,7 +1561,158 @@
         cost_estimate=pl.CostEstimate(
             flops=9 * 10**9, bytes_accessed=26 * 10**6, transcendentals=0
         ),
-    )(grad, latent, gain, wide, wideout, active, slope, low)
+    )(*map(in_hbm, (grad, latent, gain, wide, wideout, active, slope, low)))
+
+
+def write_kernel(stage, held, raws, results, scratch):
+    (
+        scalars_ref,
+        latent_ref,
+        noisy_ref,
+        noise_ref,
+        keep_ref,
+        place_ref,
+        pixels_ref,
+        wide_gain_ref,
+        gain_ref,
+        key_weight_ref,
+        value_weight_ref,
+        query_weight_ref,
+        out_weight_ref,
+    ) = held
+    (
+        latent_grad_ref,
+        key_grad_ref,
+        value_grad_ref,
+        query_grad_ref,
+        out_grad_ref,
+        wide_gain_grad_ref,
+        gain_grad_ref,
+        embed_grad_ref,
+        head_grad_ref,
+        loss_ref,
+    ) = results
+    queries, outputs, upstream, query_grads, normed_ref, scale_ref = scratch
+    stage.wait(*range(9))
+    patches, width = queries.shape
+    group = 4 * HEAD_DIM
+    groups = width // group
+    latents = latent_ref.shape[0]
+    rows = 4 * latents
+    weight, weight_total = scalars_ref[:1, :1], scalars_ref[:1, 1:2]
+
+    latent_normed, latent_scale = norm_rows(latent_ref[...])
+    latent_low = (latent_normed * wide_gain_ref[...]).astype(jnp.bfloat16)
+    interface = embed(noisy_ref[...], pixels_ref[0], place_ref[...])
+    normed, scale = norm_rows(interface)
+    normed_ref[...] = normed
+    scale_ref[...] = scale
+    outer_low = (normed * gain_ref[1:2]).astype(jnp.bfloat16)
+    stage.wait(9, 10)
+    keys = dot(latent_low, key_weight_ref[...]).astype(jnp.bfloat16)
+    values = dot(latent_low, value_weight_ref[...]).astype(jnp.bfloat16)
+    stage.wait(11, 12)
+    queries[...] = dot(outer_low, query_weight_ref[...]).astype(jnp.bfloat16)
+
+    def part(values, index):
+        return values[:, index * group : (index + 1) * group]
+
+    def by_head(values):
+        return values.reshape(4, latents, patches)
+
+    def group_probs(index):
+        scores = by_head(dot(scaled_heads(part(keys, index)), part(queries, index), 1, 1))
+        grown = jnp.exp(scores - jnp.max(scores, 1, keepdims=True))
+        return grown / jnp.sum(grown, 1, keepdims=True)
+
+    for index in range(groups):
+        probs = group_probs(index).reshape(rows, patches).astype(jnp.bfloat16)
+        output = dot(probs, spread_heads(part(values, index)), 0, 0)
+        outputs[:, index * group : (index + 1) * group] = output.astype(jnp.bfloat16)
+
+    outer = interface + dot(outputs[...], out_weight_ref[...], 1, 1)
+    final_normed, final_scale = norm_rows(outer)
+    final_low = (final_normed * gain_ref[2:3]).astype(jnp.bfloat16)
+    head = pixels_ref[1]
+    difference = dot(head, final_low, 1, 1) - noise_ref[...]
+    masked = weight * keep_ref[...] * difference
+    loss_ref[...] = jnp.full(loss_ref.shape, jnp.sum(masked * difference))
+    predict_grad = (2.0 * masked / weight_total).astype(jnp.bfloat16)
+    head_grad_ref[...] = dot(predict_grad, final_low)
+    final_grad = dot(predict_grad, head, 0, 0)
+    gain_final = jnp.sum(final_grad * final_normed, 0, keepdims=True)
+    outer_grad = norm_rows_back(final_grad, gain_ref[2:3], final_normed, final_scale)
+    branch = outer_grad.astype(jnp.bfloat16)
+    out_grad_ref[...] = dot(branch, outputs[...], 0, 0)
+    stage.store(4)
+    upstream[...] = dot(branch, out_weight_ref[...]).astype(jnp.bfloat16)
+
+    key_grads, value_grads = [], []
+    for index in range(groups):
+        probs = group_probs(index)
+        low = probs.reshape(rows, patches).astype(jnp.bfloat16)
+        above = part(upstream, index)
+        value_grads.append(join_heads(dot(low, above), 4).astype(jnp.bfloat16))
+        prob_grad = by_head(dot(spread_heads(part(values, index)), above, 1, 1))
+        inner = jnp.sum(prob_grad * probs, 1, keepdims=True)
+        score_grad = (probs * (prob_grad - inner)).reshape(rows, patches).astype(jnp.bfloat16)
+        key_grad = join_heads(dot(score_grad, part(queries, index)), 4) * HEAD_DIM ** (-0.5)
+        key_grads.append(key_grad.astype(jnp.bfloat16))
+        query_grad = dot(score_grad, scaled_heads(part(keys, index)), 0, 0)
+        query_grads[:, index * group : (index + 1) * group] = query_grad.astype(jnp.bfloat16)
+    key_grad, value_grad = (jnp.concatenate(item, 1) for item in (key_grads, value_grads))
+
+    turned = latent_low.T
+    key_grad_ref[...] = dot(turned, key_grad)
+    value_grad_ref[...] = dot(turned, value_grad)
+    stage.store(1, 2)
+    latent_part = dot(key_grad, key_weight_ref[...], 1, 1) + dot(
+        value_grad, value_weight_ref[...], 1, 1
+    )
+    wide_gain_grad_ref[...] = jnp.sum(latent_part * latent_normed, 0, keepdims=True)
+    latent_grad_ref[...] = norm_rows_back(
+        latent_part, wide_gain_ref[...], latent_normed, latent_scale
+    )
+    normed, scale = normed_ref[...], scale_ref[...]
+    outer_low = (normed * gain_ref[1:2]).astype(jnp.bfloat16)
+    query_grad_ref[...] = dot(outer_low, query_grads[...], 0, 0)
+    stage.store(3)
+    outer_part = dot(query_grads[...], query_weight_ref[...], 1, 1)
+    gain_outer = jnp.sum(outer_part * normed, 0, keepdims=True)
+    gain_grad_ref[...] = jnp.concatenate([gain_outer, gain_final], 0)
+    back = outer_grad + norm_rows_back(outer_part, gain_ref[1:2], normed, scale)
+    embed_grad_ref[...] = embed_back(noisy_ref[...], back)
+
+
+def write_stage(
+    scalars, latent, noisy, noise, keep, place, pixels, wide_gain, gains, weights
+):
+    latents, d_lat = latent.shape
+    rows, patches = noisy.shape
+    d_if = place.shape[1]
+    width = weights[0].shape[1]
+    results = [
+        (latents, d_lat),
+        (d_lat, width),
+        (d_lat, width),
+        (d_if, width),
+        (d_if, width),
+        (1, d_lat),
+        (2, d_if),
+        (rows, d_if),
+        (rows, d_if),
+        (8, 128),
+    ]
+    wide = pltpu.VMEM((patches, width), jnp.bfloat16)
+    return staged(
+        write_kernel,
+        [scalars, latent, noisy, noise, keep, place, pixels, wide_gain, gains, *weights],
+        [jax.ShapeDtypeStruct(shape, jnp.float32) for shape in results],
+        [wide] * 4
+        + [pltpu.VMEM((patches, d_if), jnp.float32), pltpu.VMEM((patches, 1), jnp.float32)],
+        15 * 10**9,
+        length=27,
+    )
 
 
 def adam_update(master, first, second, gradient, scale):
@@ -1544,17 +1731,18 @@
     return jnp.sum(values.reshape(-1, 8, values.shape[-1]), 0)
 
 
-def closing_kernel(count, count_dp, sizes, *refs):
-    refs = list(refs)
+def closing_kernel(count, count_dp, number, stage, held, raws, results, scratch):
+    refs = list(scratch)
 
     def pull(number):
         taken = refs[:number]
         del refs[:number]
         return taken
 
-    number, finished = sizes
-    items, (columns, tile), done = pull(number), pull(2), pull(finished)
-    wide_out, narrow_out, turned_out, last_out, latents_out, rest_out, stats = pull(7)
+    items, (columns, tile), done = views(held[:number]), held[number : number + 2], held[number + 2 :]
+    done = views(done, 2)
+    number = len(items)
+    wide_out, narrow_out, turned_out, last_out, latents_out, rest_out, stats = results
     shares = pull(number)
     sums = PieceSums(count_dp, items, shares, pull(number * (count_dp.bit_length() + 1)))
     (write_share,) = pull(1)
@@ -1567,6 +1755,7 @@
     others += [over_mp.peer(step) for step in range(1, count)]
     signal_all(barrier, others)
     pl.semaphore_wait(barrier, len(others))
+    stage.wait()
 
     sums.begin()
     scatter.run(lambda: sums.advance(1))
@@ -1577,7 +1766,7 @@
         spread.start()
     scatter.settle()
 
-    self_in_2, self_out, read_query, read_key, read_value, read_out = shares[:6]
+    self_in_2, self_out, read_query, read_out, read_key, read_value = shares[:6]
     self_in_0, self_in_1 = done[:2]
     up, down = done[2:6], done[6:10]
     lat_rows, if_rows = self_out.shape[0], read_key.shape[0]
@@ -1601,6 +1790,7 @@
     for slot, gradient in enumerate([read_out, self_out] + down):
         keep(turned_out.at[slot], gradient, True)
     keep(last_out, write_out)
+    stage.store(0, 1, 2, 3)
     for spread in small:
         spread.take()
     latents, rest = (spread.total() for spread in small)
@@ -1627,8 +1817,8 @@
 def closing(items, columns, tile, done, call_id):
     items, shapes, shares = piece_shapes(items)
     count, count_dp = lax.axis_size("mp"), lax.axis_size("dp")
-    lat_rows, local = done[0].shape
-    if_rows = shapes[3][0]
+    lat_rows, local = done[0].shape[1:]
+    if_rows = shapes[4][0]
     outs = [
         (10, lat_rows, local),
         (3, if_rows, local),
@@ -1639,7 +1829,7 @@
         (8, 128),
     ]
     outs = [jax.ShapeDtypeStruct(shape, jnp.float32) for shape in outs]
-    shares = [pltpu.VMEM(item.shape, jnp.float32) for item in shares]
+    shares = [pltpu.VMEM(shape, jnp.float32) for shape in shapes]
     scratch = (
         shares
         + PieceSums.scratch(count_dp, shapes)
@@ -1650,88 +1840,220 @@
         + Spread.scratch(count_dp, tile.shape)
         + Spread.scratch(count, tile.shape)
     )
-    here = [*items, columns, tile, *done]
-    return pl.pallas_call(
-        partial(closing_kernel, count, count_dp, (len(items), len(done))),
-        out_shape=outs,
-        in_specs=[VMEM_SPEC] * len(here),
-        out_specs=[VMEM_SPEC] * len(outs),
-        scratch_shapes=scratch,
-        compiler_params=pltpu.CompilerParams(
-            collective_id=call_id,
-            has_side_effects=True,
-            vmem_limit_bytes=room(here, outs, room_of(scratch)),
-        ),
-        cost_estimate=pl.CostEstimate(
-            flops=10**7, bytes_accessed=150 * 10**6, transcendentals=0
-        ),
-    )(*here)
+    return staged(
+        partial(closing_kernel, count, count_dp, len(items)),
+        [*items, columns, tile, *done],
+        outs,
+        scratch,
+        10**7,
+        call_id=call_id,
+        length=50,
+    )
 
 
 def clip_scale(norm):
     return clip_level / jnp.maximum(norm, clip_level)
 
 
-def update_kernel(kinds, stats, *refs):
-    gradients, refs = refs[:kinds], refs[kinds:]
-    states, outs, held = (refs[index * 3 * kinds : (index + 1) * 3 * kinds] for index in range(3))
-    sems = refs[9 * kinds]
+def update_kernel(kinds, *refs):
+    number = 3 * kinds
+    sources, states, refs = refs[: 1 + kinds], refs[1 + kinds :][:number], refs[1 + kinds + number :]
+    outs, local, refs = refs[:number], refs[number:][: 1 + kinds], refs[number + 1 + kinds :]
+    local_sems, held, (in_sems, out_sems) = refs[0], refs[1 : 1 + number], refs[1 + number :]
+    stats, gradients = local[0], local[1:]
+    firsts = [
+        pltpu.make_async_copy(source, target, local_sems.at[index])
+        for index, (source, target) in enumerate(zip(sources, local))
+    ]
+    for first in firsts:
+        first.start()
     lane = lax.broadcasted_iota(jnp.int32, (8, 128), 1)
-    first = jnp.logical_and(lane == 0, lax.broadcasted_iota(jnp.int32, (8, 128), 0) == 0)
-    scale = jnp.sum(jnp.where(first, clip_scale(stats[...]), 0.0))
-    copies = []
-
-    def update(kind, at, gradient):
-        refs = [3 * kind + index for index in range(3)]
-        results = adam_update(*(states[index][at] for index in refs), gradient, scale)
-        for index, result in zip(refs, results):
-            held[index][at] = result
-
-    def send(kind, slot):
-        for index in range(3 * kind, 3 * kind + 3):
-            source, target = held[index], outs[index]
-            if slot is not None:
-                source, target = source.at[slot], target.at[slot]
-            copies.append(pltpu.make_async_copy(source, target, sems.at[len(copies)]))
-            copies[-1].start()
-
+    corner = jnp.logical_and(lane == 0, lax.broadcasted_iota(jnp.int32, (8, 128), 0) == 0)
+    loads, copies = [], []
+    pieces = []
     for kind, gradient in enumerate(gradients):
         slots = range(gradient.shape[0]) if len(gradient.shape) == 3 else [None]
-        for slot in slots:
-            rows, width = states[3 * kind].shape[-2:]
-            step = math.gcd(rows, max(8, 8192 // width)) if rows % 8 == 0 else rows
-            source = gradient if slot is None else gradient.at[slot]
-
-            def one(index, carry, kind=kind, slot=slot, source=source, step=step, width=width):
-                where = pl.ds(pl.multiple_of(index * step, step), step)
-                update(kind, (where,) if slot is None else (slot, where), source[where, :width])
-                return carry
-
-            lax.fori_loop(0, rows // step, one, 0)
-            send(kind, slot)
+        pieces += [(kind, slot) for slot in slots]
+
+    def at(ref, slot):
+        return ref if slot is None else ref.at[slot]
+
+    for kind, slot in pieces:
+        for index in range(3 * kind, 3 * kind + 3):
+            source, target = at(states[index], slot), at(held[index], slot)
+            loads.append(pltpu.make_async_copy(source, target, in_sems.at[len(loads)]))
+            loads[-1].start()
+    for load in firsts:
+        load.wait()
+    scale = jnp.sum(jnp.where(corner, clip_scale(stats[...]), 0.0))
+    for order, (kind, slot) in enumerate(pieces):
+        for load in loads[3 * order : 3 * order + 3]:
+            load.wait()
+        refs = [at(held[index], slot) for index in range(3 * kind, 3 * kind + 3)]
+        source = at(gradients[kind], slot)
+        rows, width = refs[0].shape
+        step = math.gcd(rows, max(8, 8192 // width)) if rows % 8 == 0 else rows
+
+        def one(index, carry, refs=refs, source=source, step=step, width=width):
+            where = pl.ds(pl.multiple_of(index * step, step), step)
+            state = [ref[where] for ref in refs]
+            for ref, result in zip(refs, adam_update(*state, source[where, :width], scale)):
+                ref[where] = result
+            return carry
+
+        lax.fori_loop(0, rows // step, one, 0)
+        for index in range(3 * kind, 3 * kind + 3):
+            source, target = at(held[index], slot), at(outs[index], slot)
+            copies.append(pltpu.make_async_copy(source, target, out_sems.at[len(copies)]))
+            copies[-1].start()
     for copy in copies:
         copy.wait()
 
 
 def update_states(stats, gradients, states):
     kinds = len(gradients)
-    hbm = pl.BlockSpec(memory_space=pltpu.HBM)
-    outs = [jax.ShapeDtypeStruct(item.shape, jnp.float32) for item in states]
     copies = sum(3 * (item.shape[0] if item.ndim == 3 else 1) for item in gradients)
+    sems = pltpu.SemaphoreType.DMA((copies,))
     return pl.pallas_call(
         partial(update_kernel, kinds),
-        out_shape=outs,
-        in_specs=[VMEM_SPEC] * (1 + kinds + len(states)),
-        out_specs=[hbm] * len(states),
-        scratch_shapes=[pltpu.VMEM(item.shape, jnp.float32) for item in states]
-        + [pltpu.SemaphoreType.DMA((copies,))],
-        compiler_params=pltpu.CompilerParams(
-            vmem_limit_bytes=room(gradients, states, outs)
-        ),
+        out_shape=[pltpu.HBM(item.shape, item.dtype) for item in states],
+        in_specs=[HBM_SPEC] * (1 + kinds + len(states)),
+        out_specs=[HBM_SPEC] * len(states),
+        scratch_shapes=[pltpu.VMEM(item.shape, jnp.float32) for item in (stats, *gradients)]
+        + [pltpu.SemaphoreType.DMA((1 + kinds,))]
+        + [pltpu.VMEM(item.shape, jnp.float32) for item in states]
+        + [sems] * 2,
+        compiler_params=pltpu.CompilerParams(vmem_limit_bytes=24 << 20),
         cost_estimate=pl.CostEstimate(
             flops=2 * 10**7, bytes_accessed=14 * 10**6, transcendentals=0
         ),
-    )(stats, *gradients, *states)
+    )(*(in_hbm(item) for item in (stats, *gradients, *states)))
+
+
+def write_apart(
+    latent_three,
+    own_noisy,
+    own_noise,
+    own_keep,
+    own_weight,
+    weight_total,
+    place,
+    copy_pixels,
+    gain,
+    gain_rows,
+    weights,
+    layout,
+    timesteps,
+):
+    write_key_weight, write_value_weight, write_query_weight, write_out_weight = weights
+    images, latents, first_image, sharers = layout
+    own_images, own_latents, d_lat = latent_three.shape
+    write_norm, write_stats = layer_norm(latent_three, gain)
+    write_low = write_norm.astype(jnp.bfloat16)
+
+    own_interface = (
+        jnp.einsum(
+            "bcp,cd->bpd", own_noisy, copy_pixels[0].astype(jnp.float32), precision=precise
+        )
+        + place
+    )
+
+    outer_norm, outer_stats = layer_norm(own_interface, gain_rows[9])
+    outer_low = outer_norm.astype(jnp.bfloat16)
+
+    def join(spec, values, weight):
+        product = jnp.einsum(spec, values, weight, preferred_element_type=jnp.float32)
+        return product.astype(jnp.bfloat16)
+
+    def image_rows(values):
+        if sharers == 1:
+            return values
+        nothing = jnp.where(timesteps[0] > 0, 0.0, -0.0)
+        whole = lax.all_gather(values.astype(jnp.float32), "mp", axis=0, tiled=True)
+        whole = whole + nothing
+        whole = whole.reshape(images, latents, d_lat).astype(jnp.bfloat16)
+        return lax.dynamic_slice_in_dim(whole, first_image, own_images, 0)
+
+    write_query = join("bpd,dc->bpc", outer_low, write_query_weight)
+    write_key = image_rows(join("bld,dc->blc", write_low, write_key_weight))
+    write_value = image_rows(join("bld,dc->blc", write_low, write_value_weight))
+    write_out, write_total = attend_forward(write_query, write_key, write_value, None)
+    outer = own_interface + jnp.einsum(
+        "bpc,dc->bpd", write_out, write_out_weight, preferred_element_type=jnp.float32
+    )
+    final_norm, final_stats = layer_norm(outer, gain_rows[10])
+    final_low = final_norm.astype(jnp.bfloat16)
+    predicted = jnp.einsum(
+        "bpd,cd->bcp", final_low, copy_pixels[1], preferred_element_type=jnp.float32
+    )
+    difference = predicted - own_noise
+    masked = own_weight[:, None, None] * own_keep[:, None, :] * difference
+    loss_local = jnp.sum(masked * difference)
+    predict_grad = (2.0 * masked / weight_total).astype(jnp.bfloat16)
+    head_grad = jnp.einsum(
+        "bcp,bpd->cd", predict_grad, final_low, preferred_element_type=jnp.float32
+    )
+    final_grad = jnp.einsum(
+        "bcp,cd->bpd", predict_grad, copy_pixels[1], preferred_element_type=jnp.float32
+    )
+    outer_grad, gain_final = norm_back(final_grad, gain_rows[10], final_stats)
+    branch_low = outer_grad.astype(jnp.bfloat16)
+    narrowout_grad = jnp.einsum(
+        "bpd,bpc->dc", branch_low, write_out, preferred_element_type=jnp.float32
+    )
+    write_upstream = join("bpd,dc->bpc", branch_low, write_out_weight)
+    query_grad, key_grad, value_grad = attend_back(
+        write_query, write_key, write_value, None, write_total, write_upstream
+    )
+    write_query_grad = jnp.einsum(
+        "bpd,bpc->dc", outer_low, query_grad, preferred_element_type=jnp.float32
+    )
+    outer_part = jnp.einsum(
+        "bpc,dc->bpd", query_grad, write_query_weight, preferred_element_type=jnp.float32
+    )
+
+    def row_grad(values):
+        if sharers > 1:
+            whole = jnp.zeros((images, latents, d_lat), jnp.float32)
+            whole = lax.dynamic_update_slice_in_dim(whole, values, first_image, 0)
+            values = lax.psum_scatter(
+                whole.reshape(images * sharers, own_latents, d_lat),
+                "mp",
+                scatter_dimension=0,
+                tiled=True,
+            )
+        return values.astype(jnp.bfloat16)
+
+    key_grad, value_grad = row_grad(key_grad), row_grad(value_grad)
+    write_key_grad = jnp.einsum(
+        "bld,blc->dc", write_low, key_grad, preferred_element_type=jnp.float32
+    )
+    write_value_grad = jnp.einsum(
+        "bld,blc->dc", write_low, value_grad, preferred_element_type=jnp.float32
+    )
+    write_part = jnp.einsum(
+        "blc,dc->bld", key_grad, write_key_weight, preferred_element_type=jnp.float32
+    ) + jnp.einsum(
+        "blc,dc->bld", value_grad, write_value_weight, preferred_element_type=jnp.float32
+    )
+    own_grad, gain_write = norm_back(write_part, gain, write_stats)
+    outer_back, gain_outer = norm_back(outer_part, gain_rows[9], outer_stats)
+    embed_grad = jnp.einsum(
+        "bcp,bpd->cd", own_noisy, outer_grad + outer_back, precision=precise
+    )
+    return (
+        own_grad,
+        write_key_grad,
+        write_value_grad,
+        write_query_grad,
+        narrowout_grad,
+        gain_write,
+        gain_outer,
+        gain_final,
+        embed_grad,
+        head_grad,
+        loss_local,
+    )
 
 
 def body(
@@ -1807,20 +2129,25 @@
     def wide_gain(index):
         return gain_rows[2 * index : 2 * index + 2].reshape(-1)
 
-    wide_in = jnp.swapaxes(copy_widein, 0, 1)
-    narrow_in = jnp.swapaxes(copy_narrowin, 0, 1)
+    wide_in = in_hbm(jnp.swapaxes(copy_widein, 0, 1))
+    narrow_in = in_hbm(jnp.swapaxes(copy_narrowin, 0, 1))
+    wide_out = in_hbm(copy_wideout)
     place = position_table(patches, d_if)
+    noisy_rows, pixel_rows, noise_rows = (
+        jnp.pad(item, ((0, 0), (0, 16 - PIX), (0, 0)))
+        for item in (noisy, copy_pixels, noise_patches)
+    )
     read_args = (
-        jnp.pad(noisy, ((0, 0), (0, 16 - PIX), (0, 0))),
+        noisy_rows,
         keep_float[:, :, None],
         place,
-        jnp.pad(copy_pixels[0], ((0, 16 - PIX), (0, 0))),
+        pixel_rows[0],
         copy_latents,
         wide_gain(0)[None],
         gain_rows[8:9],
         wide_in,
         narrow_in,
-        copy_wideout,
+        wide_out,
     )
     read_part, *read_kept = read_forward(*read_args)
     gathered, read_part = lax.optimization_barrier((gathered, read_part))
@@ -1832,150 +2159,99 @@
     )
     weight_total = weight_tile[0, 0]
     self_part, *self_kept = self_forward(
-        latent_one, wide_gain(1)[None], wide_in, copy_wideout, images
+        latent_one, wide_gain(1)[None], wide_in, wide_out, images
     )
     latent_two, write_weights = line_sum(
         self_part, latent_one, 3, blocks=(gathered, [d_lat, d_lat, d_if, d_if])
     )
-    write_key_weight, write_value_weight, write_query_weight, write_out_weight = write_weights
-    feed_part, *feed_kept = feed_forward(latent_two, wide_gain(2)[None], wide_in, copy_wideout)
+    feed_part, *feed_kept = feed_forward(latent_two, wide_gain(2)[None], wide_in, wide_out)
     own_two = lax.dynamic_slice_in_dim(
         latent_two, mp_index * (own_images * own_latents), own_images * own_latents, 0
     )
     latent_three = (own_two + line_scatter(feed_part, 4)).reshape(own_images, own_latents, d_lat)
-    write_norm, write_stats = layer_norm(latent_three, wide_gain(3))
-    write_low = write_norm.astype(jnp.bfloat16)
-
     def own_tokens(values, axis):
         values = lax.dynamic_slice_in_dim(values, first_image, own_images, 0)
         return lax.dynamic_slice_in_dim(values, share * own_patches, own_patches, axis)
 
-    own_noisy, own_noise = own_tokens(noisy, 2), own_tokens(noise_patches, 2)
-    own_interface = jnp.einsum(
-        "bcp,cd->bpd", own_noisy, copy_pixels[0].astype(jnp.float32), precision=precise
-    ) + lax.dynamic_slice_in_dim(place, share * own_patches, own_patches, 0)
-    own_keep = own_tokens(keep_float, 1)
     own_weight = lax.dynamic_slice_in_dim(loss_weight, first_image, own_images, 0)
-
-    outer_norm, outer_stats = layer_norm(own_interface, gain_rows[9])
-    outer_low = outer_norm.astype(jnp.bfloat16)
-
-    def join(spec, values, weight):
-        product = jnp.einsum(spec, values, weight, preferred_element_type=jnp.float32)
-        return product.astype(jnp.bfloat16)
-
-    def image_rows(values):
-        if sharers == 1:
-            return values
-        nothing = jnp.where(timesteps[0] > 0, 0.0, -0.0)
-        whole = lax.all_gather(values.astype(jnp.float32), "mp", axis=0, tiled=True)
-        whole = whole + nothing
-        whole = whole.reshape(images, latents, d_lat).astype(jnp.bfloat16)
-        return lax.dynamic_slice_in_dim(whole, first_image, own_images, 0)
-
-    write_query = join("bpd,dc->bpc", outer_low, write_query_weight)
-    write_key = image_rows(join("bld,dc->blc", write_low, write_key_weight))
-    write_value = image_rows(join("bld,dc->blc", write_low, write_value_weight))
-    write_out, write_total = attend_forward(write_query, write_key, write_value, None)
-    outer = own_interface + jnp.einsum(
-        "bpc,dc->bpd", write_out, write_out_weight, preferred_element_type=jnp.float32
-    )
-    final_norm, final_stats = layer_norm(outer, gain_rows[10])
-    final_low = final_norm.astype(jnp.bfloat16)
-    predicted = jnp.einsum(
-        "bpd,cd->bcp", final_low, copy_pixels[1], preferred_element_type=jnp.float32
-    )
-    difference = predicted - own_noise
-    masked = own_weight[:, None, None] * own_keep[:, None, :] * difference
-    loss_local = jnp.sum(masked * difference)
-    predict_grad = (2.0 * masked / weight_total).astype(jnp.bfloat16)
-    head_grad = jnp.einsum(
-        "bcp,bpd->cd", predict_grad, final_low, preferred_element_type=jnp.float32
-    )
-    final_grad = jnp.einsum(
-        "bcp,cd->bpd", predict_grad, copy_pixels[1], preferred_element_type=jnp.float32
-    )
-    outer_grad, gain_final = norm_back(final_grad, gain_rows[10], final_stats)
-    branch_low = outer_grad.astype(jnp.bfloat16)
-    narrowout_grad = jnp.einsum(
-        "bpd,bpc->dc", branch_low, write_out, preferred_element_type=jnp.float32
-    )
-    write_upstream = join("bpd,dc->bpc", branch_low, write_out_weight)
-    query_grad, key_grad, value_grad = attend_back(
-        write_query, write_key, write_value, None, write_total, write_upstream
-    )
-    write_query_grad = jnp.einsum(
-        "bpd,bpc->dc", outer_low, query_grad, preferred_element_type=jnp.float32
-    )
-    outer_part = jnp.einsum(
-        "bpc,dc->bpd", query_grad, write_query_weight, preferred_element_type=jnp.float32
-    )
-
-    def row_grad(values):
-        if sharers > 1:
-            whole = jnp.zeros((images, latents, d_lat), jnp.float32)
-            whole = lax.dynamic_update_slice_in_dim(whole, values, first_image, 0)
-            values = lax.psum_scatter(
-                whole.reshape(images * sharers, own_latents, d_lat),
-                "mp",
-                scatter_dimension=0,
-                tiled=True,
-            )
-        return values.astype(jnp.bfloat16)
-
-    key_grad, value_grad = row_grad(key_grad), row_grad(value_grad)
-    write_key_grad = jnp.einsum(
-        "bld,blc->dc", write_low, key_grad, preferred_element_type=jnp.float32
-    )
-    write_value_grad = jnp.einsum(
-        "bld,blc->dc", write_low, value_grad, preferred_element_type=jnp.float32
-    )
-    write_part = jnp.einsum(
-        "blc,dc->bld", key_grad, write_key_weight, preferred_element_type=jnp.float32
-    ) + jnp.einsum(
-        "blc,dc->bld", value_grad, write_value_weight, preferred_element_type=jnp.float32
-    )
-    own_grad, gain_write = norm_back(write_part, wide_gain(3), write_stats)
-    outer_back, gain_outer = norm_back(outer_part, gain_rows[9], outer_stats)
-
+    if sharers == 1 and own_images == 1:
+        (
+            own_grad,
+            write_key_grad,
+            write_value_grad,
+            write_query_grad,
+            narrowout_grad,
+            gain_write,
+            gain_pair,
+            own_embed,
+            head_grad,
+            loss_tile,
+        ) = write_stage(
+            jnp.pad(jnp.stack([own_weight[0], weight_total])[None], ((0, 7), (0, 126))),
+            latent_three[0],
+            own_tokens(noisy_rows, 2)[0],
+            own_tokens(noise_rows, 2)[0],
+            own_tokens(keep_float, 1),
+            place,
+            pixel_rows,
+            wide_gain(3)[None],
+            gain_rows[8:11],
+            write_weights,
+        )
+        gain_outer, gain_final = gain_pair[0], gain_pair[1]
+        head_grad, own_embed = head_grad[:PIX], own_embed[:PIX]
+        loss_local = loss_tile[0, 0]
+    else:
+        (
+            own_grad,
+            write_key_grad,
+            write_value_grad,
+            write_query_grad,
+            narrowout_grad,
+            gain_write,
+            gain_outer,
+            gain_final,
+            own_embed,
+            head_grad,
+            loss_local,
+        ) = write_apart(
+            latent_three,
+            own_tokens(noisy, 2),
+            own_tokens(noise_patches, 2),
+            own_tokens(keep_float, 1),
+            own_weight,
+            weight_total,
+            lax.dynamic_slice_in_dim(place, share * own_patches, own_patches, 0),
+            copy_pixels,
+            wide_gain(3),
+            gain_rows,
+            write_weights,
+            (images, latents, first_image, sharers),
+            timesteps,
+        )
     latent_grad, (key_share, query_share) = line_gather(
         own_grad.reshape(-1, d_lat), 5, [write_key_grad, write_query_grad]
     )
-    outer_back, gain_outer = norm_back(outer_part, gain_rows[9], outer_stats)
-
-    latent_grad, (key_share, query_share) = line_gather(
-        own_grad.reshape(-1, d_lat), 5, [write_key_grad, write_query_grad]
-    )
     latent_grad = latent_grad.reshape(latent_one.shape)
-    outer_back, gain_outer = norm_back(outer_part, gain_rows[9], outer_stats)
 
     latent_part, up_first, up_last, down_grad, gain_feed = feed_backward(
-        latent_grad, latent_two, wide_gain(2)[None], wide_in, copy_wideout, *feed_kept
+        latent_grad, latent_two, wide_gain(2)[None], wide_in, wide_out, *feed_kept
     )
     latent_grad, five_shares = line_sum(
         latent_part, latent_grad, 6, [write_value_grad, narrowout_grad, up_first]
     )
-    latent_part, self_query_grad, self_key_grad, self_value_grad, self_out_grad, gain_self = (
-        self_backward(latent_grad, latent_one, wide_gain(1)[None], wide_in, copy_wideout, *self_kept)
+    latent_part, self_first, self_last, gain_self = self_backward(
+        latent_grad, latent_one, wide_gain(1)[None], wide_in, wide_out, *self_kept
     )
     latent_grad, six_shares = line_sum(
-        latent_part, latent_grad, 7, [up_last, down_grad, self_query_grad, self_key_grad]
+        latent_part, latent_grad, 7, [up_last, down_grad, self_first]
     )
     write_share = jnp.concatenate([key_share, five_shares[0], query_share, five_shares[1]], 0)
     write_columns = jnp.concatenate(jnp.split(write_share, count_mp, 1), 0)
-    (
-        read_query_grad,
-        read_key_grad,
-        read_value_grad,
-        read_out_grad,
-        latent_total,
-        gain_read,
-        gain_side,
-        side_embed,
-    ) = read_backward(*read_args, *read_kept, latent_grad, lead.reshape(1, 1))
-    embed_grad = side_embed[:PIX] + jnp.einsum(
-        "bcp,bpd->cd", own_noisy, outer_grad + outer_back, precision=precise
-    )
+    read_wide, read_narrow, latent_total, gain_read, gain_side, side_embed = read_backward(
+        *read_args, *read_kept, latent_grad, lead.reshape(1, 1)
+    )
+    embed_grad = side_embed[:PIX] + own_embed
     gains_grad = jnp.concatenate(
         [
             gain_read.reshape(2, -1),
@@ -2001,18 +2277,15 @@
 
     *gradients, rest_grad, stats = closing(
         [
-            self_value_grad,
-            self_out_grad,
-            read_query_grad,
-            read_key_grad,
-            read_value_grad,
-            read_out_grad,
+            self_last,
+            read_wide,
+            read_narrow,
             latents_item.reshape(-1, latents_item.shape[2]),
             rest.reshape(-1, rest.shape[2]),
         ],
         write_columns,
         jnp.full((8, 128), loss_local),
-        [*six_shares[6:8], *five_shares[2:], *six_shares[:6]],
+        [six_shares[2], five_shares[2], six_shares[0], six_shares[1]],
         8,
     )
     states = (

time: 702 us -> 584 us (0.83)
  local copies, waits for them, and re-layouts: 118 us -> 29.6 us
  matrix products: 52.6 us -> 0 us
  Pallas kernels: 474 us -> 499 us
  waiting for transfers between devices: 10.9 us -> 18.8 us
    unnamed x392 -> x52, local copies, waits for them, and re-layouts: 99.4 us -> 6.52 us
    dot_general x23 -> x0, matrix products: 52.6 us -> none  [the longest x4 8.64 us: join(): jnp.einsum(spec, values, weight, preferred_element_type=jnp.float32)]
    pallas_call x15, Pallas kernels: 474 us -> 499 us  [the longest x8 403 us: staged(): pl.pallas_call(partial(staged_kernel, body, (len(inputs), len(raw), len(o...]
    all_gather x1, waiting for transfers between devices: 10.8 us -> 18.7 us  [body(): lax.all_gather(jnp.concatenate([key_piece, value_piece, query_piece, out_...]
  transfers between devices with their start and end apart: 2 -> 2, of which waited for: 1 -> 1; matrix products, arithmetic and copies ran while one was open for 2% -> 3% of each run, Pallas kernels for 11% -> 14%
where the time goes in v5:
time: 584 us; the launch traced here: 576 us
  Pallas kernels  499 us (85%)
  local copies, waits for them, and re-layouts  29.6 us (5%)
  waiting for transfers between devices  18.8 us (3%)
  between operations  18.2 us (3%)
  other arithmetic  10.7 us (2%)
    pallas_call x8, Pallas kernels, staged(): pl.pallas_call(partial(staged_kernel, body, (len(inputs), len(raw), len(o...  403 us
    pallas_call x1, Pallas kernels, read_backward(): pl.pallas_call(read_backward_kernel, grid=(images,), out_shape=[pltpu.HBM...  26.3 us
    all_gather x1, waiting for transfers between devices, body(): lax.all_gather(jnp.concatenate([key_piece, value_piece, query_piece, out_...  18.7 us
    pallas_call x1, Pallas kernels, read_forward(): pl.pallas_call(read_forward_kernel, grid=(images,), out_shape=[pltpu.HBM(...  16 us
    pallas_call x1, Pallas kernels, feed_backward(): pl.pallas_call(feed_backward_kernel, grid=(4,), out_shape=[pltpu.HBM((row...  14.1 us
    pallas_call x1, Pallas kernels, self_backward(): pl.pallas_call(self_backward_kernel, grid=(images,), out_shape=[pltpu.HBM...  13.1 us
  transfers between devices with their start and end apart: 2, of which 1 were waited for; matrix products, arithmetic and copies ran while one was open for 3% of the time, Pallas kernels for 14%

profile of v5, /device:TPU:0, one launch (start us, length us, event | category | flops | bytes accessed | tf_op | source)
XLA Modules:
  0.0 576.4 jit_solution(3642424565040306280)
XLA Ops:
  7.3 1.3 fusion.8
  8.9 0.8 maximum_convert_fusion
  11.0 2.0 copy.88.keep_ref
  13.1 0.6 multiply_reduce_fusion
  14.0 0.7 pad.30.noisy_ref
  14.7 0.6 slice_bitcast_fusion.pixels_ref
  15.3 16.0 %shard_map.488 = (f32[512,1024]{1,0:T(8,128)}, bf16[4,2,1024,256]{3,2,1,0:T(8,128)(2,1)}, bf16[4,128,256]{2,1,0:T(8,128)(2,1)}, f32[4,1,512]{2,1,0:T(1,128)}, bf16[512,256]{1,0:T(8,128)(2,1)}) custom-call(f32[4,16,1024]{2,1,0:T(8,128)} %pad.30.noisy_ref, f32[4,1024,1]{2,1,0:T(8,128)} %copy.88.keep_ref, f32[1024,512]{1,0:T(8,128)} %constant.68.clone.place_ref.refs_5_, ...), custom_call_target="tpu_custom_call" | custom-call | flops 10000000000 | bytes 30000000 | tf_op jit(solution)/shard_map/pallas_call | solution.py:1057
  31.3 18.7 %all-gather.5.cloned.1.call-done = f32[1536,256]{1,0:T(8,128)} async-done(((f32[384,256]{1,0:T(8,128)}), f32[1536,256]{1,0:T(8,128)}) %all-gather.5.cloned.1.call-update) | async-done | bytes 1572880 | tf_op jit(solution)/shard_map/all_gather | solution.py:2115
  52.5 0.6 pad.31.refs_6_
  54.3 0.7 fusion.3
  54.9 1.2 broadcast_in_dim.22.refs_2_
  56.2 1.7 broadcast_in_dim.21
  57.8 58.9 %shard_map.489 = (f32[512,1024]{1,0:T(8,128)}, f32[8,128]{1,0:T(8,128)}) custom-call(f32[512,1024]{1,0:T(8,128)} %get-tuple-element.108.refs_0_, f32[512,1024]{1,0:T(8,128)} %bitcast.91, f32[8,128]{1,0:T(8,128)} %broadcast_in_dim.22.refs_2_), custom_call_target="tpu_custom_call" | custom-call | flops 2097152 | bytes 192500000 | tf_op jit(solution)/shard_map/pallas_call | solution.py:429
  116.7 1.2 slice.68
  117.9 1.4 maximum_bitcast_fusion
  119.9 7.6 %shard_map.490 = (f32[512,1024]{1,0:T(8,128)}, bf16[4,3,128,256]{3,2,1,0:T(8,128)(2,1)}, bf16[4,128,256]{2,1,0:T(8,128)(2,1)}, f32[4,1,512]{2,1,0:T(1,128)}, bf16[512,1024]{1,0:T(8,128)(2,1)}) custom-call(f32[512,1024]{1,0:T(8,128)} %get-tuple-element.110.latent_ref.refs_1_, f32[1,1024]{1,0:T(1,128)} %bitcast.118, bf16[10,1024,256]{2,1,0:T(8,128)(2,1)} %bitcast.82, ...), custom_call_target="tpu_custom_call" | custom-call | flops 3000000000 | bytes 12000000 | tf_op jit(solution)/shard_map/pallas_call | solution.py:1295
  127.5 60.3 %shard_map.491 = (f32[512,1024]{1,0:T(8,128)}, bf16[1024,1024]{1,0:T(8,128)(2,1)}, bf16[1024,1024]{1,0:T(8,128)(2,1)}, bf16[512,1024]{1,0:T(8,128)(2,1)}, bf16[512,1024]{1,0:T(8,128)(2,1)}) custom-call(f32[512,1024]{1,0:T(8,128)} %get-tuple-element.111.refs_0_, f32[512,1024]{1,0:T(8,128)} %get-tuple-element.110.latent_ref.refs_1_, ...), custom_call_target="tpu_custom_call" | custom-call | flops 2097152 | bytes 192500000 | tf_op jit(solution)/shard_map/pallas_call | solution.py:429
  187.8 10.6 %shard_map.492 = (f32[512,1024]{1,0:T(8,128)}, bf16[4,512,256]{2,1,0:T(8,128)(2,1)}, f32[4,512,256]{2,1,0:T(8,128)}, bf16[512,1024]{1,0:T(8,128)(2,1)}) custom-call(f32[512,1024]{1,0:T(8,128)} %get-tuple-element.113.latent_ref, f32[1,1024]{1,0:T(1,128)} %bitcast.122, bf16[10,1024,256]{2,1,0:T(8,128)(2,1)} %bitcast.85, bf16[6,256,1024]{2,1,0:T(8,128)(2,1)} %out_weight_ref.7), custom_call_target="tpu_custom_call" | custom-call | flops 4000000000 | bytes 14000000 | tf_op jit(solution)/shard_map/pallas_call | solution.py:1445
  198.4 35.5 %shard_map.493 = f32[128,1024]{1,0:T(8,128)} custom-call(f32[512,1024]{1,0:T(8,128)} %get-tuple-element.114.refs_0_), custom_call_target="tpu_custom_call" | custom-call | flops 1048576 | bytes 115500000 | tf_op jit(solution)/shard_map/pallas_call | solution.py:429
  233.9 2.1 dynamic-slice_add_fusion.refs_1_
  236.0 26.3 %shard_map.494 = (f32[128,1024]{1,0:T(8,128)}, f32[1024,1024]{1,0:T(8,128)}, f32[1024,1024]{1,0:T(8,128)}, f32[512,1024]{1,0:T(8,128)}, f32[512,1024]{1,0:T(8,12...) custom-call(f32[8,128]{1,0:T(8,128)} %pad.32.refs_0_, ...), custom_call_target="tpu_custom_call" | custom-call | flops 15000000512 | bytes 94500000 | tf_op jit(solution)/shard_map/pallas_call | solution.py:429
  262.3 42.8 %shard_map.495 = (f32[512,1024]{1,0:T(8,128)}, f32[128,1024]{1,0:T(8,128)}, f32[64,1024]{1,0:T(8,128)}) custom-call(f32[128,1024]{1,0:T(8,128)} %get-tuple-element.119.refs_0_, f32[8,128,1024]{2,1,0:T(8,128)} %bitcast.94, f32[8,64,1024]{2,1,0:T(8,128)} %bitcast.96), custom_call_target="tpu_custom_call" | custom-call | flops 131072 | bytes 133000000 | tf_op jit(solution)/shard_map/pallas_call | solution.py:429
  305.1 1.1 constant_dynamic-update-slice_fusion.3
  306.2 14.1 %shard_map.496 = (f32[512,1024]{1,0:T(8,128)}, f32[2,1024,256]{2,1,0:T(8,128)}, f32[2,1024,256]{2,1,0:T(8,128)}, f32[4,1024,256]{2,1,0:T(8,128)}, f32[1,1024]{1,0:T(1,128)}) custom-call(f32[512,1024]{1,0:T(8,128)} %get-tuple-element.122.grad_ref.refs_1_, f32[512,1024]{1,0:T(8,128)} %get-tuple-element.113.latent_ref, f32[1,1024]{1,0:T(1,128)} %bitcast.123, ...), custom_call_target="tpu_custom_call" | custom-call | flops 8999999488 | bytes 26000000 | tf_op jit(solution)/shard_map/pallas_call | solution.py:1527
  320.3 62.2 %shard_map.497 = (f32[512,1024]{1,0:T(8,128)}, f32[128,1024]{1,0:T(8,128)}, f32[64,1024]{1,0:T(8,128)}, f32[2,128,256]{2,1,0:T(8,128)}) custom-call(f32[512,1024]{1,0:T(8,128)} %get-tuple-element.126.refs_0_, f32[512,1024]{1,0:T(8,128)} %get-tuple-element.122.grad_ref.refs_1_, f32[8,128,1024]{2,1,0:T(8,128)} %bitcast.93, f32[8,64,1024]{2,1,0:T(8,128)} %bitcast.101, ...), custom_call_target="tpu_custom_call" | custom-call | flops 2097152 | bytes 192500000 | tf_op jit(solution)/shard_map/pallas_call | solution.py:429
  382.5 1.1 constant_dynamic-update-slice_fusion.2
  383.6 1.0 constant_dynamic-update-slice_fusion
  384.7 13.1 %shard_map.498 = (f32[512,1024]{1,0:T(8,128)}, f32[2,1024,256]{2,1,0:T(8,128)}, f32[2,1024,256]{2,1,0:T(8,128)}, f32[1,1024]{1,0:T(1,128)}) custom-call(f32[512,1024]{1,0:T(8,128)} %get-tuple-element.130.grad_ref.refs_1_, f32[512,1024]{1,0:T(8,128)} %get-tuple-element.110.latent_ref.refs_1_, f32[1,1024]{1,0:T(1,128)} %bitcast.119, ...), custom_call_target="tpu_custom_call" | custom-call | flops 6000000000 | bytes 16000000 | tf_op jit(solution)/shard_map/pallas_call | solution.py:1388
  397.9 62.4 %shard_map.499 = (f32[512,1024]{1,0:T(8,128)}, f32[2,128,256]{2,1,0:T(8,128)}, f32[4,128,256]{2,1,0:T(8,128)}, f32[2,128,256]{2,1,0:T(8,128)}) custom-call(f32[512,1024]{1,0:T(8,128)} %get-tuple-element.140.refs_0_, f32[512,1024]{1,0:T(8,128)} %get-tuple-element.130.grad_ref.refs_1_, f32[2,8,128,256]{3,2,1,0:T(8,128)} %bitcast.100, ...), custom_call_target="tpu_custom_call" | custom-call | flops 2097152 | bytes 192500000 | tf_op jit(solution)/shard_map/pallas_call | solution.py:429
  460.3 26.3 %shard_map.500 = (f32[2,1024,256]{2,1,0:T(8,128)}, f32[2,512,256]{2,1,0:T(8,128)}, f32[128,1024]{1,0:T(8,128)}, f32[1,1024]{1,0:T(1,128)}, f32[1,512]{1,0:T(1,128)}, /*index=5*/f32[16,512]{1,0:T(8,128)}) custom-call(f32[4,16,1024]{2,1,0:T(8,128)} %pad.30.noisy_ref, f32[4,1024,1]{2,1,0:T(8,128)} %copy.88.keep_ref, ...), custom_call_target="tpu_custom_call" | custom-call | flops 20000000000 | bytes 30000000 | tf_op jit(solution)/shard_map/pallas_call | solution.py:1209
  487.2 1.3 reduce.12
  488.6 0.7 reduce.13
  489.2 0.7 reduce.14
  489.9 0.7 reduce.15
  490.6 0.8 slice_add_fusion
  491.5 0.7 concatenate.18
  492.4 0.7 pad.37.refs_4_
  493.1 1.2 copy.91
  494.3 1.0 copy.92
  495.3 1.2 slice.75
  496.5 1.3 pad_maximum_fusion.refs_5_
  497.8 1.2 broadcast_in_dim.24.refs_6_
  499.0 54.1 %shard_map.501 = (f32[10,128,256]{2,1,0:T(8,128)}, f32[3,64,256]{2,1,0:T(8,128)}, f32[6,256,128]{2,1,0:T(8,128)}, f32[64,256]{1,0:T(8,128)}, f32[128,128]{1,0:T(...) custom-call(f32[2,8,128,256]{3,2,1,0:T(8,128)} %bitcast.98, f32[2,8,128,256]{3,2,1,0:T(8,128)} %bitcast.99, ...), custom_call_target="tpu_custom_call" | custom-call | flops 10000000 | bytes 175000000 | tf_op jit(solution)/shard_map/pallas_call | solution.py:429
  553.1 0.7 slice_bitcast_fusion.2
  553.8 1.3 fusion.12
  555.9 0.6 copy.100
  556.5 0.6 copy.98
  559.1 8.9 %shard_map.502 = (f32[10,128,256]{2,1,0:T(8,128)}, f32[10,128,256]{2,1,0:T(8,128)}, f32[10,128,256]{2,1,0:T(8,128)}, f32[3,64,256]{2,1,0:T(8,128)}, f32[3,64,256...) custom-call(f32[8,128]{1,0:T(8,128)} %get-tuple-element.166.refs_0_,, ...), custom_call_target="tpu_custom_call" | custom-call | flops 20000000 | bytes 14000000 | tf_op jit(solution)/shard_map/pallas_call | solution.py:1917
  (80 shorter events, 7.8 us)
Async XLA Ops:
  7.2 1.5 copy-start
  7.2 1.5 slice-start
  7.2 42.8 %all-gather.5.cloned.1.call-start = ((), (), s32[]{:S(2)}) async-start(), calls=%async_computation | async-start | bytes 1966080 | tf_op jit(solution)/shard_map/all_gather | solution.py:2115
  7.3 2.5 copy-start.7
  7.3 3.7 copy-start.6
  8.6 4.3 copy-start.10
  8.6 4.5 copy-start.19
  8.6 5.1 copy-start.4
  8.7 5.1 copy-start.5
  9.7 117.7 %all-gather.7.cloned.1.call-start = ((), (), s32[]{:S(2)}) async-start(), calls=%async_computation.1 | async-start | bytes 14155776 | tf_op jit(solution)/shard_map/all_gather | solution.py:2154
  31.3 24.9 %copy-start.2 = (bf16[128,1024]{1,0:T(8,128)(2,1)S(1)}, bf16[128,1024]{1,0:T(8,128)(2,1)}, u32[]{:S(2)}) copy-start(bf16[128,1024]{1,0:T(8,128)(2,1)} %latents_ref.3) | copy-start | bytes 786436
  320.3 63.3 %copy-start.3 = (f32[64,1024]{1,0:T(8,128)S(1)}, f32[64,1024]{1,0:T(8,128)}, u32[]{:S(2)}) copy-start(f32[64,1024]{1,0:T(8,128)} %get-tuple-element.159) | copy-start | bytes 786436
  460.3 28.3 %copy-start.17 = (f32[1,1024]{1,0:T(1,128)S(1)}, f32[1,1024]{1,0:T(1,128)}, u32[]{:S(2)}) copy-start(f32[1,1024]{1,0:T(1,128)} %get-tuple-element.149) | copy-start | bytes 12292
  460.3 29.0 %copy-start.16 = (f32[1,1024]{1,0:T(1,128)S(1)}, f32[1,1024]{1,0:T(1,128)}, u32[]{:S(2)}) copy-start(f32[1,1024]{1,0:T(1,128)} %get-tuple-element.150) | copy-start | bytes 12292
  460.3 29.6 %copy-start.15 = (f32[1,1024]{1,0:T(1,128)S(1)}, f32[1,1024]{1,0:T(1,128)}, u32[]{:S(2)}) copy-start(f32[1,1024]{1,0:T(1,128)} %get-tuple-element.151) | copy-start | bytes 12292
  460.3 30.3 %copy-start.8 = (f32[16,512]{1,0:T(8,128)S(1)}, f32[16,512]{1,0:T(8,128)}, u32[]{:S(2)}) copy-start(f32[16,512]{1,0:T(8,128)} %get-tuple-element.155) | copy-start | bytes 98308
  460.3 31.1 %copy-start.9 = (f32[16,512]{1,0:T(8,128)S(1)}, f32[16,512]{1,0:T(8,128)}, u32[]{:S(2)}) copy-start(f32[16,512]{1,0:T(8,128)} %get-tuple-element.156) | copy-start | bytes 98308
  460.3 31.1 %copy-start.18 = (pred[16]{0:T(512)(128)(4,1)S(1)}, pred[16]{0:T(512)(128)(4,1)}, u32[]{:S(2)}) copy-start(pred[16]{0:T(512)(128)(4,1)} %constant.62.clone.1) | copy-start | bytes 52
  460.3 31.2 %copy-start.14 = (f32[2,512]{1,0:T(2,128)S(1)}, f32[2,512]{1,0:T(2,128)}, u32[]{:S(2)}) copy-start(f32[2,512]{1,0:T(2,128)} %get-tuple-element.153) | copy-start | bytes 12292
  499.0 56.9 %copy-start.11 = (f32[2,12,64]{2,0,1:T(2,128)S(1)}, f32[2,12,64]{2,0,1:T(2,128)}, u32[]{:S(2)}) copy-start(f32[2,12,64]{2,0,1:T(2,128)} %param.62) | copy-start | bytes 18436
  499.0 56.9 %copy-start.12 = (f32[2,12,64]{2,0,1:T(2,128)S(1)}, f32[2,12,64]{2,0,1:T(2,128)}, u32[]{:S(2)}) copy-start(f32[2,12,64]{2,0,1:T(2,128)} %param.63) | copy-start | bytes 18436
  499.0 56.9 %copy-start.13 = (f32[2,12,64]{2,0,1:T(2,128)S(1)}, f32[2,12,64]{2,0,1:T(2,128)}, u32[]{:S(2)}) copy-start(f32[2,12,64]{2,0,1:T(2,128)} %param.64) | copy-start | bytes 18436
  559.1 8.9 %copy-start.1 = (bf16[256,512]{1,0:T(8,128)(2,1)S(1)}, bf16[256,512]{1,0:T(8,128)(2,1)}, u32[]{:S(2)}) copy-start(bf16[256,512]{1,0:T(8,128)(2,1)} %param.40) | copy-start | bytes 786436
Sparse Core Ops, SparseCore 0:
  10.2 39.7 all-gather.4
  51.9 70.9 all-gather.6

commit v6 on v5

--- a/solution.py
+++ b/solution.py
@@ -122,6 +122,10 @@
 
 def in_hbm(values):
     return pltpu.with_memory_space_constraint(values, pltpu.HBM)
+
+
+def in_vmem(values):
+    return pltpu.with_memory_space_constraint(values, pltpu.VMEM)
 
 
 def remote(source, target, send_sem, recv_sem, device):
@@ -379,7 +383,7 @@
             pltpu.make_async_copy(source, target, out_sems.at[index])
             for index, (source, target) in enumerate(zip(results, targets))
         ]
-        self.stored = []
+        self.stored, self.waited = [], []
 
     def start(self):
         for load in self.loads:
@@ -387,7 +391,9 @@
 
     def wait(self, *indices):
         for index in indices or range(len(self.loads)):
-            self.loads[index].wait()
+            if index not in self.waited:
+                self.loads[index].wait()
+                self.waited.append(index)
 
     def store(self, *indices):
         for index in indices:
@@ -408,35 +414,43 @@
         del refs[:number]
         return taken
 
-    number, raw, results = counts
-    sources, raws, targets = pull(number), pull(raw), pull(results)
+    close, number, raw, close_outs, results = counts
+    near, sources, raws = pull(close), pull(number), pull(raw)
+    near_outs, targets, echoes = pull(close_outs), pull(results), pull(close_outs)
     held, outs, (in_sems, out_sems) = pull(number), pull(results), pull(2)
-    stage = Stage(sources, held, in_sems, outs, targets, out_sems)
+    stage = Stage(
+        sources, held, in_sems, [*near_outs, *outs], [*echoes, *targets], out_sems
+    )
     stage.start()
-    body(stage, held, raws, outs, refs)
+    body(stage, [*near, *held], raws, [*near_outs, *outs], refs)
     stage.finish()
 
 
-def staged(body, inputs, outs, scratch, flops, raw=(), call_id=None, length=0):
+def staged(
+    body, inputs, outs, scratch, flops, raw=(), call_id=None, length=0, near=(), near_outs=()
+):
     copies = [pltpu.VMEM(item.shape, item.dtype) for item in (*inputs, *outs)]
-    sems = [pltpu.SemaphoreType.DMA((max(1, len(group)),)) for group in (inputs, outs)]
+    stores = [*outs, *near_outs]
+    sems = [pltpu.SemaphoreType.DMA((max(1, len(group)),)) for group in (inputs, stores)]
     needed = sum(
         math.prod(item.shape) * jnp.dtype(item.dtype).itemsize
         for item in copies + list(scratch)
         if getattr(item, "dtype", None) in (jnp.float32, jnp.bfloat16)
     )
     params = {} if call_id is None else {"collective_id": call_id, "has_side_effects": True}
+    counts = (len(near), len(inputs), len(raw), len(near_outs), len(outs))
     results = pl.pallas_call(
-        partial(staged_kernel, body, (len(inputs), len(raw), len(outs))),
-        out_shape=[pltpu.HBM(item.shape, item.dtype) for item in outs],
-        in_specs=[HBM_SPEC] * (len(inputs) + len(raw)),
-        out_specs=[HBM_SPEC] * len(outs),
+        partial(staged_kernel, body, counts),
+        out_shape=[pltpu.VMEM(item.shape, item.dtype) for item in near_outs]
+        + [pltpu.HBM(item.shape, item.dtype) for item in stores],
+        in_specs=[VMEM_SPEC] * len(near) + [HBM_SPEC] * (len(inputs) + len(raw)),
+        out_specs=[VMEM_SPEC] * len(near_outs) + [HBM_SPEC] * len(stores),
         scratch_shapes=copies + sems + list(scratch),
         compiler_params=pltpu.CompilerParams(vmem_limit_bytes=needed + (6 << 20), **params),
         cost_estimate=pl.CostEstimate(
             flops=flops, bytes_accessed=length * 3_500_000, transcendentals=0
         ),
-    )(*(in_hbm(item) for item in (*inputs, *raw)))
+    )(*map(in_vmem, near), *map(in_hbm, (*inputs, *raw)))
     return list(results)
 
 
@@ -474,7 +488,7 @@
     return result
 
 
-def line_sum_kernel(count, count_dp, extra, tiled, stage, held, blocks, results, scratch):
+def line_sum_kernel(count, count_dp, extra, tiled, stage, held, raws, results, scratch):
     refs = list(scratch)
 
     def pull(number):
@@ -485,6 +499,7 @@
     part_ref, base_ref, tile = held[0], held[1], held[2 + extra :]
     items, outs = views(held[2 : 2 + extra]), views(results[1 : 1 + extra], 2)
     out_ref, tile_out = results[0], results[1 + extra : 1 + extra + tiled]
+    blocks, base_rows = raws, base_ref.shape[0]
     wide = results[1 + extra + tiled :]
     converted = len(wide)
     inner, from_away, from_toward, toward_send, away_send, away_recv, toward_recv = pull(7)
@@ -502,16 +517,13 @@
     rows = part_ref.shape[0] // chunks
     others = [spread.peer(step) for step in range(1, count_dp)] if tiled else sums.peers()
     greet(place, count, others)
-    stage.wait()
-    if tiled:
-        spread.held[spread.place] = tile[0][...]
-        spread.start()
-    if converted:
-        convert.begin()
-    sums.begin()
 
     def window(step):
         return pl.ds(pl.multiple_of(step * rows, rows), rows)
+
+    def put(step, total):
+        first = lax.rem(step * rows, base_rows)
+        out_ref[window(step)] = total + base_ref[pl.ds(pl.multiple_of(first, rows), rows)]
 
     def push(step, source, inside):
         target = from_toward if inside else from_away
@@ -545,9 +557,20 @@
 
         lax.fori_loop(0, chunks, leave, 0)
 
+    stage.wait()
+    if tiled:
+        spread.held[spread.place] = tile[0][...]
+        spread.start()
+    if converted:
+        convert.begin()
+    sums.begin()
+
+    @pl.when(outermost)
+    def _():
+
         def arrive(step, carry):
             push(step, part_ref, True).wait_recv()
-            out_ref[window(step)] = from_toward[window(step)] + base_ref[window(step)]
+            put(step, from_toward[window(step)])
             push(step, part_ref, False).wait_send()
             if converted:
                 convert.step(step)
@@ -567,7 +590,7 @@
             total = inner[window(step)] + from_toward[window(step)]
             inner[window(step)] = total
             back(step, inner).start()
-            out_ref[window(step)] = total + base_ref[window(step)]
+            put(step, total)
 
         def first(step, carry):
             gather_in(step)
@@ -609,7 +632,7 @@
             def outwards(step, carry):
                 push(step, inner, True).wait_recv()
                 back(step, from_toward).start()
-                out_ref[window(step)] = from_toward[window(step)] + base_ref[window(step)]
+                put(step, from_toward[window(step)])
                 if converted:
                     convert.step(step)
                 return carry
@@ -643,14 +666,13 @@
 
 
 def line_sum(part, base, call_id, items=(), tile=None, blocks=None):
-    shape = part.shape
     items, shapes, shares = piece_shapes(items)
     count, count_dp = lax.axis_size("mp"), lax.axis_size("dp")
     rows, width = part.shape
     buffer = pltpu.VMEM((rows, width), jnp.float32)
     sems = pltpu.SemaphoreType.DMA((CHUNKS,))
-    inputs, raw = [part, base, *items], []
-    outs = [jax.ShapeDtypeStruct((rows, width), jnp.float32)] + shares
+    inputs, raw = [base, *items], []
+    outs = list(shares)
     scratch = [buffer] * 3 + [sems] * 4
     if tile is not None:
         inputs.append(tile)
@@ -664,6 +686,7 @@
         ]
         scratch += Convert.scratch(blocks.shape[1:])
     scratch += PieceSums.scratch(count_dp, shapes)
+    total = jax.ShapeDtypeStruct((rows, width), jnp.float32)
     results = staged(
         partial(line_sum_kernel, count, count_dp, len(items), int(tile is not None)),
         inputs,
@@ -673,8 +696,10 @@
         raw,
         call_id,
         55,
-    )
-    return results[0], results[1:]
+        [part],
+        [total],
+    )
+    return results[0], results[-1], results[1:-1]
 
 
 class LineScatter:
@@ -818,25 +843,36 @@
 
 
 def line_scatter_kernel(count, stage, held, raws, results, scratch):
-    scatter = LineScatter(count, held[0], results[0], scratch[:4], scratch[4:])
+    own, sem = scratch[8:]
+    scatter = LineScatter(count, held[0], results[0], scratch[:4], scratch[4:8])
+    rows = own.shape[0]
+    load = pltpu.make_async_copy(
+        raws[0].at[pl.ds(pl.multiple_of(scatter.place * rows, rows), rows)], own, sem
+    )
+    load.start()
     greet(scatter.place, count)
-    stage.wait()
     scatter.run()
     scatter.settle()
+    load.wait()
+    results[0][...] += own[...]
     scatter.finish()
 
 
-def line_scatter(part, call_id):
+def line_scatter(part, base, call_id):
     rows, width = part.shape
     count = lax.axis_size("mp")
+    own = (rows // count, width)
     (result,) = staged(
         partial(line_scatter_kernel, count),
-        [part],
-        [jax.ShapeDtypeStruct((rows // count, width), jnp.float32)],
-        LineScatter.scratch(count, (rows, width), 8),
+        [],
+        [jax.ShapeDtypeStruct(own, jnp.float32)],
+        LineScatter.scratch(count, (rows, width), 8)
+        + [pltpu.VMEM(own, jnp.float32), pltpu.SemaphoreType.DMA],
         2 * rows * width,
+        [base],
         call_id=call_id,
         length=33,
+        near=[part],
     )
     return result
 
@@ -852,8 +888,7 @@
     rows = block // steps
     below, above = {"mp": place - 1}, {"mp": place + 1}
     greet(place, count, sums.peers())
-    stage.wait()
-    sums.begin()
+    stage.wait(0)
 
     def window(owner, step):
         return pl.ds(pl.multiple_of(owner * block + step * rows, rows), rows)
@@ -880,6 +915,8 @@
         return carry
 
     lax.fori_loop(0, steps, begin, 0)
+    stage.wait(*range(1, len(stage.loads)))
+    sums.begin()
 
     def pass_on(index, carry):
         away, step = 1 + index // steps, lax.rem(index, steps)
@@ -931,13 +968,14 @@
     results = staged(
         partial(line_gather_kernel, count, count_dp, len(items)),
         [own, *items],
-        [jax.ShapeDtypeStruct((rows * count, width), jnp.float32)] + shares,
+        shares,
         [sems] * 4 + PieceSums.scratch(count_dp, shapes),
         rows * width,
         call_id=call_id,
         length=38,
-    )
-    return results[0], results[1:]
+        near_outs=[jax.ShapeDtypeStruct((rows * count, width), jnp.float32)],
+    )
+    return results[0], results[-1], results[1:-1]
 
 
 def dot(left, right, left_dim=1, right_dim=0):
@@ -1058,7 +1096,7 @@
         read_forward_kernel,
         grid=(images,),
         out_shape=[
-            pltpu.HBM((images * count, d_lat), jnp.float32),
+            pltpu.VMEM((images * count, d_lat), jnp.float32),
             pltpu.HBM((images, 2, patches, local), jnp.bfloat16),
             pltpu.HBM((images, count, local), jnp.bfloat16),
             pltpu.HBM((images, 1, stacked), jnp.float32),
@@ -1087,7 +1125,7 @@
         cost_estimate=pl.CostEstimate(
             flops=10**10, bytes_accessed=30 * 10**6, transcendentals=2 * 10**6
         ),
-    )(*map(in_hbm, (noisy, keep, place, pixels, latents, wide_gain, gain, wide, narrow, wideout)))
+    )(in_hbm(noisy), in_hbm(keep), in_hbm(place), in_hbm(pixels), in_hbm(latents), in_hbm(wide_gain), in_hbm(gain), in_hbm(wide), in_hbm(narrow), in_hbm(wideout))
 
 
 def read_backward_kernel(
@@ -1237,22 +1275,7 @@
         cost_estimate=pl.CostEstimate(
             flops=2 * 10**10, bytes_accessed=30 * 10**6, transcendentals=2 * 10**6
         ),
-    )(*map(in_hbm, (noisy,
-        keep,
-        place,
-        pixels,
-        latents,
-        wide_gain,
-        gain,
-        wide,
-        narrow,
-        wideout,
-        pairs,
-        output,
-        total,
-        queries,
-        grad,
-        lead)))
+    )(in_hbm(noisy), in_hbm(keep), in_hbm(place), in_hbm(pixels), in_hbm(latents), in_hbm(wide_gain), in_hbm(gain), in_hbm(wide), in_hbm(narrow), in_hbm(wideout), in_hbm(pairs), in_hbm(output), in_hbm(total), in_hbm(queries), in_vmem(grad), in_hbm(lead))
 
 
 def rows_of(rows, width):
@@ -1296,7 +1319,7 @@
         self_forward_kernel,
         grid=(images,),
         out_shape=[
-            pltpu.HBM((total, d_lat), jnp.float32),
+            pltpu.VMEM((total, d_lat), jnp.float32),
             pltpu.HBM((images, 3, count, local), jnp.bfloat16),
             pltpu.HBM((images, count, local), jnp.bfloat16),
             pltpu.HBM((images, 1, stacked), jnp.float32),
@@ -1316,7 +1339,7 @@
         cost_estimate=pl.CostEstimate(
             flops=3 * 10**9, bytes_accessed=12 * 10**6, transcendentals=3 * 10**5
         ),
-    )(*map(in_hbm, (latent, gain, wide, wide, wide, wideout)))
+    )(in_vmem(latent), in_hbm(gain), in_hbm(wide), in_hbm(wide), in_hbm(wide), in_hbm(wideout))
 
 
 def self_backward_kernel(
@@ -1388,7 +1411,7 @@
     return pl.pallas_call(
         self_backward_kernel,
         grid=(images,),
-        out_shape=[pltpu.HBM((rows, d_lat), jnp.float32)]
+        out_shape=[pltpu.VMEM((rows, d_lat), jnp.float32)]
         + [weight] * 2
         + [pltpu.HBM((1, d_lat), jnp.float32)],
         in_specs=[rows_of(count, d_lat), rows_of(count, d_lat), whole((1, d_lat))]
@@ -1411,7 +1434,7 @@
         cost_estimate=pl.CostEstimate(
             flops=6 * 10**9, bytes_accessed=16 * 10**6, transcendentals=3 * 10**5
         ),
-    )(*map(in_hbm, (grad, latent, gain, wide, wide, wide, wideout, triple, output, total, low)))
+    )(in_vmem(grad), in_hbm(latent), in_hbm(gain), in_hbm(wide), in_hbm(wide), in_hbm(wide), in_hbm(wideout), in_hbm(triple), in_hbm(output), in_hbm(total), in_hbm(low))
 
 
 def feed_forward_kernel(
@@ -1446,7 +1469,7 @@
         feed_forward_kernel,
         grid=(4,),
         out_shape=[
-            pltpu.HBM((rows, d_lat), jnp.float32),
+            pltpu.VMEM((rows, d_lat), jnp.float32),
             pltpu.HBM((4, rows, local), jnp.bfloat16),
             pltpu.HBM((4, rows, local), jnp.float32),
             pltpu.HBM((rows, d_lat), jnp.bfloat16),
@@ -1467,7 +1490,7 @@
         cost_estimate=pl.CostEstimate(
             flops=4 * 10**9, bytes_accessed=14 * 10**6, transcendentals=10**6
         ),
-    )(*map(in_hbm, (latent, gain, wide, wideout)))
+    )(in_vmem(latent), in_hbm(gain), in_hbm(wide), in_hbm(wideout))
 
 
 def feed_backward_kernel(
@@ -1528,7 +1551,7 @@
         feed_backward_kernel,
         grid=(4,),
         out_shape=[
-            pltpu.HBM((rows, d_lat), jnp.float32),
+            pltpu.VMEM((rows, d_lat), jnp.float32),
             pltpu.HBM((2, d_lat, local), jnp.float32),
             pltpu.HBM((2, d_lat, local), jnp.float32),
             pltpu.HBM((4, d_lat, local), jnp.float32),
@@ -1561,12 +1584,13 @@
         cost_estimate=pl.CostEstimate(
             flops=9 * 10**9, bytes_accessed=26 * 10**6, transcendentals=0
         ),
-    )(*map(in_hbm, (grad, latent, gain, wide, wideout, active, slope, low)))
+    )(in_vmem(grad), in_hbm(latent), in_hbm(gain), in_hbm(wide), in_hbm(wideout), in_hbm(active), in_hbm(slope), in_hbm(low))
 
 
 def write_kernel(stage, held, raws, results, scratch):
     (
-        scalars_ref,
+        own_weight_ref,
+        weight_total_ref,
         latent_ref,
         noisy_ref,
         noise_ref,
@@ -1593,13 +1617,13 @@
         loss_ref,
     ) = results
     queries, outputs, upstream, query_grads, normed_ref, scale_ref = scratch
-    stage.wait(*range(9))
+    stage.wait(*range(10))
     patches, width = queries.shape
     group = 4 * HEAD_DIM
     groups = width // group
     latents = latent_ref.shape[0]
     rows = 4 * latents
-    weight, weight_total = scalars_ref[:1, :1], scalars_ref[:1, 1:2]
+    weight, weight_total = own_weight_ref[:1, :1], weight_total_ref[:1, :1]
 
     latent_normed, latent_scale = norm_rows(latent_ref[...])
     latent_low = (latent_normed * wide_gain_ref[...]).astype(jnp.bfloat16)
@@ -1608,10 +1632,10 @@
     normed_ref[...] = normed
     scale_ref[...] = scale
     outer_low = (normed * gain_ref[1:2]).astype(jnp.bfloat16)
-    stage.wait(9, 10)
+    stage.wait(10, 11)
     keys = dot(latent_low, key_weight_ref[...]).astype(jnp.bfloat16)
     values = dot(latent_low, value_weight_ref[...]).astype(jnp.bfloat16)
-    stage.wait(11, 12)
+    stage.wait(12, 13)
     queries[...] = dot(outer_low, query_weight_ref[...]).astype(jnp.bfloat16)
 
     def part(values, index):
@@ -1685,7 +1709,7 @@
 
 
 def write_stage(
-    scalars, latent, noisy, noise, keep, place, pixels, wide_gain, gains, weights
+    own_weight, weight_total, latent, noisy, noise, keep, place, pixels, wide_gain, gains, weights
 ):
     latents, d_lat = latent.shape
     rows, patches = noisy.shape
@@ -1706,7 +1730,19 @@
     wide = pltpu.VMEM((patches, width), jnp.bfloat16)
     return staged(
         write_kernel,
-        [scalars, latent, noisy, noise, keep, place, pixels, wide_gain, gains, *weights],
+        [
+            own_weight,
+            weight_total,
+            latent,
+            noisy,
+            noise,
+            keep,
+            place,
+            pixels,
+            wide_gain,
+            gains,
+            *weights,
+        ],
         [jax.ShapeDtypeStruct(shape, jnp.float32) for shape in results],
         [wide] * 4
         + [pltpu.VMEM((patches, d_if), jnp.float32), pltpu.VMEM((patches, 1), jnp.float32)],
@@ -1731,18 +1767,23 @@
     return jnp.sum(values.reshape(-1, 8, values.shape[-1]), 0)
 
 
-def closing_kernel(count, count_dp, number, stage, held, raws, results, scratch):
-    refs = list(scratch)
-
-    def pull(number):
-        taken = refs[:number]
-        del refs[:number]
+def closing_kernel(count, count_dp, sizes, stage, held, raws, results, scratch):
+    refs, given = list(scratch), list(held)
+
+    def pull(number, source=None):
+        source = refs if source is None else source
+        taken = source[:number]
+        del source[:number]
         return taken
 
-    items, (columns, tile), done = views(held[:number]), held[number : number + 2], held[number + 2 :]
-    done = views(done, 2)
+    number, finished = sizes
+    items, small_parts = views(pull(number, given)), pull(10, given)
+    loss_tile, weight_tile = pull(2, given)
+    done = views(pull(finished, given), 2)
+    wide_out, narrow_out, turned_out, last_out, latents_out, rest_out, stats = results
+    latents_item, rest_item, columns, column_sems = pull(4)
+    items += [latents_item, rest_item]
     number = len(items)
-    wide_out, narrow_out, turned_out, last_out, latents_out, rest_out, stats = results
     shares = pull(number)
     sums = PieceSums(count_dp, items, shares, pull(number * (count_dp.bit_length() + 1)))
     (write_share,) = pull(1)
@@ -1750,14 +1791,47 @@
     small = [Spread("mp", count, *pull(3)) for _ in range(2)]
     over_dp, over_mp = Spread("dp", count_dp, *pull(3)), Spread("mp", count, *pull(3))
 
+    column_loads, low = [], 0
+    block, local = columns.shape[0] // count, columns.shape[1]
+    for source in raws:
+        rows = source.shape[0]
+        for owner in range(count):
+            column_loads.append(
+                pltpu.make_async_copy(
+                    source.at[:, pl.ds(owner * local, local)],
+                    columns.at[pl.ds(owner * block + low, rows)],
+                    column_sems.at[len(column_loads)],
+                )
+            )
+        low += rows
+    for load in column_loads:
+        load.start()
     barrier = pltpu.get_barrier_semaphore()
     others = [over_dp.peer(step) for step in range(1, count_dp)]
     others += [over_mp.peer(step) for step in range(1, count)]
     signal_all(barrier, others)
+    stage.wait()
+    (latent_total, *gains, gain_side, gain_pair, side_embed, own_embed, head_grad) = small_parts
+    d_if = gain_side.shape[1]
+    lanes = d_if // count_dp
+    width = latents_item.shape[2]
+    rest_item[...] = jnp.zeros_like(rest_item)
+    rows = []
+    for gain in gains:
+        rows += [gain[:, :d_if], gain[:, d_if:]]
+    rows += [gain_side[...], gain_pair[...]]
+    blocks = [(0, jnp.concatenate(rows, 0)), (16, side_embed[...] + own_embed[...]), (32, head_grad[...])]
+    for piece in range(count_dp):
+        latents_item[piece] = latent_total[:, piece * width : (piece + 1) * width]
+        for first, block in blocks:
+            rest_item[piece, pl.ds(first, block.shape[0]), :lanes] = block[
+                :, piece * lanes : (piece + 1) * lanes
+            ]
     pl.semaphore_wait(barrier, len(others))
-    stage.wait()
 
     sums.begin()
+    for load in column_loads:
+        load.wait()
     scatter.run(lambda: sums.advance(1))
     for phase in range(2, sums.bits + 1):
         sums.advance(phase)
@@ -1801,53 +1875,61 @@
         jnp.sum(sum_rows(latents * latents)) + jnp.sum(sum_rows(rest * rest))
     )
     lane = lax.broadcasted_iota(jnp.int32, (8, 128), 1)
-    value = jnp.where(lane == 0, local, tile[...])
+    value = jnp.where(lane == 0, local, loss_tile[...])
     for spread in (over_dp, over_mp):
         spread.held[spread.place] = value
         spread.start()
         spread.take()
         value = spread.total()
-    stats[...] = jnp.where(lane == 0, jnp.sqrt(value), value)
+    stats[...] = jnp.where(lane == 0, jnp.sqrt(value), value / weight_tile[...])
     sums.finish()
     scatter.finish()
     for spread in small + [over_dp, over_mp]:
         spread.finish()
 
 
-def closing(items, columns, tile, done, call_id):
-    items, shapes, shares = piece_shapes(items)
+def closing(items, small_parts, tiles, done, write_shares, call_id):
+    items, shapes, _ = piece_shapes(items)
     count, count_dp = lax.axis_size("mp"), lax.axis_size("dp")
+    latents, d_lat = small_parts[0].shape
     lat_rows, local = done[0].shape[1:]
-    if_rows = shapes[4][0]
+    if_rows = write_shares[2].shape[0]
+    extra = [(latents, d_lat // count_dp), (48, 128)]
+    block = (sum(item.shape[0] for item in write_shares), local)
+    columns = (count * block[0], local)
     outs = [
         (10, lat_rows, local),
         (3, if_rows, local),
         (6, local, lat_rows),
         (if_rows, local),
-        shapes[-2],
-        shapes[-1],
+        *extra,
         (8, 128),
     ]
-    outs = [jax.ShapeDtypeStruct(shape, jnp.float32) for shape in outs]
-    shares = [pltpu.VMEM(shape, jnp.float32) for shape in shapes]
+    shapes = shapes + extra
     scratch = (
-        shares
+        [pltpu.VMEM((count_dp,) + shape, jnp.float32) for shape in extra]
+        + [
+            pltpu.VMEM(columns, jnp.float32),
+            pltpu.SemaphoreType.DMA((count * len(write_shares),)),
+        ]
+        + [pltpu.VMEM(shape, jnp.float32) for shape in shapes]
         + PieceSums.scratch(count_dp, shapes)
-        + [pltpu.VMEM((columns.shape[0] // count, columns.shape[1]), jnp.float32)]
-        + LineScatter.scratch(count, columns.shape, 4)
-        + Spread.scratch(count, tuple(shapes[-2]))
-        + Spread.scratch(count, tuple(shapes[-1]))
-        + Spread.scratch(count_dp, tile.shape)
-        + Spread.scratch(count, tile.shape)
+        + [pltpu.VMEM(block, jnp.float32)]
+        + LineScatter.scratch(count, columns, 4)
+        + Spread.scratch(count, extra[0])
+        + Spread.scratch(count, extra[1])
+        + Spread.scratch(count_dp, (8, 128))
+        + Spread.scratch(count, (8, 128))
     )
     return staged(
-        partial(closing_kernel, count, count_dp, len(items)),
-        [*items, columns, tile, *done],
-        outs,
+        partial(closing_kernel, count, count_dp, (len(items), len(done))),
+        [*items, *small_parts, *tiles, *done],
+        [jax.ShapeDtypeStruct(shape, jnp.float32) for shape in outs],
         scratch,
         10**7,
-        call_id=call_id,
-        length=50,
+        write_shares,
+        call_id,
+        50,
     )
 
 
@@ -1856,11 +1938,12 @@
 
 
 def update_kernel(kinds, *refs):
-    number = 3 * kinds
+    number = 3 * (kinds + 1)
     sources, states, refs = refs[: 1 + kinds], refs[1 + kinds :][:number], refs[1 + kinds + number :]
     outs, local, refs = refs[:number], refs[number:][: 1 + kinds], refs[number + 1 + kinds :]
     local_sems, held, (in_sems, out_sems) = refs[0], refs[1 : 1 + number], refs[1 + number :]
     stats, gradients = local[0], local[1:]
+    kinds += 1
     firsts = [
         pltpu.make_async_copy(source, target, local_sems.at[index])
         for index, (source, target) in enumerate(zip(sources, local))
@@ -1886,6 +1969,12 @@
     for load in firsts:
         load.wait()
     scale = jnp.sum(jnp.where(corner, clip_scale(stats[...]), 0.0))
+    pixel_loads = [
+        pltpu.make_async_copy(states[index], held[index], in_sems.at[len(loads) + index - 18])
+        for index in range(18, 21)
+    ]
+    for load in pixel_loads:
+        load.start()
     for order, (kind, slot) in enumerate(pieces):
         for load in loads[3 * order : 3 * order + 3]:
             load.wait()
@@ -1906,13 +1995,24 @@
             source, target = at(held[index], slot), at(outs[index], slot)
             copies.append(pltpu.make_async_copy(source, target, out_sems.at[len(copies)]))
             copies[-1].start()
+    for load in pixel_loads:
+        load.wait()
+    pixels, rest = held[18:21], gradients[-1]
+    for slot in range(2):
+        gradient = rest[16 * (slot + 1) : 16 * (slot + 1) + PIX, : pixels[0].shape[2]]
+        state = [ref[:, slot, :] for ref in pixels]
+        for ref, result in zip(pixels, adam_update(*state, gradient, scale)):
+            ref[:, slot, :] = result
+    for index in range(18, 21):
+        copies.append(pltpu.make_async_copy(held[index], outs[index], out_sems.at[len(copies)]))
+        copies[-1].start()
     for copy in copies:
         copy.wait()
 
 
 def update_states(stats, gradients, states):
     kinds = len(gradients)
-    copies = sum(3 * (item.shape[0] if item.ndim == 3 else 1) for item in gradients)
+    copies = sum(3 * (item.shape[0] if item.ndim == 3 else 1) for item in gradients) + 3
     sems = pltpu.SemaphoreType.DMA((copies,))
     return pl.pallas_call(
         partial(update_kernel, kinds),
@@ -2152,28 +2252,25 @@
     read_part, *read_kept = read_forward(*read_args)
     gathered, read_part = lax.optimization_barrier((gathered, read_part))
     gathered = lax.all_gather(gathered, "dp").reshape(count_dp * count_mp, -1, local)
-    latent_zero = copy_latents.astype(jnp.float32)
-    latent_base = jnp.broadcast_to(latent_zero[None], (images, latents, d_lat))
-    latent_one, (weight_tile,) = line_sum(
-        read_part, latent_base.reshape(-1, d_lat), 2, tile=jnp.full((8, 128), weight_here)
-    )
-    weight_total = weight_tile[0, 0]
+    latent_near, latent_one, (weight_tile,) = line_sum(
+        read_part, copy_latents.astype(jnp.float32), 2, tile=jnp.full((8, 128), weight_here)
+    )
     self_part, *self_kept = self_forward(
-        latent_one, wide_gain(1)[None], wide_in, wide_out, images
-    )
-    latent_two, write_weights = line_sum(
+        latent_near, wide_gain(1)[None], wide_in, wide_out, images
+    )
+    latent_near, latent_two, write_weights = line_sum(
         self_part, latent_one, 3, blocks=(gathered, [d_lat, d_lat, d_if, d_if])
     )
-    feed_part, *feed_kept = feed_forward(latent_two, wide_gain(2)[None], wide_in, wide_out)
-    own_two = lax.dynamic_slice_in_dim(
-        latent_two, mp_index * (own_images * own_latents), own_images * own_latents, 0
-    )
-    latent_three = (own_two + line_scatter(feed_part, 4)).reshape(own_images, own_latents, d_lat)
+    feed_part, *feed_kept = feed_forward(latent_near, wide_gain(2)[None], wide_in, wide_out)
+    latent_three = line_scatter(feed_part, latent_two, 4)
+    latent_three = latent_three.reshape(own_images, own_latents, d_lat)
+
     def own_tokens(values, axis):
         values = lax.dynamic_slice_in_dim(values, first_image, own_images, 0)
         return lax.dynamic_slice_in_dim(values, share * own_patches, own_patches, axis)
 
     own_weight = lax.dynamic_slice_in_dim(loss_weight, first_image, own_images, 0)
+    own_scalar = jnp.broadcast_to(own_weight[0], (8, 128))
     if sharers == 1 and own_images == 1:
         (
             own_grad,
@@ -2187,7 +2284,8 @@
             head_grad,
             loss_tile,
         ) = write_stage(
-            jnp.pad(jnp.stack([own_weight[0], weight_total])[None], ((0, 7), (0, 126))),
+            own_scalar,
+            weight_tile,
             latent_three[0],
             own_tokens(noisy_rows, 2)[0],
             own_tokens(noise_rows, 2)[0],
@@ -2198,9 +2296,6 @@
             gain_rows[8:11],
             write_weights,
         )
-        gain_outer, gain_final = gain_pair[0], gain_pair[1]
-        head_grad, own_embed = head_grad[:PIX], own_embed[:PIX]
-        loss_local = loss_tile[0, 0]
     else:
         (
             own_grad,
@@ -2220,7 +2315,7 @@
             own_tokens(noise_patches, 2),
             own_tokens(keep_float, 1),
             own_weight,
-            weight_total,
+            weight_tile[0, 0],
             lax.dynamic_slice_in_dim(place, share * own_patches, own_patches, 0),
             copy_pixels,
             wide_gain(3),
@@ -2229,63 +2324,46 @@
             (images, latents, first_image, sharers),
             timesteps,
         )
-    latent_grad, (key_share, query_share) = line_gather(
+        gain_write, gain_pair = gain_write[None], jnp.stack([gain_outer, gain_final])
+        own_embed, head_grad = (
+            jnp.pad(item, ((0, 16 - PIX), (0, 0))) for item in (own_embed, head_grad)
+        )
+        loss_tile = jnp.full((8, 128), loss_local)
+    latent_near, latent_grad, (key_share, query_share) = line_gather(
         own_grad.reshape(-1, d_lat), 5, [write_key_grad, write_query_grad]
     )
-    latent_grad = latent_grad.reshape(latent_one.shape)
-
     latent_part, up_first, up_last, down_grad, gain_feed = feed_backward(
-        latent_grad, latent_two, wide_gain(2)[None], wide_in, wide_out, *feed_kept
-    )
-    latent_grad, five_shares = line_sum(
+        latent_near, latent_two, wide_gain(2)[None], wide_in, wide_out, *feed_kept
+    )
+    latent_near, latent_grad, five_shares = line_sum(
         latent_part, latent_grad, 6, [write_value_grad, narrowout_grad, up_first]
     )
     latent_part, self_first, self_last, gain_self = self_backward(
-        latent_grad, latent_one, wide_gain(1)[None], wide_in, wide_out, *self_kept
-    )
-    latent_grad, six_shares = line_sum(
+        latent_near, latent_one, wide_gain(1)[None], wide_in, wide_out, *self_kept
+    )
+    latent_near, latent_grad, six_shares = line_sum(
         latent_part, latent_grad, 7, [up_last, down_grad, self_first]
     )
-    write_share = jnp.concatenate([key_share, five_shares[0], query_share, five_shares[1]], 0)
-    write_columns = jnp.concatenate(jnp.split(write_share, count_mp, 1), 0)
     read_wide, read_narrow, latent_total, gain_read, gain_side, side_embed = read_backward(
-        *read_args, *read_kept, latent_grad, lead.reshape(1, 1)
-    )
-    embed_grad = side_embed[:PIX] + own_embed
-    gains_grad = jnp.concatenate(
+        *read_args, *read_kept, latent_near, lead.reshape(1, 1)
+    )
+    *gradients, stats = closing(
+        [self_last, read_wide, read_narrow],
         [
-            gain_read.reshape(2, -1),
-            gain_self.reshape(2, -1),
-            gain_feed.reshape(2, -1),
-            gain_write.reshape(2, -1),
+            latent_total,
+            gain_read,
+            gain_self,
+            gain_feed,
+            gain_write,
             gain_side,
-            gain_outer[None],
-            gain_final[None],
+            gain_pair,
+            side_embed,
+            own_embed,
+            head_grad,
         ],
-        0,
-    )
-
-    def dp_pieces(values):
-        values = values.reshape(values.shape[0], count_dp, -1)
-        return jnp.swapaxes(values, 0, 1)
-
-    low_rows = [gains_grad, embed_grad, head_grad]
-    low_rows = [jnp.pad(item, ((0, 16 - item.shape[0]), (0, 0))) for item in low_rows]
-    rest = dp_pieces(jnp.concatenate(low_rows, 0))
-    rest = jnp.pad(rest, ((0, 0), (0, 0), (0, 128 - rest.shape[2])))
-    latents_item = dp_pieces(latent_total)
-
-    *gradients, rest_grad, stats = closing(
-        [
-            self_last,
-            read_wide,
-            read_narrow,
-            latents_item.reshape(-1, latents_item.shape[2]),
-            rest.reshape(-1, rest.shape[2]),
-        ],
-        write_columns,
-        jnp.full((8, 128), loss_local),
+        [loss_tile, weight_tile],
         [six_shares[2], five_shares[2], six_shares[0], six_shares[1]],
+        [key_share, five_shares[0], query_share, five_shares[1]],
         8,
     )
     states = (
@@ -2301,18 +2379,14 @@
         master_gains,
         first_gains,
         second_gains,
-    )
-    results = update_states(stats, [*gradients, rest_grad], states)
+        *(jnp.swapaxes(item, 0, 1) for item in (master_pixels, first_pixels, second_pixels)),
+    )
+    results = update_states(stats, gradients, states)
     results = [
-        jnp.swapaxes(item, 0, 1) if index < 6 or 9 <= index < 12 else item
+        jnp.swapaxes(item, 0, 1) if index < 6 or 9 <= index < 12 or index >= 18 else item
         for index, item in enumerate(results)
     ]
-    lanes = master_pixels.shape[2]
-    pixels_grad = jnp.stack([rest_grad[16 : 16 + PIX, :lanes], rest_grad[32 : 32 + PIX, :lanes]])
-    results += adam_update(
-        master_pixels, first_pixels, second_pixels, pixels_grad, clip_scale(stats[0, 0])
-    )
-    return (stats[0, 1] / weight_total, stats[0, 0], *results)
+    return (stats[0, 1], stats[0, 0], *results)
 
 
 def solution(mesh):

time: 584 us -> 548 us (0.938)
  local copies, waits for them, and re-layouts: 29.6 us -> 16.6 us
  Pallas kernels: 499 us -> 488 us
  other arithmetic: 10.7 us -> 2.64 us
    pallas_call x13, Pallas kernels: 464 us -> 453 us  [the longest x8 396 us: staged(): pl.pallas_call(partial(staged_kernel, body, counts), out_shape=[pltpu.VME...]
  transfers between devices with their start and end apart: 2 -> 2, of which waited for: 1 -> 1; matrix products, arithmetic and copies ran while one was open for 3% -> 2% of each run, Pallas kernels for 14% -> 15%
where the time goes in v6:
time: 548 us; the launch traced here: 541 us
  Pallas kernels  488 us (89%)
  waiting for transfers between devices  18.7 us (3%)
  local copies, waits for them, and re-layouts  16.6 us (3%)
  between operations  14.8 us (3%)
    pallas_call x8, Pallas kernels, staged(): pl.pallas_call(partial(staged_kernel, body, counts), out_shape=[pltpu.VME...  396 us
    pallas_call x1, Pallas kernels, read_backward(): pl.pallas_call(read_backward_kernel, grid=(images,), out_shape=[pltpu.HBM...  26.2 us
    all_gather x1, waiting for transfers between devices, body(): lax.all_gather(jnp.concatenate([key_piece, value_piece, query_piece, out_...  18.7 us
    pallas_call x1, Pallas kernels, read_forward(): pl.pallas_call(read_forward_kernel, grid=(images,), out_shape=[pltpu.VMEM...  15.6 us
    pallas_call x1, Pallas kernels, feed_backward(): pl.pallas_call(feed_backward_kernel, grid=(4,), out_shape=[pltpu.VMEM((ro...  12.9 us
    pallas_call x1, Pallas kernels, self_backward(): pl.pallas_call(self_backward_kernel, grid=(images,), out_shape=[pltpu.VME...  12.7 us
  transfers between devices with their start and end apart: 2, of which 1 were waited for; matrix products, arithmetic and copies ran while one was open for 2% of the time, Pallas kernels for 15%

profile of v6, /device:TPU:0, one launch (start us, length us, event | category | flops | bytes accessed | tf_op | source)
XLA Modules:
  0.0 541.2 jit_solution(1023824684138611121)
XLA Ops:
  7.2 0.0 copy-start
  7.2 0.0 all-gather.5.cloned.1.call-start
  7.3 0.9 copy-done
  8.2 0.1 dynamic-slice_bitcast_fusion.1
  8.3 0.1 copy.67
  8.4 1.0 slice.40
  9.3 1.3 fusion.2
  10.6 0.0 copy-start.3
  10.7 0.8 maximum_convert_fusion
  11.5 0.0 all-gather.5.cloned.1.call-update
  11.5 0.0 all-gather.7.cloned.1.call-start
  11.5 0.6 slice.51.gain_ref
  12.2 0.6 copy.74
  12.8 2.0 copy.71.keep_ref
  14.8 0.1 convert_reduce_fusion
  14.9 0.7 multiply_reduce_fusion
  15.6 0.2 fusion.3
  15.8 0.7 pad.11.noisy_ref
  16.6 0.6 slice_bitcast_fusion.pixels_ref
  17.2 15.6 %shard_map.488 = (f32[512,1024]{1,0:T(8,128)S(1)}, bf16[4,2,1024,256]{3,2,1,0:T(8,128)(2,1)}, bf16[4,128,256]{2,1,0:T(8,128)(2,1)}, f32[4,1,512]{2,1,0:T(1,128)}, bf16[512,256]{1,0:T(8,128)(2,1)}) custom-call(f32[4,16,1024]{2,1,0:T(8,128)} %pad.11.noisy_ref, f32[4,1024,1]{2,1,0:T(8,128)} %copy.71.keep_ref, f32[1024,512]{1,0:T(8,128)} %constant.53.clone.place_ref.refs_6_, ...), custom_call_target="tpu_custom_call" | custom-call | flops 10000000000 | bytes 30000000 | tf_op jit(solution)/shard_map/pallas_call | solution.py:1095
  32.8 18.7 %all-gather.5.cloned.1.call-done = f32[1536,256]{1,0:T(8,128)} async-done(((f32[384,256]{1,0:T(8,128)}), f32[1536,256]{1,0:T(8,128)}) %all-gather.5.cloned.1.call-update) | async-done | bytes 1572880 | tf_op jit(solution)/shard_map/all_gather | solution.py:2215
  51.5 0.0 all-gather.7.cloned.1.call-update
  51.5 0.6 slice.55.refs_9_
  52.1 0.8 convert_element_type.37.refs_1_
  52.9 0.6 pad.12.refs_7_
  53.6 0.6 copy.77
  54.2 0.6 copy.76
  54.8 0.6 copy.75
  55.3 0.6 dynamic_slice.27
  55.9 0.6 constant_dynamic-slice_fusion.refs_5_
  56.5 0.7 fusion.1
  57.2 1.2 broadcast_in_dim.13.refs_2_
  58.4 58.9 %shard_map.489 = (f32[512,1024]{1,0:T(8,128)S(1)}, f32[8,128]{1,0:T(8,128)}, f32[512,1024]{1,0:T(8,128)}) custom-call(f32[512,1024]{1,0:T(8,128)S(1)} %get-tuple-element.115.refs_0_, f32[128,1024]{1,0:T(8,128)} %convert_element_type.37.refs_1_, f32[8,128]{1,0:T(8,128)} %broadcast_in_dim.13.refs_2_), custom_call_target="tpu_custom_call" | custom-call | flops 2097152 | bytes 192500000 | tf_op jit(solution)/shard_map/pallas_call | solution.py:442
  117.3 7.1 %shard_map.490 = (f32[512,1024]{1,0:T(8,128)S(1)}, bf16[4,3,128,256]{3,2,1,0:T(8,128)(2,1)}, bf16[4,128,256]{2,1,0:T(8,128)(2,1)}, f32[4,1,512]{2,1,0:T(1,128)}, bf16[512,1024]{1,0:T(8,128)(2,1)}) custom-call(f32[512,1024]{1,0:T(8,128)S(1)} %get-tuple-element.117.latent_ref, f32[1,1024]{1,0:T(1,128)} %bitcast.107, bf16[10,1024,256]{2,1,0:T(8,128)(2,1)} %bitcast.75, ...), custom_call_target="tpu_custom_call" | custom-call | flops 3000000000 | bytes 12000000 | tf_op jit(solution)/shard_map/pallas_call | solution.py:1318
  124.5 59.8 %shard_map.491 = (f32[512,1024]{1,0:T(8,128)S(1)}, bf16[1024,1024]{1,0:T(8,128)(2,1)}, bf16[1024,1024]{1,0:T(8,128)(2,1)}, bf16[512,1024]{1,0:T(8,128)(2,1)}, bf...) custom-call(f32[512,1024]{1,0:T(8,128)S(1)} %get-tuple-element.118.refs_0_, ...), custom_call_target="tpu_custom_call" | custom-call | flops 2097152 | bytes 192500000 | tf_op jit(solution)/shard_map/pallas_call | solution.py:442
  184.3 9.1 %shard_map.492 = (f32[512,1024]{1,0:T(8,128)S(1)}, bf16[4,512,256]{2,1,0:T(8,128)(2,1)}, f32[4,512,256]{2,1,0:T(8,128)}, bf16[512,1024]{1,0:T(8,128)(2,1)}) custom-call(f32[512,1024]{1,0:T(8,128)S(1)} %get-tuple-element.121.latent_ref, f32[1,1024]{1,0:T(1,128)} %bitcast.114, bf16[10,1024,256]{2,1,0:T(8,128)(2,1)} %bitcast.78, ...), custom_call_target="tpu_custom_call" | custom-call | flops 4000000000 | bytes 14000000 | tf_op jit(solution)/shard_map/pallas_call | solution.py:1468
  193.5 34.7 %shard_map.493.refs_2_ = f32[128,1024]{1,0:T(8,128)} custom-call(f32[512,1024]{1,0:T(8,128)S(1)} %get-tuple-element.122.refs_0_, f32[512,1024]{1,0:T(8,128)} %get-tuple-element.123.refs_1_.latent_ref), custom_call_target="tpu_custom_call" | custom-call | flops 1048576 | bytes 115500000 | tf_op jit(solution)/shard_map/pallas_call | solution.py:442
  228.2 1.2 broadcast_in_dim.11.refs_0_
  229.4 26.3 %shard_map.494 = (f32[128,1024]{1,0:T(8,128)}, f32[1024,1024]{1,0:T(8,128)}, f32[1024,1024]{1,0:T(8,128)}, f32[512,1024]{1,0:T(8,128)}, f32[512,1024]{1,0:T(8,12...) custom-call(f32[8,128]{1,0:T(8,128)} %broadcast_in_dim.11.refs_0_, ...), custom_call_target="tpu_custom_call" | custom-call | flops 15000000512 | bytes 94500000 | tf_op jit(solution)/shard_map/pallas_call | solution.py:442
  255.7 42.4 %shard_map.495 = (f32[512,1024]{1,0:T(8,128)S(1)}, f32[128,1024]{1,0:T(8,128)}, f32[64,1024]{1,0:T(8,128)}, f32[512,1024]{1,0:T(8,128)}) custom-call(f32[128,1024]{1,0:T(8,128)} %get-tuple-element.128.refs_0_, f32[8,128,1024]{2,1,0:T(8,128)} %bitcast.86, f32[8,64,1024]{2,1,0:T(8,128)} %bitcast.87), custom_call_target="tpu_custom_call" | custom-call | flops 131072 | bytes 133000000 | tf_op jit(solution)/shard_map/pallas_call | solution.py:442
  298.2 12.9 %shard_map.496 = (f32[512,1024]{1,0:T(8,128)S(1)}, f32[2,1024,256]{2,1,0:T(8,128)}, f32[2,1024,256]{2,1,0:T(8,128)}, f32[4,1024,256]{2,1,0:T(8,128)}, f32[1,1024]{1,0:T(1,128)}) custom-call(f32[512,1024]{1,0:T(8,128)S(1)} %get-tuple-element.131.grad_ref, f32[512,1024]{1,0:T(8,128)} %get-tuple-element.123.refs_1_.latent_ref, f32[1,1024]{1,0:T(1,128)} %bitcast.115, ...), custom_call_target="tpu_custom_call" | custom-call | flops 8999999488 | bytes 26000000 | tf_op jit(solution)/shard_map/pallas_call | solution.py:1550
  311.1 58.5 %shard_map.497 = (f32[512,1024]{1,0:T(8,128)S(1)}, f32[128,1024]{1,0:T(8,128)}, f32[64,1024]{1,0:T(8,128)}, f32[2,128,256]{2,1,0:T(8,128)}, f32[512,1024]{1,0:T(8,128)}) custom-call(f32[512,1024]{1,0:T(8,128)S(1)} %get-tuple-element.135.refs_0_, f32[512,1024]{1,0:T(8,128)} %get-tuple-element.136.refs_1_, f32[8,128,1024]{2,1,0:T(8,128)} %bitcast.84, ...), custom_call_target="tpu_custom_call" | custom-call | flops 2097152 | bytes 192500000 | tf_op jit(solution)/shard_map/pallas_call | solution.py:442
  369.6 12.7 %shard_map.498 = (f32[512,1024]{1,0:T(8,128)S(1)}, f32[2,1024,256]{2,1,0:T(8,128)}, f32[2,1024,256]{2,1,0:T(8,128)}, f32[1,1024]{1,0:T(1,128)}) custom-call(f32[512,1024]{1,0:T(8,128)S(1)} %get-tuple-element.140.grad_ref, f32[512,1024]{1,0:T(8,128)} %get-tuple-element.119.refs_1_.latent_ref, f32[1,1024]{1,0:T(1,128)} %bitcast.108, ...), custom_call_target="tpu_custom_call" | custom-call | flops 6000000000 | bytes 16000000 | tf_op jit(solution)/shard_map/pallas_call | solution.py:1411
  382.3 60.5 %shard_map.499 = (f32[512,1024]{1,0:T(8,128)S(1)}, f32[2,128,256]{2,1,0:T(8,128)}, f32[4,128,256]{2,1,0:T(8,128)}, f32[2,128,256]{2,1,0:T(8,128)}, f32[512,1024]{1,0:T(8,128)}) custom-call(f32[512,1024]{1,0:T(8,128)S(1)} %get-tuple-element.150.refs_0_, f32[512,1024]{1,0:T(8,128)} %get-tuple-element.151.refs_1_, f32[2,8,128,256]{3,2,1,0:T(8,128)} %bitcast.91, ...), custom_call_target="tpu_custom_call" | custom-call | flops 2097152 | bytes 192500000 | tf_op jit(solution)/shard_map/pallas_call | solution.py:442
  442.8 26.2 %shard_map.500 = (f32[2,1024,256]{2,1,0:T(8,128)}, f32[2,512,256]{2,1,0:T(8,128)}, f32[128,1024]{1,0:T(8,128)}, f32[1,1024]{1,0:T(1,128)}, f32[1,512]{1,0:T(1,128)}, /*index=5*/f32[16,512]{1,0:T(8,128)}) custom-call(f32[4,16,1024]{2,1,0:T(8,128)} %pad.11.noisy_ref, f32[4,1024,1]{2,1,0:T(8,128)} %copy.71.keep_ref, ...), custom_call_target="tpu_custom_call" | custom-call | flops 20000000000 | bytes 30000000 | tf_op jit(solution)/shard_map/pallas_call | solution.py:1247
  469.0 54.6 %shard_map.501 = (f32[10,128,256]{2,1,0:T(8,128)}, f32[3,64,256]{2,1,0:T(8,128)}, f32[6,256,128]{2,1,0:T(8,128)}, f32[64,256]{1,0:T(8,128)}, f32[128,128]{1,0:T(...) custom-call(f32[2,8,128,256]{3,2,1,0:T(8,128)} %bitcast.88, f32[2,8,128,256]{3,2,1,0:T(8,128)} %bitcast.89, ...), custom_call_target="tpu_custom_call" | custom-call | flops 10000000 | bytes 175000000 | tf_op jit(solution)/shard_map/pallas_call | solution.py:442
  523.6 1.3 fusion.5
  524.9 9.0 %shard_map.502 = (f32[10,128,256]{2,1,0:T(8,128)}, f32[10,128,256]{2,1,0:T(8,128)}, f32[10,128,256]{2,1,0:T(8,128)}, f32[3,64,256]{2,1,0:T(8,128)}, f32[3,64,256...) custom-call(f32[8,128]{1,0:T(8,128)} %get-tuple-element.177.refs_0_,, ...), custom_call_target="tpu_custom_call" | custom-call | flops 20000000 | bytes 14000000 | tf_op jit(solution)/shard_map/pallas_call | solution.py:2017
  (23 shorter events, 0.1 us)
Async XLA Ops:
  7.2 1.0 copy-start
  7.2 44.2 %all-gather.5.cloned.1.call-start = ((), (), s32[]{:S(2)}) async-start(), calls=%async_computation | async-start | bytes 1966080 | tf_op jit(solution)/shard_map/all_gather | solution.py:2215
  7.3 4.3 copy-start.6
  8.2 4.0 copy-start.7
  8.2 4.5 copy-start.5
  10.6 4.3 copy-start.8
  10.6 4.9 copy-start.3
  10.6 4.9 copy-start.4
  11.5 113.0 %all-gather.7.cloned.1.call-start = ((), (), s32[]{:S(2)}) async-start(), calls=%async_computation.1 | async-start | bytes 14155776 | tf_op jit(solution)/shard_map/all_gather | solution.py:2254
  17.2 34.9 %copy-start.2 = (bf16[128,1024]{1,0:T(8,128)(2,1)S(1)}, bf16[128,1024]{1,0:T(8,128)(2,1)}, u32[]{:S(2)}) copy-start(bf16[128,1024]{1,0:T(8,128)(2,1)} %latents_ref.3) | copy-start | bytes 786436
  524.9 9.0 %copy-start.1 = (bf16[256,512]{1,0:T(8,128)(2,1)S(1)}, bf16[256,512]{1,0:T(8,128)(2,1)}, u32[]{:S(2)}) copy-start(bf16[256,512]{1,0:T(8,128)(2,1)} %param.40) | copy-start | bytes 786436
Sparse Core Ops, SparseCore 0:
  11.6 39.8 all-gather.4
  53.3 71.0 all-gather.6

commit v7 on v6

--- a/solution.py
+++ b/solution.py
@@ -116,7 +116,7 @@
 MESH_ID = pl.DeviceIdType.MESH
 HBM_SPEC = pl.BlockSpec(memory_space=pltpu.HBM)
 VMEM_SPEC = pl.BlockSpec(memory_space=pltpu.VMEM)
-CHUNKS = 32
+CHUNKS = 64
 VMEM_LIMIT = 56 << 20
 
 
@@ -330,7 +330,7 @@
         self.count_mp, self.blocks, self.outs = count_mp, blocks, outs
         self.buffer, self.sems = buffer, sems
         self.number = blocks.shape[0]
-        self.each = -(-self.number // steps)
+        self.each, self.stride = max(1, self.number // steps), max(1, steps // self.number)
 
     @staticmethod
     def scratch(block):
@@ -364,8 +364,10 @@
             low += rows
 
     def step(self, index):
-        for entry in range(self.each):
-            self.one(index * self.each + entry)
+        @pl.when(lax.rem(index, self.stride) == 0)
+        def _():
+            for entry in range(self.each):
+                self.one(index // self.stride * self.each + entry)
 
 
 def signal_all(barrier, others):
@@ -1045,8 +1047,11 @@
     part_ref,
     pairs_ref,
     output_ref,
-    total_ref,
     queries_ref,
+    normed_ref,
+    scale_ref,
+    side_ref,
+    probs_ref,
 ):
     heads = query_weight_ref.shape[2] // HEAD_DIM
 
@@ -1057,8 +1062,11 @@
         queries = dot(low, query_weight_ref[0]).astype(jnp.bfloat16)
         queries_ref[...] = spread_heads(queries * jnp.bfloat16(HEAD_DIM ** (-0.5)))
 
-    normed, _ = norm_rows(embed(noisy_ref[0], pixels_ref[...], place_ref[...]))
+    normed, scale = norm_rows(embed(noisy_ref[0], pixels_ref[...], place_ref[...]))
+    normed_ref[0] = normed
+    scale_ref[0] = scale
     side = (normed * gain_ref[...]).astype(jnp.bfloat16)
+    side_ref[0] = side.T
     keys = dot(side, pair_weight_ref[0]).astype(jnp.bfloat16)
     values = dot(side, pair_weight_ref[1]).astype(jnp.bfloat16)
     pairs_ref[0, 0] = keys
@@ -1067,10 +1075,10 @@
     scores = jnp.where(keep_ref[0] > 0, scores, -1e30)
     top = jnp.max(scores, 0, keepdims=True)
     grown = jnp.exp(scores - top)
-    summed = jnp.sum(grown, 0, keepdims=True)
-    total_ref[0] = top + jnp.log(summed)
-    probs = (grown / summed).astype(jnp.bfloat16)
-    output = join_heads(dot(probs, values, 0, 0), heads).astype(jnp.bfloat16)
+    probs = grown / jnp.sum(grown, 0, keepdims=True)
+    probs_ref[0] = probs
+    output = join_heads(dot(probs.astype(jnp.bfloat16), values, 0, 0), heads)
+    output = output.astype(jnp.bfloat16)
     output_ref[0] = output
     part_ref[...] = dot(output, out_weight_ref[0])
 
@@ -1099,8 +1107,11 @@
             pltpu.VMEM((images * count, d_lat), jnp.float32),
             pltpu.HBM((images, 2, patches, local), jnp.bfloat16),
             pltpu.HBM((images, count, local), jnp.bfloat16),
-            pltpu.HBM((images, 1, stacked), jnp.float32),
             pltpu.HBM((stacked, local), jnp.bfloat16),
+            pltpu.HBM((images, patches, d_if), jnp.float32),
+            pltpu.HBM((images, patches, 1), jnp.float32),
+            pltpu.HBM((images, d_if, patches), jnp.bfloat16),
+            pltpu.HBM((images, patches, stacked), jnp.float32),
         ],
         in_specs=[
             each(noisy.shape[1:]),
@@ -1118,10 +1129,13 @@
             pl.BlockSpec((count, d_lat), lambda b: (b, 0)),
             each((2, patches, local)),
             each((count, local)),
-            each((1, stacked)),
             whole((stacked, local)),
+            each((patches, d_if)),
+            each((patches, 1)),
+            each((d_if, patches)),
+            each((patches, stacked)),
         ],
-        compiler_params=pltpu.CompilerParams(vmem_limit_bytes=40 << 20),
+        compiler_params=pltpu.CompilerParams(vmem_limit_bytes=52 << 20),
         cost_estimate=pl.CostEstimate(
             flops=10**10, bytes_accessed=30 * 10**6, transcendentals=2 * 10**6
         ),
@@ -1130,9 +1144,6 @@
 
 def read_backward_kernel(
     noisy_ref,
-    keep_ref,
-    place_ref,
-    pixels_ref,
     latents_ref,
     wide_gain_ref,
     gain_ref,
@@ -1141,8 +1152,11 @@
     out_weight_ref,
     pairs_ref,
     output_ref,
-    total_ref,
     queries_ref,
+    normed_ref,
+    scale_ref,
+    side_ref,
+    probs_ref,
     grad_ref,
     lead_ref,
     wide_grad_ref,
@@ -1171,16 +1185,12 @@
         ):
             ref[...] = jnp.zeros_like(ref)
 
-    normed, scale = norm_rows(embed(noisy_ref[0], pixels_ref[...], place_ref[...]))
-    side = (normed * gain_ref[...]).astype(jnp.bfloat16)
+    normed, scale, side, probs = normed_ref[0], scale_ref[0], side_ref[0], probs_ref[0]
     keys, values, queries = pairs_ref[0, 0], pairs_ref[0, 1], queries_ref[...]
     branch = grad_ref[...].astype(jnp.bfloat16)
     latents_grad_ref[...] += lead_ref[...] * grad_ref[...]
     wide_grad_ref[1] += dot(branch, output_ref[0], 0, 0)
     upstream = spread_heads(dot(branch, out_weight_ref[0], 1, 1).astype(jnp.bfloat16))
-    scores = dot(keys, queries, 1, 1)
-    scores = jnp.where(keep_ref[0] > 0, scores, -1e30)
-    probs = jnp.exp(scores - total_ref[0])
     value_grad = dot(probs.astype(jnp.bfloat16), upstream).astype(jnp.bfloat16)
     prob_grad = dot(values, upstream, 1, 1)
     inner = jnp.sum(prob_grad * probs, 0, keepdims=True)
@@ -1190,8 +1200,8 @@
     query_grad = query_grad.astype(jnp.bfloat16)
     wide_grad_ref[0] += dot(low_ref[...], query_grad, 0, 0)
     returned_ref[...] += dot(query_grad, query_weight_ref[0], 1, 1)
-    narrow_grad_ref[0] += dot(side, key_grad, 0, 0)
-    narrow_grad_ref[1] += dot(side, value_grad, 0, 0)
+    narrow_grad_ref[0] += dot(side, key_grad)
+    narrow_grad_ref[1] += dot(side, value_grad)
     side_grad = dot(key_grad, pair_weight_ref[0], 1, 1) + dot(value_grad, pair_weight_ref[1], 1, 1)
     gain_grad_ref[...] += jnp.sum(side_grad * normed, 0, keepdims=True)
     back = norm_rows_back(side_grad, gain_ref[...], normed, scale)
@@ -1216,9 +1226,6 @@
 
 def read_backward(
     noisy,
-    keep,
-    place,
-    pixels,
     latents,
     wide_gain,
     gain,
@@ -1227,8 +1234,11 @@
     wideout,
     pairs,
     output,
-    total,
     queries,
+    normed,
+    scale,
+    side,
+    probs,
     grad,
     lead,
 ):
@@ -1250,9 +1260,6 @@
         out_shape=[pltpu.HBM(shape, jnp.float32) for shape in results],
         in_specs=[
             each(noisy.shape[1:]),
-            each((patches, 1)),
-            whole((patches, d_if)),
-            whole(pixels.shape),
             whole(latents.shape),
             whole((1, d_lat)),
             whole((1, d_if)),
@@ -1261,8 +1268,11 @@
             slot_of((1, local, d_lat), 0),
             each((2, patches, local)),
             each((count, local)),
-            each((1, stacked)),
             whole((stacked, local)),
+            each((patches, d_if)),
+            each((patches, 1)),
+            each((d_if, patches)),
+            each((patches, stacked)),
             pl.BlockSpec((count, d_lat), lambda b: (b, 0)),
             whole((1, 1)),
         ],
@@ -1271,11 +1281,11 @@
             pltpu.VMEM((count, d_lat), jnp.bfloat16),
             pltpu.VMEM((count, d_lat), jnp.float32),
         ],
-        compiler_params=pltpu.CompilerParams(vmem_limit_bytes=48 << 20),
+        compiler_params=pltpu.CompilerParams(vmem_limit_bytes=52 << 20),
         cost_estimate=pl.CostEstimate(
             flops=2 * 10**10, bytes_accessed=30 * 10**6, transcendentals=2 * 10**6
         ),
-    )(in_hbm(noisy), in_hbm(keep), in_hbm(place), in_hbm(pixels), in_hbm(latents), in_hbm(wide_gain), in_hbm(gain), in_hbm(wide), in_hbm(narrow), in_hbm(wideout), in_hbm(pairs), in_hbm(output), in_hbm(total), in_hbm(queries), in_vmem(grad), in_hbm(lead))
+    )(*map(in_hbm, (noisy, latents, wide_gain, gain, wide, narrow, wideout, pairs, output, queries, normed, scale, side, probs)), in_vmem(grad), in_hbm(lead))
 
 
 def rows_of(rows, width):
@@ -1782,10 +1792,11 @@
     done = views(pull(finished, given), 2)
     wide_out, narrow_out, turned_out, last_out, latents_out, rest_out, stats = results
     latents_item, rest_item, columns, column_sems = pull(4)
-    items += [latents_item, rest_item]
     number = len(items)
-    shares = pull(number)
-    sums = PieceSums(count_dp, items, shares, pull(number * (count_dp.bit_length() + 1)))
+    shares = pull(number + 2)
+    each = count_dp.bit_length() + 1
+    sums = PieceSums(count_dp, items, shares[:number], pull(number * each))
+    tiny = PieceSums(count_dp, [latents_item, rest_item], shares[number:], pull(2 * each))
     (write_share,) = pull(1)
     scatter = LineScatter(count, columns, write_share, pull(4), pull(4))
     small = [Spread("mp", count, *pull(3)) for _ in range(2)]
@@ -1829,15 +1840,24 @@
             ]
     pl.semaphore_wait(barrier, len(others))
 
+    tiny.begin()
     sums.begin()
     for load in column_loads:
         load.wait()
-    scatter.run(lambda: sums.advance(1))
-    for phase in range(2, sums.bits + 1):
-        sums.advance(phase)
+    tiny.advance(1)
+
+    def between():
+        sums.advance(1)
+        tiny.advance(2)
+
+    scatter.run(between)
+    for phase in range(3, tiny.bits + 1):
+        tiny.advance(phase)
     for spread, share in zip(small, shares[-2:]):
         spread.held[spread.place] = share[...]
         spread.start()
+    for phase in range(2, sums.bits + 1):
+        sums.advance(phase)
     scatter.settle()
 
     self_in_2, self_out, read_query, read_out, read_key, read_value = shares[:6]
@@ -1883,6 +1903,7 @@
         value = spread.total()
     stats[...] = jnp.where(lane == 0, jnp.sqrt(value), value / weight_tile[...])
     sums.finish()
+    tiny.finish()
     scatter.finish()
     for spread in small + [over_dp, over_mp]:
         spread.finish()
@@ -2250,20 +2271,8 @@
         wide_out,
     )
     read_part, *read_kept = read_forward(*read_args)
-    gathered, read_part = lax.optimization_barrier((gathered, read_part))
-    gathered = lax.all_gather(gathered, "dp").reshape(count_dp * count_mp, -1, local)
-    latent_near, latent_one, (weight_tile,) = line_sum(
-        read_part, copy_latents.astype(jnp.float32), 2, tile=jnp.full((8, 128), weight_here)
-    )
-    self_part, *self_kept = self_forward(
-        latent_near, wide_gain(1)[None], wide_in, wide_out, images
-    )
-    latent_near, latent_two, write_weights = line_sum(
-        self_part, latent_one, 3, blocks=(gathered, [d_lat, d_lat, d_if, d_if])
-    )
-    feed_part, *feed_kept = feed_forward(latent_near, wide_gain(2)[None], wide_in, wide_out)
-    latent_three = line_scatter(feed_part, latent_two, 4)
-    latent_three = latent_three.reshape(own_images, own_latents, d_lat)
+    wide_gains = [wide_gain(index)[None] for index in range(1, 4)]
+    latent_base = copy_latents.astype(jnp.float32)
 
     def own_tokens(values, axis):
         values = lax.dynamic_slice_in_dim(values, first_image, own_images, 0)
@@ -2271,6 +2280,29 @@
 
     own_weight = lax.dynamic_slice_in_dim(loss_weight, first_image, own_images, 0)
     own_scalar = jnp.broadcast_to(own_weight[0], (8, 128))
+    own_pieces = [
+        own_tokens(noisy_rows, 2),
+        own_tokens(noise_rows, 2),
+        own_tokens(keep_float, 1),
+    ]
+    side_gains = gain_rows[8:11]
+    here_tile, lead = jnp.full((8, 128), weight_here), lead.reshape(1, 1)
+    ready = (own_pieces, own_scalar, wide_gains, side_gains, latent_base, here_tile, lead, pixel_rows)
+    gathered, read_part, ready = lax.optimization_barrier((gathered, read_part, ready))
+    own_pieces, own_scalar, wide_gains, side_gains, latent_base, here_tile, lead, pixel_rows = ready
+    gathered = lax.all_gather(gathered, "dp").reshape(count_dp * count_mp, -1, local)
+    latent_near, latent_one, (weight_tile,) = line_sum(
+        read_part, latent_base, 2, tile=here_tile
+    )
+    self_part, *self_kept = self_forward(
+        latent_near, wide_gains[0], wide_in, wide_out, images
+    )
+    latent_near, latent_two, write_weights = line_sum(
+        self_part, latent_one, 3, blocks=(gathered, [d_lat, d_lat, d_if, d_if])
+    )
+    feed_part, *feed_kept = feed_forward(latent_near, wide_gains[1], wide_in, wide_out)
+    latent_three = line_scatter(feed_part, latent_two, 4)
+    latent_three = latent_three.reshape(own_images, own_latents, d_lat)
     if sharers == 1 and own_images == 1:
         (
             own_grad,
@@ -2287,13 +2319,13 @@
             own_scalar,
             weight_tile,
             latent_three[0],
-            own_tokens(noisy_rows, 2)[0],
-            own_tokens(noise_rows, 2)[0],
-            own_tokens(keep_float, 1),
+            own_pieces[0][0],
+            own_pieces[1][0],
+            own_pieces[2],
             place,
             pixel_rows,
-            wide_gain(3)[None],
-            gain_rows[8:11],
+            wide_gains[2],
+            side_gains,
             write_weights,
         )
     else:
@@ -2333,19 +2365,19 @@
         own_grad.reshape(-1, d_lat), 5, [write_key_grad, write_query_grad]
     )
     latent_part, up_first, up_last, down_grad, gain_feed = feed_backward(
-        latent_near, latent_two, wide_gain(2)[None], wide_in, wide_out, *feed_kept
+        latent_near, latent_two, wide_gains[1], wide_in, wide_out, *feed_kept
     )
     latent_near, latent_grad, five_shares = line_sum(
         latent_part, latent_grad, 6, [write_value_grad, narrowout_grad, up_first]
     )
     latent_part, self_first, self_last, gain_self = self_backward(
-        latent_near, latent_one, wide_gain(1)[None], wide_in, wide_out, *self_kept
+        latent_near, latent_one, wide_gains[0], wide_in, wide_out, *self_kept
     )
     latent_near, latent_grad, six_shares = line_sum(
         latent_part, latent_grad, 7, [up_last, down_grad, self_first]
     )
     read_wide, read_narrow, latent_total, gain_read, gain_side, side_embed = read_backward(
-        *read_args, *read_kept, latent_near, lead.reshape(1, 1)
+        read_args[0], *read_args[4:], *read_kept, latent_near, lead
     )
     *gradients, stats = closing(
         [self_last, read_wide, read_narrow],

time: 548 us -> 608 us (1.11)
  Pallas kernels: 488 us -> 557 us
  waiting for transfers between devices: 18.7 us -> 9.41 us
    pallas_call x8, Pallas kernels: 396 us -> 462 us  [staged(): pl.pallas_call(partial(staged_kernel, body, counts), out_shape=[pltpu.VME...]
    all_gather x1, waiting for transfers between devices: 18.7 us -> 9.37 us  [body(): lax.all_gather(jnp.concatenate([key_piece, value_piece, query_piece, out_...]
  transfers between devices with their start and end apart: 2 -> 2, of which waited for: 1 -> 1; matrix products, arithmetic and copies ran while one was open for 2% -> 2% of each run, Pallas kernels for 15% -> 18%
where the time goes in v7:
time: 608 us; the launch traced here: 601 us
  Pallas kernels  557 us (92%)
  local copies, waits for them, and re-layouts  16.6 us (3%)
  between operations  14.8 us (2%)
  waiting for transfers between devices  9.41 us (2%)
    pallas_call x8, Pallas kernels, staged(): pl.pallas_call(partial(staged_kernel, body, counts), out_shape=[pltpu.VME...  462 us
    pallas_call x1, Pallas kernels, read_backward(): pl.pallas_call(read_backward_kernel, grid=(images,), out_shape=[pltpu.HBM...  25.6 us
    pallas_call x1, Pallas kernels, read_forward(): pl.pallas_call(read_forward_kernel, grid=(images,), out_shape=[pltpu.VMEM...  19.2 us
    pallas_call x1, Pallas kernels, feed_backward(): pl.pallas_call(feed_backward_kernel, grid=(4,), out_shape=[pltpu.VMEM((ro...  12.8 us
    pallas_call x1, Pallas kernels, self_backward(): pl.pallas_call(self_backward_kernel, grid=(images,), out_shape=[pltpu.VME...  12.7 us
  transfers between devices with their start and end apart: 2, of which 1 were waited for; matrix products, arithmetic and copies ran while one was open for 2% of the time, Pallas kernels for 18%

profile of v7, /device:TPU:0, one launch (start us, length us, event | category | flops | bytes accessed | tf_op | source)
XLA Modules:
  0.0 600.9 jit_solution(11215961257942158552)
XLA Ops:
  7.2 0.0 copy-start
  7.2 0.0 all-gather.5.cloned.1.call-start
  7.3 0.9 copy-done
  8.2 0.1 dynamic-slice_bitcast_fusion
  8.3 0.1 copy.62
  8.4 1.0 slice.38
  9.4 1.3 fusion.1
  10.7 0.0 copy-start.3
  10.8 0.8 maximum_convert_fusion
  11.5 0.0 all-gather.5.cloned.1.call-update
  11.6 0.0 all-gather.7.cloned.1.call-start
  11.6 0.6 slice.49.gain_ref
  12.2 0.6 slice.53.refs_9_
  12.9 0.6 copy.71
  13.5 0.6 copy.70
  14.1 0.6 copy.69
  14.6 0.6 copy.68
  15.2 0.8 convert_element_type.37.refs_1_
  16.1 2.0 copy.66.keep_ref
  18.1 0.1 convert_reduce_fusion
  18.2 0.6 multiply_reduce_fusion
  18.9 0.6 dynamic_slice.34
  19.5 0.6 pad.12.refs_7_
  20.1 0.2 fusion.2
  20.3 0.7 pad.11.noisy_ref
  21.1 0.6 constant_dynamic-slice_fusion.refs_5_
  21.7 0.6 slice_bitcast_fusion.pixels_ref
  22.3 0.7 pad_dynamic-slice_fusion
  22.9 19.2 %shard_map.488 = (f32[512,1024]{1,0:T(8,128)S(1)}, bf16[4,2,1024,256]{3,2,1,0:T(8,128)(2,1)}, bf16[4,128,256]{2,1,0:T(8,128)(2,1)}, bf16[512,256]{1,0:T(8,128)(2...) custom-call(f32[4,16,1024]{2,1,0:T(8,128)} %pad.11.noisy_ref, ...), custom_call_target="tpu_custom_call" | custom-call | flops 10000000000 | bytes 30000000 | tf_op jit(solution)/shard_map/pallas_call | solution.py:1103
  42.1 9.4 %all-gather.5.cloned.1.call-done = f32[1536,256]{1,0:T(8,128)} async-done(((f32[384,256]{1,0:T(8,128)}), f32[1536,256]{1,0:T(8,128)}) %all-gather.5.cloned.1.call-update) | async-done | bytes 1572880 | tf_op jit(solution)/shard_map/all_gather | solution.py:2236
  51.5 1.2 broadcast_in_dim.12.refs_0_
  52.7 1.2 broadcast_in_dim.13.refs_2_
  54.0 0.0 all-gather.7.cloned.1.call-update
  54.0 79.8 %shard_map.489 = (f32[512,1024]{1,0:T(8,128)S(1)}, f32[8,128]{1,0:T(8,128)}, f32[512,1024]{1,0:T(8,128)}) custom-call(f32[512,1024]{1,0:T(8,128)S(1)} %get-tuple-element.131.refs_0_, f32[128,1024]{1,0:T(8,128)} %convert_element_type.37.refs_1_, f32[8,128]{1,0:T(8,128)} %broadcast_in_dim.13.refs_2_), custom_call_target="tpu_custom_call" | custom-call | flops 2097152 | bytes 192500000 | tf_op jit(solution)/shard_map/pallas_call | solution.py:444
  133.8 7.1 %shard_map.490 = (f32[512,1024]{1,0:T(8,128)S(1)}, bf16[4,3,128,256]{3,2,1,0:T(8,128)(2,1)}, bf16[4,128,256]{2,1,0:T(8,128)(2,1)}, f32[4,1,512]{2,1,0:T(1,128)}, bf16[512,1024]{1,0:T(8,128)(2,1)}) custom-call(f32[512,1024]{1,0:T(8,128)S(1)} %get-tuple-element.135.latent_ref, f32[1,1024]{1,0:T(1,128)} %bitcast.107, bf16[10,1024,256]{2,1,0:T(8,128)(2,1)} %bitcast.73, ...), custom_call_target="tpu_custom_call" | custom-call | flops 3000000000 | bytes 12000000 | tf_op jit(solution)/shard_map/pallas_call | solution.py:1328
  140.9 79.8 %shard_map.491 = (f32[512,1024]{1,0:T(8,128)S(1)}, bf16[1024,1024]{1,0:T(8,128)(2,1)}, bf16[1024,1024]{1,0:T(8,128)(2,1)}, bf16[512,1024]{1,0:T(8,128)(2,1)}, bf...) custom-call(f32[512,1024]{1,0:T(8,128)S(1)} %get-tuple-element.137.refs_0_, ...), custom_call_target="tpu_custom_call" | custom-call | flops 2097152 | bytes 192500000 | tf_op jit(solution)/shard_map/pallas_call | solution.py:444
  220.7 9.1 %shard_map.492 = (f32[512,1024]{1,0:T(8,128)S(1)}, bf16[4,512,256]{2,1,0:T(8,128)(2,1)}, f32[4,512,256]{2,1,0:T(8,128)}, bf16[512,1024]{1,0:T(8,128)(2,1)}) custom-call(f32[512,1024]{1,0:T(8,128)S(1)} %get-tuple-element.140.latent_ref, f32[1,1024]{1,0:T(1,128)} %bitcast.114, bf16[10,1024,256]{2,1,0:T(8,128)(2,1)} %bitcast.76, ...), custom_call_target="tpu_custom_call" | custom-call | flops 4000000000 | bytes 14000000 | tf_op jit(solution)/shard_map/pallas_call | solution.py:1478
  229.9 20.1 %shard_map.493.refs_2_ = f32[128,1024]{1,0:T(8,128)} custom-call(f32[512,1024]{1,0:T(8,128)S(1)} %get-tuple-element.142.refs_0_, f32[512,1024]{1,0:T(8,128)} %get-tuple-element.143.refs_1_.latent_ref), custom_call_target="tpu_custom_call" | custom-call | flops 1048576 | bytes 115500000 | tf_op jit(solution)/shard_map/pallas_call | solution.py:444
  249.9 26.3 %shard_map.494 = (f32[128,1024]{1,0:T(8,128)}, f32[1024,1024]{1,0:T(8,128)}, f32[1024,1024]{1,0:T(8,128)}, f32[512,1024]{1,0:T(8,128)}, f32[512,1024]{1,0:T(8,12...) custom-call(f32[8,128]{1,0:T(8,128)} %broadcast_in_dim.12.refs_0_, ...), custom_call_target="tpu_custom_call" | custom-call | flops 15000000512 | bytes 94500000 | tf_op jit(solution)/shard_map/pallas_call | solution.py:444
  276.3 42.1 %shard_map.495 = (f32[512,1024]{1,0:T(8,128)S(1)}, f32[128,1024]{1,0:T(8,128)}, f32[64,1024]{1,0:T(8,128)}, f32[512,1024]{1,0:T(8,128)}) custom-call(f32[128,1024]{1,0:T(8,128)} %get-tuple-element.154.refs_0_, f32[8,128,1024]{2,1,0:T(8,128)} %bitcast.84, f32[8,64,1024]{2,1,0:T(8,128)} %bitcast.85), custom_call_target="tpu_custom_call" | custom-call | flops 131072 | bytes 133000000 | tf_op jit(solution)/shard_map/pallas_call | solution.py:444
  318.3 12.8 %shard_map.496 = (f32[512,1024]{1,0:T(8,128)S(1)}, f32[2,1024,256]{2,1,0:T(8,128)}, f32[2,1024,256]{2,1,0:T(8,128)}, f32[4,1024,256]{2,1,0:T(8,128)}, f32[1,1024]{1,0:T(1,128)}) custom-call(f32[512,1024]{1,0:T(8,128)S(1)} %get-tuple-element.157.grad_ref, f32[512,1024]{1,0:T(8,128)} %get-tuple-element.143.refs_1_.latent_ref, f32[1,1024]{1,0:T(1,128)} %bitcast.115, ...), custom_call_target="tpu_custom_call" | custom-call | flops 8999999488 | bytes 26000000 | tf_op jit(solution)/shard_map/pallas_call | solution.py:1560
  331.1 79.7 %shard_map.497 = (f32[512,1024]{1,0:T(8,128)S(1)}, f32[128,1024]{1,0:T(8,128)}, f32[64,1024]{1,0:T(8,128)}, f32[2,128,256]{2,1,0:T(8,128)}, f32[512,1024]{1,0:T(8,128)}) custom-call(f32[512,1024]{1,0:T(8,128)S(1)} %get-tuple-element.161.refs_0_, f32[512,1024]{1,0:T(8,128)} %get-tuple-element.162.refs_1_, f32[8,128,1024]{2,1,0:T(8,128)} %bitcast.82, ...), custom_call_target="tpu_custom_call" | custom-call | flops 2097152 | bytes 192500000 | tf_op jit(solution)/shard_map/pallas_call | solution.py:444
  410.9 12.7 %shard_map.498 = (f32[512,1024]{1,0:T(8,128)S(1)}, f32[2,1024,256]{2,1,0:T(8,128)}, f32[2,1024,256]{2,1,0:T(8,128)}, f32[1,1024]{1,0:T(1,128)}) custom-call(f32[512,1024]{1,0:T(8,128)S(1)} %get-tuple-element.166.grad_ref, f32[512,1024]{1,0:T(8,128)} %get-tuple-element.138.refs_1_.latent_ref, f32[1,1024]{1,0:T(1,128)} %bitcast.108, ...), custom_call_target="tpu_custom_call" | custom-call | flops 6000000000 | bytes 16000000 | tf_op jit(solution)/shard_map/pallas_call | solution.py:1421
  423.5 81.3 %shard_map.499 = (f32[512,1024]{1,0:T(8,128)S(1)}, f32[2,128,256]{2,1,0:T(8,128)}, f32[4,128,256]{2,1,0:T(8,128)}, f32[2,128,256]{2,1,0:T(8,128)}, f32[512,1024]{1,0:T(8,128)}) custom-call(f32[512,1024]{1,0:T(8,128)S(1)} %get-tuple-element.179.refs_0_, f32[512,1024]{1,0:T(8,128)} %get-tuple-element.180.refs_1_, f32[2,8,128,256]{3,2,1,0:T(8,128)} %bitcast.89, ...), custom_call_target="tpu_custom_call" | custom-call | flops 2097152 | bytes 192500000 | tf_op jit(solution)/shard_map/pallas_call | solution.py:444
  504.8 25.6 %shard_map.500 = (f32[2,1024,256]{2,1,0:T(8,128)}, f32[2,512,256]{2,1,0:T(8,128)}, f32[128,1024]{1,0:T(8,128)}, f32[1,1024]{1,0:T(1,128)}, f32[1,512]{1,0:T(1,128)}, /*index=5*/f32[16,512]{1,0:T(8,128)}) custom-call(f32[4,16,1024]{2,1,0:T(8,128)} %pad.11.noisy_ref, bf16[128,1024]{1,0:T(8,128)(2,1)} %latents_ref.3, f32[1,1024]{1,0:T(1,128)} %bitcast.113, ...), custom_call_target="tpu_custom_call" | custom-call | flops 20000000000 | bytes 30000000 | tf_op jit(solution)/shard_map/pallas_call | solution.py:1257
  530.4 52.9 %shard_map.501 = (f32[10,128,256]{2,1,0:T(8,128)}, f32[3,64,256]{2,1,0:T(8,128)}, f32[6,256,128]{2,1,0:T(8,128)}, f32[64,256]{1,0:T(8,128)}, f32[128,128]{1,0:T(...) custom-call(f32[2,8,128,256]{3,2,1,0:T(8,128)} %bitcast.86, f32[2,8,128,256]{3,2,1,0:T(8,128)} %bitcast.87, ...), custom_call_target="tpu_custom_call" | custom-call | flops 10000000 | bytes 175000000 | tf_op jit(solution)/shard_map/pallas_call | solution.py:444
  583.3 1.3 fusion.4
  584.6 9.0 %shard_map.502 = (f32[10,128,256]{2,1,0:T(8,128)}, f32[10,128,256]{2,1,0:T(8,128)}, f32[10,128,256]{2,1,0:T(8,128)}, f32[3,64,256]{2,1,0:T(8,128)}, f32[3,64,256...) custom-call(f32[8,128]{1,0:T(8,128)} %get-tuple-element.207.refs_0_,, ...), custom_call_target="tpu_custom_call" | custom-call | flops 20000000 | bytes 14000000 | tf_op jit(solution)/shard_map/pallas_call | solution.py:2038
  (23 shorter events, 0.1 us)
Async XLA Ops:
  7.2 1.0 copy-start
  7.2 44.3 %all-gather.5.cloned.1.call-start = ((), (), s32[]{:S(2)}) async-start(), calls=%async_computation | async-start | bytes 1966080 | tf_op jit(solution)/shard_map/all_gather | solution.py:2236
  7.3 4.3 copy-start.6
  8.2 4.6 copy-start.7
  8.4 6.9 %copy-start.2 = (bf16[128,1024]{1,0:T(8,128)(2,1)S(1)}, bf16[128,1024]{1,0:T(8,128)(2,1)}, u32[]{:S(2)}) copy-start(bf16[128,1024]{1,0:T(8,128)(2,1)} %latents_ref.3) | copy-start | bytes 786436
  9.4 6.7 %copy-start.5 = (s32[4,1024]{1,0:T(4,128)S(1)}, s32[4,1024]{1,0:T(4,128)}, u32[]{:S(2)}) copy-start(s32[4,1024]{1,0:T(4,128)} %param.36) | copy-start | bytes 49156
  10.7 7.5 %copy-start.8 = (s32[4]{0:T(128)S(1)}, s32[4]{0:T(128)}, u32[]{:S(2)}) copy-start(s32[4]{0:T(128)} %param.35) | copy-start | bytes 52
  10.7 9.4 %copy-start.3 = (f32[4,12,1024]{2,0,1:T(4,128)S(1)}, f32[4,12,1024]{2,0,1:T(4,128)}, u32[]{:S(2)}) copy-start(f32[4,12,1024]{2,0,1:T(4,128)} %param.34) | copy-start | bytes 589828
  10.7 9.4 %copy-start.4 = (f32[4,12,1024]{2,0,1:T(4,128)S(1)}, f32[4,12,1024]{2,0,1:T(4,128)}, u32[]{:S(2)}) copy-start(f32[4,12,1024]{2,0,1:T(4,128)} %param.33) | copy-start | bytes 589828
  11.6 129.4 %all-gather.7.cloned.1.call-start = ((), (), s32[]{:S(2)}) async-start(), calls=%async_computation.1 | async-start | bytes 14155776 | tf_op jit(solution)/shard_map/all_gather | solution.py:2293
  584.6 9.0 %copy-start.1 = (bf16[256,512]{1,0:T(8,128)(2,1)S(1)}, bf16[256,512]{1,0:T(8,128)(2,1)}, u32[]{:S(2)}) copy-start(bf16[256,512]{1,0:T(8,128)(2,1)} %param.40) | copy-start | bytes 786436
Sparse Core Ops, SparseCore 0:
  11.7 39.7 all-gather.4
  54.1 70.9 all-gather.6

commit v8 on v7

--- a/solution.py
+++ b/solution.py
@@ -116,7 +116,7 @@
 MESH_ID = pl.DeviceIdType.MESH
 HBM_SPEC = pl.BlockSpec(memory_space=pltpu.HBM)
 VMEM_SPEC = pl.BlockSpec(memory_space=pltpu.VMEM)
-CHUNKS = 64
+CHUNKS = 32
 VMEM_LIMIT = 56 << 20
 
 
@@ -501,13 +501,11 @@
     part_ref, base_ref, tile = held[0], held[1], held[2 + extra :]
     items, outs = views(held[2 : 2 + extra]), views(results[1 : 1 + extra], 2)
     out_ref, tile_out = results[0], results[1 + extra : 1 + extra + tiled]
-    blocks, base_rows = raws, base_ref.shape[0]
-    wide = results[1 + extra + tiled :]
-    converted = len(wide)
+    base_rows = base_ref.shape[0]
     inner, from_away, from_toward, toward_send, away_send, away_recv, toward_recv = pull(7)
     chunks = toward_send.shape[0]
     spread = Spread("dp", count_dp, *pull(3)) if tiled else None
-    convert = Convert(count, chunks, blocks[0], wide, *pull(2)) if converted else None
+    turn = pull(1)[0] if tiled else None
     sums = PieceSums(count_dp, items, outs, refs)
     place = lax.axis_index("mp")
     half = count // 2
@@ -551,6 +549,25 @@
         push(step, part_ref, False).wait_recv()
         inner[window(step)] = part_ref[window(step)] + from_away[window(step)]
 
+    odd = lax.rem(lax.axis_index("dp"), 2) == 1
+    if tiled:
+        stage.wait()
+        spread.held[spread.place] = tile[0][...]
+        spread.start()
+
+        @pl.when(jnp.logical_and(outermost, odd))
+        def _():
+            pl.semaphore_wait(turn, 1)
+
+    def pass_turn():
+        if tiled:
+
+            @pl.when(jnp.logical_not(odd))
+            def _():
+                pl.semaphore_signal(
+                    turn, inc=1, device_id=spread.peer(1), device_id_type=MESH_ID
+                )
+
     @pl.when(outermost)
     def _():
         def leave(step, carry):
@@ -560,11 +577,6 @@
         lax.fori_loop(0, chunks, leave, 0)
 
     stage.wait()
-    if tiled:
-        spread.held[spread.place] = tile[0][...]
-        spread.start()
-    if converted:
-        convert.begin()
     sums.begin()
 
     @pl.when(outermost)
@@ -574,13 +586,17 @@
             push(step, part_ref, True).wait_recv()
             put(step, from_toward[window(step)])
             push(step, part_ref, False).wait_send()
-            if converted:
-                convert.step(step)
             return carry
 
-        for low, high, phase in sums.moments(chunks):
-            lax.fori_loop(low, high, arrive, 0)
-            sums.advance(phase)
+        if tiled:
+            early = chunks * 3 // 8
+            lax.fori_loop(0, early, arrive, 0)
+            pass_turn()
+            lax.fori_loop(early, chunks, arrive, 0)
+        else:
+            for low, high, phase in sums.moments(chunks):
+                lax.fori_loop(low, high, arrive, 0)
+                sums.advance(phase)
 
     lag = 2
 
@@ -597,8 +613,6 @@
         def first(step, carry):
             gather_in(step)
             push(step, inner, True).start()
-            if converted:
-                convert.step(step)
             return carry
 
         def both(step, carry):
@@ -635,8 +649,6 @@
                 push(step, inner, True).wait_recv()
                 back(step, from_toward).start()
                 put(step, from_toward[window(step)])
-                if converted:
-                    convert.step(step)
                 return carry
 
             def drain(step, carry):
@@ -667,26 +679,19 @@
     return items, shapes, shares
 
 
-def line_sum(part, base, call_id, items=(), tile=None, blocks=None):
+def line_sum(part, base, call_id, items=(), tile=None):
     items, shapes, shares = piece_shapes(items)
     count, count_dp = lax.axis_size("mp"), lax.axis_size("dp")
     rows, width = part.shape
     buffer = pltpu.VMEM((rows, width), jnp.float32)
     sems = pltpu.SemaphoreType.DMA((CHUNKS,))
-    inputs, raw = [base, *items], []
+    inputs = [base, *items]
     outs = list(shares)
     scratch = [buffer] * 3 + [sems] * 4
     if tile is not None:
         inputs.append(tile)
         outs.append(jax.ShapeDtypeStruct(tile.shape, jnp.float32))
-        scratch += Spread.scratch(count_dp, tile.shape)
-    if blocks is not None:
-        blocks, sizes = blocks
-        raw.append(blocks)
-        outs += [
-            jax.ShapeDtypeStruct((size, count * blocks.shape[2]), jnp.bfloat16) for size in sizes
-        ]
-        scratch += Convert.scratch(blocks.shape[1:])
+        scratch += Spread.scratch(count_dp, tile.shape) + [pltpu.SemaphoreType.REGULAR]
     scratch += PieceSums.scratch(count_dp, shapes)
     total = jax.ShapeDtypeStruct((rows, width), jnp.float32)
     results = staged(
@@ -695,11 +700,10 @@
         outs,
         scratch,
         4 * rows * width,
-        raw,
-        call_id,
-        55,
-        [part],
-        [total],
+        call_id=call_id,
+        length=55,
+        near=[part],
+        near_outs=[total],
     )
     return results[0], results[-1], results[1:-1]
 
@@ -772,17 +776,21 @@
             self.down_acc[where] = part[where] + self.from_above[where]
             self.down(owner, step, self.down_acc).start()
 
-    def run(self, pause=None):
+    def run(self, pause=None, beside=None):
         turns, lag = self.count * self.steps, self.steps
 
         def staggered(first, second):
             def begin(index, carry):
                 first(index)
+                if beside is not None:
+                    beside(index)
                 return carry
 
             def both(index, carry):
                 first(index)
                 second(index - lag)
+                if beside is not None:
+                    beside(index)
                 return carry
 
             def end(index, carry):
@@ -845,38 +853,46 @@
 
 
 def line_scatter_kernel(count, stage, held, raws, results, scratch):
-    own, sem = scratch[8:]
+    own, sem = scratch[8:10]
+    base, blocks = raws
     scatter = LineScatter(count, held[0], results[0], scratch[:4], scratch[4:8])
+    convert = Convert(
+        count, count * scatter.steps, blocks, results[1:], scratch[10], scratch[11]
+    )
     rows = own.shape[0]
     load = pltpu.make_async_copy(
-        raws[0].at[pl.ds(pl.multiple_of(scatter.place * rows, rows), rows)], own, sem
+        base.at[pl.ds(pl.multiple_of(scatter.place * rows, rows), rows)], own, sem
     )
     load.start()
+    convert.begin()
     greet(scatter.place, count)
-    scatter.run()
+    scatter.run(None, convert.step)
+    stage.store(1, 2, 3, 4)
     scatter.settle()
     load.wait()
     results[0][...] += own[...]
     scatter.finish()
 
 
-def line_scatter(part, base, call_id):
+def line_scatter(part, base, blocks, sizes, call_id):
     rows, width = part.shape
     count = lax.axis_size("mp")
     own = (rows // count, width)
-    (result,) = staged(
+    result, *weights = staged(
         partial(line_scatter_kernel, count),
         [],
-        [jax.ShapeDtypeStruct(own, jnp.float32)],
+        [jax.ShapeDtypeStruct(own, jnp.float32)]
+        + [jax.ShapeDtypeStruct((size, count * blocks.shape[2]), jnp.bfloat16) for size in sizes],
         LineScatter.scratch(count, (rows, width), 8)
-        + [pltpu.VMEM(own, jnp.float32), pltpu.SemaphoreType.DMA],
+        + [pltpu.VMEM(own, jnp.float32), pltpu.SemaphoreType.DMA]
+        + Convert.scratch(blocks.shape[1:]),
         2 * rows * width,
-        [base],
+        [base, blocks],
         call_id=call_id,
         length=33,
         near=[part],
     )
-    return result
+    return result, weights
 
 
 def line_gather_kernel(count, count_dp, extra, stage, held, raws, results, scratch):
@@ -2297,11 +2313,11 @@
     self_part, *self_kept = self_forward(
         latent_near, wide_gains[0], wide_in, wide_out, images
     )
-    latent_near, latent_two, write_weights = line_sum(
-        self_part, latent_one, 3, blocks=(gathered, [d_lat, d_lat, d_if, d_if])
-    )
+    latent_near, latent_two, _ = line_sum(self_part, latent_one, 3)
     feed_part, *feed_kept = feed_forward(latent_near, wide_gains[1], wide_in, wide_out)
-    latent_three = line_scatter(feed_part, latent_two, 4)
+    latent_three, write_weights = line_scatter(
+        feed_part, latent_two, gathered, [d_lat, d_lat, d_if, d_if], 4
+    )
     latent_three = latent_three.reshape(own_images, own_latents, d_lat)
     if sharers == 1 and own_images == 1:
         (

time: 608 us -> 537 us (0.88)
  Pallas kernels: 557 us -> 486 us
    pallas_call x8, Pallas kernels: 462 us -> 390 us  [staged(): pl.pallas_call(partial(staged_kernel, body, counts), out_shape=[pltpu.VME...]
  transfers between devices with their start and end apart: 2 -> 2, of which waited for: 1 -> 1; matrix products, arithmetic and copies ran while one was open for 2% -> 2% of each run, Pallas kernels for 18% -> 26%
where the time goes in v8:
time: 537 us; the launch traced here: 529 us
  Pallas kernels  486 us (91%)
  local copies, waits for them, and re-layouts  16.7 us (3%)
  between operations  14.8 us (3%)
  waiting for transfers between devices  9.43 us (2%)
    pallas_call x8, Pallas kernels, staged(): pl.pallas_call(partial(staged_kernel, body, counts), out_shape=[pltpu.VME...  390 us
    pallas_call x1, Pallas kernels, read_backward(): pl.pallas_call(read_backward_kernel, grid=(images,), out_shape=[pltpu.HBM...  25.8 us
    pallas_call x1, Pallas kernels, read_forward(): pl.pallas_call(read_forward_kernel, grid=(images,), out_shape=[pltpu.VMEM...  19.2 us
    pallas_call x1, Pallas kernels, feed_backward(): pl.pallas_call(feed_backward_kernel, grid=(4,), out_shape=[pltpu.VMEM((ro...  12.8 us
    pallas_call x1, Pallas kernels, self_backward(): pl.pallas_call(self_backward_kernel, grid=(images,), out_shape=[pltpu.VME...  12.7 us
  transfers between devices with their start and end apart: 2, of which 1 were waited for; matrix products, arithmetic and copies ran while one was open for 2% of the time, Pallas kernels for 26%

profile of v8, /device:TPU:0, one launch (start us, length us, event | category | flops | bytes accessed | tf_op | source)
XLA Modules:
  0.0 529.1 jit_solution(10010435994446925110)
XLA Ops:
  7.2 0.0 copy-start
  7.2 0.0 all-gather.5.cloned.1.call-start
  7.3 0.9 copy-done
  8.2 0.1 dynamic-slice_bitcast_fusion
  8.3 0.1 copy.62
  8.4 1.0 slice.38
  9.4 1.3 fusion.1
  10.8 0.8 maximum_convert_fusion
  11.5 0.0 all-gather.5.cloned.1.call-update
  11.6 0.0 all-gather.7.cloned.1.call-start
  11.6 0.6 slice.49.gain_ref
  12.2 0.6 slice.53.refs_9_
  12.9 0.6 copy.71
  13.5 0.6 copy.70
  14.1 0.6 copy.69
  14.7 0.6 copy.68
  15.3 0.8 convert_element_type.37.refs_1_
  16.1 2.0 copy.66.keep_ref
  18.1 0.1 convert_reduce_fusion
  18.2 0.6 multiply_reduce_fusion
  18.9 0.6 dynamic_slice.34
  19.5 0.6 pad.12.refs_7_
  20.1 0.2 fusion.2
  20.3 0.7 pad.11.noisy_ref
  21.1 0.6 constant_dynamic-slice_fusion.refs_5_
  21.7 0.6 slice_bitcast_fusion.pixels_ref
  22.3 0.7 pad_dynamic-slice_fusion
  22.9 19.2 %shard_map.488 = (f32[512,1024]{1,0:T(8,128)S(1)}, bf16[4,2,1024,256]{3,2,1,0:T(8,128)(2,1)}, bf16[4,128,256]{2,1,0:T(8,128)(2,1)}, bf16[512,256]{1,0:T(8,128)(2...) custom-call(f32[4,16,1024]{2,1,0:T(8,128)} %pad.11.noisy_ref, ...), custom_call_target="tpu_custom_call" | custom-call | flops 10000000000 | bytes 30000000 | tf_op jit(solution)/shard_map/pallas_call | solution.py:1119
  42.1 9.4 %all-gather.5.cloned.1.call-done = f32[1536,256]{1,0:T(8,128)} async-done(((f32[384,256]{1,0:T(8,128)}), f32[1536,256]{1,0:T(8,128)}) %all-gather.5.cloned.1.call-update) | async-done | bytes 1572880 | tf_op jit(solution)/shard_map/all_gather | solution.py:2252
  51.5 1.2 broadcast_in_dim.12.refs_0_
  52.7 1.2 broadcast_in_dim.13.refs_2_
  54.0 0.0 all-gather.7.cloned.1.call-update
  54.0 52.6 %shard_map.489 = (f32[512,1024]{1,0:T(8,128)S(1)}, f32[8,128]{1,0:T(8,128)}, f32[512,1024]{1,0:T(8,128)}) custom-call(f32[512,1024]{1,0:T(8,128)S(1)} %get-tuple-element.132.refs_0_, f32[128,1024]{1,0:T(8,128)} %convert_element_type.37.refs_1_, f32[8,128]{1,0:T(8,128)} %broadcast_in_dim.13.refs_2_), custom_call_target="tpu_custom_call" | custom-call | flops 2097152 | bytes 192500000 | tf_op jit(solution)/shard_map/pallas_call | solution.py:444
  106.6 7.3 %shard_map.490 = (f32[512,1024]{1,0:T(8,128)S(1)}, bf16[4,3,128,256]{3,2,1,0:T(8,128)(2,1)}, bf16[4,128,256]{2,1,0:T(8,128)(2,1)}, f32[4,1,512]{2,1,0:T(1,128)}, bf16[512,1024]{1,0:T(8,128)(2,1)}) custom-call(f32[512,1024]{1,0:T(8,128)S(1)} %get-tuple-element.136.latent_ref, f32[1,1024]{1,0:T(1,128)} %bitcast.107, bf16[10,1024,256]{2,1,0:T(8,128)(2,1)} %bitcast.73, ...), custom_call_target="tpu_custom_call" | custom-call | flops 3000000000 | bytes 12000000 | tf_op jit(solution)/shard_map/pallas_call | solution.py:1344
  113.9 51.8 %shard_map.491 = (f32[512,1024]{1,0:T(8,128)S(1)}, f32[512,1024]{1,0:T(8,128)}) custom-call(f32[512,1024]{1,0:T(8,128)S(1)} %get-tuple-element.138.refs_0_, f32[512,1024]{1,0:T(8,128)} %get-tuple-element.139.refs_1_.latent_ref), custom_call_target="tpu_custom_call" | custom-call | flops 2097152 | bytes 192500000 | tf_op jit(solution)/shard_map/pallas_call | solution.py:444
  165.7 9.1 %shard_map.492 = (f32[512,1024]{1,0:T(8,128)S(1)}, bf16[4,512,256]{2,1,0:T(8,128)(2,1)}, f32[4,512,256]{2,1,0:T(8,128)}, bf16[512,1024]{1,0:T(8,128)(2,1)}) custom-call(f32[512,1024]{1,0:T(8,128)S(1)} %get-tuple-element.140.latent_ref, f32[1,1024]{1,0:T(1,128)} %bitcast.114, bf16[10,1024,256]{2,1,0:T(8,128)(2,1)} %bitcast.76, ...), custom_call_target="tpu_custom_call" | custom-call | flops 4000000000 | bytes 14000000 | tf_op jit(solution)/shard_map/pallas_call | solution.py:1494
  174.9 0.0 all-gather.7.cloned.1.call-done.refs_2_
  174.9 26.7 %shard_map.493 = (f32[128,1024]{1,0:T(8,128)}, bf16[1024,1024]{1,0:T(8,128)(2,1)}, bf16[1024,1024]{1,0:T(8,128)(2,1)}, bf16[512,1024]{1,0:T(8,128)(2,1)}, bf16[512,1024]{1,0:T(8,128)(2,1)}) custom-call(f32[512,1024]{1,0:T(8,128)S(1)} %get-tuple-element.142.refs_0_, f32[512,1024]{1,0:T(8,128)} %get-tuple-element.143.refs_1_.latent_ref, ...), custom_call_target="tpu_custom_call" | custom-call | flops 1048576 | bytes 115500000 | tf_op jit(solution)/shard_map/pallas_call | solution.py:444
  201.6 26.3 %shard_map.494 = (f32[128,1024]{1,0:T(8,128)}, f32[1024,1024]{1,0:T(8,128)}, f32[1024,1024]{1,0:T(8,128)}, f32[512,1024]{1,0:T(8,128)}, f32[512,1024]{1,0:T(8,12...) custom-call(f32[8,128]{1,0:T(8,128)} %broadcast_in_dim.12.refs_0_, ...), custom_call_target="tpu_custom_call" | custom-call | flops 15000000512 | bytes 94500000 | tf_op jit(solution)/shard_map/pallas_call | solution.py:444
  227.9 61.2 %shard_map.495 = (f32[512,1024]{1,0:T(8,128)S(1)}, f32[128,1024]{1,0:T(8,128)}, f32[64,1024]{1,0:T(8,128)}, f32[512,1024]{1,0:T(8,128)}) custom-call(f32[128,1024]{1,0:T(8,128)} %get-tuple-element.156.refs_0_, f32[8,128,1024]{2,1,0:T(8,128)} %bitcast.84, f32[8,64,1024]{2,1,0:T(8,128)} %bitcast.85), custom_call_target="tpu_custom_call" | custom-call | flops 131072 | bytes 133000000 | tf_op jit(solution)/shard_map/pallas_call | solution.py:444
  289.1 12.8 %shard_map.496 = (f32[512,1024]{1,0:T(8,128)S(1)}, f32[2,1024,256]{2,1,0:T(8,128)}, f32[2,1024,256]{2,1,0:T(8,128)}, f32[4,1024,256]{2,1,0:T(8,128)}, f32[1,1024]{1,0:T(1,128)}) custom-call(f32[512,1024]{1,0:T(8,128)S(1)} %get-tuple-element.159.grad_ref, f32[512,1024]{1,0:T(8,128)} %get-tuple-element.143.refs_1_.latent_ref, f32[1,1024]{1,0:T(1,128)} %bitcast.115, ...), custom_call_target="tpu_custom_call" | custom-call | flops 8999999488 | bytes 26000000 | tf_op jit(solution)/shard_map/pallas_call | solution.py:1576
  301.9 58.7 %shard_map.497 = (f32[512,1024]{1,0:T(8,128)S(1)}, f32[128,1024]{1,0:T(8,128)}, f32[64,1024]{1,0:T(8,128)}, f32[2,128,256]{2,1,0:T(8,128)}, f32[512,1024]{1,0:T(8,128)}) custom-call(f32[512,1024]{1,0:T(8,128)S(1)} %get-tuple-element.163.refs_0_, f32[512,1024]{1,0:T(8,128)} %get-tuple-element.164.refs_1_, f32[8,128,1024]{2,1,0:T(8,128)} %bitcast.82, ...), custom_call_target="tpu_custom_call" | custom-call | flops 2097152 | bytes 192500000 | tf_op jit(solution)/shard_map/pallas_call | solution.py:444
  360.6 12.7 %shard_map.498 = (f32[512,1024]{1,0:T(8,128)S(1)}, f32[2,1024,256]{2,1,0:T(8,128)}, f32[2,1024,256]{2,1,0:T(8,128)}, f32[1,1024]{1,0:T(1,128)}) custom-call(f32[512,1024]{1,0:T(8,128)S(1)} %get-tuple-element.168.grad_ref, f32[512,1024]{1,0:T(8,128)} %get-tuple-element.139.refs_1_.latent_ref, f32[1,1024]{1,0:T(1,128)} %bitcast.108, ...), custom_call_target="tpu_custom_call" | custom-call | flops 6000000000 | bytes 16000000 | tf_op jit(solution)/shard_map/pallas_call | solution.py:1437
  373.3 59.6 %shard_map.499 = (f32[512,1024]{1,0:T(8,128)S(1)}, f32[2,128,256]{2,1,0:T(8,128)}, f32[4,128,256]{2,1,0:T(8,128)}, f32[2,128,256]{2,1,0:T(8,128)}, f32[512,1024]{1,0:T(8,128)}) custom-call(f32[512,1024]{1,0:T(8,128)S(1)} %get-tuple-element.181.refs_0_, f32[512,1024]{1,0:T(8,128)} %get-tuple-element.182.refs_1_, f32[2,8,128,256]{3,2,1,0:T(8,128)} %bitcast.89, ...), custom_call_target="tpu_custom_call" | custom-call | flops 2097152 | bytes 192500000 | tf_op jit(solution)/shard_map/pallas_call | solution.py:444
  432.9 25.8 %shard_map.500 = (f32[2,1024,256]{2,1,0:T(8,128)}, f32[2,512,256]{2,1,0:T(8,128)}, f32[128,1024]{1,0:T(8,128)}, f32[1,1024]{1,0:T(1,128)}, f32[1,512]{1,0:T(1,128)}, /*index=5*/f32[16,512]{1,0:T(8,128)}) custom-call(f32[4,16,1024]{2,1,0:T(8,128)} %pad.11.noisy_ref, bf16[128,1024]{1,0:T(8,128)(2,1)} %latents_ref.3, f32[1,1024]{1,0:T(1,128)} %bitcast.113, ...), custom_call_target="tpu_custom_call" | custom-call | flops 20000000000 | bytes 30000000 | tf_op jit(solution)/shard_map/pallas_call | solution.py:1273
  458.7 52.8 %shard_map.501 = (f32[10,128,256]{2,1,0:T(8,128)}, f32[3,64,256]{2,1,0:T(8,128)}, f32[6,256,128]{2,1,0:T(8,128)}, f32[64,256]{1,0:T(8,128)}, f32[128,128]{1,0:T(...) custom-call(f32[2,8,128,256]{3,2,1,0:T(8,128)} %bitcast.86, f32[2,8,128,256]{3,2,1,0:T(8,128)} %bitcast.87, ...), custom_call_target="tpu_custom_call" | custom-call | flops 10000000 | bytes 175000000 | tf_op jit(solution)/shard_map/pallas_call | solution.py:444
  511.5 1.3 fusion.4
  512.8 9.0 %shard_map.502 = (f32[10,128,256]{2,1,0:T(8,128)}, f32[10,128,256]{2,1,0:T(8,128)}, f32[10,128,256]{2,1,0:T(8,128)}, f32[3,64,256]{2,1,0:T(8,128)}, f32[3,64,256...) custom-call(f32[8,128]{1,0:T(8,128)} %get-tuple-element.209.refs_0_,, ...), custom_call_target="tpu_custom_call" | custom-call | flops 20000000 | bytes 14000000 | tf_op jit(solution)/shard_map/pallas_call | solution.py:2054
  (23 shorter events, 0.1 us)
Async XLA Ops:
  7.2 1.0 copy-start
  7.2 44.3 %all-gather.5.cloned.1.call-start = ((), (), s32[]{:S(2)}) async-start(), calls=%async_computation | async-start | bytes 1966080 | tf_op jit(solution)/shard_map/all_gather | solution.py:2252
  7.3 4.3 copy-start.6
  8.2 4.6 copy-start.7
  8.4 6.9 %copy-start.2 = (bf16[128,1024]{1,0:T(8,128)(2,1)S(1)}, bf16[128,1024]{1,0:T(8,128)(2,1)}, u32[]{:S(2)}) copy-start(bf16[128,1024]{1,0:T(8,128)(2,1)} %latents_ref.3) | copy-start | bytes 786436
  9.4 6.7 %copy-start.5 = (s32[4,1024]{1,0:T(4,128)S(1)}, s32[4,1024]{1,0:T(4,128)}, u32[]{:S(2)}) copy-start(s32[4,1024]{1,0:T(4,128)} %param.36) | copy-start | bytes 49156
  10.7 7.5 %copy-start.8 = (s32[4]{0:T(128)S(1)}, s32[4]{0:T(128)}, u32[]{:S(2)}) copy-start(s32[4]{0:T(128)} %param.35) | copy-start | bytes 52
  10.7 9.4 %copy-start.3 = (f32[4,12,1024]{2,0,1:T(4,128)S(1)}, f32[4,12,1024]{2,0,1:T(4,128)}, u32[]{:S(2)}) copy-start(f32[4,12,1024]{2,0,1:T(4,128)} %param.34) | copy-start | bytes 589828
  10.7 9.4 %copy-start.4 = (f32[4,12,1024]{2,0,1:T(4,128)S(1)}, f32[4,12,1024]{2,0,1:T(4,128)}, u32[]{:S(2)}) copy-start(f32[4,12,1024]{2,0,1:T(4,128)} %param.33) | copy-start | bytes 589828
  11.6 163.3 %all-gather.7.cloned.1.call-start = ((), (), s32[]{:S(2)}) async-start(), calls=%async_computation.1 | async-start | bytes 14155776 | tf_op jit(solution)/shard_map/all_gather | solution.py:2309
  512.8 9.0 %copy-start.1 = (bf16[256,512]{1,0:T(8,128)(2,1)S(1)}, bf16[256,512]{1,0:T(8,128)(2,1)}, u32[]{:S(2)}) copy-start(bf16[256,512]{1,0:T(8,128)(2,1)} %param.40) | copy-start | bytes 786436
Sparse Core Ops, SparseCore 0:
  11.7 39.7 all-gather.4
  54.1 70.9 all-gather.6

commit v9 on v8

--- a/solution.py
+++ b/solution.py
@@ -589,7 +589,7 @@
             return carry
 
         if tiled:
-            early = chunks * 3 // 8
+            early = chunks // 4
             lax.fori_loop(0, early, arrive, 0)
             pass_turn()
             lax.fori_loop(early, chunks, arrive, 0)
@@ -604,10 +604,9 @@
     def _():
         def finish(step):
             push(step, inner, True).wait_recv()
-            push(step, inner, True).wait_send()
             total = inner[window(step)] + from_toward[window(step)]
-            inner[window(step)] = total
-            back(step, inner).start()
+            from_away[window(step)] = total
+            back(step, from_away).start()
             put(step, total)
 
         def first(step, carry):
@@ -625,7 +624,8 @@
             return carry
 
         def drain(step, carry):
-            back(step, inner).wait_send()
+            push(step, inner, True).wait_send()
+            back(step, from_away).wait_send()
             return carry
 
         lax.fori_loop(0, lag, first, 0)
@@ -1183,6 +1183,7 @@
     embed_grad_ref,
     low_ref,
     returned_ref,
+    pair_ref,
 ):
     step, steps = pl.program_id(0), pl.num_programs(0)
     heads = query_weight_ref.shape[2] // HEAD_DIM
@@ -1191,6 +1192,7 @@
     def _():
         normed, _ = norm_rows(latents_ref[...].astype(jnp.float32))
         low_ref[...] = (normed * wide_gain_ref[...]).astype(jnp.bfloat16)
+        pair_ref[...] = jnp.concatenate([pair_weight_ref[0], pair_weight_ref[1]], 1)
         for ref in (
             wide_grad_ref,
             narrow_grad_ref,
@@ -1216,9 +1218,11 @@
     query_grad = query_grad.astype(jnp.bfloat16)
     wide_grad_ref[0] += dot(low_ref[...], query_grad, 0, 0)
     returned_ref[...] += dot(query_grad, query_weight_ref[0], 1, 1)
-    narrow_grad_ref[0] += dot(side, key_grad)
-    narrow_grad_ref[1] += dot(side, value_grad)
-    side_grad = dot(key_grad, pair_weight_ref[0], 1, 1) + dot(value_grad, pair_weight_ref[1], 1, 1)
+    pair_grad = jnp.concatenate([key_grad, value_grad], 1)
+    narrow_grad = dot(side, pair_grad)
+    narrow_grad_ref[0] += narrow_grad[:, : keys.shape[1]]
+    narrow_grad_ref[1] += narrow_grad[:, keys.shape[1] :]
+    side_grad = dot(pair_grad, pair_ref[...], 1, 1)
     gain_grad_ref[...] += jnp.sum(side_grad * normed, 0, keepdims=True)
     back = norm_rows_back(side_grad, gain_ref[...], normed, scale)
     embed_grad_ref[...] += embed_back(noisy_ref[0], back)
@@ -1296,6 +1300,7 @@
         scratch_shapes=[
             pltpu.VMEM((count, d_lat), jnp.bfloat16),
             pltpu.VMEM((count, d_lat), jnp.float32),
+            pltpu.VMEM((d_if, 2 * local), jnp.bfloat16),
         ],
         compiler_params=pltpu.CompilerParams(vmem_limit_bytes=52 << 20),
         cost_estimate=pl.CostEstimate(
@@ -1670,14 +1675,19 @@
     def by_head(values):
         return values.reshape(4, latents, patches)
 
+    def probs_of(index):
+        later = (key_grad_ref, value_grad_ref)[index * rows // key_grad_ref.shape[0]]
+        return later.at[pl.ds(index * rows % key_grad_ref.shape[0], rows)]
+
     def group_probs(index):
         scores = by_head(dot(scaled_heads(part(keys, index)), part(queries, index), 1, 1))
         grown = jnp.exp(scores - jnp.max(scores, 1, keepdims=True))
         return grown / jnp.sum(grown, 1, keepdims=True)
 
     for index in range(groups):
-        probs = group_probs(index).reshape(rows, patches).astype(jnp.bfloat16)
-        output = dot(probs, spread_heads(part(values, index)), 0, 0)
+        probs = group_probs(index).reshape(rows, patches)
+        probs_of(index)[...] = probs
+        output = dot(probs.astype(jnp.bfloat16), spread_heads(part(values, index)), 0, 0)
         outputs[:, index * group : (index + 1) * group] = output.astype(jnp.bfloat16)
 
     outer = interface + dot(outputs[...], out_weight_ref[...], 1, 1)
@@ -1699,8 +1709,8 @@
 
     key_grads, value_grads = [], []
     for index in range(groups):
-        probs = group_probs(index)
-        low = probs.reshape(rows, patches).astype(jnp.bfloat16)
+        probs = probs_of(index)[...]
+        low, probs = probs.astype(jnp.bfloat16), by_head(probs)
         above = part(upstream, index)
         value_grads.append(join_heads(dot(low, above), 4).astype(jnp.bfloat16))
         prob_grad = by_head(dot(spread_heads(part(values, index)), above, 1, 1))
@@ -1771,7 +1781,10 @@
         ],
         [jax.ShapeDtypeStruct(shape, jnp.float32) for shape in results],
         [wide] * 4
-        + [pltpu.VMEM((patches, d_if), jnp.float32), pltpu.VMEM((patches, 1), jnp.float32)],
+        + [
+            pltpu.VMEM((patches, d_if), jnp.float32),
+            pltpu.VMEM((patches, 1), jnp.float32),
+        ],
         15 * 10**9,
         length=27,
     )
@@ -2319,7 +2332,8 @@
         feed_part, latent_two, gathered, [d_lat, d_lat, d_if, d_if], 4
     )
     latent_three = latent_three.reshape(own_images, own_latents, d_lat)
-    if sharers == 1 and own_images == 1:
+    fits = patches == count_mp * local and d_lat % (4 * latents) == 0
+    if sharers == 1 and own_images == 1 and fits:
         (
             own_grad,
             write_key_grad,

time: 537 us -> 549 us (1.022)
  Pallas kernels: 486 us -> 498 us
    pallas_call x8, Pallas kernels: 390 us -> 403 us  [staged(): pl.pallas_call(partial(staged_kernel, body, counts), out_shape=[pltpu.VME...]
where the time goes in v9:
time: 549 us; the launch traced here: 542 us
  Pallas kernels  498 us (91%)
  local copies, waits for them, and re-layouts  16.7 us (3%)
  between operations  14.7 us (3%)
  waiting for transfers between devices  9.43 us (2%)
    pallas_call x8, Pallas kernels, staged(): pl.pallas_call(partial(staged_kernel, body, counts), out_shape=[pltpu.VME...  403 us
    pallas_call x1, Pallas kernels, read_backward(): pl.pallas_call(read_backward_kernel, grid=(images,), out_shape=[pltpu.HBM...  25.6 us
    pallas_call x1, Pallas kernels, read_forward(): pl.pallas_call(read_forward_kernel, grid=(images,), out_shape=[pltpu.VMEM...  19.2 us
    pallas_call x1, Pallas kernels, feed_backward(): pl.pallas_call(feed_backward_kernel, grid=(4,), out_shape=[pltpu.VMEM((ro...  12.8 us
    pallas_call x1, Pallas kernels, self_backward(): pl.pallas_call(self_backward_kernel, grid=(images,), out_shape=[pltpu.VME...  12.7 us
  transfers between devices with their start and end apart: 2, of which 1 were waited for; matrix products, arithmetic and copies ran while one was open for 2% of the time, Pallas kernels for 26%

profile of v9, /device:TPU:0, one launch (start us, length us, event | category | flops | bytes accessed | tf_op | source)
XLA Modules:
  0.0 542.0 jit_solution(6246161243947648277)
XLA Ops:
  7.2 0.0 copy-start
  7.2 0.0 all-gather.5.cloned.1.call-start
  7.3 0.9 copy-done
  8.2 0.1 dynamic-slice_bitcast_fusion
  8.3 0.1 copy.62
  8.4 1.0 slice.38
  9.4 1.3 fusion.1
  10.8 0.8 maximum_convert_fusion
  11.5 0.0 all-gather.5.cloned.1.call-update
  11.6 0.0 all-gather.7.cloned.1.call-start
  11.6 0.6 slice.49.gain_ref
  12.2 0.6 slice.53.refs_9_
  12.9 0.6 copy.71
  13.5 0.6 copy.70
  14.1 0.6 copy.69
  14.7 0.6 copy.68
  15.3 0.8 convert_element_type.37.refs_1_
  16.1 2.0 copy.66.keep_ref
  18.1 0.1 convert_reduce_fusion
  18.2 0.6 multiply_reduce_fusion
  18.9 0.6 dynamic_slice.34
  19.5 0.6 pad.12.refs_7_
  20.1 0.2 fusion.2
  20.3 0.7 pad.11.noisy_ref
  21.1 0.6 constant_dynamic-slice_fusion.refs_5_
  21.7 0.6 slice_bitcast_fusion.pixels_ref
  22.3 0.7 pad_dynamic-slice_fusion
  22.9 19.2 %shard_map.488 = (f32[512,1024]{1,0:T(8,128)S(1)}, bf16[4,2,1024,256]{3,2,1,0:T(8,128)(2,1)}, bf16[4,128,256]{2,1,0:T(8,128)(2,1)}, bf16[512,256]{1,0:T(8,128)(2...) custom-call(f32[4,16,1024]{2,1,0:T(8,128)} %pad.11.noisy_ref, ...), custom_call_target="tpu_custom_call" | custom-call | flops 10000000000 | bytes 30000000 | tf_op jit(solution)/shard_map/pallas_call | solution.py:1119
  42.1 9.4 %all-gather.5.cloned.1.call-done = f32[1536,256]{1,0:T(8,128)} async-done(((f32[384,256]{1,0:T(8,128)}), f32[1536,256]{1,0:T(8,128)}) %all-gather.5.cloned.1.call-update) | async-done | bytes 1572880 | tf_op jit(solution)/shard_map/all_gather | solution.py:2265
  51.5 1.2 broadcast_in_dim.12.refs_0_
  52.7 1.2 broadcast_in_dim.13.refs_2_
  54.0 0.0 all-gather.7.cloned.1.call-update
  54.0 54.5 %shard_map.489 = (f32[512,1024]{1,0:T(8,128)S(1)}, f32[8,128]{1,0:T(8,128)}, f32[512,1024]{1,0:T(8,128)}) custom-call(f32[512,1024]{1,0:T(8,128)S(1)} %get-tuple-element.132.refs_0_, f32[128,1024]{1,0:T(8,128)} %convert_element_type.37.refs_1_, f32[8,128]{1,0:T(8,128)} %broadcast_in_dim.13.refs_2_), custom_call_target="tpu_custom_call" | custom-call | flops 2097152 | bytes 192500000 | tf_op jit(solution)/shard_map/pallas_call | solution.py:444
  108.5 7.1 %shard_map.490 = (f32[512,1024]{1,0:T(8,128)S(1)}, bf16[4,3,128,256]{3,2,1,0:T(8,128)(2,1)}, bf16[4,128,256]{2,1,0:T(8,128)(2,1)}, f32[4,1,512]{2,1,0:T(1,128)}, bf16[512,1024]{1,0:T(8,128)(2,1)}) custom-call(f32[512,1024]{1,0:T(8,128)S(1)} %get-tuple-element.136.latent_ref, f32[1,1024]{1,0:T(1,128)} %bitcast.107, bf16[10,1024,256]{2,1,0:T(8,128)(2,1)} %bitcast.73, ...), custom_call_target="tpu_custom_call" | custom-call | flops 3000000000 | bytes 12000000 | tf_op jit(solution)/shard_map/pallas_call | solution.py:1349
  115.7 53.1 %shard_map.491 = (f32[512,1024]{1,0:T(8,128)S(1)}, f32[512,1024]{1,0:T(8,128)}) custom-call(f32[512,1024]{1,0:T(8,128)S(1)} %get-tuple-element.138.refs_0_, f32[512,1024]{1,0:T(8,128)} %get-tuple-element.139.refs_1_.latent_ref), custom_call_target="tpu_custom_call" | custom-call | flops 2097152 | bytes 192500000 | tf_op jit(solution)/shard_map/pallas_call | solution.py:444
  168.8 9.1 %shard_map.492 = (f32[512,1024]{1,0:T(8,128)S(1)}, bf16[4,512,256]{2,1,0:T(8,128)(2,1)}, f32[4,512,256]{2,1,0:T(8,128)}, bf16[512,1024]{1,0:T(8,128)(2,1)}) custom-call(f32[512,1024]{1,0:T(8,128)S(1)} %get-tuple-element.140.latent_ref, f32[1,1024]{1,0:T(1,128)} %bitcast.114, bf16[10,1024,256]{2,1,0:T(8,128)(2,1)} %bitcast.76, ...), custom_call_target="tpu_custom_call" | custom-call | flops 4000000000 | bytes 14000000 | tf_op jit(solution)/shard_map/pallas_call | solution.py:1499
  178.0 0.0 all-gather.7.cloned.1.call-done.refs_2_
  178.0 30.0 %shard_map.493 = (f32[128,1024]{1,0:T(8,128)}, bf16[1024,1024]{1,0:T(8,128)(2,1)}, bf16[1024,1024]{1,0:T(8,128)(2,1)}, bf16[512,1024]{1,0:T(8,128)(2,1)}, bf16[512,1024]{1,0:T(8,128)(2,1)}) custom-call(f32[512,1024]{1,0:T(8,128)S(1)} %get-tuple-element.142.refs_0_, f32[512,1024]{1,0:T(8,128)} %get-tuple-element.143.refs_1_.latent_ref, ...), custom_call_target="tpu_custom_call" | custom-call | flops 1048576 | bytes 115500000 | tf_op jit(solution)/shard_map/pallas_call | solution.py:444
  208.0 37.5 %shard_map.494 = (f32[128,1024]{1,0:T(8,128)}, f32[1024,1024]{1,0:T(8,128)}, f32[1024,1024]{1,0:T(8,128)}, f32[512,1024]{1,0:T(8,128)}, f32[512,1024]{1,0:T(8,12...) custom-call(f32[8,128]{1,0:T(8,128)} %broadcast_in_dim.12.refs_0_, ...), custom_call_target="tpu_custom_call" | custom-call | flops 15000000512 | bytes 94500000 | tf_op jit(solution)/shard_map/pallas_call | solution.py:444
  245.5 56.7 %shard_map.495 = (f32[512,1024]{1,0:T(8,128)S(1)}, f32[128,1024]{1,0:T(8,128)}, f32[64,1024]{1,0:T(8,128)}, f32[512,1024]{1,0:T(8,128)}) custom-call(f32[128,1024]{1,0:T(8,128)} %get-tuple-element.156.refs_0_, f32[8,128,1024]{2,1,0:T(8,128)} %bitcast.84, f32[8,64,1024]{2,1,0:T(8,128)} %bitcast.85), custom_call_target="tpu_custom_call" | custom-call | flops 131072 | bytes 133000000 | tf_op jit(solution)/shard_map/pallas_call | solution.py:444
  302.3 12.8 %shard_map.496 = (f32[512,1024]{1,0:T(8,128)S(1)}, f32[2,1024,256]{2,1,0:T(8,128)}, f32[2,1024,256]{2,1,0:T(8,128)}, f32[4,1024,256]{2,1,0:T(8,128)}, f32[1,1024]{1,0:T(1,128)}) custom-call(f32[512,1024]{1,0:T(8,128)S(1)} %get-tuple-element.159.grad_ref, f32[512,1024]{1,0:T(8,128)} %get-tuple-element.143.refs_1_.latent_ref, f32[1,1024]{1,0:T(1,128)} %bitcast.115, ...), custom_call_target="tpu_custom_call" | custom-call | flops 8999999488 | bytes 26000000 | tf_op jit(solution)/shard_map/pallas_call | solution.py:1581
  315.0 58.8 %shard_map.497 = (f32[512,1024]{1,0:T(8,128)S(1)}, f32[128,1024]{1,0:T(8,128)}, f32[64,1024]{1,0:T(8,128)}, f32[2,128,256]{2,1,0:T(8,128)}, f32[512,1024]{1,0:T(8,128)}) custom-call(f32[512,1024]{1,0:T(8,128)S(1)} %get-tuple-element.163.refs_0_, f32[512,1024]{1,0:T(8,128)} %get-tuple-element.164.refs_1_, f32[8,128,1024]{2,1,0:T(8,128)} %bitcast.82, ...), custom_call_target="tpu_custom_call" | custom-call | flops 2097152 | bytes 192500000 | tf_op jit(solution)/shard_map/pallas_call | solution.py:444
  373.9 12.7 %shard_map.498 = (f32[512,1024]{1,0:T(8,128)S(1)}, f32[2,1024,256]{2,1,0:T(8,128)}, f32[2,1024,256]{2,1,0:T(8,128)}, f32[1,1024]{1,0:T(1,128)}) custom-call(f32[512,1024]{1,0:T(8,128)S(1)} %get-tuple-element.168.grad_ref, f32[512,1024]{1,0:T(8,128)} %get-tuple-element.139.refs_1_.latent_ref, f32[1,1024]{1,0:T(1,128)} %bitcast.108, ...), custom_call_target="tpu_custom_call" | custom-call | flops 6000000000 | bytes 16000000 | tf_op jit(solution)/shard_map/pallas_call | solution.py:1442
  386.5 59.7 %shard_map.499 = (f32[512,1024]{1,0:T(8,128)S(1)}, f32[2,128,256]{2,1,0:T(8,128)}, f32[4,128,256]{2,1,0:T(8,128)}, f32[2,128,256]{2,1,0:T(8,128)}, f32[512,1024]{1,0:T(8,128)}) custom-call(f32[512,1024]{1,0:T(8,128)S(1)} %get-tuple-element.181.refs_0_, f32[512,1024]{1,0:T(8,128)} %get-tuple-element.182.refs_1_, f32[2,8,128,256]{3,2,1,0:T(8,128)} %bitcast.89, ...), custom_call_target="tpu_custom_call" | custom-call | flops 2097152 | bytes 192500000 | tf_op jit(solution)/shard_map/pallas_call | solution.py:444
  446.2 25.6 %shard_map.500 = (f32[2,1024,256]{2,1,0:T(8,128)}, f32[2,512,256]{2,1,0:T(8,128)}, f32[128,1024]{1,0:T(8,128)}, f32[1,1024]{1,0:T(1,128)}, f32[1,512]{1,0:T(1,128)}, /*index=5*/f32[16,512]{1,0:T(8,128)}) custom-call(f32[4,16,1024]{2,1,0:T(8,128)} %pad.11.noisy_ref, bf16[128,1024]{1,0:T(8,128)(2,1)} %latents_ref.3, f32[1,1024]{1,0:T(1,128)} %bitcast.113, ...), custom_call_target="tpu_custom_call" | custom-call | flops 20000000000 | bytes 30000000 | tf_op jit(solution)/shard_map/pallas_call | solution.py:1277
  471.8 52.6 %shard_map.501 = (f32[10,128,256]{2,1,0:T(8,128)}, f32[3,64,256]{2,1,0:T(8,128)}, f32[6,256,128]{2,1,0:T(8,128)}, f32[64,256]{1,0:T(8,128)}, f32[128,128]{1,0:T(...) custom-call(f32[2,8,128,256]{3,2,1,0:T(8,128)} %bitcast.86, f32[2,8,128,256]{3,2,1,0:T(8,128)} %bitcast.87, ...), custom_call_target="tpu_custom_call" | custom-call | flops 10000000 | bytes 175000000 | tf_op jit(solution)/shard_map/pallas_call | solution.py:444
  524.4 1.3 fusion.4
  525.8 9.0 %shard_map.502 = (f32[10,128,256]{2,1,0:T(8,128)}, f32[10,128,256]{2,1,0:T(8,128)}, f32[10,128,256]{2,1,0:T(8,128)}, f32[3,64,256]{2,1,0:T(8,128)}, f32[3,64,256...) custom-call(f32[8,128]{1,0:T(8,128)} %get-tuple-element.209.refs_0_,, ...), custom_call_target="tpu_custom_call" | custom-call | flops 20000000 | bytes 14000000 | tf_op jit(solution)/shard_map/pallas_call | solution.py:2067
  (23 shorter events, 0.1 us)
Async XLA Ops:
  7.2 1.0 copy-start
  7.2 44.3 %all-gather.5.cloned.1.call-start = ((), (), s32[]{:S(2)}) async-start(), calls=%async_computation | async-start | bytes 1966080 | tf_op jit(solution)/shard_map/all_gather | solution.py:2265
  7.3 4.3 copy-start.6
  8.2 4.6 copy-start.7
  8.4 6.9 %copy-start.2 = (bf16[128,1024]{1,0:T(8,128)(2,1)S(1)}, bf16[128,1024]{1,0:T(8,128)(2,1)}, u32[]{:S(2)}) copy-start(bf16[128,1024]{1,0:T(8,128)(2,1)} %latents_ref.3) | copy-start | bytes 786436
  9.4 6.7 %copy-start.5 = (s32[4,1024]{1,0:T(4,128)S(1)}, s32[4,1024]{1,0:T(4,128)}, u32[]{:S(2)}) copy-start(s32[4,1024]{1,0:T(4,128)} %param.36) | copy-start | bytes 49156
  10.7 7.5 %copy-start.8 = (s32[4]{0:T(128)S(1)}, s32[4]{0:T(128)}, u32[]{:S(2)}) copy-start(s32[4]{0:T(128)} %param.35) | copy-start | bytes 52
  10.7 9.4 %copy-start.3 = (f32[4,12,1024]{2,0,1:T(4,128)S(1)}, f32[4,12,1024]{2,0,1:T(4,128)}, u32[]{:S(2)}) copy-start(f32[4,12,1024]{2,0,1:T(4,128)} %param.34) | copy-start | bytes 589828
  10.7 9.4 %copy-start.4 = (f32[4,12,1024]{2,0,1:T(4,128)S(1)}, f32[4,12,1024]{2,0,1:T(4,128)}, u32[]{:S(2)}) copy-start(f32[4,12,1024]{2,0,1:T(4,128)} %param.33) | copy-start | bytes 589828
  11.6 166.4 %all-gather.7.cloned.1.call-start = ((), (), s32[]{:S(2)}) async-start(), calls=%async_computation.1 | async-start | bytes 14155776 | tf_op jit(solution)/shard_map/all_gather | solution.py:2322
  525.8 9.0 %copy-start.1 = (bf16[256,512]{1,0:T(8,128)(2,1)S(1)}, bf16[256,512]{1,0:T(8,128)(2,1)}, u32[]{:S(2)}) copy-start(bf16[256,512]{1,0:T(8,128)(2,1)} %param.40) | copy-start | bytes 786436
Sparse Core Ops, SparseCore 0:
  11.7 39.7 all-gather.4
  54.1 70.9 all-gather.6

commit v10 on v8

--- a/solution.py
+++ b/solution.py
@@ -776,7 +776,7 @@
             self.down_acc[where] = part[where] + self.from_above[where]
             self.down(owner, step, self.down_acc).start()
 
-    def run(self, pause=None, beside=None):
+    def run(self, pauses=(), beside=None):
         turns, lag = self.count * self.steps, self.steps
 
         def staggered(first, second):
@@ -798,9 +798,13 @@
                 return carry
 
             lax.fori_loop(0, lag, begin, 0)
-            if pause is not None:
-                pause()
-            lax.fori_loop(lag, turns, both, 0)
+            low = lag
+            for share, action in pauses:
+                high = lag + int((turns - lag) * share)
+                lax.fori_loop(low, high, both, 0)
+                action()
+                low = high
+            lax.fori_loop(low, turns, both, 0)
             lax.fori_loop(turns - lag, turns, end, 0)
 
         @pl.when(self.place < self.count // 2)
@@ -866,7 +870,7 @@
     load.start()
     convert.begin()
     greet(scatter.place, count)
-    scatter.run(None, convert.step)
+    scatter.run((), convert.step)
     stage.store(1, 2, 3, 4)
     scatter.settle()
     load.wait()
@@ -1862,17 +1866,19 @@
         load.wait()
     tiny.advance(1)
 
-    def between():
+    def early():
         sums.advance(1)
         tiny.advance(2)
 
-    scatter.run(between)
-    for phase in range(3, tiny.bits + 1):
-        tiny.advance(phase)
-    for spread, share in zip(small, shares[-2:]):
-        spread.held[spread.place] = share[...]
-        spread.start()
-    for phase in range(2, sums.bits + 1):
+    def middle():
+        for phase in range(3, tiny.bits + 1):
+            tiny.advance(phase)
+        for spread, share in zip(small, shares[-2:]):
+            spread.held[spread.place] = share[...]
+            spread.start()
+
+    scatter.run([(0.0, early), (0.35, middle), (0.75, lambda: sums.advance(2))])
+    for phase in range(3, sums.bits + 1):
         sums.advance(phase)
     scatter.settle()
 
@@ -1989,51 +1995,64 @@
         first.start()
     lane = lax.broadcasted_iota(jnp.int32, (8, 128), 1)
     corner = jnp.logical_and(lane == 0, lax.broadcasted_iota(jnp.int32, (8, 128), 0) == 0)
-    loads, copies = [], []
-    pieces = []
+    loads, copies, pieces = [], [], []
     for kind, gradient in enumerate(gradients):
-        slots = range(gradient.shape[0]) if len(gradient.shape) == 3 else [None]
-        pieces += [(kind, slot) for slot in slots]
-
-    def at(ref, slot):
-        return ref if slot is None else ref.at[slot]
-
-    for kind, slot in pieces:
+        if len(gradient.shape) == 2:
+            pieces.append((kind, None))
+        else:
+            slots = gradient.shape[0]
+            size = 2 if slots % 2 == 0 else slots
+            pieces += [(kind, pl.ds(low, size)) for low in range(0, slots, size)]
+
+    def at(ref, group):
+        return ref if group is None else ref.at[group]
+
+    def load(order):
+        kind, group = pieces[order]
         for index in range(3 * kind, 3 * kind + 3):
-            source, target = at(states[index], slot), at(held[index], slot)
+            source, target = at(states[index], group), at(held[index], group)
             loads.append(pltpu.make_async_copy(source, target, in_sems.at[len(loads)]))
             loads[-1].start()
-    for load in firsts:
-        load.wait()
+
+    ahead = 4
+    for order in range(ahead):
+        load(order)
+    for copy in firsts:
+        copy.wait()
     scale = jnp.sum(jnp.where(corner, clip_scale(stats[...]), 0.0))
+    for order, (kind, group) in enumerate(pieces):
+        if order + ahead < len(pieces):
+            load(order + ahead)
+        for copy in loads[3 * order : 3 * order + 3]:
+            copy.wait()
+        for slot in [None] if group is None else range(group.start, group.start + group.size):
+            refs = [
+                ref if slot is None else ref.at[slot] for ref in held[3 * kind : 3 * kind + 3]
+            ]
+            source = gradients[kind] if slot is None else gradients[kind].at[slot]
+            rows, width = refs[0].shape
+            step = math.gcd(rows, max(8, 8192 // width)) if rows % 8 == 0 else rows
+
+            def one(index, carry, refs=refs, source=source, step=step, width=width):
+                where = pl.ds(pl.multiple_of(index * step, step), step)
+                state = [ref[where] for ref in refs]
+                for ref, result in zip(refs, adam_update(*state, source[where, :width], scale)):
+                    ref[where] = result
+                return carry
+
+            lax.fori_loop(0, rows // step, one, 0)
+        for index in range(3 * kind, 3 * kind + 3):
+            source, target = at(held[index], group), at(outs[index], group)
+            copies.append(pltpu.make_async_copy(source, target, out_sems.at[len(copies)]))
+            copies[-1].start()
     pixel_loads = [
         pltpu.make_async_copy(states[index], held[index], in_sems.at[len(loads) + index - 18])
         for index in range(18, 21)
     ]
-    for load in pixel_loads:
-        load.start()
-    for order, (kind, slot) in enumerate(pieces):
-        for load in loads[3 * order : 3 * order + 3]:
-            load.wait()
-        refs = [at(held[index], slot) for index in range(3 * kind, 3 * kind + 3)]
-        source = at(gradients[kind], slot)
-        rows, width = refs[0].shape
-        step = math.gcd(rows, max(8, 8192 // width)) if rows % 8 == 0 else rows
-
-        def one(index, carry, refs=refs, source=source, step=step, width=width):
-            where = pl.ds(pl.multiple_of(index * step, step), step)
-            state = [ref[where] for ref in refs]
-            for ref, result in zip(refs, adam_update(*state, source[where, :width], scale)):
-                ref[where] = result
-            return carry
-
-        lax.fori_loop(0, rows // step, one, 0)
-        for index in range(3 * kind, 3 * kind + 3):
-            source, target = at(held[index], slot), at(outs[index], slot)
-            copies.append(pltpu.make_async_copy(source, target, out_sems.at[len(copies)]))
-            copies[-1].start()
-    for load in pixel_loads:
-        load.wait()
+    for copy in pixel_loads:
+        copy.start()
+    for copy in pixel_loads:
+        copy.wait()
     pixels, rest = held[18:21], gradients[-1]
     for slot in range(2):
         gradient = rest[16 * (slot + 1) : 16 * (slot + 1) + PIX, : pixels[0].shape[2]]

time: 537 us -> 538 us (level)
  no operation moved by 1% of the time
where the time goes in v10:
time: 538 us; the launch traced here: 530 us
  Pallas kernels  487 us (91%)
  local copies, waits for them, and re-layouts  16.7 us (3%)
  between operations  14.8 us (3%)
  waiting for transfers between devices  9.43 us (2%)
    pallas_call x8, Pallas kernels, staged(): pl.pallas_call(partial(staged_kernel, body, counts), out_shape=[pltpu.VME...  390 us
    pallas_call x1, Pallas kernels, read_backward(): pl.pallas_call(read_backward_kernel, grid=(images,), out_shape=[pltpu.HBM...  25.8 us
    pallas_call x1, Pallas kernels, read_forward(): pl.pallas_call(read_forward_kernel, grid=(images,), out_shape=[pltpu.VMEM...  19.2 us
    pallas_call x1, Pallas kernels, feed_backward(): pl.pallas_call(feed_backward_kernel, grid=(4,), out_shape=[pltpu.VMEM((ro...  12.8 us
    pallas_call x1, Pallas kernels, self_backward(): pl.pallas_call(self_backward_kernel, grid=(images,), out_shape=[pltpu.VME...  12.7 us
  transfers between devices with their start and end apart: 2, of which 1 were waited for; matrix products, arithmetic and copies ran while one was open for 2% of the time, Pallas kernels for 26%

profile of v10, /device:TPU:0, one launch (start us, length us, event | category | flops | bytes accessed | tf_op | source)
XLA Modules:
  0.0 530.2 jit_solution(3731565009574957277)
XLA Ops:
  7.2 0.0 copy-start
  7.2 0.0 all-gather.5.cloned.1.call-start
  7.3 0.9 copy-done
  8.2 0.1 dynamic-slice_bitcast_fusion
  8.3 0.1 copy.62
  8.4 1.0 slice.38
  9.4 1.3 fusion.1
  10.8 0.8 maximum_convert_fusion
  11.5 0.0 all-gather.5.cloned.1.call-update
  11.6 0.0 all-gather.7.cloned.1.call-start
  11.6 0.6 slice.49.gain_ref
  12.2 0.6 slice.53.refs_9_
  12.9 0.6 copy.71
  13.5 0.6 copy.70
  14.1 0.6 copy.69
  14.7 0.6 copy.68
  15.3 0.8 convert_element_type.37.refs_1_
  16.1 2.0 copy.66.keep_ref
  18.1 0.1 convert_reduce_fusion
  18.2 0.6 multiply_reduce_fusion
  18.9 0.6 dynamic_slice.34
  19.5 0.6 pad.12.refs_7_
  20.1 0.2 fusion.2
  20.3 0.7 pad.11.noisy_ref
  21.1 0.6 constant_dynamic-slice_fusion.refs_5_
  21.7 0.6 slice_bitcast_fusion.pixels_ref
  22.3 0.7 pad_dynamic-slice_fusion
  22.9 19.2 %shard_map.488 = (f32[512,1024]{1,0:T(8,128)S(1)}, bf16[4,2,1024,256]{3,2,1,0:T(8,128)(2,1)}, bf16[4,128,256]{2,1,0:T(8,128)(2,1)}, bf16[512,256]{1,0:T(8,128)(2...) custom-call(f32[4,16,1024]{2,1,0:T(8,128)} %pad.11.noisy_ref, ...), custom_call_target="tpu_custom_call" | custom-call | flops 10000000000 | bytes 30000000 | tf_op jit(solution)/shard_map/pallas_call | solution.py:1123
  42.1 9.4 %all-gather.5.cloned.1.call-done = f32[1536,256]{1,0:T(8,128)} async-done(((f32[384,256]{1,0:T(8,128)}), f32[1536,256]{1,0:T(8,128)}) %all-gather.5.cloned.1.call-update) | async-done | bytes 1572880 | tf_op jit(solution)/shard_map/all_gather | solution.py:2271
  51.5 1.2 broadcast_in_dim.12.refs_0_
  52.7 1.2 broadcast_in_dim.13.refs_2_
  54.0 0.0 all-gather.7.cloned.1.call-update
  54.0 52.6 %shard_map.489 = (f32[512,1024]{1,0:T(8,128)S(1)}, f32[8,128]{1,0:T(8,128)}, f32[512,1024]{1,0:T(8,128)}) custom-call(f32[512,1024]{1,0:T(8,128)S(1)} %get-tuple-element.132.refs_0_, f32[128,1024]{1,0:T(8,128)} %convert_element_type.37.refs_1_, f32[8,128]{1,0:T(8,128)} %broadcast_in_dim.13.refs_2_), custom_call_target="tpu_custom_call" | custom-call | flops 2097152 | bytes 192500000 | tf_op jit(solution)/shard_map/pallas_call | solution.py:444
  106.6 7.3 %shard_map.490 = (f32[512,1024]{1,0:T(8,128)S(1)}, bf16[4,3,128,256]{3,2,1,0:T(8,128)(2,1)}, bf16[4,128,256]{2,1,0:T(8,128)(2,1)}, f32[4,1,512]{2,1,0:T(1,128)}, bf16[512,1024]{1,0:T(8,128)(2,1)}) custom-call(f32[512,1024]{1,0:T(8,128)S(1)} %get-tuple-element.136.latent_ref, f32[1,1024]{1,0:T(1,128)} %bitcast.107, bf16[10,1024,256]{2,1,0:T(8,128)(2,1)} %bitcast.73, ...), custom_call_target="tpu_custom_call" | custom-call | flops 3000000000 | bytes 12000000 | tf_op jit(solution)/shard_map/pallas_call | solution.py:1348
  113.9 51.8 %shard_map.491 = (f32[512,1024]{1,0:T(8,128)S(1)}, f32[512,1024]{1,0:T(8,128)}) custom-call(f32[512,1024]{1,0:T(8,128)S(1)} %get-tuple-element.138.refs_0_, f32[512,1024]{1,0:T(8,128)} %get-tuple-element.139.refs_1_.latent_ref), custom_call_target="tpu_custom_call" | custom-call | flops 2097152 | bytes 192500000 | tf_op jit(solution)/shard_map/pallas_call | solution.py:444
  165.7 9.1 %shard_map.492 = (f32[512,1024]{1,0:T(8,128)S(1)}, bf16[4,512,256]{2,1,0:T(8,128)(2,1)}, f32[4,512,256]{2,1,0:T(8,128)}, bf16[512,1024]{1,0:T(8,128)(2,1)}) custom-call(f32[512,1024]{1,0:T(8,128)S(1)} %get-tuple-element.140.latent_ref, f32[1,1024]{1,0:T(1,128)} %bitcast.114, bf16[10,1024,256]{2,1,0:T(8,128)(2,1)} %bitcast.76, ...), custom_call_target="tpu_custom_call" | custom-call | flops 4000000000 | bytes 14000000 | tf_op jit(solution)/shard_map/pallas_call | solution.py:1498
  174.9 0.0 all-gather.7.cloned.1.call-done.refs_2_
  174.9 26.7 %shard_map.493 = (f32[128,1024]{1,0:T(8,128)}, bf16[1024,1024]{1,0:T(8,128)(2,1)}, bf16[1024,1024]{1,0:T(8,128)(2,1)}, bf16[512,1024]{1,0:T(8,128)(2,1)}, bf16[512,1024]{1,0:T(8,128)(2,1)}) custom-call(f32[512,1024]{1,0:T(8,128)S(1)} %get-tuple-element.142.refs_0_, f32[512,1024]{1,0:T(8,128)} %get-tuple-element.143.refs_1_.latent_ref, ...), custom_call_target="tpu_custom_call" | custom-call | flops 1048576 | bytes 115500000 | tf_op jit(solution)/shard_map/pallas_call | solution.py:444
  201.6 26.3 %shard_map.494 = (f32[128,1024]{1,0:T(8,128)}, f32[1024,1024]{1,0:T(8,128)}, f32[1024,1024]{1,0:T(8,128)}, f32[512,1024]{1,0:T(8,128)}, f32[512,1024]{1,0:T(8,12...) custom-call(f32[8,128]{1,0:T(8,128)} %broadcast_in_dim.12.refs_0_, ...), custom_call_target="tpu_custom_call" | custom-call | flops 15000000512 | bytes 94500000 | tf_op jit(solution)/shard_map/pallas_call | solution.py:444
  227.9 61.2 %shard_map.495 = (f32[512,1024]{1,0:T(8,128)S(1)}, f32[128,1024]{1,0:T(8,128)}, f32[64,1024]{1,0:T(8,128)}, f32[512,1024]{1,0:T(8,128)}) custom-call(f32[128,1024]{1,0:T(8,128)} %get-tuple-element.156.refs_0_, f32[8,128,1024]{2,1,0:T(8,128)} %bitcast.84, f32[8,64,1024]{2,1,0:T(8,128)} %bitcast.85), custom_call_target="tpu_custom_call" | custom-call | flops 131072 | bytes 133000000 | tf_op jit(solution)/shard_map/pallas_call | solution.py:444
  289.1 12.8 %shard_map.496 = (f32[512,1024]{1,0:T(8,128)S(1)}, f32[2,1024,256]{2,1,0:T(8,128)}, f32[2,1024,256]{2,1,0:T(8,128)}, f32[4,1024,256]{2,1,0:T(8,128)}, f32[1,1024]{1,0:T(1,128)}) custom-call(f32[512,1024]{1,0:T(8,128)S(1)} %get-tuple-element.159.grad_ref, f32[512,1024]{1,0:T(8,128)} %get-tuple-element.143.refs_1_.latent_ref, f32[1,1024]{1,0:T(1,128)} %bitcast.115, ...), custom_call_target="tpu_custom_call" | custom-call | flops 8999999488 | bytes 26000000 | tf_op jit(solution)/shard_map/pallas_call | solution.py:1580
  301.9 58.7 %shard_map.497 = (f32[512,1024]{1,0:T(8,128)S(1)}, f32[128,1024]{1,0:T(8,128)}, f32[64,1024]{1,0:T(8,128)}, f32[2,128,256]{2,1,0:T(8,128)}, f32[512,1024]{1,0:T(8,128)}) custom-call(f32[512,1024]{1,0:T(8,128)S(1)} %get-tuple-element.163.refs_0_, f32[512,1024]{1,0:T(8,128)} %get-tuple-element.164.refs_1_, f32[8,128,1024]{2,1,0:T(8,128)} %bitcast.82, ...), custom_call_target="tpu_custom_call" | custom-call | flops 2097152 | bytes 192500000 | tf_op jit(solution)/shard_map/pallas_call | solution.py:444
  360.6 12.7 %shard_map.498 = (f32[512,1024]{1,0:T(8,128)S(1)}, f32[2,1024,256]{2,1,0:T(8,128)}, f32[2,1024,256]{2,1,0:T(8,128)}, f32[1,1024]{1,0:T(1,128)}) custom-call(f32[512,1024]{1,0:T(8,128)S(1)} %get-tuple-element.168.grad_ref, f32[512,1024]{1,0:T(8,128)} %get-tuple-element.139.refs_1_.latent_ref, f32[1,1024]{1,0:T(1,128)} %bitcast.108, ...), custom_call_target="tpu_custom_call" | custom-call | flops 6000000000 | bytes 16000000 | tf_op jit(solution)/shard_map/pallas_call | solution.py:1441
  373.3 59.6 %shard_map.499 = (f32[512,1024]{1,0:T(8,128)S(1)}, f32[2,128,256]{2,1,0:T(8,128)}, f32[4,128,256]{2,1,0:T(8,128)}, f32[2,128,256]{2,1,0:T(8,128)}, f32[512,1024]{1,0:T(8,128)}) custom-call(f32[512,1024]{1,0:T(8,128)S(1)} %get-tuple-element.181.refs_0_, f32[512,1024]{1,0:T(8,128)} %get-tuple-element.182.refs_1_, f32[2,8,128,256]{3,2,1,0:T(8,128)} %bitcast.89, ...), custom_call_target="tpu_custom_call" | custom-call | flops 2097152 | bytes 192500000 | tf_op jit(solution)/shard_map/pallas_call | solution.py:444
  432.9 25.8 %shard_map.500 = (f32[2,1024,256]{2,1,0:T(8,128)}, f32[2,512,256]{2,1,0:T(8,128)}, f32[128,1024]{1,0:T(8,128)}, f32[1,1024]{1,0:T(1,128)}, f32[1,512]{1,0:T(1,128)}, /*index=5*/f32[16,512]{1,0:T(8,128)}) custom-call(f32[4,16,1024]{2,1,0:T(8,128)} %pad.11.noisy_ref, bf16[128,1024]{1,0:T(8,128)(2,1)} %latents_ref.3, f32[1,1024]{1,0:T(1,128)} %bitcast.113, ...), custom_call_target="tpu_custom_call" | custom-call | flops 20000000000 | bytes 30000000 | tf_op jit(solution)/shard_map/pallas_call | solution.py:1277
  458.7 53.3 %shard_map.501 = (f32[10,128,256]{2,1,0:T(8,128)}, f32[3,64,256]{2,1,0:T(8,128)}, f32[6,256,128]{2,1,0:T(8,128)}, f32[64,256]{1,0:T(8,128)}, f32[128,128]{1,0:T(...) custom-call(f32[2,8,128,256]{3,2,1,0:T(8,128)} %bitcast.86, f32[2,8,128,256]{3,2,1,0:T(8,128)} %bitcast.87, ...), custom_call_target="tpu_custom_call" | custom-call | flops 10000000 | bytes 175000000 | tf_op jit(solution)/shard_map/pallas_call | solution.py:444
  512.0 1.3 fusion.4
  513.3 9.6 %shard_map.502 = (f32[10,128,256]{2,1,0:T(8,128)}, f32[10,128,256]{2,1,0:T(8,128)}, f32[10,128,256]{2,1,0:T(8,128)}, f32[3,64,256]{2,1,0:T(8,128)}, f32[3,64,256...) custom-call(f32[8,128]{1,0:T(8,128)} %get-tuple-element.209.refs_0_,, ...), custom_call_target="tpu_custom_call" | custom-call | flops 20000000 | bytes 14000000 | tf_op jit(solution)/shard_map/pallas_call | solution.py:2073
  (23 shorter events, 0.1 us)
Async XLA Ops:
  7.2 1.0 copy-start
  7.2 44.3 %all-gather.5.cloned.1.call-start = ((), (), s32[]{:S(2)}) async-start(), calls=%async_computation | async-start | bytes 1966080 | tf_op jit(solution)/shard_map/all_gather | solution.py:2271
  7.3 4.3 copy-start.6
  8.2 4.6 copy-start.7
  8.4 6.9 %copy-start.2 = (bf16[128,1024]{1,0:T(8,128)(2,1)S(1)}, bf16[128,1024]{1,0:T(8,128)(2,1)}, u32[]{:S(2)}) copy-start(bf16[128,1024]{1,0:T(8,128)(2,1)} %latents_ref.3) | copy-start | bytes 786436
  9.4 6.7 %copy-start.5 = (s32[4,1024]{1,0:T(4,128)S(1)}, s32[4,1024]{1,0:T(4,128)}, u32[]{:S(2)}) copy-start(s32[4,1024]{1,0:T(4,128)} %param.36) | copy-start | bytes 49156
  10.7 7.5 %copy-start.8 = (s32[4]{0:T(128)S(1)}, s32[4]{0:T(128)}, u32[]{:S(2)}) copy-start(s32[4]{0:T(128)} %param.35) | copy-start | bytes 52
  10.7 9.4 %copy-start.3 = (f32[4,12,1024]{2,0,1:T(4,128)S(1)}, f32[4,12,1024]{2,0,1:T(4,128)}, u32[]{:S(2)}) copy-start(f32[4,12,1024]{2,0,1:T(4,128)} %param.34) | copy-start | bytes 589828
  10.7 9.4 %copy-start.4 = (f32[4,12,1024]{2,0,1:T(4,128)S(1)}, f32[4,12,1024]{2,0,1:T(4,128)}, u32[]{:S(2)}) copy-start(f32[4,12,1024]{2,0,1:T(4,128)} %param.33) | copy-start | bytes 589828
  11.6 163.3 %all-gather.7.cloned.1.call-start = ((), (), s32[]{:S(2)}) async-start(), calls=%async_computation.1 | async-start | bytes 14155776 | tf_op jit(solution)/shard_map/all_gather | solution.py:2328
  513.3 9.6 %copy-start.1 = (bf16[256,512]{1,0:T(8,128)(2,1)S(1)}, bf16[256,512]{1,0:T(8,128)(2,1)}, u32[]{:S(2)}) copy-start(bf16[256,512]{1,0:T(8,128)(2,1)} %param.40) | copy-start | bytes 786436
Sparse Core Ops, SparseCore 0:
  11.7 39.7 all-gather.4
  54.1 70.9 all-gather.6

commit v11 on v8

--- a/solution.py
+++ b/solution.py
@@ -684,7 +684,7 @@
     count, count_dp = lax.axis_size("mp"), lax.axis_size("dp")
     rows, width = part.shape
     buffer = pltpu.VMEM((rows, width), jnp.float32)
-    sems = pltpu.SemaphoreType.DMA((CHUNKS,))
+    sems = pltpu.SemaphoreType.DMA((CHUNKS if items else CHUNKS // 2,))
     inputs = [base, *items]
     outs = list(shares)
     scratch = [buffer] * 3 + [sems] * 4

time: 537 us -> 519 us (0.966)
  Pallas kernels: 486 us -> 468 us
    pallas_call x8, Pallas kernels: 390 us -> 372 us  [staged(): pl.pallas_call(partial(staged_kernel, body, counts), out_shape=[pltpu.VME...]
  transfers between devices with their start and end apart: 2 -> 2, of which waited for: 1 -> 1; matrix products, arithmetic and copies ran while one was open for 2% -> 2% of each run, Pallas kernels for 26% -> 24%
where the time goes in v11:
time: 519 us; the launch traced here: 512 us
  Pallas kernels  468 us (90%)
  local copies, waits for them, and re-layouts  16.7 us (3%)
  between operations  14.8 us (3%)
  waiting for transfers between devices  9.43 us (2%)
    pallas_call x8, Pallas kernels, staged(): pl.pallas_call(partial(staged_kernel, body, counts), out_shape=[pltpu.VME...  372 us
    pallas_call x1, Pallas kernels, read_backward(): pl.pallas_call(read_backward_kernel, grid=(images,), out_shape=[pltpu.HBM...  25.8 us
    pallas_call x1, Pallas kernels, read_forward(): pl.pallas_call(read_forward_kernel, grid=(images,), out_shape=[pltpu.VMEM...  19.2 us
    pallas_call x1, Pallas kernels, feed_backward(): pl.pallas_call(feed_backward_kernel, grid=(4,), out_shape=[pltpu.VMEM((ro...  12.8 us
    pallas_call x1, Pallas kernels, self_backward(): pl.pallas_call(self_backward_kernel, grid=(images,), out_shape=[pltpu.VME...  12.7 us
  transfers between devices with their start and end apart: 2, of which 1 were waited for; matrix products, arithmetic and copies ran while one was open for 2% of the time, Pallas kernels for 24%

profile of v11, /device:TPU:0, one launch (start us, length us, event | category | flops | bytes accessed | tf_op | source)
XLA Modules:
  0.0 511.7 jit_solution(9406535338171275974)
XLA Ops:
  7.2 0.0 copy-start
  7.2 0.0 all-gather.5.cloned.1.call-start
  7.3 0.9 copy-done
  8.2 0.1 dynamic-slice_bitcast_fusion
  8.3 0.1 copy.62
  8.4 1.0 slice.38
  9.4 1.3 fusion.1
  10.8 0.8 maximum_convert_fusion
  11.5 0.0 all-gather.5.cloned.1.call-update
  11.6 0.0 all-gather.7.cloned.1.call-start
  11.6 0.6 slice.49.gain_ref
  12.2 0.6 slice.53.refs_9_
  12.9 0.6 copy.71
  13.5 0.6 copy.70
  14.1 0.6 copy.69
  14.7 0.6 copy.68
  15.3 0.8 convert_element_type.37.refs_1_
  16.1 2.0 copy.66.keep_ref
  18.1 0.1 convert_reduce_fusion
  18.2 0.6 multiply_reduce_fusion
  18.9 0.6 dynamic_slice.34
  19.5 0.6 pad.12.refs_7_
  20.1 0.2 fusion.2
  20.3 0.7 pad.11.noisy_ref
  21.1 0.6 constant_dynamic-slice_fusion.refs_5_
  21.7 0.6 slice_bitcast_fusion.pixels_ref
  22.3 0.7 pad_dynamic-slice_fusion
  22.9 19.2 %shard_map.488 = (f32[512,1024]{1,0:T(8,128)S(1)}, bf16[4,2,1024,256]{3,2,1,0:T(8,128)(2,1)}, bf16[4,128,256]{2,1,0:T(8,128)(2,1)}, bf16[512,256]{1,0:T(8,128)(2...) custom-call(f32[4,16,1024]{2,1,0:T(8,128)} %pad.11.noisy_ref, ...), custom_call_target="tpu_custom_call" | custom-call | flops 10000000000 | bytes 30000000 | tf_op jit(solution)/shard_map/pallas_call | solution.py:1119
  42.1 9.4 %all-gather.5.cloned.1.call-done = f32[1536,256]{1,0:T(8,128)} async-done(((f32[384,256]{1,0:T(8,128)}), f32[1536,256]{1,0:T(8,128)}) %all-gather.5.cloned.1.call-update) | async-done | bytes 1572880 | tf_op jit(solution)/shard_map/all_gather | solution.py:2252
  51.5 1.2 broadcast_in_dim.12.refs_0_
  52.7 1.2 broadcast_in_dim.13.refs_2_
  54.0 0.0 all-gather.7.cloned.1.call-update
  54.0 44.6 %shard_map.489 = (f32[512,1024]{1,0:T(8,128)S(1)}, f32[8,128]{1,0:T(8,128)}, f32[512,1024]{1,0:T(8,128)}) custom-call(f32[512,1024]{1,0:T(8,128)S(1)} %get-tuple-element.132.refs_0_, f32[128,1024]{1,0:T(8,128)} %convert_element_type.37.refs_1_, f32[8,128]{1,0:T(8,128)} %broadcast_in_dim.13.refs_2_), custom_call_target="tpu_custom_call" | custom-call | flops 2097152 | bytes 192500000 | tf_op jit(solution)/shard_map/pallas_call | solution.py:444
  98.7 7.1 %shard_map.490 = (f32[512,1024]{1,0:T(8,128)S(1)}, bf16[4,3,128,256]{3,2,1,0:T(8,128)(2,1)}, bf16[4,128,256]{2,1,0:T(8,128)(2,1)}, f32[4,1,512]{2,1,0:T(1,128)}, bf16[512,1024]{1,0:T(8,128)(2,1)}) custom-call(f32[512,1024]{1,0:T(8,128)S(1)} %get-tuple-element.136.latent_ref, f32[1,1024]{1,0:T(1,128)} %bitcast.107, bf16[10,1024,256]{2,1,0:T(8,128)(2,1)} %bitcast.73, ...), custom_call_target="tpu_custom_call" | custom-call | flops 3000000000 | bytes 12000000 | tf_op jit(solution)/shard_map/pallas_call | solution.py:1344
  105.8 42.8 %shard_map.491 = (f32[512,1024]{1,0:T(8,128)S(1)}, f32[512,1024]{1,0:T(8,128)}) custom-call(f32[512,1024]{1,0:T(8,128)S(1)} %get-tuple-element.138.refs_0_, f32[512,1024]{1,0:T(8,128)} %get-tuple-element.139.refs_1_.latent_ref), custom_call_target="tpu_custom_call" | custom-call | flops 2097152 | bytes 192500000 | tf_op jit(solution)/shard_map/pallas_call | solution.py:444
  148.6 9.1 %shard_map.492 = (f32[512,1024]{1,0:T(8,128)S(1)}, bf16[4,512,256]{2,1,0:T(8,128)(2,1)}, f32[4,512,256]{2,1,0:T(8,128)}, bf16[512,1024]{1,0:T(8,128)(2,1)}) custom-call(f32[512,1024]{1,0:T(8,128)S(1)} %get-tuple-element.140.latent_ref, f32[1,1024]{1,0:T(1,128)} %bitcast.114, bf16[10,1024,256]{2,1,0:T(8,128)(2,1)} %bitcast.76, ...), custom_call_target="tpu_custom_call" | custom-call | flops 4000000000 | bytes 14000000 | tf_op jit(solution)/shard_map/pallas_call | solution.py:1494
  157.7 0.0 all-gather.7.cloned.1.call-done.refs_2_
  157.8 21.4 %shard_map.493 = (f32[128,1024]{1,0:T(8,128)}, bf16[1024,1024]{1,0:T(8,128)(2,1)}, bf16[1024,1024]{1,0:T(8,128)(2,1)}, bf16[512,1024]{1,0:T(8,128)(2,1)}, bf16[512,1024]{1,0:T(8,128)(2,1)}) custom-call(f32[512,1024]{1,0:T(8,128)S(1)} %get-tuple-element.142.refs_0_, f32[512,1024]{1,0:T(8,128)} %get-tuple-element.143.refs_1_.latent_ref, ...), custom_call_target="tpu_custom_call" | custom-call | flops 1048576 | bytes 115500000 | tf_op jit(solution)/shard_map/pallas_call | solution.py:444
  179.1 26.3 %shard_map.494 = (f32[128,1024]{1,0:T(8,128)}, f32[1024,1024]{1,0:T(8,128)}, f32[1024,1024]{1,0:T(8,128)}, f32[512,1024]{1,0:T(8,128)}, f32[512,1024]{1,0:T(8,12...) custom-call(f32[8,128]{1,0:T(8,128)} %broadcast_in_dim.12.refs_0_, ...), custom_call_target="tpu_custom_call" | custom-call | flops 15000000512 | bytes 94500000 | tf_op jit(solution)/shard_map/pallas_call | solution.py:444
  205.5 65.6 %shard_map.495 = (f32[512,1024]{1,0:T(8,128)S(1)}, f32[128,1024]{1,0:T(8,128)}, f32[64,1024]{1,0:T(8,128)}, f32[512,1024]{1,0:T(8,128)}) custom-call(f32[128,1024]{1,0:T(8,128)} %get-tuple-element.156.refs_0_, f32[8,128,1024]{2,1,0:T(8,128)} %bitcast.84, f32[8,64,1024]{2,1,0:T(8,128)} %bitcast.85), custom_call_target="tpu_custom_call" | custom-call | flops 131072 | bytes 133000000 | tf_op jit(solution)/shard_map/pallas_call | solution.py:444
  271.1 12.8 %shard_map.496 = (f32[512,1024]{1,0:T(8,128)S(1)}, f32[2,1024,256]{2,1,0:T(8,128)}, f32[2,1024,256]{2,1,0:T(8,128)}, f32[4,1024,256]{2,1,0:T(8,128)}, f32[1,1024]{1,0:T(1,128)}) custom-call(f32[512,1024]{1,0:T(8,128)S(1)} %get-tuple-element.159.grad_ref, f32[512,1024]{1,0:T(8,128)} %get-tuple-element.143.refs_1_.latent_ref, f32[1,1024]{1,0:T(1,128)} %bitcast.115, ...), custom_call_target="tpu_custom_call" | custom-call | flops 8999999488 | bytes 26000000 | tf_op jit(solution)/shard_map/pallas_call | solution.py:1576
  283.9 59.1 %shard_map.497 = (f32[512,1024]{1,0:T(8,128)S(1)}, f32[128,1024]{1,0:T(8,128)}, f32[64,1024]{1,0:T(8,128)}, f32[2,128,256]{2,1,0:T(8,128)}, f32[512,1024]{1,0:T(8,128)}) custom-call(f32[512,1024]{1,0:T(8,128)S(1)} %get-tuple-element.163.refs_0_, f32[512,1024]{1,0:T(8,128)} %get-tuple-element.164.refs_1_, f32[8,128,1024]{2,1,0:T(8,128)} %bitcast.82, ...), custom_call_target="tpu_custom_call" | custom-call | flops 2097152 | bytes 192500000 | tf_op jit(solution)/shard_map/pallas_call | solution.py:444
  343.0 12.7 %shard_map.498 = (f32[512,1024]{1,0:T(8,128)S(1)}, f32[2,1024,256]{2,1,0:T(8,128)}, f32[2,1024,256]{2,1,0:T(8,128)}, f32[1,1024]{1,0:T(1,128)}) custom-call(f32[512,1024]{1,0:T(8,128)S(1)} %get-tuple-element.168.grad_ref, f32[512,1024]{1,0:T(8,128)} %get-tuple-element.139.refs_1_.latent_ref, f32[1,1024]{1,0:T(1,128)} %bitcast.108, ...), custom_call_target="tpu_custom_call" | custom-call | flops 6000000000 | bytes 16000000 | tf_op jit(solution)/shard_map/pallas_call | solution.py:1437
  355.6 59.8 %shard_map.499 = (f32[512,1024]{1,0:T(8,128)S(1)}, f32[2,128,256]{2,1,0:T(8,128)}, f32[4,128,256]{2,1,0:T(8,128)}, f32[2,128,256]{2,1,0:T(8,128)}, f32[512,1024]{1,0:T(8,128)}) custom-call(f32[512,1024]{1,0:T(8,128)S(1)} %get-tuple-element.181.refs_0_, f32[512,1024]{1,0:T(8,128)} %get-tuple-element.182.refs_1_, f32[2,8,128,256]{3,2,1,0:T(8,128)} %bitcast.89, ...), custom_call_target="tpu_custom_call" | custom-call | flops 2097152 | bytes 192500000 | tf_op jit(solution)/shard_map/pallas_call | solution.py:444
  415.4 25.8 %shard_map.500 = (f32[2,1024,256]{2,1,0:T(8,128)}, f32[2,512,256]{2,1,0:T(8,128)}, f32[128,1024]{1,0:T(8,128)}, f32[1,1024]{1,0:T(1,128)}, f32[1,512]{1,0:T(1,128)}, /*index=5*/f32[16,512]{1,0:T(8,128)}) custom-call(f32[4,16,1024]{2,1,0:T(8,128)} %pad.11.noisy_ref, bf16[128,1024]{1,0:T(8,128)(2,1)} %latents_ref.3, f32[1,1024]{1,0:T(1,128)} %bitcast.113, ...), custom_call_target="tpu_custom_call" | custom-call | flops 20000000000 | bytes 30000000 | tf_op jit(solution)/shard_map/pallas_call | solution.py:1273
  441.2 52.8 %shard_map.501 = (f32[10,128,256]{2,1,0:T(8,128)}, f32[3,64,256]{2,1,0:T(8,128)}, f32[6,256,128]{2,1,0:T(8,128)}, f32[64,256]{1,0:T(8,128)}, f32[128,128]{1,0:T(...) custom-call(f32[2,8,128,256]{3,2,1,0:T(8,128)} %bitcast.86, f32[2,8,128,256]{3,2,1,0:T(8,128)} %bitcast.87, ...), custom_call_target="tpu_custom_call" | custom-call | flops 10000000 | bytes 175000000 | tf_op jit(solution)/shard_map/pallas_call | solution.py:444
  494.0 1.3 fusion.4
  495.4 9.0 %shard_map.502 = (f32[10,128,256]{2,1,0:T(8,128)}, f32[10,128,256]{2,1,0:T(8,128)}, f32[10,128,256]{2,1,0:T(8,128)}, f32[3,64,256]{2,1,0:T(8,128)}, f32[3,64,256...) custom-call(f32[8,128]{1,0:T(8,128)} %get-tuple-element.209.refs_0_,, ...), custom_call_target="tpu_custom_call" | custom-call | flops 20000000 | bytes 14000000 | tf_op jit(solution)/shard_map/pallas_call | solution.py:2054
  (23 shorter events, 0.1 us)
Async XLA Ops:
  7.2 1.0 copy-start
  7.2 44.3 %all-gather.5.cloned.1.call-start = ((), (), s32[]{:S(2)}) async-start(), calls=%async_computation | async-start | bytes 1966080 | tf_op jit(solution)/shard_map/all_gather | solution.py:2252
  7.3 4.3 copy-start.6
  8.2 4.6 copy-start.7
  8.4 6.9 %copy-start.2 = (bf16[128,1024]{1,0:T(8,128)(2,1)S(1)}, bf16[128,1024]{1,0:T(8,128)(2,1)}, u32[]{:S(2)}) copy-start(bf16[128,1024]{1,0:T(8,128)(2,1)} %latents_ref.3) | copy-start | bytes 786436
  9.4 6.7 %copy-start.5 = (s32[4,1024]{1,0:T(4,128)S(1)}, s32[4,1024]{1,0:T(4,128)}, u32[]{:S(2)}) copy-start(s32[4,1024]{1,0:T(4,128)} %param.36) | copy-start | bytes 49156
  10.7 7.5 %copy-start.8 = (s32[4]{0:T(128)S(1)}, s32[4]{0:T(128)}, u32[]{:S(2)}) copy-start(s32[4]{0:T(128)} %param.35) | copy-start | bytes 52
  10.7 9.4 %copy-start.3 = (f32[4,12,1024]{2,0,1:T(4,128)S(1)}, f32[4,12,1024]{2,0,1:T(4,128)}, u32[]{:S(2)}) copy-start(f32[4,12,1024]{2,0,1:T(4,128)} %param.34) | copy-start | bytes 589828
  10.7 9.4 %copy-start.4 = (f32[4,12,1024]{2,0,1:T(4,128)S(1)}, f32[4,12,1024]{2,0,1:T(4,128)}, u32[]{:S(2)}) copy-start(f32[4,12,1024]{2,0,1:T(4,128)} %param.33) | copy-start | bytes 589828
  11.6 146.2 %all-gather.7.cloned.1.call-start = ((), (), s32[]{:S(2)}) async-start(), calls=%async_computation.1 | async-start | bytes 14155776 | tf_op jit(solution)/shard_map/all_gather | solution.py:2309
  495.4 9.0 %copy-start.1 = (bf16[256,512]{1,0:T(8,128)(2,1)S(1)}, bf16[256,512]{1,0:T(8,128)(2,1)}, u32[]{:S(2)}) copy-start(bf16[256,512]{1,0:T(8,128)(2,1)} %param.40) | copy-start | bytes 786436
Sparse Core Ops, SparseCore 0:
  11.7 39.7 all-gather.4
  54.1 70.9 all-gather.6
